TPU v7x, 128 devices: a whole 4x4x4 slice. The times are simulated.
128 devices in a mesh: member: 8 (over y, z_hi), lat: 16 (over z_lo, x, core).
Axes of the slice: x: 4, y: 4, z: 4 (z_hi: 2, z_lo: 2; z = z_hi * 2 + z_lo), core: 2. Of those that a mesh axis runs over, the one named last changes fastest.
Arguments:
- initial_states: float32 [8, 32, 80, 128], P('member', 'lat'), may hold values from -6 to 6
- targets: float32 [2, 32, 80, 128], P(None, 'lat'), may hold values from -6 to 6
- lat_weight: float32 [32], P('lat'), may hold values from 0.3 to 3
- weight_in: float32 [256, 720], replicated, may hold values from -0.21875 to 0.21875
- weight_out: float32 [80, 2304], replicated, may hold values from -0.125 to 0.125
- hidden_bias: float32 [256], replicated, may hold values from -4 to 4
Outputs:
- state_grad: float32 [8, 32, 80, 128], P('member', 'lat')
- loss: float32 [], replicated
All inputs are finite; a program needn't handle non-finite values.
Results may differ from a plain program's by a relative error of at most 0.00023.
Values sent between devices are 32-bit elements; how exact they have to be, the bound alone decides.
No kernel may reach another device: no remote copies, remote signals or barrier semaphores. Data moves between devices by JAX's collectives and lax.ppermute only.
A program may use at most 64 MiB of HBM per device.

v0:
```python
import functools

import jax
import jax.numpy as jnp
from jax import lax
from jax.sharding import Mesh
from jax.sharding import PartitionSpec as P

MEMBER = ("member_0", "member_1")
LAT = ("lat_0", "lat_1", "lat_2")
MEMBER_LAT = ("member_0", "member_1", "lat_0", "lat_1", "lat_2")


smooth_width = 0.1


def padded_2(cells, sides, width):
    for axis, dim in sides:
        count = lax.axis_size(axis)
        ends = count - 1
        head = lax.slice_in_dim(cells, 0, width, axis=dim)
        tail = lax.slice_in_dim(cells, cells.shape[dim] - width, cells.shape[dim], axis=dim)
        cells = jnp.concatenate(
            [
                lax.ppermute(tail, axis, [(i, (i + 1) % count) for i in range(ends)]),
                cells,
                lax.ppermute(head, axis, [((i + 1) % count, i) for i in range(ends)]),
            ],
            axis=dim,
        )
    return cells


def from_everyone(value, axis):
    copies = jnp.broadcast_to(value, (lax.axis_size(axis), *value.shape))
    return lax.all_to_all(copies, axis, split_axis=0, concat_axis=0, tiled=True)


def laid_out(pieces, dim):
    shape = list(pieces.shape[1:])
    shape[dim] *= pieces.shape[0]
    return jnp.moveaxis(pieces, 0, dim).reshape(shape)


def gather_directly(value, axis, dim):
    pieces = from_everyone(value, axis)
    return laid_out(pieces, dim)


def over_axes(value, axes):
    return functools.reduce(lax.psum, axes, value)


def smooth(spread):
    return jnp.sqrt(spread * spread + smooth_width * smooth_width)


def convolve(matrix, padded, height, flipped):
    members = padded.shape[0]
    channels = padded.shape[2]
    columns = padded.shape[3]
    outer = matrix.shape[0]
    widened = jnp.pad(padded, ((0, 0), (0, 0), (0, 0), (1, 1)))
    blocks = matrix.reshape(outer, 9, channels)
    result = jnp.zeros((members, height, outer, columns), jnp.float32)
    for across in range(3):
        for along in range(3):
            top_row = 2 - across if flipped else across
            left_col = 2 - along if flipped else along
            window = widened[:, top_row : top_row + height, :, left_col : left_col + columns]
            result = result + jnp.einsum(
                "oc,mrcl->mrol",
                blocks[:, 3 * across + along],
                window,
                precision=lax.Precision.HIGHEST,
            )
    return result


def flip_taps(matrix, inner):
    outer = matrix.shape[0]
    return matrix.reshape(outer, 9, inner).transpose(2, 1, 0).reshape(inner, 9 * outer)


def pair_terms(mine, others, initial):

    def add_member(position, accum):
        summed, slopes = accum
        other = lax.dynamic_index_in_dim(others, position, 0, keepdims=True)
        spread = mine - other
        width = smooth(spread)
        return (summed + width, slopes + spread / width)

    return lax.fori_loop(0, others.shape[0], add_member, initial)


def on_device(initial_states, targets, lat_weight, weight_in, weight_out, hidden_bias):
    field = initial_states
    members = field.shape[0] * lax.axis_size(MEMBER)
    slab_rows = field.shape[1]
    vars_count = field.shape[2]
    columns = field.shape[3]
    hidden_count = weight_in.shape[0]
    weight_out_back = flip_taps(weight_out, hidden_count)
    weight_in_back = flip_taps(weight_in, vars_count)
    first_row = lax.axis_index(LAT) * slab_rows - 1
    row_index = first_row + jnp.arange(slab_rows + 2, dtype=jnp.int32)
    inside = ((row_index >= 0) & (row_index < slab_rows * lax.axis_size(LAT))).astype(jnp.float32)[
        None, :, None, None
    ]
    weights = lat_weight[None, :, None, None]
    biases = hidden_bias[None, None, :, None]
    saved = []
    loss_grads = []
    partial_value = jnp.zeros((), jnp.float32)
    for rollout in range(targets.shape[0]):
        padded = padded_2(field, ((LAT, 1),), 2)
        before = convolve(weight_in, padded, slab_rows + 2, False) + biases
        hidden = jax.nn.gelu(before) * inside
        field = field + convolve(weight_out, hidden, slab_rows, False)
        saved.append(before)
        blanks = jnp.zeros_like(field)
        current = field

        def fold_pairs(accum, shards, offset, current=current):
            return pair_terms(current, shards, accum)

        summed, slopes = fold_pairs(
            (blanks, blanks), gather_directly(field, MEMBER, 0), jnp.int32(0)
        )
        pair_total = jnp.sum(weights * summed)
        error = field - targets[rollout][None]
        direct = smooth(error)
        partial_value = (
            partial_value + jnp.sum(weights * direct) - pair_total / (2.0 * (members - 1))
        )
        loss_grads.append(weights * (error / direct - slopes / (members - 1)))
    overall = over_axes(partial_value, MEMBER_LAT)
    loss = overall / (
        members * targets.shape[0] * slab_rows * lax.axis_size(LAT) * vars_count * columns
    )
    gradient = jnp.zeros_like(field)
    for rollout in range(targets.shape[0] - 1, -1, -1):
        gradient = gradient + loss_grads[rollout]
        before = saved[rollout]
        padded = padded_2(gradient, ((LAT, 1),), 2)
        hidden_grad = convolve(weight_out_back, padded, slab_rows + 2, True) * inside
        unused, pullback = jax.vjp(jax.nn.gelu, before)
        before_grad = pullback(hidden_grad)[0]
        gradient = gradient + convolve(weight_in_back, before_grad, slab_rows, True)
    return (gradient, loss)


def solution(mesh):
    torus = Mesh(
        mesh.devices.reshape(4, 2, 2, 4, 2), ("member_0", "member_1", "lat_0", "lat_1", "lat_2")
    )
    placed = (P(MEMBER, LAT, None, None), P(None, LAT, None, None), P(LAT), P(), P(), P())
    return jax.shard_map(
        on_device,
        mesh=torus,
        in_specs=placed,
        out_specs=(P(MEMBER, LAT, None, None), P()),
        check_vma=False,
    )
```

profile of v0, /device:TPU:0, one launch (start us, length us, event | category | flops | bytes accessed | tf_op | source)
XLA Modules:
  0.0 147.8 jit_solution(2369679199676485740)
XLA Ops:
  0.6 1.3 collective-permute-start
  1.9 1.3 collective-permute-start.1
  3.3 1.3 copy.176
  4.6 0.9 copy-done.1
  5.4 1.7 %collective-permute-done.1 = f32[1,2,80,128]{3,2,1,0:T(8,128)S(1)} collective-permute-done((f32[1,2,80,128]{3,2,1,0:T(8,128)}, f32[1,2,80,128]{3,2,1,0:T(8,128)S(1)}, u32[]{:S(2)}, u32[]{:S(2)}) %collective-permute-start.1) | collective-permute-done | bytes 81952 | tf_op jit(solution)/shard_map/ppermute | solution.py:27
  7.9 0.8 fusion.102
  9.4 0.8 convolution_add_fusion.26
  11.0 0.8 convolution_add_fusion.24
  12.5 0.8 convolution_add_fusion.22
  13.3 1.6 %multiply_multiply_fusion.5 = (f32[1,4,256,128]{2,3,1,0:T(8,128)S(1)}, f32[1,4,256,128]{2,3,1,0:T(8,128)}) fusion(f32[4]{0:T(128)S(1)} %and_convert_fusion, f32[256]{0:T(256)S(1)} %copy-done.5, f32[4,128,256]{2,1,0:T(8,128)S(1)} %fusion.102, f32[4,128,256]{2,1,0:T(8,128)S(1)} %convolution_add_fusion.22, f32[256,9,80]{0,2,1:T(8,128)S(1)} %bitcast.531, ...), kind=kOutput, calls=%fused_computation.135 | convolution fusion | flops 127442944 | bytes 2344448 | tf_op jit(solution)/shard_map/oc,mrcl->mrol/dot_general | solution.py:71
  18.3 5.0 %collective-permute-start.2 = (f32[1,2,80,128]{3,2,1,0:T(8,128)S(1)}, f32[1,2,80,128]{3,2,1,0:T(8,128)S(1)}, u32[]{:S(2)}, u32[]{:S(2)}) collective-permute-start(f32[1,2,80,128]{3,2,1,0:T(8,128)S(1)} %fusion.21), channel_id=1, source_target_pairs={{0,1},{1,2},{2,3},{3,4},{4,5},{5,6},{6,7},{7,8},{8,9},{9,10},{10,1... | collective-permute-start | bytes 245768 | tf_op jit(solution)/shard_map/ppermute | solution.py:25
  23.3 1.3 collective-permute-start.3
  24.7 0.9 broadcast_in_dim.10
  25.6 7.8 %all-to-all-start.1 = ((f32[8,1,2,80,128]{4,3,2,1,0:T(8,128)}), f32[8,1,2,80,128]{4,3,2,1,0:T(8,128)S(1)}, u32[]{:S(2)}, u32[]{:S(2)}) async-start(f32[8,1,2,80,128]{4,3,2,1,0:T(8,128)} %broadcast_in_dim.10), calls=%async_computation.1 | async-start | bytes 1310720 | tf_op jit(solution)/shard_map/all_to_all | solution.py:36
  34.2 0.8 fusion.116
  35.6 0.8 convolution_add_fusion.19
  36.4 0.8 convolution_add_fusion.18
  37.9 0.8 convolution_add_fusion.16
  38.7 0.8 convolution_add_fusion.15
  39.5 1.6 %multiply_multiply_fusion.4 = (f32[1,4,256,128]{2,3,1,0:T(8,128)S(1)}, f32[1,4,256,128]{2,3,1,0:T(8,128)}) fusion(f32[4]{0:T(128)S(1)} %and_convert_fusion, f32[256]{0:T(256)S(1)} %copy-done.5, f32[4,128,256]{2,1,0:T(8,128)S(1)} %fusion.116, f32[4,128,256]{2,1,0:T(8,128)S(1)} %convolution_add_fusion.15, f32[256,9,80]{0,2,1:T(8,128)S(1)} %bitcast.540, ...), kind=kOutput, calls=%fused_computation.134 | convolution fusion | flops 127442944 | bytes 2344448 | tf_op jit(solution)/shard_map/oc,mrcl->mrol/dot_general | solution.py:71
  44.6 1.9 %all-to-all-done.1 = f32[8,1,2,80,128]{4,3,2,1,0:T(8,128)S(1)} async-done(((f32[8,1,2,80,128]{4,3,2,1,0:T(8,128)}), f32[8,1,2,80,128]{4,3,2,1,0:T(8,128)S(1)}, u32[]{:S(2)}, u32[]{:S(2)}) %all-to-all-start.1) | async-done | bytes 655392 | tf_op jit(solution)/shard_map/all_to_all | solution.py:36
  46.4 0.9 broadcast_in_dim.4
  47.3 5.3 %all-to-all-start = ((f32[8,1,2,80,128]{4,3,2,1,0:T(8,128)}), f32[8,1,2,80,128]{4,3,2,1,0:T(8,128)S(1)}, u32[]{:S(2)}, u32[]{:S(2)}) async-start(f32[8,1,2,80,128]{4,3,2,1,0:T(8,128)} %broadcast_in_dim.4), calls=%async_computation | async-start | bytes 1310720 | tf_op jit(solution)/shard_map/all_to_all | solution.py:36
  53.4 11.8 %all-to-all-done = f32[8,1,2,80,128]{4,3,2,1,0:T(8,128)S(1)} async-done(((f32[8,1,2,80,128]{4,3,2,1,0:T(8,128)}), f32[8,1,2,80,128]{4,3,2,1,0:T(8,128)S(1)}, u32[]{:S(2)}, u32[]{:S(2)}) %all-to-all-start) | async-done | bytes 655392 | tf_op jit(solution)/shard_map/all_to_all | solution.py:36
  66.6 0.8 multiply_reduce_fusion
  67.4 1.4 collective-permute-start.4
  68.8 1.5 %collective-permute-start.5 = (f32[1,2,80,128]{3,2,1,0:T(8,128)S(1)}, f32[1,2,80,128]{3,2,1,0:T(8,128)S(1)}, u32[]{:S(2)}, u32[]{:S(2)}) collective-permute-start(f32[1,2,80,128]{3,2,1,0:T(8,128)S(1)} %get-tuple-element.264), channel_id=1, source_target_pairs={{1,0},{2,1},{3,2},{4,3},{5,4},{6,5},{7,6},{8,7},{9,8},{10,9},{11,1... | collective-permute-start | bytes 245768 | tf_op jit(solution)/shard_map/ppermute | solution.py:27
  70.3 3.6 %collective-permute-done.5 = f32[1,2,80,128]{3,2,1,0:T(8,128)S(1)} collective-permute-done((f32[1,2,80,128]{3,2,1,0:T(8,128)S(1)}, f32[1,2,80,128]{3,2,1,0:T(8,128)S(1)}, u32[]{:S(2)}, u32[]{:S(2)}) %collective-permute-start.5) | collective-permute-done | bytes 81952 | tf_op jit(solution)/shard_map/ppermute | solution.py:27
  74.7 0.8 fusion.130
  76.2 0.8 convolution_add_fusion.12
  77.0 0.8 convolution_add_fusion.11
  78.4 0.8 convolution_add_fusion.9
  79.2 0.8 convolution_add_fusion.8
  80.3 0.9 fusion.37
  84.7 5.0 %collective-permute-start.6 = (f32[1,2,80,128]{3,2,1,0:T(8,128)S(1)}, f32[1,2,80,128]{3,2,1,0:T(8,128)S(1)}, u32[]{:S(2)}, u32[]{:S(2)}) collective-permute-start(f32[1,2,80,128]{3,2,1,0:T(8,128)S(1)} %fusion.24), channel_id=1, source_target_pairs={{0,1},{1,2},{2,3},{3,4},{4,5},{5,6},{6,7},{7,8},{8,9},{9,10},{10,1... | collective-permute-start | bytes 245768 | tf_op jit(solution)/shard_map/ppermute | solution.py:25
  89.7 1.3 collective-permute-start.7
  93.5 9.7 %psum.35 = f32[]{:T(128)} all-reduce(f32[]{:T(128)S(6)} %sub.49), channel_id=1, replica_groups=mesh['member_0'=4,'member_1'=2,'lat_0'=2,'lat_1'=4,'lat_2'=2] {'member_0'}, use_global_device_ids=true, to_apply=%region_8.9 | all-reduce | flops 1 | bytes 8 | tf_op jit(solution)/shard_map/psum | solution.py:51
  103.2 7.1 %psum.36 = f32[]{:T(128)} all-reduce(f32[]{:T(128)} %psum.35), channel_id=1, replica_groups=mesh['member_0'=4,'member_1'=2,'lat_0'=2,'lat_1'=4,'lat_2'=2] {'member_1'}, use_global_device_ids=true, to_apply=%region_9.10 | all-reduce | flops 1 | bytes 8 | tf_op jit(solution)/shard_map/psum | solution.py:51
  110.2 11.7 %psum.37 = f32[]{:T(128)} all-reduce(f32[]{:T(128)} %psum.36), channel_id=1, replica_groups=mesh['member_0'=4,'member_1'=2,'lat_0'=2,'lat_1'=4,'lat_2'=2] {'lat_0'}, use_global_device_ids=true, to_apply=%region_10.11 | all-reduce | flops 1 | bytes 8 | tf_op jit(solution)/shard_map/psum | solution.py:51
  122.0 9.3 %psum.38 = f32[]{:T(128)} all-reduce(f32[]{:T(128)} %psum.37), channel_id=1, replica_groups=mesh['member_0'=4,'member_1'=2,'lat_0'=2,'lat_1'=4,'lat_2'=2] {'lat_1'}, use_global_device_ids=true, to_apply=%region_11.12 | all-reduce | flops 1 | bytes 8 | tf_op jit(solution)/shard_map/psum | solution.py:51
  131.3 3.3 %psum.39 = f32[]{:T(128)} all-reduce(f32[]{:T(128)} %psum.38), channel_id=1, replica_groups=mesh['member_0'=4,'member_1'=2,'lat_0'=2,'lat_1'=4,'lat_2'=2] {'lat_2'}, use_global_device_ids=true, to_apply=%region_12.13 | all-reduce | flops 1 | bytes 8 | tf_op jit(solution)/shard_map/psum | solution.py:51
  136.1 0.8 fusion.144
  137.6 0.8 convolution_add_fusion.5
  138.4 0.8 convolution_add_fusion.4
  139.8 0.8 convolution_add_fusion.2
  140.6 0.8 convolution_add_fusion.1
  141.7 0.9 fusion.31
  145.7 1.0 fusion.25
  (96 shorter events, 26.1 us)
Async XLA Ops:
  0.6 3.9 %collective-permute-start = (f32[1,2,80,128]{3,2,1,0:T(8,128)}, f32[1,2,80,128]{3,2,1,0:T(8,128)S(1)}, u32[]{:S(2)}, u32[]{:S(2)}) collective-permute-start(f32[1,2,80,128]{3,2,1,0:T(8,128)} %param.10), channel_id=1, source_target_pairs={{0,1},{1,2},{2,3},{3,4},{4,5},{5,6},{6,7},{7,8},{8,9},{9,10},{10,1... | collective-permute-start | bytes 245768 | tf_op jit(solution)/shard_map/ppermute | solution.py:25
  1.9 5.2 %collective-permute-start.1 = (f32[1,2,80,128]{3,2,1,0:T(8,128)}, f32[1,2,80,128]{3,2,1,0:T(8,128)S(1)}, u32[]{:S(2)}, u32[]{:S(2)}) collective-permute-start(f32[1,2,80,128]{3,2,1,0:T(8,128)} %param.10), channel_id=1, source_target_pairs={{1,0},{2,1},{3,2},{4,3},{5,4},{6,5},{7,6},{8,7},{9,8},{10,9},{11,1... | collective-permute-start | bytes 245768 | tf_op jit(solution)/shard_map/ppermute | solution.py:27
  3.2 3.9 %copy-start = (f32[256,720]{0,1:T(8,128)S(1)}, f32[256,720]{0,1:T(8,128)}, u32[]{:S(2)}) copy-start(f32[256,720]{0,1:T(8,128)} %param.13) | copy-start | bytes 2211844
  4.5 0.9 copy-start.1
  12.4 0.8 copy-start.5
  18.3 15.0 %collective-permute-start.2 = (f32[1,2,80,128]{3,2,1,0:T(8,128)S(1)}, f32[1,2,80,128]{3,2,1,0:T(8,128)S(1)}, u32[]{:S(2)}, u32[]{:S(2)}) collective-permute-start(f32[1,2,80,128]{3,2,1,0:T(8,128)S(1)} %fusion.21), channel_id=1, source_target_pairs={{0,1},{1,2},{2,3},{3,4},{4,5},{5,6},{6,7},{7,8},{8,9},{9,10},{10,1... | collective-permute-start | bytes 245768 | tf_op jit(solution)/shard_map/ppermute | solution.py:25
  23.3 10.0 %collective-permute-start.3 = (f32[1,2,80,128]{3,2,1,0:T(8,128)S(1)}, f32[1,2,80,128]{3,2,1,0:T(8,128)S(1)}, u32[]{:S(2)}, u32[]{:S(2)}) collective-permute-start(f32[1,2,80,128]{3,2,1,0:T(8,128)S(1)} %fusion.21), channel_id=1, source_target_pairs={{1,0},{2,1},{3,2},{4,3},{5,4},{6,5},{7,6},{8,7},{9,8},{10,9},{11,1... | collective-permute-start | bytes 245768 | tf_op jit(solution)/shard_map/ppermute | solution.py:27
  25.6 20.9 %all-to-all-start.1 = ((f32[8,1,2,80,128]{4,3,2,1,0:T(8,128)}), f32[8,1,2,80,128]{4,3,2,1,0:T(8,128)S(1)}, u32[]{:S(2)}, u32[]{:S(2)}) async-start(f32[8,1,2,80,128]{4,3,2,1,0:T(8,128)} %broadcast_in_dim.10), calls=%async_computation.1 | async-start | bytes 1310720 | tf_op jit(solution)/shard_map/all_to_all | solution.py:36
  47.3 17.9 %all-to-all-start = ((f32[8,1,2,80,128]{4,3,2,1,0:T(8,128)}), f32[8,1,2,80,128]{4,3,2,1,0:T(8,128)S(1)}, u32[]{:S(2)}, u32[]{:S(2)}) async-start(f32[8,1,2,80,128]{4,3,2,1,0:T(8,128)} %broadcast_in_dim.4), calls=%async_computation | async-start | bytes 1310720 | tf_op jit(solution)/shard_map/all_to_all | solution.py:36
  65.2 0.9 copy-start.4
  65.9 0.7 copy-start.6
  67.4 2.9 %collective-permute-start.4 = (f32[1,2,80,128]{3,2,1,0:T(8,128)S(1)}, f32[1,2,80,128]{3,2,1,0:T(8,128)S(1)}, u32[]{:S(2)}, u32[]{:S(2)}) collective-permute-start(f32[1,2,80,128]{3,2,1,0:T(8,128)S(1)} %get-tuple-element.264), channel_id=1, source_target_pairs={{0,1},{1,2},{2,3},{3,4},{4,5},{5,6},{6,7},{7,8},{8,9},{9,10},{10,1... | collective-permute-start | bytes 245768 | tf_op jit(solution)/shard_map/ppermute | solution.py:25
  68.8 5.1 %collective-permute-start.5 = (f32[1,2,80,128]{3,2,1,0:T(8,128)S(1)}, f32[1,2,80,128]{3,2,1,0:T(8,128)S(1)}, u32[]{:S(2)}, u32[]{:S(2)}) collective-permute-start(f32[1,2,80,128]{3,2,1,0:T(8,128)S(1)} %get-tuple-element.264), channel_id=1, source_target_pairs={{1,0},{2,1},{3,2},{4,3},{5,4},{6,5},{7,6},{8,7},{9,8},{10,9},{11,1... | collective-permute-start | bytes 245768 | tf_op jit(solution)/shard_map/ppermute | solution.py:27
  79.2 1.0 copy-start.3
  84.7 50.6 %collective-permute-start.6 = (f32[1,2,80,128]{3,2,1,0:T(8,128)S(1)}, f32[1,2,80,128]{3,2,1,0:T(8,128)S(1)}, u32[]{:S(2)}, u32[]{:S(2)}) collective-permute-start(f32[1,2,80,128]{3,2,1,0:T(8,128)S(1)} %fusion.24), channel_id=1, source_target_pairs={{0,1},{1,2},{2,3},{3,4},{4,5},{5,6},{6,7},{7,8},{8,9},{9,10},{10,1... | collective-permute-start | bytes 245768 | tf_op jit(solution)/shard_map/ppermute | solution.py:25
  89.7 45.6 %collective-permute-start.7 = (f32[1,2,80,128]{3,2,1,0:T(8,128)S(1)}, f32[1,2,80,128]{3,2,1,0:T(8,128)S(1)}, u32[]{:S(2)}, u32[]{:S(2)}) collective-permute-start(f32[1,2,80,128]{3,2,1,0:T(8,128)S(1)} %fusion.24), channel_id=1, source_target_pairs={{1,0},{2,1},{3,2},{4,3},{5,4},{6,5},{7,6},{8,7},{9,8},{10,9},{11,1... | collective-permute-start | bytes 245768 | tf_op jit(solution)/shard_map/ppermute | solution.py:27
  140.6 1.0 copy-start.2
where the time goes:
time: 150 us; the launch traced here: 148 us
  matrix products  43.5 us (29%)
  blocking collectives  41.1 us (27%)
  starting transfers between devices  31.1 us (21%)
  waiting for transfers between devices  19 us (13%)
  between operations  5.73 us (4%)
  local copies, waits for them, and re-layouts  5.02 us (3%)
  other arithmetic  1.98 us (1%)
    dot_general x72, matrix products, convolve(): jnp.einsum('oc,mrcl->mrol', blocks[:, 3 * across + along], window, precis...  43.5 us
    psum x5, blocking collectives, over_axes(): return functools.reduce(lax.psum, axes, value)  41.1 us
    all_to_all x2, waiting for transfers between devices, from_everyone(): return lax.all_to_all(copies, axis, split_axis=0, concat_axis=0, tiled=True)  13.7 us
    all_to_all x2, starting transfers between devices, from_everyone(): return lax.all_to_all(copies, axis, split_axis=0, concat_axis=0, tiled=True)  13.1 us
    ppermute x4, starting transfers between devices, padded_2(): lax.ppermute(tail, axis, [(i, (i + 1) % count) for i in range(ends)])  12.7 us
    ppermute x4, starting transfers between devices, padded_2(): lax.ppermute(head, axis, [((i + 1) % count, i) for i in range(ends)])  5.39 us
    ppermute x4, waiting for transfers between devices, padded_2(): lax.ppermute(head, axis, [((i + 1) % count, i) for i in range(ends)])  5.27 us
  transfers between devices with their start and end apart: 10, of which 4 were waited for; matrix products, arithmetic and copies ran while one was open for 9% of the time, Pallas kernels for 0%

commit v1 on v0

v1 whole, which is shorter than its diff:
```python
import functools

import jax
import jax.numpy as jnp
from jax import lax
from jax.experimental import pallas as pl
from jax.experimental.pallas import tpu as pltpu
from jax.sharding import Mesh
from jax.sharding import PartitionSpec as P

MEMBER = ("member_0", "member_1")
LAT = ("lat_0", "lat_1", "lat_2")

smooth_width = 0.1
gelu_scale = 0.7978845608028654
gelu_cubic = 0.044715

f32 = jnp.float32
bf16 = jnp.bfloat16
params = pltpu.CompilerParams(vmem_limit_bytes=40 * 1024 * 1024)


def split(value):
    high = value.astype(bf16)
    return high, (value - high.astype(f32)).astype(bf16)


def product(left, right):
    dot = functools.partial(jnp.dot, preferred_element_type=f32)
    return dot(left[0], right[0]) + (dot(left[0], right[1]) + dot(left[1], right[0]))


def from_left(row):
    lane = lax.broadcasted_iota(jnp.int32, row.shape, 1)
    return jnp.where(lane == 0, 0.0, pltpu.roll(row, 1, 1))


def from_right(row):
    lane = lax.broadcasted_iota(jnp.int32, row.shape, 1)
    return jnp.where(lane == row.shape[1] - 1, 0.0, pltpu.roll(row, row.shape[1] - 1, 1))


def put_twice(refs, index, height, part, values):
    width = values[0].shape[1]
    size = values[0].shape[0]
    for ref, value in zip(refs, values):
        base = index * height + part * size
        if base + size <= ref.shape[0]:
            ref[base : base + size, :width] = value
        if index:
            ref[base - height : base - height + size, width:] = value


def put_windows(refs, index, row):
    height = 3 * row.shape[0]
    for part, shifted in enumerate((from_left(row), row, from_right(row))):
        put_twice(refs, index, height, part, split(shifted))


def read(refs, start, size):
    return tuple(ref[start : start + size, :] for ref in refs)


def to_channels(weights, windows, pair, channels):
    return product(weights, read(windows, pair * 3 * channels, 9 * channels))


def from_channels(weights, hidden, pair, channels, outer):
    mixed = product(weights, read(hidden, pair * channels, 3 * channels))
    width = mixed.shape[1] // 2
    rows = []
    for half in range(2):
        part = mixed[:, half * width : (half + 1) * width]
        rows.append(
            from_left(part[:outer])
            + part[outer : 2 * outer]
            + from_right(part[2 * outer :])
        )
    return rows


def gelu(x):
    return 0.5 * x * (1.0 + jnp.tanh(gelu_scale * (x + gelu_cubic * x * x * x)))


def gelu_slope(x):
    t = jnp.tanh(gelu_scale * (x + gelu_cubic * x * x * x))
    inner = gelu_scale * (1.0 + 3.0 * gelu_cubic * x * x)
    return 0.5 * (1.0 + t) + 0.5 * x * (1.0 - t * t) * inner


def prepare_kernel(win_ref, wout_ref, in_hi, in_lo, out_hi, out_lo, outb_hi, outb_lo, inb_hi, inb_lo, stack):
    outer, width = wout_ref.shape
    hidden = width // 9
    inner = win_ref.shape[1] // 9
    high, low = split(win_ref[...])
    in_hi[...] = high
    in_lo[...] = low
    for a in range(3):
        for b in range(3):
            tap = 3 * a + b
            block = wout_ref[:, tap * hidden : (tap + 1) * hidden]
            high, low = split(block)
            out_hi[b * outer : (b + 1) * outer, a * hidden : (a + 1) * hidden] = high
            out_lo[b * outer : (b + 1) * outer, a * hidden : (a + 1) * hidden] = low
            stack[(8 - tap) * outer : (9 - tap) * outer, :] = block
    high, low = split(stack[...].T)
    outb_hi[...] = high
    outb_lo[...] = low
    turned = win_ref[...].T
    for a in range(3):
        for b in range(3):
            tap = 3 * a + b
            high, low = split(turned[tap * inner : (tap + 1) * inner, :])
            j, k = 2 - a, 2 - b
            inb_hi[k * inner : (k + 1) * inner, j * hidden : (j + 1) * hidden] = high
            inb_lo[k * inner : (k + 1) * inner, j * hidden : (j + 1) * hidden] = low


def prepare(weight_in, weight_out):
    hidden, taps_in = weight_in.shape
    outer = weight_out.shape[0]
    inner = taps_in // 9
    shapes = [(hidden, 9 * inner)] * 2 + [(3 * outer, 3 * hidden)] * 2
    shapes = shapes + [(hidden, 9 * outer)] * 2 + [(3 * inner, 3 * hidden)] * 2
    return pl.pallas_call(
        prepare_kernel,
        out_shape=[jax.ShapeDtypeStruct(shape, bf16) for shape in shapes],
        scratch_shapes=[pltpu.VMEM((9 * outer, hidden), f32)],
        compiler_params=params,
        name="prepare",
    )(weight_in, weight_out)


def inside(at_ref, row, rows):
    index = at_ref[0] + row
    return (index >= 0) & (index < rows)


def forward_kernel(rows, at_ref, own_ref, near_ref, across_ref, far_across_ref, far_near_ref, bias_ref,
                   in_hi, in_lo, out_hi, out_lo, before_ref, fields_ref, wide_hi, wide_lo, hid_hi, hid_lo):
    channels, width = own_ref.shape[1:]
    hidden = in_hi.shape[0]
    even = at_ref[1] == 0
    wide = (wide_hi, wide_lo)
    hid = (hid_hi, hid_lo)
    w_in = (in_hi[...], in_lo[...])
    w_out = (out_hi[...], out_lo[...])
    bias = bias_ref[...]

    def initial(index):
        slab, row = index // 2, index % 2
        if slab == 2:
            return own_ref[row]
        first, second = {
            0: (far_across_ref, far_near_ref),
            1: (across_ref, near_ref),
            3: (near_ref, across_ref),
            4: (far_near_ref, far_across_ref),
        }[slab]
        return jnp.where(even, first[row], second[row])

    def advance(field, first, count, keep, step):
        for index in range(count):
            put_windows(wide, index, field(index))
        for pair in range(0, count - 2, 2):
            before = to_channels(w_in, wide, pair, channels) + bias
            if pair in keep:
                before_ref[step, keep.index(pair)] = before
            active = gelu(before)
            for half in range(2):
                row = active[:, half * width : (half + 1) * width]
                row = jnp.where(inside(at_ref, first + 1 + pair + half, rows), row, 0.0)
                put_twice(hid, pair + half, hidden, 0, split(row))
        result = []
        for pair in range(0, count - 4, 2):
            moved = from_channels(w_out, hid, pair, hidden, channels)
            for half in range(2):
                row = field(pair + 2 + half) + moved[half]
                result.append(jnp.where(inside(at_ref, first + 2 + pair + half, rows), row, 0.0))
        return result

    first = advance(initial, -4, 10, (2, 4), 0)
    for half in range(2):
        fields_ref[half * channels : (half + 1) * channels, :] = first[2 + half]
    second = advance(lambda index: first[index], -2, 6, (0, 2), 1)
    for half in range(2):
        fields_ref[(2 + half) * channels : (3 + half) * channels, :] = second[half]


def forward(rows, at, own, near, across, far_across, far_near, bias, w_in, w_out):
    channels, width = own.shape[1:]
    hidden = w_in[0].shape[0]
    vmem = pl.BlockSpec(memory_space=pltpu.VMEM)
    return pl.pallas_call(
        functools.partial(forward_kernel, rows),
        in_specs=[pl.BlockSpec(memory_space=pltpu.SMEM)] + [vmem] * 10,
        out_shape=[
            jax.ShapeDtypeStruct((2, 2, hidden, 2 * width), f32),
            jax.ShapeDtypeStruct((4 * channels, width), f32),
        ],
        scratch_shapes=[pltpu.VMEM((30 * channels, 2 * width), bf16)] * 2
        + [pltpu.VMEM((8 * hidden, 2 * width), bf16)] * 2,
        compiler_params=params,
        name="forward",
    )(at, own, near, across, far_across, far_near, bias, *w_in, *w_out)


def crps_kernel(at_ref, weight_ref, fields_ref, targets_ref, out_ref):
    members, height, width = fields_ref.shape
    mine = at_ref[2]
    weight = jnp.where((lax.rem(mine, 4) // 2) == 0, weight_ref[0], weight_ref[1])
    softness = smooth_width * smooth_width
    loss = jnp.zeros((8, width), f32)
    for tile in range(0, height, 8):
        values = [fields_ref[m, tile : tile + 8, :] for m in range(members)]
        truth = targets_ref[mine, tile : tile + 8, :]
        direct = jnp.zeros((8, width), f32)
        pairs = jnp.full((8, width), members * smooth_width, f32)
        slopes = [jnp.zeros((8, width), f32) for m in range(members)]
        grads = []
        for m in range(members):
            error = values[m] - truth
            spread = jnp.sqrt(error * error + softness)
            direct = direct + spread
            grads.append(error / spread)
            for other in range(m + 1, members):
                gap = values[m] - values[other]
                spread = jnp.sqrt(gap * gap + softness)
                pairs = pairs + 2.0 * spread
                slope = gap / spread
                slopes[m] = slopes[m] + slope
                slopes[other] = slopes[other] - slope
        loss = loss + weight * (direct - pairs / (2.0 * (members - 1)))
        for m in range(members):
            out_ref[m, tile : tile + 8, :] = weight * (grads[m] - slopes[m] / (members - 1))
    for m in range(members):
        out_ref[m, height : height + 8, :] = loss


def crps(at, weights, fields, targets):
    members, height, width = fields.shape
    smem = pl.BlockSpec(memory_space=pltpu.SMEM)
    vmem = pl.BlockSpec(memory_space=pltpu.VMEM)
    return pl.pallas_call(
        crps_kernel,
        in_specs=[smem, smem, vmem, vmem],
        out_shape=jax.ShapeDtypeStruct((members, height + 8, width), f32),
        compiler_params=params,
        name="crps",
    )(at, weights, fields, targets)


def backward_kernel(rows, step, at_ref, own_ref, near_ref, across_ref, before_ref, outb_hi, outb_lo, inb_hi, inb_lo,
                    *rest):
    added = rest[:-5]
    out_ref, wide_hi, wide_lo, hid_hi, hid_lo = rest[-5:]
    channels, width = own_ref.shape[1:]
    hidden = outb_hi.shape[0]
    even = at_ref[1] == 0
    wide = (wide_hi, wide_lo)
    hid = (hid_hi, hid_lo)
    w_out = (outb_hi[...], outb_lo[...])
    w_in = (inb_hi[...], inb_lo[...])
    for row in range(2):
        put_windows(wide, row, jnp.where(even, across_ref[row], near_ref[row]))
        put_windows(wide, 2 + row, own_ref[row])
    for row in range(2):
        put_windows(wide, 4 + row, jnp.where(even, near_ref[row], across_ref[row]))
    for pair in (0, 2):
        grads = to_channels(w_out, wide, pair, channels) * gelu_slope(before_ref[step, pair // 2])
        for half in range(2):
            row = grads[:, half * width : (half + 1) * width]
            row = jnp.where(inside(at_ref, pair + half - 1, rows), row, 0.0)
            put_twice(hid, pair + half, hidden, 0, split(row))
    moved = from_channels(w_in, hid, 0, hidden, channels)
    for row in range(2):
        total = own_ref[row] + moved[row]
        for extra in added:
            total = total + extra[row]
        out_ref[row] = total


def backward(rows, step, at, own, near, across, before, w_out, w_in, *added):
    channels, width = own.shape[1:]
    hidden = w_out[0].shape[0]
    vmem = pl.BlockSpec(memory_space=pltpu.VMEM)
    return pl.pallas_call(
        functools.partial(backward_kernel, rows, step),
        in_specs=[pl.BlockSpec(memory_space=pltpu.SMEM)] + [vmem] * (8 + len(added)),
        out_shape=jax.ShapeDtypeStruct((2, channels, width), f32),
        scratch_shapes=[pltpu.VMEM((18 * channels, 2 * width), bf16)] * 2
        + [pltpu.VMEM((4 * hidden, 2 * width), bf16)] * 2,
        compiler_params=params,
        name="backward",
    )(at, own, near, across, before, *w_out, *w_in, *added)


def on_device(initial_states, targets, lat_weight, weight_in, weight_out, hidden_bias):
    members = lax.axis_size(MEMBER)
    slabs = lax.axis_size(LAT)
    steps, slab_rows, channels, width = targets.shape
    rows = slabs * slab_rows
    near = [(i, i ^ 1) for i in range(slabs)]
    across = [(i, i + 1 if i % 2 else i - 1) for i in range(1, slabs - 1)]

    slab = lax.axis_index(LAT)
    at = jnp.stack([slab * slab_rows, lax.rem(slab, 2), lax.axis_index(MEMBER)]).astype(jnp.int32)
    own = initial_states[0]
    beside = lax.ppermute(own, LAT, near)
    crossed = lax.ppermute(own, LAT, across)
    far_crossed = lax.ppermute(beside, LAT, across)
    far_beside = lax.ppermute(crossed, LAT, near)
    ready = prepare(weight_in, weight_out)
    w_in, w_out, w_out_back, w_in_back = (ready[2 * i : 2 * i + 2] for i in range(4))
    bias = hidden_bias[:, None]
    before, fields = forward(
        rows, at, own, beside, crossed, far_crossed, far_beside, bias, w_in, w_out
    )
    height = steps * slab_rows * channels // members
    chunks = lax.all_to_all(
        fields.reshape(members, height, width), MEMBER, split_axis=0, concat_axis=0, tiled=True
    )
    grads = crps(at, lat_weight, chunks, targets.reshape(members, height, width))
    grads = lax.all_to_all(grads, MEMBER, split_axis=0, concat_axis=0, tiled=True)
    partial = jnp.sum(grads[:, height:, :], axis=0)
    loss_grads = grads[:, :height, :].reshape(steps, slab_rows, channels, width)

    total = partial
    total = total + lax.ppermute(total, LAT, near)
    for turn in (2, 6, 8):
        total = total + lax.ppermute(total, LAT, [(i, i ^ turn) for i in range(slabs)])
    loss = jnp.sum(total) / (members * steps * rows * channels * width)

    gradient = loss_grads[1]
    beside = lax.ppermute(gradient, LAT, near)
    crossed = lax.ppermute(gradient, LAT, across)
    gradient = backward(
        rows, 1, at, gradient, beside, crossed, before, w_out_back, w_in_back, loss_grads[0]
    )
    beside = lax.ppermute(gradient, LAT, near)
    crossed = lax.ppermute(gradient, LAT, across)
    gradient = backward(rows, 0, at, gradient, beside, crossed, before, w_out_back, w_in_back)
    return gradient[None], loss


def solution(mesh):
    torus = Mesh(
        mesh.devices.reshape(4, 2, 2, 4, 2), ("member_0", "member_1", "lat_0", "lat_1", "lat_2")
    )
    placed = (P(MEMBER, LAT, None, None), P(None, LAT, None, None), P(LAT), P(), P(), P())
    return jax.shard_map(
        on_device,
        mesh=torus,
        in_specs=placed,
        out_specs=(P(MEMBER, LAT, None, None), P()),
        check_vma=False,
    )
```

time: 150 us -> 78.3 us (0.52)
  the two profiles are of different devices: /device:TPU:0 before, /device:TPU:32 now
where the time goes in v1:
time: 78.3 us; the launch traced here: 77.9 us
  blocking collectives  25.8 us (33%)
  waiting for transfers between devices  18.5 us (24%)
  starting transfers between devices  13.4 us (17%)
  Pallas kernels  12.5 us (16%)
  local copies, waits for them, and re-layouts  4.45 us (6%)
  between operations  2.61 us (3%)
    all_to_all x1, blocking collectives, on_device(): lax.all_to_all(fields.reshape(members, height, width), MEMBER, split_axis...  14.9 us
    all_to_all x1, blocking collectives, on_device(): lax.all_to_all(grads, MEMBER, split_axis=0, concat_axis=0, tiled=True)  10.9 us
    ppermute x3, waiting for transfers between devices, on_device(): lax.ppermute(total, LAT, [(i, i ^ turn) for i in range(slabs)])  8.42 us
    pallas_call x2, Pallas kernels, backward(): pl.pallas_call(functools.partial(backward_kernel, rows, step), in_specs=[...  5.68 us
    pallas_call x1, Pallas kernels, forward(): pl.pallas_call(functools.partial(forward_kernel, rows), in_specs=[pl.Bloc...  5.17 us
    ppermute x2, starting transfers between devices, on_device(): crossed = lax.ppermute(gradient, LAT, across)  4.6 us
    ppermute x2, waiting for transfers between devices, on_device(): crossed = lax.ppermute(gradient, LAT, across)  4.44 us
    unnamed x15, local copies, waits for them, and re-layouts  4.31 us
  transfers between devices with their start and end apart: 12, of which 6 were waited for; matrix products, arithmetic and copies ran while one was open for 3% of the time, Pallas kernels for 4%

profile of v1, /device:TPU:32, one launch (start us, length us, event | category | flops | bytes accessed | tf_op | source)
XLA Modules:
  0.0 77.9 jit_solution(4377935560629137872)
XLA Ops:
  0.6 3.7 %collective-permute-start.1 = (f32[2,80,128]{2,1,0:T(8,128)}, f32[2,80,128]{2,1,0:T(8,128)S(1)}, u32[]{:S(2)}, u32[]{:S(2)}) collective-permute-start(f32[2,80,128]{2,1,0:T(8,128)} %bitcast.16), channel_id=1, source_target_pairs={{1,2},{2,1},{3,4},{4,3},{5,6},{6,5},{7,8},{8,7},{9,10},{10,9},{11,... | collective-permute-start | bytes 245768 | tf_op jit(solution)/shard_map/ppermute | solution.py:311
  4.3 0.1 collective-permute-start
  4.4 0.0 copy-start.6
  4.4 0.7 copy-done.6
  5.1 0.1 copy.12.bias_ref
  5.2 0.0 copy-start
  5.2 1.4 %copy.11.win_ref = f32[256,720]{1,0:T(8,128)S(1)} copy(f32[256,720]{0,1:T(8,128)} %param.9) | data formatting | bytes 1474560 | tf_op args[3]
  6.7 0.0 copy-done
  6.7 0.0 copy-start.2
  6.7 0.7 prepare.1
  7.4 1.3 %collective-permute-done.1.across_ref = f32[2,80,128]{2,1,0:T(8,128)S(1)} collective-permute-done((f32[2,80,128]{2,1,0:T(8,128)}, f32[2,80,128]{2,1,0:T(8,128)S(1)}, u32[]{:S(2)}, u32[]{:S(2)}) %collective-permute-start.1) | collective-permute-done | bytes 81952 | tf_op jit(solution)/shard_map/ppermute | solution.py:311
  8.7 0.0 collective-permute-start.3
  8.7 0.0 collective-permute-done.near_ref
  8.7 3.6 %collective-permute-start.2 = (f32[2,80,128]{2,1,0:T(8,128)S(1)}, f32[2,80,128]{2,1,0:T(8,128)S(1)}, u32[]{:S(2)}, u32[]{:S(2)}) collective-permute-start(f32[2,80,128]{2,1,0:T(8,128)S(1)} %collective-permute-done.near_ref), channel_id=1, source_target_pairs={{1,2},{2,1},{3,4},{4,3},{5,6},{6,5},{7,8},{8,7},{9,10},{10,9},{11,... | collective-permute-start | bytes 245768 | tf_op jit(solution)/shard_map/ppermute | solution.py:312
  12.4 0.0 copy-start.3
  12.4 0.6 copy-done.3
  13.0 0.1 pad_add_fusion.at_ref
  13.1 0.0 collective-permute-done.3.far_near_ref
  13.1 3.5 %collective-permute-done.2.far_across_ref = f32[2,80,128]{2,1,0:T(8,128)S(1)} collective-permute-done((f32[2,80,128]{2,1,0:T(8,128)S(1)}, f32[2,80,128]{2,1,0:T(8,128)S(1)}, u32[]{:S(2)}, u32[]{:S(2)}) %collective-permute-start.2) | collective-permute-done | bytes 81952 | tf_op jit(solution)/shard_map/ppermute | solution.py:312
  16.6 0.0 copy-done.2
  16.6 0.0 copy-start.4
  16.6 0.9 %copy-done.4 = f32[2,80,128]{2,1,0:T(8,128)S(1)} copy-done((f32[2,80,128]{2,1,0:T(8,128)S(1)}, f32[2,80,128]{2,1,0:T(8,128)}, u32[]{:S(2)}) %copy-start.4) | copy-done | bytes 81944
  17.5 5.2 %forward.1 = (f32[2,2,256,256]{3,2,1,0:T(8,128)S(1)}, f32[320,128]{1,0:T(8,128)S(1)}) custom-call(s32[3]{0:T(128)S(1)} %pad_add_fusion.at_ref, f32[2,80,128]{2,1,0:T(8,128)S(1)} %bitcast.18, f32[2,80,128]{2,1,0:T(8,128)S(1)} %copy-done.4, f32[2,80,128]{2,1,0:T(8,128)S(1)} %collective-permute-done.1.across_ref, ...), custom_call_target="tpu_custom_call" | custom-call | tf_op jit(solution)/shard_map/forward/pallas_call | solution.py:195
  22.6 0.0 copy-start.1
  22.7 14.9 %all_to_all.10.fields_ref = f32[8,40,128]{2,1,0:T(8,128)S(1)} all-to-all(f32[8,40,128]{2,1,0:T(8,128)S(1)} %bitcast.15), channel_id=1, replica_groups=mesh['member_0'=4,'member_1'=2,'lat_0'=2,'lat_1'=4,'lat_2'=2] {'member_0..., dimensions={0} | all-to-all | bytes 327680 | tf_op jit(solution)/shard_map/all_to_all | solution.py:321
  37.5 0.0 copy-done.1
  37.5 0.7 copy-done.5
  38.2 0.9 %crps.1 = f32[8,48,128]{2,1,0:T(8,128)S(1)} custom-call(s32[3]{0:T(128)S(1)} %pad_add_fusion.at_ref, f32[2]{0:T(128)S(1)} %copy-done.5, f32[8,40,128]{2,1,0:T(8,128)S(1)} %all_to_all.10.fields_ref, f32[8,40,128]{2,1,0:T(8,128)S(1)} %bitcast.14), custom_call_target="tpu_custom_call" | custom-call | tf_op jit(solution)/shard_map/crps/pallas_call | solution.py:245
  39.1 10.9 %all_to_all.11 = f32[8,48,128]{2,1,0:T(8,128)S(1)} all-to-all(f32[8,48,128]{2,1,0:T(8,128)S(1)} %crps.1), channel_id=1, replica_groups=mesh['member_0'=4,'member_1'=2,'lat_0'=2,'lat_1'=4,'lat_2'=2] {'member_0..., dimensions={0} | all-to-all | bytes 393216 | tf_op jit(solution)/shard_map/all_to_all | solution.py:325
  50.1 2.5 %collective-permute-start.5 = (f32[2,80,128]{2,1,0:T(8,128)S(1)}, f32[2,80,128]{2,1,0:T(8,128)S(1)}, u32[]{:S(2)}, u32[]{:S(2)}) collective-permute-start(f32[2,80,128]{2,1,0:T(8,128)S(1)} %bitcast.11), channel_id=1, source_target_pairs={{1,2},{2,1},{3,4},{4,3},{5,6},{6,5},{7,8},{8,7},{9,10},{10,9},{11,... | collective-permute-start | bytes 245768 | tf_op jit(solution)/shard_map/ppermute | solution.py:337
  52.6 0.1 collective-permute-start.4
  52.7 0.5 collective-permute-start.8
  53.2 0.8 %collective-permute-done.8 = f32[8,128]{1,0:T(8,128)S(1)} collective-permute-done((f32[8,128]{1,0:T(8,128)S(1)}, f32[8,128]{1,0:T(8,128)S(1)}, u32[]{:S(2)}, u32[]{:S(2)}) %collective-permute-start.8) | collective-permute-done | bytes 4128 | tf_op jit(solution)/shard_map/ppermute | solution.py:330
  54.0 0.0 collective-permute-start.9
  54.0 3.6 %collective-permute-done.9 = f32[8,128]{1,0:T(8,128)S(1)} collective-permute-done((f32[8,128]{1,0:T(8,128)S(1)}, f32[8,128]{1,0:T(8,128)S(1)}, u32[]{:S(2)}, u32[]{:S(2)}) %collective-permute-start.9) | collective-permute-done | bytes 4128 | tf_op jit(solution)/shard_map/ppermute | solution.py:332
  57.6 0.0 collective-permute-start.10
  57.6 4.8 %collective-permute-done.10 = f32[8,128]{1,0:T(8,128)S(1)} collective-permute-done((f32[8,128]{1,0:T(8,128)S(1)}, f32[8,128]{1,0:T(8,128)S(1)}, u32[]{:S(2)}, u32[]{:S(2)}) %collective-permute-start.10) | collective-permute-done | bytes 4128 | tf_op jit(solution)/shard_map/ppermute | solution.py:332
  62.5 0.8 %collective-permute-start.11 = (f32[8,128]{1,0:T(8,128)S(1)}, f32[8,128]{1,0:T(8,128)S(1)}, u32[]{:S(2)}, u32[]{:S(2)}) collective-permute-start(f32[8,128]{1,0:T(8,128)S(1)} %add.26), channel_id=1, source_target_pairs={{0,8},{1,9},{2,10},{3,11},{4,12},{5,13},{6,14},{7,15},{8,0},{9,1},... | collective-permute-start | bytes 12296 | tf_op jit(solution)/shard_map/ppermute | solution.py:332
  63.2 0.0 collective-permute-done.5.across_ref
  63.2 0.0 collective-permute-done.4.near_ref
  63.3 2.5 %backward.2.own_ref = f32[2,80,128]{2,1,0:T(8,128)S(1)} custom-call(s32[3]{0:T(128)S(1)} %pad_add_fusion.at_ref, f32[2,80,128]{2,1,0:T(8,128)S(1)} %bitcast.13, f32[2,80,128]{2,1,0:T(8,128)S(1)} %collective-permute-done.4.near_ref, f32[2,80,128]{2,1,0:T(8,128)S(1)} %collective-permute-done.5.across_ref, f32[2,2,256,256]{3,2,1,0:T(8,128)S(1)} %get-tuple-element.17.before_ref, ...), custom_call_target="tpu_custom_call" | custom-call | tf_op jit(solution)/shard_map/backward/pallas_call | solution.py:288
  65.8 2.1 %collective-permute-start.7 = (f32[2,80,128]{2,1,0:T(8,128)S(1)}, f32[2,80,128]{2,1,0:T(8,128)S(1)}, u32[]{:S(2)}, u32[]{:S(2)}) collective-permute-start(f32[2,80,128]{2,1,0:T(8,128)S(1)} %backward.2.own_ref), channel_id=1, source_target_pairs={{1,2},{2,1},{3,4},{4,3},{5,6},{6,5},{7,8},{8,7},{9,10},{10,9},{11,... | collective-permute-start | bytes 245768 | tf_op jit(solution)/shard_map/ppermute | solution.py:342
  67.9 0.1 collective-permute-start.6
  67.9 0.0 collective-permute-done.11
  68.0 0.6 add_reduce_fusion
  69.2 4.4 %collective-permute-done.7.across_ref = f32[2,80,128]{2,1,0:T(8,128)S(1)} collective-permute-done((f32[2,80,128]{2,1,0:T(8,128)S(1)}, f32[2,80,128]{2,1,0:T(8,128)S(1)}, u32[]{:S(2)}, u32[]{:S(2)}) %collective-permute-start.7) | collective-permute-done | bytes 81952 | tf_op jit(solution)/shard_map/ppermute | solution.py:342
  73.7 0.0 collective-permute-done.6.near_ref
  73.7 3.2 %backward.3 = f32[2,80,128]{2,1,0:T(8,128)} custom-call(s32[3]{0:T(128)S(1)} %pad_add_fusion.at_ref, f32[2,80,128]{2,1,0:T(8,128)S(1)} %backward.2.own_ref, f32[2,80,128]{2,1,0:T(8,128)S(1)} %collective-permute-done.6.near_ref, f32[2,80,128]{2,1,0:T(8,128)S(1)} %collective-permute-done.7.across_ref, f32[2,2,256,256]{3,2,1,0:T(8,128)S(1)} %get-tuple-element.17.before_ref, ...), custom_call_target="tpu_custom_call" | custom-call | tf_op jit(solution)/shard_map/backward/pallas_call | solution.py:288
  (6 shorter events, 0.0 us)
Async XLA Ops:
  0.6 8.1 %collective-permute-start.1 = (f32[2,80,128]{2,1,0:T(8,128)}, f32[2,80,128]{2,1,0:T(8,128)S(1)}, u32[]{:S(2)}, u32[]{:S(2)}) collective-permute-start(f32[2,80,128]{2,1,0:T(8,128)} %bitcast.16), channel_id=1, source_target_pairs={{1,2},{2,1},{3,4},{4,3},{5,6},{6,5},{7,8},{8,7},{9,10},{10,9},{11,... | collective-permute-start | bytes 245768 | tf_op jit(solution)/shard_map/ppermute | solution.py:311
  4.3 4.4 %collective-permute-start = (f32[2,80,128]{2,1,0:T(8,128)}, f32[2,80,128]{2,1,0:T(8,128)S(1)}, u32[]{:S(2)}, u32[]{:S(2)}) collective-permute-start(f32[2,80,128]{2,1,0:T(8,128)} %bitcast.17), channel_id=1, source_target_pairs={{0,1},{1,0},{2,3},{3,2},{4,5},{5,4},{6,7},{7,6},{8,9},{9,8},{10,11... | collective-permute-start | bytes 245768 | tf_op jit(solution)/shard_map/ppermute | solution.py:310
  4.4 0.7 copy-start.6
  5.2 1.5 %copy-start = (f32[80,2304]{1,0:T(8,128)S(1)}, f32[80,2304]{1,0:T(8,128)}, u32[]{:S(2)}) copy-start(f32[80,2304]{1,0:T(8,128)} %wout_ref.1) | copy-start | bytes 2211844
  6.7 9.9 %copy-start.2 = (f32[1,2,80,128]{3,2,1,0:T(8,128)S(1)}, f32[1,2,80,128]{3,2,1,0:T(8,128)}, u32[]{:S(2)}) copy-start(f32[1,2,80,128]{3,2,1,0:T(8,128)} %param.6) | copy-start | bytes 245764
  8.7 4.4 %collective-permute-start.3 = (f32[2,80,128]{2,1,0:T(8,128)S(1)}, f32[2,80,128]{2,1,0:T(8,128)S(1)}, u32[]{:S(2)}, u32[]{:S(2)}) collective-permute-start(f32[2,80,128]{2,1,0:T(8,128)S(1)} %collective-permute-done.1.across_ref), channel_id=1, source_target_pairs={{0,1},{1,0},{2,3},{3,2},{4,5},{5,4},{6,7},{7,6},{8,9},{9,8},{10,11... | collective-permute-start | bytes 245768 | tf_op jit(solution)/shard_map/ppermute | solution.py:313
  8.7 7.9 %collective-permute-start.2 = (f32[2,80,128]{2,1,0:T(8,128)S(1)}, f32[2,80,128]{2,1,0:T(8,128)S(1)}, u32[]{:S(2)}, u32[]{:S(2)}) collective-permute-start(f32[2,80,128]{2,1,0:T(8,128)S(1)} %collective-permute-done.near_ref), channel_id=1, source_target_pairs={{1,2},{2,1},{3,4},{4,3},{5,6},{6,5},{7,8},{8,7},{9,10},{10,9},{11,... | collective-permute-start | bytes 245768 | tf_op jit(solution)/shard_map/ppermute | solution.py:312
  12.4 0.6 copy-start.3
  16.6 0.9 %copy-start.4 = (f32[2,80,128]{2,1,0:T(8,128)S(1)}, f32[2,80,128]{2,1,0:T(8,128)}, u32[]{:S(2)}) copy-start(f32[2,80,128]{2,1,0:T(8,128)} %copy-done.3) | copy-start | bytes 245764
  22.6 14.9 %copy-start.1 = (f32[2,2,80,128]{3,2,1,0:T(8,128)S(1)}, f32[2,2,80,128]{3,2,1,0:T(8,128)}, u32[]{:S(2)}) copy-start(f32[2,2,80,128]{3,2,1,0:T(8,128)} %param.7) | copy-start | bytes 491524
  37.5 0.7 copy-start.5
  50.1 13.2 %collective-permute-start.5 = (f32[2,80,128]{2,1,0:T(8,128)S(1)}, f32[2,80,128]{2,1,0:T(8,128)S(1)}, u32[]{:S(2)}, u32[]{:S(2)}) collective-permute-start(f32[2,80,128]{2,1,0:T(8,128)S(1)} %bitcast.11), channel_id=1, source_target_pairs={{1,2},{2,1},{3,4},{4,3},{5,6},{6,5},{7,8},{8,7},{9,10},{10,9},{11,... | collective-permute-start | bytes 245768 | tf_op jit(solution)/shard_map/ppermute | solution.py:337
  52.6 10.7 %collective-permute-start.4 = (f32[2,80,128]{2,1,0:T(8,128)S(1)}, f32[2,80,128]{2,1,0:T(8,128)S(1)}, u32[]{:S(2)}, u32[]{:S(2)}) collective-permute-start(f32[2,80,128]{2,1,0:T(8,128)S(1)} %bitcast.12), channel_id=1, source_target_pairs={{0,1},{1,0},{2,3},{3,2},{4,5},{5,4},{6,7},{7,6},{8,9},{9,8},{10,11... | collective-permute-start | bytes 245768 | tf_op jit(solution)/shard_map/ppermute | solution.py:336
  52.7 1.3 %collective-permute-start.8 = (f32[8,128]{1,0:T(8,128)S(1)}, f32[8,128]{1,0:T(8,128)S(1)}, u32[]{:S(2)}, u32[]{:S(2)}) collective-permute-start(f32[8,128]{1,0:T(8,128)S(1)} %slice_reduce_fusion), channel_id=1, source_target_pairs={{0,1},{1,0},{2,3},{3,2},{4,5},{5,4},{6,7},{7,6},{8,9},{9,8},{10,11... | collective-permute-start | bytes 12296 | tf_op jit(solution)/shard_map/ppermute | solution.py:330
  54.0 3.6 %collective-permute-start.9 = (f32[8,128]{1,0:T(8,128)S(1)}, f32[8,128]{1,0:T(8,128)S(1)}, u32[]{:S(2)}, u32[]{:S(2)}) collective-permute-start(f32[8,128]{1,0:T(8,128)S(1)} %add.24), channel_id=1, source_target_pairs={{0,2},{1,3},{2,0},{3,1},{4,6},{5,7},{6,4},{7,5},{8,10},{9,11},{10,... | collective-permute-start | bytes 12296 | tf_op jit(solution)/shard_map/ppermute | solution.py:332
  57.6 4.8 %collective-permute-start.10 = (f32[8,128]{1,0:T(8,128)S(1)}, f32[8,128]{1,0:T(8,128)S(1)}, u32[]{:S(2)}, u32[]{:S(2)}) collective-permute-start(f32[8,128]{1,0:T(8,128)S(1)} %add.25), channel_id=1, source_target_pairs={{0,6},{1,7},{2,4},{3,5},{4,2},{5,3},{6,0},{7,1},{8,14},{9,15},{10,... | collective-permute-start | bytes 12296 | tf_op jit(solution)/shard_map/ppermute | solution.py:332
  62.5 5.5 %collective-permute-start.11 = (f32[8,128]{1,0:T(8,128)S(1)}, f32[8,128]{1,0:T(8,128)S(1)}, u32[]{:S(2)}, u32[]{:S(2)}) collective-permute-start(f32[8,128]{1,0:T(8,128)S(1)} %add.26), channel_id=1, source_target_pairs={{0,8},{1,9},{2,10},{3,11},{4,12},{5,13},{6,14},{7,15},{8,0},{9,1},... | collective-permute-start | bytes 12296 | tf_op jit(solution)/shard_map/ppermute | solution.py:332
  65.8 7.9 %collective-permute-start.7 = (f32[2,80,128]{2,1,0:T(8,128)S(1)}, f32[2,80,128]{2,1,0:T(8,128)S(1)}, u32[]{:S(2)}, u32[]{:S(2)}) collective-permute-start(f32[2,80,128]{2,1,0:T(8,128)S(1)} %backward.2.own_ref), channel_id=1, source_target_pairs={{1,2},{2,1},{3,4},{4,3},{5,6},{6,5},{7,8},{8,7},{9,10},{10,9},{11,... | collective-permute-start | bytes 245768 | tf_op jit(solution)/shard_map/ppermute | solution.py:342
  67.9 5.8 %collective-permute-start.6 = (f32[2,80,128]{2,1,0:T(8,128)S(1)}, f32[2,80,128]{2,1,0:T(8,128)S(1)}, u32[]{:S(2)}, u32[]{:S(2)}) collective-permute-start(f32[2,80,128]{2,1,0:T(8,128)S(1)} %backward.2.own_ref), channel_id=1, source_target_pairs={{0,1},{1,0},{2,3},{3,2},{4,5},{5,4},{6,7},{7,6},{8,9},{9,8},{10,11... | collective-permute-start | bytes 245768 | tf_op jit(solution)/shard_map/ppermute | solution.py:341

commit v2 on v1

--- a/solution.py
+++ b/solution.py
@@ -14,10 +14,11 @@
 smooth_width = 0.1
 gelu_scale = 0.7978845608028654
 gelu_cubic = 0.044715
+slab_count = 16
 
 f32 = jnp.float32
 bf16 = jnp.bfloat16
-params = pltpu.CompilerParams(vmem_limit_bytes=40 * 1024 * 1024)
+params = pltpu.CompilerParams(vmem_limit_bytes=16 * 1024 * 1024)
 
 
 def split(value):
@@ -89,11 +90,18 @@
     return 0.5 * (1.0 + t) + 0.5 * x * (1.0 - t * t) * inner
 
 
-def prepare_kernel(win_ref, wout_ref, in_hi, in_lo, out_hi, out_lo, outb_hi, outb_lo, inb_hi, inb_lo, stack):
+def prepare_kernel(win_hbm, wout_hbm, bias_hbm, in_hi, in_lo, out_hi, out_lo, outb_hi, outb_lo, inb_hi, inb_lo,
+                   wide_bias_ref, stack, win_ref, wout_ref, bias_ref, arrived):
+    pairs = ((win_hbm, win_ref), (wout_hbm, wout_ref), (bias_hbm, bias_ref))
+    copies = [pltpu.make_async_copy(*pair, arrived.at[i]) for i, pair in enumerate(pairs)]
+    for copy in copies:
+        copy.start()
+    for copy in copies:
+        copy.wait()
     outer, width = wout_ref.shape
     hidden = width // 9
-    inner = win_ref.shape[1] // 9
-    high, low = split(win_ref[...])
+    inner = win_ref.shape[0] // 9
+    high, low = split(win_ref[...].T)
     in_hi[...] = high
     in_lo[...] = low
     for a in range(3):
@@ -104,32 +112,37 @@
             out_hi[b * outer : (b + 1) * outer, a * hidden : (a + 1) * hidden] = high
             out_lo[b * outer : (b + 1) * outer, a * hidden : (a + 1) * hidden] = low
             stack[(8 - tap) * outer : (9 - tap) * outer, :] = block
+            high, low = split(win_ref[tap * inner : (tap + 1) * inner, :])
+            j, k = 2 - a, 2 - b
+            inb_hi[k * inner : (k + 1) * inner, j * hidden : (j + 1) * hidden] = high
+            inb_lo[k * inner : (k + 1) * inner, j * hidden : (j + 1) * hidden] = low
     high, low = split(stack[...].T)
     outb_hi[...] = high
     outb_lo[...] = low
-    turned = win_ref[...].T
-    for a in range(3):
-        for b in range(3):
-            tap = 3 * a + b
-            high, low = split(turned[tap * inner : (tap + 1) * inner, :])
-            j, k = 2 - a, 2 - b
-            inb_hi[k * inner : (k + 1) * inner, j * hidden : (j + 1) * hidden] = high
-            inb_lo[k * inner : (k + 1) * inner, j * hidden : (j + 1) * hidden] = low
-
-
-def prepare(weight_in, weight_out):
-    hidden, taps_in = weight_in.shape
+    wide_bias_ref[...] = jnp.broadcast_to(bias_ref[...], wide_bias_ref.shape[::-1]).T
+
+
+def prepare(weight_in, weight_out, bias, width):
+    taps_in, hidden = weight_in.shape
     outer = weight_out.shape[0]
     inner = taps_in // 9
     shapes = [(hidden, 9 * inner)] * 2 + [(3 * outer, 3 * hidden)] * 2
     shapes = shapes + [(hidden, 9 * outer)] * 2 + [(3 * inner, 3 * hidden)] * 2
     return pl.pallas_call(
         prepare_kernel,
-        out_shape=[jax.ShapeDtypeStruct(shape, bf16) for shape in shapes],
-        scratch_shapes=[pltpu.VMEM((9 * outer, hidden), f32)],
+        out_shape=[jax.ShapeDtypeStruct(shape, bf16) for shape in shapes]
+        + [jax.ShapeDtypeStruct((hidden, width), f32)],
+        in_specs=[pl.BlockSpec(memory_space=pltpu.HBM)] * 3,
+        scratch_shapes=[
+            pltpu.VMEM((9 * outer, hidden), f32),
+            pltpu.VMEM(weight_in.shape, f32),
+            pltpu.VMEM(weight_out.shape, f32),
+            pltpu.VMEM(bias.shape, f32),
+            pltpu.SemaphoreType.DMA((3,)),
+        ],
         compiler_params=params,
         name="prepare",
-    )(weight_in, weight_out)
+    )(weight_in, weight_out, bias)
 
 
 def inside(at_ref, row, rows):
@@ -146,7 +159,7 @@
     hid = (hid_hi, hid_lo)
     w_in = (in_hi[...], in_lo[...])
     w_out = (out_hi[...], out_lo[...])
-    bias = bias_ref[...]
+    bias = jnp.concatenate([bias_ref[...]] * 2, axis=1)
 
     def initial(index):
         slab, row = index // 2, index % 2
@@ -158,7 +171,8 @@
             3: (near_ref, across_ref),
             4: (far_near_ref, far_across_ref),
         }[slab]
-        return jnp.where(even, first[row], second[row])
+        value = jnp.where(even, first[row], second[row])
+        return jnp.where(inside(at_ref, index - 4, rows), value, 0.0)
 
     def advance(field, first, count, keep, step):
         for index in range(count):
@@ -251,49 +265,135 @@
     )(at, weights, fields, targets)
 
 
-def backward_kernel(rows, step, at_ref, own_ref, near_ref, across_ref, before_ref, outb_hi, outb_lo, inb_hi, inb_lo,
+def collect_kernel(at_ref, grads_ref, first_ref, second_ref):
+    chunks, height, width = grads_ref.shape
+    height = height - 8
+    half = chunks // 2
+    total = grads_ref[0, height : height + 8, :]
+    for chunk in range(1, chunks):
+        total = total + grads_ref[chunk, height : height + 8, :]
+    for chunk in range(half):
+        first_ref[chunk * height : (chunk + 1) * height, :] = grads_ref[chunk, :height, :]
+        second_ref[chunk * height : (chunk + 1) * height, :] = grads_ref[half + chunk, :height, :]
+    known = jnp.broadcast_to(jnp.sum(total, axis=0, keepdims=True), (slab_count, width))
+    slab = lax.broadcasted_iota(jnp.int32, known.shape, 0)
+    second_ref[half * height :, :] = jnp.where(slab == at_ref[3], known, 0.0)
+
+
+def collect(at, grads):
+    chunks, height, width = grads.shape
+    count = chunks // 2 * (height - 8)
+    vmem = pl.BlockSpec(memory_space=pltpu.VMEM)
+    return pl.pallas_call(
+        collect_kernel,
+        in_specs=[pl.BlockSpec(memory_space=pltpu.SMEM), vmem],
+        out_shape=[
+            jax.ShapeDtypeStruct((count, width), f32),
+            jax.ShapeDtypeStruct((count + slab_count, width), f32),
+        ],
+        compiler_params=params,
+        name="collect",
+    )(at, grads)
+
+
+def merged(*known):
+    result = known[0]
+    for other in known[1:]:
+        result = jnp.where(result != 0.0, result, other)
+    return result
+
+
+def merge_kernel(own_ref, near_ref, across_ref, far_ref, out_ref):
+    count = own_ref.shape[0] - slab_count
+    out_ref[...] = merged(own_ref[count:, :], near_ref[count:, :], across_ref[count:, :], far_ref[...])
+
+
+def merge(own, near, across, far):
+    return pl.pallas_call(
+        merge_kernel,
+        out_shape=jax.ShapeDtypeStruct(far.shape, f32),
+        compiler_params=params,
+        name="merge",
+    )(own, near, across, far)
+
+
+def slopes_kernel(before_ref, out_ref):
+    for step in range(2):
+        for pair in range(2):
+            out_ref[step, pair] = gelu_slope(before_ref[step, pair])
+
+
+def slopes_of(before):
+    return pl.pallas_call(
+        slopes_kernel,
+        out_shape=jax.ShapeDtypeStruct(before.shape, f32),
+        compiler_params=params,
+        name="slopes",
+    )(before)
+
+
+def backward_kernel(rows, step, at_ref, own_ref, near_ref, across_ref, slope_ref, outb_hi, outb_lo, inb_hi, inb_lo,
                     *rest):
-    added = rest[:-5]
-    out_ref, wide_hi, wide_lo, hid_hi, hid_lo = rest[-5:]
-    channels, width = own_ref.shape[1:]
+    outs = 1 + step
+    added = rest[: -4 - outs]
+    out_ref, *known_ref = rest[-4 - outs : -4]
+    wide_hi, wide_lo, hid_hi, hid_lo = rest[-4:]
+    width = own_ref.shape[1]
+    channels = (own_ref.shape[0] - slab_count) // 2
     hidden = outb_hi.shape[0]
     even = at_ref[1] == 0
     wide = (wide_hi, wide_lo)
     hid = (hid_hi, hid_lo)
     w_out = (outb_hi[...], outb_lo[...])
     w_in = (inb_hi[...], inb_lo[...])
+
+    def take(ref, row):
+        return ref[row * channels : (row + 1) * channels, :]
+
+    def put_beside(index, first, second, row):
+        value = jnp.where(even, take(first, row), take(second, row))
+        value = jnp.where(inside(at_ref, index - 2, rows), value, 0.0)
+        put_windows(wide, index, value)
+
     for row in range(2):
-        put_windows(wide, row, jnp.where(even, across_ref[row], near_ref[row]))
-        put_windows(wide, 2 + row, own_ref[row])
+        put_windows(wide, 2 + row, take(own_ref, row))
     for row in range(2):
-        put_windows(wide, 4 + row, jnp.where(even, near_ref[row], across_ref[row]))
+        put_beside(row, across_ref, near_ref, row)
+        put_beside(4 + row, near_ref, across_ref, row)
     for pair in (0, 2):
-        grads = to_channels(w_out, wide, pair, channels) * gelu_slope(before_ref[step, pair // 2])
+        grads = to_channels(w_out, wide, pair, channels) * slope_ref[step, pair // 2]
         for half in range(2):
             row = grads[:, half * width : (half + 1) * width]
             row = jnp.where(inside(at_ref, pair + half - 1, rows), row, 0.0)
             put_twice(hid, pair + half, hidden, 0, split(row))
     moved = from_channels(w_in, hid, 0, hidden, channels)
     for row in range(2):
-        total = own_ref[row] + moved[row]
+        total = take(own_ref, row) + moved[row]
         for extra in added:
-            total = total + extra[row]
-        out_ref[row] = total
-
-
-def backward(rows, step, at, own, near, across, before, w_out, w_in, *added):
-    channels, width = own.shape[1:]
+            total = total + take(extra, row)
+        out_ref[row * channels : (row + 1) * channels, :] = total
+    if known_ref:
+        last = 2 * channels
+        known = merged(own_ref[last:, :], near_ref[last:, :], across_ref[last:, :])
+        out_ref[last:, :] = known
+        known_ref[0][...] = known
+
+
+def backward(rows, step, at, own, near, across, slopes, w_out, w_in, *added):
+    count, width = own.shape
+    channels = (count - slab_count) // 2
     hidden = w_out[0].shape[0]
     vmem = pl.BlockSpec(memory_space=pltpu.VMEM)
     return pl.pallas_call(
         functools.partial(backward_kernel, rows, step),
         in_specs=[pl.BlockSpec(memory_space=pltpu.SMEM)] + [vmem] * (8 + len(added)),
-        out_shape=jax.ShapeDtypeStruct((2, channels, width), f32),
+        out_shape=[jax.ShapeDtypeStruct((count if step else 2 * channels, width), f32)]
+        + [jax.ShapeDtypeStruct((slab_count, width), f32)] * step,
         scratch_shapes=[pltpu.VMEM((18 * channels, 2 * width), bf16)] * 2
         + [pltpu.VMEM((4 * hidden, 2 * width), bf16)] * 2,
         compiler_params=params,
         name="backward",
-    )(at, own, near, across, before, *w_out, *w_in, *added)
+    )(at, own, near, across, slopes, *w_out, *w_in, *added)
 
 
 def on_device(initial_states, targets, lat_weight, weight_in, weight_out, hidden_bias):
@@ -302,20 +402,22 @@
     steps, slab_rows, channels, width = targets.shape
     rows = slabs * slab_rows
     near = [(i, i ^ 1) for i in range(slabs)]
-    across = [(i, i + 1 if i % 2 else i - 1) for i in range(1, slabs - 1)]
+    across = [(i, (i + 1 if i % 2 else i - 1) % slabs) for i in range(slabs)]
 
     slab = lax.axis_index(LAT)
-    at = jnp.stack([slab * slab_rows, lax.rem(slab, 2), lax.axis_index(MEMBER)]).astype(jnp.int32)
+    at = [slab * slab_rows, lax.rem(slab, 2), lax.axis_index(MEMBER), slab]
+    at = jnp.stack(at).astype(jnp.int32)
     own = initial_states[0]
     beside = lax.ppermute(own, LAT, near)
     crossed = lax.ppermute(own, LAT, across)
     far_crossed = lax.ppermute(beside, LAT, across)
+    crossed, beside = lax.optimization_barrier((crossed, beside))
     far_beside = lax.ppermute(crossed, LAT, near)
-    ready = prepare(weight_in, weight_out)
+    far_beside, weight_out = lax.optimization_barrier((far_beside, weight_out))
+    ready = prepare(weight_in.T, weight_out, hidden_bias[None, :], width)
     w_in, w_out, w_out_back, w_in_back = (ready[2 * i : 2 * i + 2] for i in range(4))
-    bias = hidden_bias[:, None]
     before, fields = forward(
-        rows, at, own, beside, crossed, far_crossed, far_beside, bias, w_in, w_out
+        rows, at, own, beside, crossed, far_crossed, far_beside, ready[8], w_in, w_out
     )
     height = steps * slab_rows * channels // members
     chunks = lax.all_to_all(
@@ -323,25 +425,24 @@
     )
     grads = crps(at, lat_weight, chunks, targets.reshape(members, height, width))
     grads = lax.all_to_all(grads, MEMBER, split_axis=0, concat_axis=0, tiled=True)
-    partial = jnp.sum(grads[:, height:, :], axis=0)
-    loss_grads = grads[:, :height, :].reshape(steps, slab_rows, channels, width)
-
-    total = partial
-    total = total + lax.ppermute(total, LAT, near)
-    for turn in (2, 6, 8):
-        total = total + lax.ppermute(total, LAT, [(i, i ^ turn) for i in range(slabs)])
-    loss = jnp.sum(total) / (members * steps * rows * channels * width)
-
-    gradient = loss_grads[1]
-    beside = lax.ppermute(gradient, LAT, near)
-    crossed = lax.ppermute(gradient, LAT, across)
-    gradient = backward(
-        rows, 1, at, gradient, beside, crossed, before, w_out_back, w_in_back, loss_grads[0]
+    grads, before = lax.optimization_barrier((grads, before))
+    slopes = slopes_of(before)
+    first_grads, message = collect(at, grads)
+
+    beside = lax.ppermute(message, LAT, near)
+    crossed = lax.ppermute(message, LAT, across)
+    message, known = backward(
+        rows, 1, at, message, beside, crossed, slopes, w_out_back, w_in_back, first_grads
     )
-    beside = lax.ppermute(gradient, LAT, near)
-    crossed = lax.ppermute(gradient, LAT, across)
-    gradient = backward(rows, 0, at, gradient, beside, crossed, before, w_out_back, w_in_back)
-    return gradient[None], loss
+    beside = lax.ppermute(message, LAT, near)
+    crossed = lax.ppermute(message, LAT, across)
+    far = lax.ppermute(known, LAT, [(i, i ^ 4) for i in range(slabs)])
+    known = merge(message, beside, crossed, far)
+    (gradient,) = backward(rows, 0, at, message, beside, crossed, slopes, w_out_back, w_in_back)
+    opposite = lax.ppermute(known, LAT, [(i, i ^ 8) for i in range(slabs)])
+    total = jnp.sum(jnp.where(known != 0.0, known, opposite))
+    loss = total / (members * steps * rows * channels * width)
+    return gradient.reshape(initial_states.shape), loss
 
 
 def solution(mesh):

time: 78.3 us -> 70.9 us (0.905)
  the two profiles are of different devices: /device:TPU:32 before, /device:TPU:0 now
where the time goes in v2:
time: 70.9 us; the launch traced here: 70.1 us
  blocking collectives  26.4 us (37%)
  waiting for transfers between devices  14.1 us (20%)
  Pallas kernels  14.1 us (20%)
  starting transfers between devices  8.71 us (12%)
  local copies, waits for them, and re-layouts  3.57 us (5%)
  between operations  2.54 us (4%)
    all_to_all x1, blocking collectives, on_device(): lax.all_to_all(fields.reshape(members, height, width), MEMBER, split_axis...  15.5 us
    all_to_all x1, blocking collectives, on_device(): lax.all_to_all(grads, MEMBER, split_axis=0, concat_axis=0, tiled=True)  10.9 us
    ppermute x2, waiting for transfers between devices, on_device(): crossed = lax.ppermute(message, LAT, across)  6.05 us
    pallas_call x2, Pallas kernels, backward(): pl.pallas_call(functools.partial(backward_kernel, rows, step), in_specs=[...  5.55 us
    pallas_call x1, Pallas kernels, forward(): pl.pallas_call(functools.partial(forward_kernel, rows), in_specs=[pl.Bloc...  5.23 us
    ppermute x1, waiting for transfers between devices, on_device(): far = lax.ppermute(known, LAT, [(i, i ^ 4) for i in range(slabs)])  5.14 us
    ppermute x1, starting transfers between devices, on_device(): crossed = lax.ppermute(own, LAT, across)  4.29 us
    ppermute x1, starting transfers between devices, on_device(): far_crossed = lax.ppermute(beside, LAT, across)  3.81 us
  transfers between devices with their start and end apart: 10, of which 5 were waited for; matrix products, arithmetic and copies ran while one was open for 0% of the time, Pallas kernels for 7%

profile of v2, /device:TPU:0, one launch (start us, length us, event | category | flops | bytes accessed | tf_op | source)
XLA Modules:
  0.0 70.1 jit_solution(13729484259139228256)
XLA Ops:
  0.6 0.1 collective-permute-start.1
  0.7 4.3 %collective-permute-start = (f32[2,80,128]{2,1,0:T(8,128)}, f32[2,80,128]{2,1,0:T(8,128)S(1)}, u32[]{:S(2)}, u32[]{:S(2)}) collective-permute-start(f32[2,80,128]{2,1,0:T(8,128)} %bitcast.14), channel_id=1, source_target_pairs={{0,15},{1,2},{2,1},{3,4},{4,3},{5,6},{6,5},{7,8},{8,7},{9,10},{10,... | collective-permute-start | bytes 245768 | tf_op jit(solution)/shard_map/ppermute | solution.py:412
  5.0 0.0 collective-permute-done.1.near_ref
  5.0 2.4 %collective-permute-done.across_ref = f32[2,80,128]{2,1,0:T(8,128)S(1)} collective-permute-done((f32[2,80,128]{2,1,0:T(8,128)}, f32[2,80,128]{2,1,0:T(8,128)S(1)}, u32[]{:S(2)}, u32[]{:S(2)}) %collective-permute-start) | collective-permute-done | bytes 81952 | tf_op jit(solution)/shard_map/ppermute | solution.py:412
  7.4 0.0 collective-permute-start.3
  7.4 3.8 %collective-permute-start.2 = (f32[2,80,128]{2,1,0:T(8,128)S(1)}, f32[2,80,128]{2,1,0:T(8,128)S(1)}, u32[]{:S(2)}, u32[]{:S(2)}) collective-permute-start(f32[2,80,128]{2,1,0:T(8,128)S(1)} %collective-permute-done.1.near_ref), channel_id=1, source_target_pairs={{0,15},{1,2},{2,1},{3,4},{4,3},{5,6},{6,5},{7,8},{8,7},{9,10},{10,... | collective-permute-start | bytes 245768 | tf_op jit(solution)/shard_map/ppermute | solution.py:413
  11.2 0.1 pad_add_fusion.at_ref
  11.3 0.0 collective-permute-done.3.far_near_ref
  11.3 0.0 copy-start.4
  11.3 0.7 copy-done.4
  12.0 0.0 copy-start
  12.0 1.1 %copy-done = f32[256,720]{0,1:T(8,128)S(1)} copy-done((f32[256,720]{0,1:T(8,128)S(1)}, f32[256,720]{0,1:T(8,128)}, u32[]{:S(2)}) %copy-start) | copy-done | bytes 737304
  13.1 0.0 copy-start.1
  13.1 1.1 %copy-done.1 = f32[80,2304]{1,0:T(8,128)S(1)} copy-done((f32[80,2304]{1,0:T(8,128)S(1)}, f32[80,2304]{1,0:T(8,128)}, u32[]{:S(2)}) %copy-start.1) | copy-done | bytes 737304
  14.2 0.0 copy-start.3
  14.2 1.2 %prepare.1 = (bf16[256,720]{1,0:T(8,128)(2,1)S(1)}, bf16[256,720]{1,0:T(8,128)(2,1)S(1)}, bf16[240,768]{1,0:T(8,128)(2,1)S(1)}, bf16[240,768]{1,0:T(8,128)(2,1)S...) custom-call(f32[720,256]{1,0:T(8,128)S(1)} %bitcast.10, ...), custom_call_target="tpu_custom_call" | custom-call | tf_op jit(solution)/shard_map/prepare/pallas_call | solution.py:131
  15.4 0.0 collective-permute-done.2.far_across_ref
  15.4 0.0 copy-done.3
  15.4 5.2 %forward.1 = (f32[2,2,256,256]{3,2,1,0:T(8,128)S(1)}, f32[320,128]{1,0:T(8,128)S(1)}) custom-call(s32[4]{0:T(128)S(1)} %pad_add_fusion.at_ref, f32[2,80,128]{2,1,0:T(8,128)S(1)} %bitcast.15, f32[2,80,128]{2,1,0:T(8,128)S(1)} %collective-permute-done.1.near_ref, f32[2,80,128]{2,1,0:T(8,128)S(1)} %collective-permute-done.across_ref, ...), custom_call_target="tpu_custom_call" | custom-call | tf_op jit(solution)/shard_map/forward/pallas_call | solution.py:209
  20.7 0.0 copy-start.2
  20.7 15.5 %all_to_all.10.fields_ref = f32[8,40,128]{2,1,0:T(8,128)S(1)} all-to-all(f32[8,40,128]{2,1,0:T(8,128)S(1)} %bitcast.12), channel_id=1, replica_groups=mesh['member_0'=4,'member_1'=2,'lat_0'=2,'lat_1'=4,'lat_2'=2] {'member_0..., dimensions={0} | all-to-all | bytes 327680 | tf_op jit(solution)/shard_map/all_to_all | solution.py:423
  36.1 0.0 copy-start.5
  36.1 0.0 copy-done.2
  36.1 0.7 copy-done.5
  36.8 0.9 %crps.1 = f32[8,48,128]{2,1,0:T(8,128)S(1)} custom-call(s32[4]{0:T(128)S(1)} %pad_add_fusion.at_ref, f32[2]{0:T(128)S(1)} %copy-done.5, f32[8,40,128]{2,1,0:T(8,128)S(1)} %all_to_all.10.fields_ref, f32[8,40,128]{2,1,0:T(8,128)S(1)} %bitcast.11), custom_call_target="tpu_custom_call" | custom-call | tf_op jit(solution)/shard_map/crps/pallas_call | solution.py:259
  37.7 10.9 %all_to_all.11.grads_ref = f32[8,48,128]{2,1,0:T(8,128)S(1)} all-to-all(f32[8,48,128]{2,1,0:T(8,128)S(1)} %crps.1), channel_id=1, replica_groups=mesh['member_0'=4,'member_1'=2,'lat_0'=2,'lat_1'=4,'lat_2'=2] {'member_0..., dimensions={0} | all-to-all | bytes 393216 | tf_op jit(solution)/shard_map/all_to_all | solution.py:427
  48.7 0.6 collect.1
  49.2 0.1 collective-permute-start.5
  49.3 0.1 collective-permute-start.4
  49.4 0.6 slopes.1.slope_ref
  50.0 5.3 %collective-permute-done.5.across_ref = f32[176,128]{1,0:T(8,128)S(1)} collective-permute-done((f32[176,128]{1,0:T(8,128)S(1)}, f32[176,128]{1,0:T(8,128)S(1)}, u32[]{:S(2)}, u32[]{:S(2)}) %collective-permute-start.5) | collective-permute-done | bytes 90144 | tf_op jit(solution)/shard_map/ppermute | solution.py:433
  55.4 0.0 collective-permute-done.4.near_ref
  55.4 2.5 %backward.2 = (f32[176,128]{1,0:T(8,128)S(1)}, f32[16,128]{1,0:T(8,128)S(1)}) custom-call(s32[4]{0:T(128)S(1)} %pad_add_fusion.at_ref, f32[176,128]{1,0:T(8,128)S(1)} %get-tuple-element.35.own_ref, f32[176,128]{1,0:T(8,128)S(1)} %collective-permute-done.4.near_ref, f32[176,128]{1,0:T(8,128)S(1)} %collective-permute-done.5.across_ref, ...), custom_call_target="tpu_custom_call" | custom-call | tf_op jit(solution)/shard_map/backward/pallas_call | solution.py:387
  57.8 0.1 collective-permute-start.7
  57.9 0.1 collective-permute-start.6
  58.0 0.1 collective-permute-start.8
  58.1 5.1 %collective-permute-done.8.far_ref = f32[16,128]{1,0:T(8,128)S(1)} collective-permute-done((f32[16,128]{1,0:T(8,128)S(1)}, f32[16,128]{1,0:T(8,128)S(1)}, u32[]{:S(2)}, u32[]{:S(2)}) %collective-permute-start.8) | collective-permute-done | bytes 8224 | tf_op jit(solution)/shard_map/ppermute | solution.py:439
  63.3 0.7 %collective-permute-done.7.across_ref = f32[176,128]{1,0:T(8,128)S(1)} collective-permute-done((f32[176,128]{1,0:T(8,128)S(1)}, f32[176,128]{1,0:T(8,128)S(1)}, u32[]{:S(2)}, u32[]{:S(2)}) %collective-permute-start.7) | collective-permute-done | bytes 90144 | tf_op jit(solution)/shard_map/ppermute | solution.py:438
  64.0 0.0 collective-permute-done.6.near_ref
  64.0 0.1 collective-permute-start.9
  64.1 3.1 %backward.3 = f32[160,128]{1,0:T(8,128)} custom-call(s32[4]{0:T(128)S(1)} %pad_add_fusion.at_ref, f32[176,128]{1,0:T(8,128)S(1)} %get-tuple-element.42.own_ref, f32[176,128]{1,0:T(8,128)S(1)} %collective-permute-done.6.near_ref, f32[176,128]{1,0:T(8,128)S(1)} %collective-permute-done.7.across_ref, f32[2,2,256,256]{3,2,1,0:T(8,128)S(1)} %slopes.1.slope_ref, ...), custom_call_target="tpu_custom_call" | custom-call | tf_op jit(solution)/shard_map/backward/pallas_call | solution.py:387
  67.2 0.5 collective-permute-done.9
  67.7 0.6 fusion
  (1 shorter events, 0.0 us)
Async XLA Ops:
  0.6 4.4 %collective-permute-start.1 = (f32[2,80,128]{2,1,0:T(8,128)}, f32[2,80,128]{2,1,0:T(8,128)S(1)}, u32[]{:S(2)}, u32[]{:S(2)}) collective-permute-start(f32[2,80,128]{2,1,0:T(8,128)} %bitcast.13), channel_id=1, source_target_pairs={{0,1},{1,0},{2,3},{3,2},{4,5},{5,4},{6,7},{7,6},{8,9},{9,8},{10,11... | collective-permute-start | bytes 245768 | tf_op jit(solution)/shard_map/ppermute | solution.py:411
  0.7 6.7 %collective-permute-start = (f32[2,80,128]{2,1,0:T(8,128)}, f32[2,80,128]{2,1,0:T(8,128)S(1)}, u32[]{:S(2)}, u32[]{:S(2)}) collective-permute-start(f32[2,80,128]{2,1,0:T(8,128)} %bitcast.14), channel_id=1, source_target_pairs={{0,15},{1,2},{2,1},{3,4},{4,3},{5,6},{6,5},{7,8},{8,7},{9,10},{10,... | collective-permute-start | bytes 245768 | tf_op jit(solution)/shard_map/ppermute | solution.py:412
  7.4 3.9 %collective-permute-start.3 = (f32[2,80,128]{2,1,0:T(8,128)S(1)}, f32[2,80,128]{2,1,0:T(8,128)S(1)}, u32[]{:S(2)}, u32[]{:S(2)}) collective-permute-start(f32[2,80,128]{2,1,0:T(8,128)S(1)} %collective-permute-done.across_ref), channel_id=1, source_target_pairs={{0,1},{1,0},{2,3},{3,2},{4,5},{5,4},{6,7},{7,6},{8,9},{9,8},{10,11... | collective-permute-start | bytes 245768 | tf_op jit(solution)/shard_map/ppermute | solution.py:415
  7.4 8.0 %collective-permute-start.2 = (f32[2,80,128]{2,1,0:T(8,128)S(1)}, f32[2,80,128]{2,1,0:T(8,128)S(1)}, u32[]{:S(2)}, u32[]{:S(2)}) collective-permute-start(f32[2,80,128]{2,1,0:T(8,128)S(1)} %collective-permute-done.1.near_ref), channel_id=1, source_target_pairs={{0,15},{1,2},{2,1},{3,4},{4,3},{5,6},{6,5},{7,8},{8,7},{9,10},{10,... | collective-permute-start | bytes 245768 | tf_op jit(solution)/shard_map/ppermute | solution.py:413
  11.3 0.7 copy-start.4
  12.0 1.1 %copy-start = (f32[256,720]{0,1:T(8,128)S(1)}, f32[256,720]{0,1:T(8,128)}, u32[]{:S(2)}) copy-start(f32[256,720]{0,1:T(8,128)} %param.9) | copy-start | bytes 2211844
  13.1 1.1 %copy-start.1 = (f32[80,2304]{1,0:T(8,128)S(1)}, f32[80,2304]{1,0:T(8,128)}, u32[]{:S(2)}) copy-start(f32[80,2304]{1,0:T(8,128)} %wout_hbm) | copy-start | bytes 2211844
  14.2 1.2 %copy-start.3 = (f32[1,2,80,128]{3,2,1,0:T(8,128)S(1)}, f32[1,2,80,128]{3,2,1,0:T(8,128)}, u32[]{:S(2)}) copy-start(f32[1,2,80,128]{3,2,1,0:T(8,128)} %param.6) | copy-start | bytes 245764
  20.7 15.5 %copy-start.2 = (f32[2,2,80,128]{3,2,1,0:T(8,128)S(1)}, f32[2,2,80,128]{3,2,1,0:T(8,128)}, u32[]{:S(2)}) copy-start(f32[2,2,80,128]{3,2,1,0:T(8,128)} %param.7) | copy-start | bytes 491524
  36.1 0.7 copy-start.5
  49.2 6.1 %collective-permute-start.5 = (f32[176,128]{1,0:T(8,128)S(1)}, f32[176,128]{1,0:T(8,128)S(1)}, u32[]{:S(2)}, u32[]{:S(2)}) collective-permute-start(f32[176,128]{1,0:T(8,128)S(1)} %get-tuple-element.35.own_ref), channel_id=1, source_target_pairs={{0,15},{1,2},{2,1},{3,4},{4,3},{5,6},{6,5},{7,8},{8,7},{9,10},{10,... | collective-permute-start | bytes 270344 | tf_op jit(solution)/shard_map/ppermute | solution.py:433
  49.3 6.1 %collective-permute-start.4 = (f32[176,128]{1,0:T(8,128)S(1)}, f32[176,128]{1,0:T(8,128)S(1)}, u32[]{:S(2)}, u32[]{:S(2)}) collective-permute-start(f32[176,128]{1,0:T(8,128)S(1)} %get-tuple-element.35.own_ref), channel_id=1, source_target_pairs={{0,1},{1,0},{2,3},{3,2},{4,5},{5,4},{6,7},{7,6},{8,9},{9,8},{10,11... | collective-permute-start | bytes 270344 | tf_op jit(solution)/shard_map/ppermute | solution.py:432
  57.8 6.1 %collective-permute-start.7 = (f32[176,128]{1,0:T(8,128)S(1)}, f32[176,128]{1,0:T(8,128)S(1)}, u32[]{:S(2)}, u32[]{:S(2)}) collective-permute-start(f32[176,128]{1,0:T(8,128)S(1)} %get-tuple-element.42.own_ref), channel_id=1, source_target_pairs={{0,15},{1,2},{2,1},{3,4},{4,3},{5,6},{6,5},{7,8},{8,7},{9,10},{10,... | collective-permute-start | bytes 270344 | tf_op jit(solution)/shard_map/ppermute | solution.py:438
  57.9 6.1 %collective-permute-start.6 = (f32[176,128]{1,0:T(8,128)S(1)}, f32[176,128]{1,0:T(8,128)S(1)}, u32[]{:S(2)}, u32[]{:S(2)}) collective-permute-start(f32[176,128]{1,0:T(8,128)S(1)} %get-tuple-element.42.own_ref), channel_id=1, source_target_pairs={{0,1},{1,0},{2,3},{3,2},{4,5},{5,4},{6,7},{7,6},{8,9},{9,8},{10,11... | collective-permute-start | bytes 270344 | tf_op jit(solution)/shard_map/ppermute | solution.py:437
  58.0 5.2 %collective-permute-start.8 = (f32[16,128]{1,0:T(8,128)S(1)}, f32[16,128]{1,0:T(8,128)S(1)}, u32[]{:S(2)}, u32[]{:S(2)}) collective-permute-start(f32[16,128]{1,0:T(8,128)S(1)} %get-tuple-element.43), channel_id=1, source_target_pairs={{0,4},{1,5},{2,6},{3,7},{4,0},{5,1},{6,2},{7,3},{8,12},{9,13},{10,... | collective-permute-start | bytes 24584 | tf_op jit(solution)/shard_map/ppermute | solution.py:439
  64.0 3.7 %collective-permute-start.9 = (f32[16,128]{1,0:T(8,128)S(1)}, f32[16,128]{1,0:T(8,128)S(1)}, u32[]{:S(2)}, u32[]{:S(2)}) collective-permute-start(f32[16,128]{1,0:T(8,128)S(1)} %merge.1), channel_id=1, source_target_pairs={{0,8},{1,9},{2,10},{3,11},{4,12},{5,13},{6,14},{7,15},{8,0},{9,1},... | collective-permute-start | bytes 24584 | tf_op jit(solution)/shard_map/ppermute | solution.py:442

commit v3 on v2

v3 whole, which is shorter than its diff:
```python
import functools

import jax
import jax.numpy as jnp
from jax import lax
from jax.experimental import pallas as pl
from jax.experimental.pallas import tpu as pltpu
from jax.sharding import Mesh
from jax.sharding import PartitionSpec as P

MEMBER = ("member_0", "member_1")
LAT = ("lat_0", "lat_1", "lat_2")

smooth_width = 0.1
gelu_scale = 0.7978845608028654
gelu_cubic = 0.044715
slab_count = 16

f32 = jnp.float32
bf16 = jnp.bfloat16
params = pltpu.CompilerParams(vmem_limit_bytes=16 * 1024 * 1024)


def split(value):
    high = value.astype(bf16)
    return high, (value - high.astype(f32)).astype(bf16)


def product(left, right):
    dot = functools.partial(jnp.dot, preferred_element_type=f32)
    return dot(left[0], right[0]) + (dot(left[0], right[1]) + dot(left[1], right[0]))


def from_left(row):
    lane = lax.broadcasted_iota(jnp.int32, row.shape, 1)
    return jnp.where(lane == 0, 0.0, pltpu.roll(row, 1, 1))


def from_right(row):
    lane = lax.broadcasted_iota(jnp.int32, row.shape, 1)
    return jnp.where(lane == row.shape[1] - 1, 0.0, pltpu.roll(row, row.shape[1] - 1, 1))


def put_twice(refs, index, height, part, values):
    width = values[0].shape[1]
    size = values[0].shape[0]
    for ref, value in zip(refs, values):
        base = index * height + part * size
        if base + size <= ref.shape[0]:
            ref[base : base + size, :width] = value
        if index:
            ref[base - height : base - height + size, width:] = value


def put_windows(refs, index, row):
    height = 3 * row.shape[0]
    for part, shifted in enumerate((from_left(row), row, from_right(row))):
        put_twice(refs, index, height, part, split(shifted))


def read(refs, start, size):
    return tuple(ref[start : start + size, :] for ref in refs)


def to_channels(weights, windows, pair, channels):
    return product(weights, read(windows, pair * 3 * channels, 9 * channels))


def from_channels(weights, hidden, pair, channels, outer):
    mixed = product(weights, read(hidden, pair * channels, 3 * channels))
    width = mixed.shape[1] // 2
    rows = []
    for half in range(2):
        part = mixed[:, half * width : (half + 1) * width]
        rows.append(
            from_left(part[:outer])
            + part[outer : 2 * outer]
            + from_right(part[2 * outer :])
        )
    return rows


def gelu(x):
    return 0.5 * x * (1.0 + jnp.tanh(gelu_scale * (x + gelu_cubic * x * x * x)))


def gelu_slope(x):
    t = jnp.tanh(gelu_scale * (x + gelu_cubic * x * x * x))
    inner = gelu_scale * (1.0 + 3.0 * gelu_cubic * x * x)
    return 0.5 * (1.0 + t) + 0.5 * x * (1.0 - t * t) * inner


def fetch(pairs, arrived):
    copies = [pltpu.make_async_copy(*pair, arrived.at[i]) for i, pair in enumerate(pairs)]
    for copy in copies:
        copy.start()
    for copy in copies:
        copy.wait()


def prepare_kernel(win_hbm, wout_hbm, bias_hbm, lat_hbm, in_hi, in_lo, out_hi, out_lo, wide_bias_ref, wide_lat_ref,
                   win_ref, wout_ref, bias_ref, lat_ref, arrived):
    fetch(((win_hbm, win_ref), (wout_hbm, wout_ref), (bias_hbm, bias_ref), (lat_hbm, lat_ref)), arrived)
    outer, width = wout_ref.shape
    hidden = width // 9
    high, low = split(win_ref[...].T)
    in_hi[...] = high
    in_lo[...] = low
    for a in range(3):
        for b in range(3):
            tap = 3 * a + b
            high, low = split(wout_ref[:, tap * hidden : (tap + 1) * hidden])
            out_hi[b * outer : (b + 1) * outer, a * hidden : (a + 1) * hidden] = high
            out_lo[b * outer : (b + 1) * outer, a * hidden : (a + 1) * hidden] = low
    wide_bias_ref[...] = jnp.broadcast_to(bias_ref[...], wide_bias_ref.shape[::-1]).T
    for row in range(2):
        one = jnp.broadcast_to(lat_ref[:, row : row + 1], (8, wide_lat_ref.shape[1]))
        wide_lat_ref[8 * row : 8 * (row + 1), :] = one


def prepare(weight_in, weight_out, bias, lat_weight, width):
    taps_in, hidden = weight_in.shape
    outer = weight_out.shape[0]
    arrays = (weight_in, weight_out, bias, lat_weight)
    shapes = [(hidden, taps_in)] * 2 + [(3 * outer, 3 * hidden)] * 2
    return pl.pallas_call(
        prepare_kernel,
        out_shape=[jax.ShapeDtypeStruct(shape, bf16) for shape in shapes]
        + [jax.ShapeDtypeStruct((hidden, width), f32), jax.ShapeDtypeStruct((16, width), f32)],
        in_specs=[pl.BlockSpec(memory_space=pltpu.HBM)] * 4,
        scratch_shapes=[pltpu.VMEM(array.shape, f32) for array in arrays] + [pltpu.SemaphoreType.DMA((4,))],
        compiler_params=params,
        name="prepare",
    )(*(pltpu.with_memory_space_constraint(array, pltpu.HBM) for array in arrays))


def prepare_back_kernel(win_hbm, wout_hbm, before_ref, outb_hi, outb_lo, inb_hi, inb_lo, slope_ref,
                        stack, win_ref, wout_ref, arrived):
    pairs = ((win_hbm, win_ref), (wout_hbm, wout_ref))
    copies = [pltpu.make_async_copy(*pair, arrived.at[i]) for i, pair in enumerate(pairs)]
    for copy in copies:
        copy.start()
    for step in range(2):
        for pair in range(2):
            slope_ref[step, pair] = gelu_slope(before_ref[step, pair])
    for copy in copies:
        copy.wait()
    outer, width = wout_ref.shape
    hidden = width // 9
    inner = win_ref.shape[0] // 9
    for a in range(3):
        for b in range(3):
            tap = 3 * a + b
            stack[(8 - tap) * outer : (9 - tap) * outer, :] = wout_ref[:, tap * hidden : (tap + 1) * hidden]
            high, low = split(win_ref[tap * inner : (tap + 1) * inner, :])
            j, k = 2 - a, 2 - b
            inb_hi[k * inner : (k + 1) * inner, j * hidden : (j + 1) * hidden] = high
            inb_lo[k * inner : (k + 1) * inner, j * hidden : (j + 1) * hidden] = low
    high, low = split(stack[...].T)
    outb_hi[...] = high
    outb_lo[...] = low


def prepare_back(weight_in, weight_out, before):
    taps_in, hidden = weight_in.shape
    outer = weight_out.shape[0]
    inner = taps_in // 9
    arrays = (weight_in, weight_out)
    shapes = [(hidden, 9 * outer)] * 2 + [(3 * inner, 3 * hidden)] * 2
    hbm = pl.BlockSpec(memory_space=pltpu.HBM)
    return pl.pallas_call(
        prepare_back_kernel,
        out_shape=[jax.ShapeDtypeStruct(shape, bf16) for shape in shapes]
        + [jax.ShapeDtypeStruct(before.shape, f32)],
        in_specs=[hbm, hbm, pl.BlockSpec(memory_space=pltpu.VMEM)],
        scratch_shapes=[pltpu.VMEM((9 * outer, hidden), f32)]
        + [pltpu.VMEM(array.shape, f32) for array in arrays]
        + [pltpu.SemaphoreType.DMA((2,))],
        compiler_params=params,
        name="prepare_back",
    )(*(pltpu.with_memory_space_constraint(array, pltpu.HBM) for array in arrays), before)


def inside(row):
    index = lax.axis_index(LAT) * 2 + row
    return (index >= 0) & (index < 2 * slab_count)


def is_even():
    return lax.rem(lax.axis_index(LAT), 2) == 0


def forward_kernel(own_ref, near_ref, across_ref, far_across_ref, far_near_ref, bias_ref,
                   in_hi, in_lo, out_hi, out_lo, before_ref, fields_ref, wide_hi, wide_lo, hid_hi, hid_lo):
    channels, width = own_ref.shape[1:]
    hidden = in_hi.shape[0]
    even = is_even()
    wide = (wide_hi, wide_lo)
    hid = (hid_hi, hid_lo)
    w_in = (in_hi[...], in_lo[...])
    w_out = (out_hi[...], out_lo[...])
    bias = jnp.concatenate([bias_ref[...]] * 2, axis=1)

    def initial(index):
        slab, row = index // 2, index % 2
        if slab == 2:
            return own_ref[row]
        first, second = {
            0: (far_across_ref, far_near_ref),
            1: (across_ref, near_ref),
            3: (near_ref, across_ref),
            4: (far_near_ref, far_across_ref),
        }[slab]
        value = jnp.where(even, first[row], second[row])
        return jnp.where(inside(index - 4), value, 0.0)

    def advance(field, first, count, keep, step):
        for index in range(count):
            put_windows(wide, index, field(index))
        for pair in range(0, count - 2, 2):
            before = to_channels(w_in, wide, pair, channels) + bias
            if pair in keep:
                before_ref[step, keep.index(pair)] = before
            active = gelu(before)
            for half in range(2):
                row = active[:, half * width : (half + 1) * width]
                row = jnp.where(inside(first + 1 + pair + half), row, 0.0)
                put_twice(hid, pair + half, hidden, 0, split(row))
        result = []
        for pair in range(0, count - 4, 2):
            moved = from_channels(w_out, hid, pair, hidden, channels)
            for half in range(2):
                row = field(pair + 2 + half) + moved[half]
                result.append(jnp.where(inside(first + 2 + pair + half), row, 0.0))
        return result

    first = advance(initial, -4, 10, (2, 4), 0)
    for half in range(2):
        fields_ref[half * channels : (half + 1) * channels, :] = first[2 + half]
    second = advance(lambda index: first[index], -2, 6, (0, 2), 1)
    for half in range(2):
        fields_ref[(2 + half) * channels : (3 + half) * channels, :] = second[half]


def forward(own, near, across, far_across, far_near, bias, w_in, w_out):
    channels, width = own.shape[1:]
    hidden = w_in[0].shape[0]
    vmem = pl.BlockSpec(memory_space=pltpu.VMEM)
    return pl.pallas_call(
        forward_kernel,
        in_specs=[vmem] * 10,
        out_shape=[
            jax.ShapeDtypeStruct((2, 2, hidden, 2 * width), f32),
            jax.ShapeDtypeStruct((4 * channels, width), f32),
        ],
        scratch_shapes=[pltpu.VMEM((30 * channels, 2 * width), bf16)] * 2
        + [pltpu.VMEM((8 * hidden, 2 * width), bf16)] * 2,
        compiler_params=params,
        name="forward",
    )(own, near, across, far_across, far_near, bias, *w_in, *w_out)


def crps_kernel(weight_ref, fields_ref, targets_ref, out_ref):
    members, height, width = fields_ref.shape
    mine = lax.axis_index(MEMBER)
    weight = jnp.where(lax.rem(lax.div(mine, 2), 2) == 0, weight_ref[:8, :], weight_ref[8:, :])
    softness = smooth_width * smooth_width
    loss = jnp.zeros((8, width), f32)
    for tile in range(0, height, 8):
        values = [fields_ref[m, tile : tile + 8, :] for m in range(members)]
        truth = targets_ref[mine, tile : tile + 8, :]
        direct = jnp.zeros((8, width), f32)
        pairs = jnp.full((8, width), members * smooth_width, f32)
        slopes = [jnp.zeros((8, width), f32) for m in range(members)]
        grads = []
        for m in range(members):
            error = values[m] - truth
            square = error * error + softness
            inverse = lax.rsqrt(square)
            direct = direct + square * inverse
            grads.append(error * inverse)
            for other in range(m + 1, members):
                gap = values[m] - values[other]
                square = gap * gap + softness
                inverse = lax.rsqrt(square)
                pairs = pairs + 2.0 * square * inverse
                slope = gap * inverse
                slopes[m] = slopes[m] + slope
                slopes[other] = slopes[other] - slope
        loss = loss + weight * (direct - pairs / (2.0 * (members - 1)))
        for m in range(members):
            out_ref[m, tile : tile + 8, :] = weight * (grads[m] - slopes[m] / (members - 1))
    for m in range(members):
        out_ref[m, height : height + 8, :] = loss


def crps(weights, fields, targets):
    members, height, width = fields.shape
    return pl.pallas_call(
        crps_kernel,
        out_shape=jax.ShapeDtypeStruct((members, height + 8, width), f32),
        compiler_params=params,
        name="crps",
    )(weights, fields, targets)


def collect_kernel(grads_ref, first_ref, second_ref):
    chunks, height, width = grads_ref.shape
    height = height - 8
    half = chunks // 2
    total = grads_ref[0, height : height + 8, :]
    for chunk in range(1, chunks):
        total = total + grads_ref[chunk, height : height + 8, :]
    for chunk in range(half):
        first_ref[chunk * height : (chunk + 1) * height, :] = grads_ref[chunk, :height, :]
        second_ref[chunk * height : (chunk + 1) * height, :] = grads_ref[half + chunk, :height, :]
    known = jnp.broadcast_to(jnp.sum(total, axis=0, keepdims=True), (slab_count, width))
    slab = lax.broadcasted_iota(jnp.int32, known.shape, 0)
    second_ref[half * height :, :] = jnp.where(slab == lax.axis_index(LAT), known, 0.0)


def collect(grads):
    chunks, height, width = grads.shape
    count = chunks // 2 * (height - 8)
    return pl.pallas_call(
        collect_kernel,
        out_shape=[
            jax.ShapeDtypeStruct((count, width), f32),
            jax.ShapeDtypeStruct((count + slab_count, width), f32),
        ],
        compiler_params=params,
        name="collect",
    )(grads)


def merged(*known):
    result = known[0]
    for other in known[1:]:
        result = jnp.where(result != 0.0, result, other)
    return result


def merge_kernel(own_ref, near_ref, across_ref, *rest):
    count = own_ref.shape[0] - slab_count
    tables = [ref[count:, :] for ref in (own_ref, near_ref, across_ref)]
    rest[-1][...] = merged(*tables, *(ref[...] for ref in rest[:-1]))


def merge(own, near, across, *far):
    return pl.pallas_call(
        merge_kernel,
        out_shape=jax.ShapeDtypeStruct((slab_count, own.shape[1]), f32),
        compiler_params=params,
        name="merge",
    )(own, near, across, *far)


def backward_kernel(step, own_ref, near_ref, across_ref, slope_ref, outb_hi, outb_lo, inb_hi, inb_lo,
                    *rest):
    added, known_ref = rest[:-5][:1], rest[:-5][1:]
    out_ref, wide_hi, wide_lo, hid_hi, hid_lo = rest[-5:]
    width = own_ref.shape[1]
    channels = (own_ref.shape[0] - slab_count) // 2
    hidden = outb_hi.shape[0]
    even = is_even()
    wide = (wide_hi, wide_lo)
    hid = (hid_hi, hid_lo)
    w_out = (outb_hi[...], outb_lo[...])
    w_in = (inb_hi[...], inb_lo[...])

    def take(ref, row):
        return ref[row * channels : (row + 1) * channels, :]

    def put_beside(index, first, second, row):
        value = jnp.where(even, take(first, row), take(second, row))
        value = jnp.where(inside(index - 2), value, 0.0)
        put_windows(wide, index, value)

    for row in range(2):
        put_windows(wide, 2 + row, take(own_ref, row))
    for row in range(2):
        put_beside(row, across_ref, near_ref, row)
        put_beside(4 + row, near_ref, across_ref, row)
    for pair in (0, 2):
        grads = to_channels(w_out, wide, pair, channels) * slope_ref[step, pair // 2]
        for half in range(2):
            row = grads[:, half * width : (half + 1) * width]
            row = jnp.where(inside(pair + half - 1), row, 0.0)
            put_twice(hid, pair + half, hidden, 0, split(row))
    moved = from_channels(w_in, hid, 0, hidden, channels)
    for row in range(2):
        total = take(own_ref, row) + moved[row]
        for extra in added:
            total = total + take(extra, row)
        out_ref[row * channels : (row + 1) * channels, :] = total
    if known_ref:
        last = 2 * channels
        out_ref[last:, :] = known_ref[0][...]


def backward(step, own, near, across, slopes, w_out, w_in, *added):
    count, width = own.shape
    channels = (count - slab_count) // 2
    hidden = w_out[0].shape[0]
    vmem = pl.BlockSpec(memory_space=pltpu.VMEM)
    return pl.pallas_call(
        functools.partial(backward_kernel, step),
        in_specs=[vmem] * (8 + len(added)),
        out_shape=jax.ShapeDtypeStruct((count if step else 2 * channels, width), f32),
        scratch_shapes=[pltpu.VMEM((18 * channels, 2 * width), bf16)] * 2
        + [pltpu.VMEM((4 * hidden, 2 * width), bf16)] * 2,
        compiler_params=params,
        name="backward",
    )(own, near, across, slopes, *w_out, *w_in, *added)


def on_device(initial_states, targets, lat_weight, weight_in, weight_out, hidden_bias):
    members = lax.axis_size(MEMBER)
    slabs = lax.axis_size(LAT)
    steps, slab_rows, channels, width = targets.shape
    rows = slabs * slab_rows
    near = [(i, i ^ 1) for i in range(slabs)]
    across = [(i, (i + 1 if i % 2 else i - 1) % slabs) for i in range(slabs)]

    own = initial_states[0]
    beside = lax.ppermute(own, LAT, near)
    crossed = lax.ppermute(own, LAT, across)
    far_crossed = lax.ppermute(beside, LAT, across)
    ready = prepare(weight_in.T, weight_out, hidden_bias[None, :], lat_weight[None, :], width)
    crossed, beside = lax.optimization_barrier((crossed, beside))
    far_beside = lax.ppermute(crossed, LAT, near)
    before, fields = forward(
        own, beside, crossed, far_crossed, far_beside, ready[4], ready[:2], ready[2:4]
    )
    height = steps * slab_rows * channels // members
    chunks = lax.all_to_all(
        fields.reshape(members, height, width), MEMBER, split_axis=0, concat_axis=0, tiled=True
    )
    grads = crps(ready[5], chunks, targets.reshape(members, height, width))
    grads = lax.all_to_all(grads, MEMBER, split_axis=0, concat_axis=0, tiled=True)
    grads, before = lax.optimization_barrier((grads, before))
    *back, slopes = prepare_back(weight_in.T, weight_out, before)
    w_out_back, w_in_back = back[:2], back[2:]
    first_grads, message = collect(grads)

    beside = lax.ppermute(message, LAT, near)
    crossed = lax.ppermute(message, LAT, across)
    known = merge(message, beside, crossed)
    far = lax.ppermute(known, LAT, [(i, i ^ 4) for i in range(slabs)])
    message = backward(1, message, beside, crossed, slopes, w_out_back, w_in_back, first_grads, known)
    message, far = lax.optimization_barrier((message, far))
    beside = lax.ppermute(message, LAT, near)
    crossed = lax.ppermute(message, LAT, across)
    known = merge(message, beside, crossed, far)
    gradient = backward(0, message, beside, crossed, slopes, w_out_back, w_in_back)
    opposite = lax.ppermute(known, LAT, [(i, i ^ 8) for i in range(slabs)])
    total = jnp.sum(jnp.where(known != 0.0, known, opposite))
    loss = total / (members * steps * rows * channels * width)
    return gradient.reshape(initial_states.shape), loss


def solution(mesh):
    torus = Mesh(
        mesh.devices.reshape(4, 2, 2, 4, 2), ("member_0", "member_1", "lat_0", "lat_1", "lat_2")
    )
    placed = (P(MEMBER, LAT, None, None), P(None, LAT, None, None), P(LAT), P(), P(), P())
    return jax.shard_map(
        on_device,
        mesh=torus,
        in_specs=placed,
        out_specs=(P(MEMBER, LAT, None, None), P()),
        check_vma=False,
    )
```

time: 70.9 us -> 68.4 us (0.965)
  local copies, waits for them, and re-layouts: 3.57 us -> 0.01 us
  waiting for transfers between devices: 14.1 us -> 16.8 us
  Pallas kernels: 14.1 us -> 12.9 us
    ppermute x1, waiting for transfers between devices: 5.14 us -> 1.55 us  [on_device(): far = lax.ppermute(known, LAT, [(i, i ^ 4) for i in range(slabs)])]
    ppermute x2, waiting for transfers between devices: 6.05 us -> 9.64 us  [on_device(): crossed = lax.ppermute(message, LAT, across)]
    unnamed x12 -> x4, local copies, waits for them, and re-layouts: 3.57 us -> 0.01 us
    ppermute x2, waiting for transfers between devices: 0.01 us -> 2.42 us  [on_device(): beside = lax.ppermute(message, LAT, near)]
    pallas_call x7 -> x8, Pallas kernels: 12.9 us -> 11.1 us  [the longest x1 4.65 us: forward(): pl.pallas_call(forward_kernel, in_specs=[vmem] * 10, out_shape=[jax.Shape...]
    ppermute x1, starting transfers between devices: 0.09 us -> 1.02 us  [on_device(): opposite = lax.ppermute(known, LAT, [(i, i ^ 8) for i in range(slabs)])]
  transfers between devices with their start and end apart: 10 -> 10, of which waited for: 5 -> 8; matrix products, arithmetic and copies ran while one was open for 0% -> 0% of each run, Pallas kernels for 7% -> 12%
where the time goes in v3:
time: 68.4 us; the launch traced here: 68.1 us
  blocking collectives  26.8 us (39%)
  waiting for transfers between devices  16.8 us (25%)
  Pallas kernels  12.9 us (19%)
  starting transfers between devices  8.6 us (13%)
  between operations  2.47 us (4%)
    all_to_all x1, blocking collectives, on_device(): lax.all_to_all(fields.reshape(members, height, width), MEMBER, split_axis...  15.8 us
    all_to_all x1, blocking collectives, on_device(): lax.all_to_all(grads, MEMBER, split_axis=0, concat_axis=0, tiled=True)  10.9 us
    ppermute x2, waiting for transfers between devices, on_device(): crossed = lax.ppermute(message, LAT, across)  9.64 us
    pallas_call x1, Pallas kernels, forward(): pl.pallas_call(forward_kernel, in_specs=[vmem] * 10, out_shape=[jax.Shape...  4.65 us
    pallas_call x2, Pallas kernels, backward(): pl.pallas_call(functools.partial(backward_kernel, step), in_specs=[vmem]...  4.49 us
    ppermute x1, starting transfers between devices, on_device(): crossed = lax.ppermute(own, LAT, across)  3.71 us
    ppermute x1, starting transfers between devices, on_device(): far_crossed = lax.ppermute(beside, LAT, across)  3.64 us
    ppermute x1, waiting for transfers between devices, on_device(): crossed = lax.ppermute(own, LAT, across)  2.55 us
  transfers between devices with their start and end apart: 10, of which 8 were waited for; matrix products, arithmetic and copies ran while one was open for 0% of the time, Pallas kernels for 12%

profile of v3, /device:TPU:0, one launch (start us, length us, event | category | flops | bytes accessed | tf_op | source)
XLA Modules:
  0.0 68.1 jit_solution(16968946548992556819)
XLA Ops:
  0.6 3.7 %collective-permute-start = (f32[2,80,128]{2,1,0:T(8,128)}, f32[2,80,128]{2,1,0:T(8,128)S(1)}, u32[]{:S(2)}, u32[]{:S(2)}) collective-permute-start(f32[2,80,128]{2,1,0:T(8,128)} %bitcast.9), channel_id=1, source_target_pairs={{0,15},{1,2},{2,1},{3,4},{4,3},{5,6},{6,5},{7,8},{8,7},{9,10},{10,... | collective-permute-start | bytes 245768 | tf_op jit(solution)/shard_map/ppermute | solution.py:427
  4.3 0.0 collective-permute-start.1
  4.3 2.5 %collective-permute-done.across_ref = f32[2,80,128]{2,1,0:T(8,128)S(1)} collective-permute-done((f32[2,80,128]{2,1,0:T(8,128)}, f32[2,80,128]{2,1,0:T(8,128)S(1)}, u32[]{:S(2)}, u32[]{:S(2)}) %collective-permute-start) | collective-permute-done | bytes 81952 | tf_op jit(solution)/shard_map/ppermute | solution.py:427
  6.9 0.0 collective-permute-done.1.near_ref
  6.9 3.6 %collective-permute-start.2 = (f32[2,80,128]{2,1,0:T(8,128)S(1)}, f32[2,80,128]{2,1,0:T(8,128)S(1)}, u32[]{:S(2)}, u32[]{:S(2)}) collective-permute-start(f32[2,80,128]{2,1,0:T(8,128)S(1)} %collective-permute-done.1.near_ref), channel_id=1, source_target_pairs={{0,15},{1,2},{2,1},{3,4},{4,3},{5,6},{6,5},{7,8},{8,7},{9,10},{10,... | collective-permute-start | bytes 245768 | tf_op jit(solution)/shard_map/ppermute | solution.py:428
  10.5 0.0 collective-permute-start.3
  10.5 0.0 copy-start.1
  10.5 1.8 %prepare.1 = (bf16[256,720]{1,0:T(8,128)(2,1)S(1)}, bf16[256,720]{1,0:T(8,128)(2,1)S(1)}, bf16[240,768]{1,0:T(8,128)(2,1)S(1)}, bf16[240,768]{1,0:T(8,128)(2,1)S...) custom-call(f32[720,256]{1,0:T(8,128)} %bitcast.12, f32[80,2304]{1,0:T(8,128)} %wout_hbm.3, f32[1,256]{1,0:T(1,128)} %bitcast.15, ...), custom_call_target="tpu_custom_call" | custom-call | tf_op jit(solution)/shard_map/prepare/pallas_call | solution.py:126
  12.3 0.6 collective-permute-done.2.far_across_ref
  12.9 0.0 collective-permute-done.3.far_near_ref
  12.9 0.0 copy-done.1
  12.9 4.7 %forward.1 = (f32[2,2,256,256]{3,2,1,0:T(8,128)S(1)}, f32[320,128]{1,0:T(8,128)S(1)}) custom-call(f32[2,80,128]{2,1,0:T(8,128)S(1)} %bitcast.11, f32[2,80,128]{2,1,0:T(8,128)S(1)} %collective-permute-done.1.near_ref, f32[2,80,128]{2,1,0:T(8,128)S(1)} %collective-permute-done.across_ref, f32[2,80,128]{2,1,0:T(8,128)S(1)} %collective-permute-done.2.far_across_ref, ...), custom_call_target="tpu_custom_call" | custom-call | tf_op jit(solution)/shard_map/forward/pallas_call | solution.py:249
  17.5 0.0 copy-start
  17.6 15.8 %all_to_all.10.fields_ref = f32[8,40,128]{2,1,0:T(8,128)S(1)} all-to-all(f32[8,40,128]{2,1,0:T(8,128)S(1)} %bitcast.8), channel_id=1, replica_groups=mesh['member_0'=4,'member_1'=2,'lat_0'=2,'lat_1'=4,'lat_2'=2] {'member_0..., dimensions={0} | all-to-all | bytes 327680 | tf_op jit(solution)/shard_map/all_to_all | solution.py:436
  33.4 0.0 copy-done
  33.4 0.2 crps.1
  33.6 10.9 %all_to_all.11.grads_ref = f32[8,48,128]{2,1,0:T(8,128)S(1)} all-to-all(f32[8,48,128]{2,1,0:T(8,128)S(1)} %crps.1), channel_id=1, replica_groups=mesh['member_0'=4,'member_1'=2,'lat_0'=2,'lat_1'=4,'lat_2'=2] {'member_0..., dimensions={0} | all-to-all | bytes 393216 | tf_op jit(solution)/shard_map/all_to_all | solution.py:440
  44.6 0.1 collective-permute-start.4
  44.7 0.1 collective-permute-start.5
  44.8 1.1 %collective-permute-done.4.near_ref = f32[176,128]{1,0:T(8,128)S(1)} collective-permute-done((f32[176,128]{1,0:T(8,128)S(1)}, f32[176,128]{1,0:T(8,128)S(1)}, u32[]{:S(2)}, u32[]{:S(2)}) %collective-permute-start.4) | collective-permute-done | bytes 90144 | tf_op jit(solution)/shard_map/ppermute | solution.py:446
  46.0 4.9 %collective-permute-done.5.across_ref = f32[176,128]{1,0:T(8,128)S(1)} collective-permute-done((f32[176,128]{1,0:T(8,128)S(1)}, f32[176,128]{1,0:T(8,128)S(1)}, u32[]{:S(2)}, u32[]{:S(2)}) %collective-permute-start.5) | collective-permute-done | bytes 90144 | tf_op jit(solution)/shard_map/ppermute | solution.py:447
  50.8 0.0 collective-permute-start.6
  50.8 1.7 %prepare_back.1 = (bf16[256,720]{1,0:T(8,128)(2,1)S(1)}, bf16[256,720]{1,0:T(8,128)(2,1)S(1)}, bf16[240,768]{1,0:T(8,128)(2,1)S(1)}, bf16[240,768]{1,0:T(8,128)(2,1)S(1)}, f32[2,2,256,256]{3,2,1,0:T(8,128)S(1)}) custom-call(f32[720,256]{1,0:T(8,128)} %bitcast.13, f32[80,2304]{1,0:T(8,128)} %wout_hbm.3, f32[2,2,256,256]{3,2,1,0:T(8,128)S(1)} %get-tuple-element.35.before_ref), custom_call_target="tpu_custom_call" | custom-call | tf_op jit(solution)/shard_map/prepare_back/pallas_call | solution.py:171
  52.5 1.9 %backward.2.own_ref = f32[176,128]{1,0:T(8,128)S(1)} custom-call(f32[176,128]{1,0:T(8,128)S(1)} %get-tuple-element.34.own_ref, f32[176,128]{1,0:T(8,128)S(1)} %collective-permute-done.4.near_ref, f32[176,128]{1,0:T(8,128)S(1)} %collective-permute-done.5.across_ref, f32[2,2,256,256]{3,2,1,0:T(8,128)S(1)} %get-tuple-element.36.slope_ref, ...), custom_call_target="tpu_custom_call" | custom-call | tf_op jit(solution)/shard_map/backward/pallas_call | solution.py:406
  54.4 1.5 %collective-permute-done.6.rest_0_ = f32[16,128]{1,0:T(8,128)S(1)} collective-permute-done((f32[16,128]{1,0:T(8,128)S(1)}, f32[16,128]{1,0:T(8,128)S(1)}, u32[]{:S(2)}, u32[]{:S(2)}) %collective-permute-start.6) | collective-permute-done | bytes 8224 | tf_op jit(solution)/shard_map/ppermute | solution.py:449
  56.0 0.0 collective-permute-start.7
  56.0 0.0 collective-permute-start.8
  56.0 1.3 %collective-permute-done.7.near_ref = f32[176,128]{1,0:T(8,128)S(1)} collective-permute-done((f32[176,128]{1,0:T(8,128)S(1)}, f32[176,128]{1,0:T(8,128)S(1)}, u32[]{:S(2)}, u32[]{:S(2)}) %collective-permute-start.7) | collective-permute-done | bytes 90144 | tf_op jit(solution)/shard_map/ppermute | solution.py:452
  57.3 4.8 %collective-permute-done.8.across_ref = f32[176,128]{1,0:T(8,128)S(1)} collective-permute-done((f32[176,128]{1,0:T(8,128)S(1)}, f32[176,128]{1,0:T(8,128)S(1)}, u32[]{:S(2)}, u32[]{:S(2)}) %collective-permute-start.8) | collective-permute-done | bytes 90144 | tf_op jit(solution)/shard_map/ppermute | solution.py:453
  62.1 1.0 %collective-permute-start.9 = (f32[16,128]{1,0:T(8,128)S(1)}, f32[16,128]{1,0:T(8,128)S(1)}, u32[]{:S(2)}, u32[]{:S(2)}) collective-permute-start(f32[16,128]{1,0:T(8,128)S(1)} %merge.3), channel_id=1, source_target_pairs={{0,8},{1,9},{2,10},{3,11},{4,12},{5,13},{6,14},{7,15},{8,0},{9,1},... | collective-permute-start | bytes 24584 | tf_op jit(solution)/shard_map/ppermute | solution.py:456
  63.1 2.6 %backward.3 = f32[160,128]{1,0:T(8,128)} custom-call(f32[176,128]{1,0:T(8,128)S(1)} %backward.2.own_ref, f32[176,128]{1,0:T(8,128)S(1)} %collective-permute-done.7.near_ref, f32[176,128]{1,0:T(8,128)S(1)} %collective-permute-done.8.across_ref, f32[2,2,256,256]{3,2,1,0:T(8,128)S(1)} %get-tuple-element.36.slope_ref, ...), custom_call_target="tpu_custom_call" | custom-call | tf_op jit(solution)/shard_map/backward/pallas_call | solution.py:406
  65.6 0.1 collective-permute-done.9
  65.7 0.6 fusion
  (3 shorter events, 0.0 us)
Async XLA Ops:
  0.6 6.3 %collective-permute-start = (f32[2,80,128]{2,1,0:T(8,128)}, f32[2,80,128]{2,1,0:T(8,128)S(1)}, u32[]{:S(2)}, u32[]{:S(2)}) collective-permute-start(f32[2,80,128]{2,1,0:T(8,128)} %bitcast.9), channel_id=1, source_target_pairs={{0,15},{1,2},{2,1},{3,4},{4,3},{5,6},{6,5},{7,8},{8,7},{9,10},{10,... | collective-permute-start | bytes 245768 | tf_op jit(solution)/shard_map/ppermute | solution.py:427
  4.3 2.6 %collective-permute-start.1 = (f32[2,80,128]{2,1,0:T(8,128)}, f32[2,80,128]{2,1,0:T(8,128)S(1)}, u32[]{:S(2)}, u32[]{:S(2)}) collective-permute-start(f32[2,80,128]{2,1,0:T(8,128)} %bitcast.10), channel_id=1, source_target_pairs={{0,1},{1,0},{2,3},{3,2},{4,5},{5,4},{6,7},{7,6},{8,9},{9,8},{10,11... | collective-permute-start | bytes 245768 | tf_op jit(solution)/shard_map/ppermute | solution.py:426
  6.9 6.0 %collective-permute-start.2 = (f32[2,80,128]{2,1,0:T(8,128)S(1)}, f32[2,80,128]{2,1,0:T(8,128)S(1)}, u32[]{:S(2)}, u32[]{:S(2)}) collective-permute-start(f32[2,80,128]{2,1,0:T(8,128)S(1)} %collective-permute-done.1.near_ref), channel_id=1, source_target_pairs={{0,15},{1,2},{2,1},{3,4},{4,3},{5,6},{6,5},{7,8},{8,7},{9,10},{10,... | collective-permute-start | bytes 245768 | tf_op jit(solution)/shard_map/ppermute | solution.py:428
  10.5 2.3 %collective-permute-start.3 = (f32[2,80,128]{2,1,0:T(8,128)S(1)}, f32[2,80,128]{2,1,0:T(8,128)S(1)}, u32[]{:S(2)}, u32[]{:S(2)}) collective-permute-start(f32[2,80,128]{2,1,0:T(8,128)S(1)} %collective-permute-done.across_ref), channel_id=1, source_target_pairs={{0,1},{1,0},{2,3},{3,2},{4,5},{5,4},{6,7},{7,6},{8,9},{9,8},{10,11... | collective-permute-start | bytes 245768 | tf_op jit(solution)/shard_map/ppermute | solution.py:431
  10.5 2.3 %copy-start.1 = (f32[1,2,80,128]{3,2,1,0:T(8,128)S(1)}, f32[1,2,80,128]{3,2,1,0:T(8,128)}, u32[]{:S(2)}) copy-start(f32[1,2,80,128]{3,2,1,0:T(8,128)} %param.6) | copy-start | bytes 245764
  17.5 15.9 %copy-start = (f32[2,2,80,128]{3,2,1,0:T(8,128)S(1)}, f32[2,2,80,128]{3,2,1,0:T(8,128)}, u32[]{:S(2)}) copy-start(f32[2,2,80,128]{3,2,1,0:T(8,128)} %param.7) | copy-start | bytes 491524
  44.6 1.4 %collective-permute-start.4 = (f32[176,128]{1,0:T(8,128)S(1)}, f32[176,128]{1,0:T(8,128)S(1)}, u32[]{:S(2)}, u32[]{:S(2)}) collective-permute-start(f32[176,128]{1,0:T(8,128)S(1)} %get-tuple-element.34.own_ref), channel_id=1, source_target_pairs={{0,1},{1,0},{2,3},{3,2},{4,5},{5,4},{6,7},{7,6},{8,9},{9,8},{10,11... | collective-permute-start | bytes 270344 | tf_op jit(solution)/shard_map/ppermute | solution.py:446
  44.7 6.1 %collective-permute-start.5 = (f32[176,128]{1,0:T(8,128)S(1)}, f32[176,128]{1,0:T(8,128)S(1)}, u32[]{:S(2)}, u32[]{:S(2)}) collective-permute-start(f32[176,128]{1,0:T(8,128)S(1)} %get-tuple-element.34.own_ref), channel_id=1, source_target_pairs={{0,15},{1,2},{2,1},{3,4},{4,3},{5,6},{6,5},{7,8},{8,7},{9,10},{10,... | collective-permute-start | bytes 270344 | tf_op jit(solution)/shard_map/ppermute | solution.py:447
  50.8 5.2 %collective-permute-start.6 = (f32[16,128]{1,0:T(8,128)S(1)}, f32[16,128]{1,0:T(8,128)S(1)}, u32[]{:S(2)}, u32[]{:S(2)}) collective-permute-start(f32[16,128]{1,0:T(8,128)S(1)} %merge.2.rest_1_), channel_id=1, source_target_pairs={{0,4},{1,5},{2,6},{3,7},{4,0},{5,1},{6,2},{7,3},{8,12},{9,13},{10,... | collective-permute-start | bytes 24584 | tf_op jit(solution)/shard_map/ppermute | solution.py:449
  56.0 1.3 %collective-permute-start.7 = (f32[176,128]{1,0:T(8,128)S(1)}, f32[176,128]{1,0:T(8,128)S(1)}, u32[]{:S(2)}, u32[]{:S(2)}) collective-permute-start(f32[176,128]{1,0:T(8,128)S(1)} %backward.2.own_ref), channel_id=1, source_target_pairs={{0,1},{1,0},{2,3},{3,2},{4,5},{5,4},{6,7},{7,6},{8,9},{9,8},{10,11... | collective-permute-start | bytes 270344 | tf_op jit(solution)/shard_map/ppermute | solution.py:452
  56.0 6.1 %collective-permute-start.8 = (f32[176,128]{1,0:T(8,128)S(1)}, f32[176,128]{1,0:T(8,128)S(1)}, u32[]{:S(2)}, u32[]{:S(2)}) collective-permute-start(f32[176,128]{1,0:T(8,128)S(1)} %backward.2.own_ref), channel_id=1, source_target_pairs={{0,15},{1,2},{2,1},{3,4},{4,3},{5,6},{6,5},{7,8},{8,7},{9,10},{10,... | collective-permute-start | bytes 270344 | tf_op jit(solution)/shard_map/ppermute | solution.py:453
  62.1 3.7 %collective-permute-start.9 = (f32[16,128]{1,0:T(8,128)S(1)}, f32[16,128]{1,0:T(8,128)S(1)}, u32[]{:S(2)}, u32[]{:S(2)}) collective-permute-start(f32[16,128]{1,0:T(8,128)S(1)} %merge.3), channel_id=1, source_target_pairs={{0,8},{1,9},{2,10},{3,11},{4,12},{5,13},{6,14},{7,15},{8,0},{9,1},... | collective-permute-start | bytes 24584 | tf_op jit(solution)/shard_map/ppermute | solution.py:456

commit v4 on v3

--- a/solution.py
+++ b/solution.py
@@ -28,7 +28,9 @@
 
 def product(left, right):
     dot = functools.partial(jnp.dot, preferred_element_type=f32)
-    return dot(left[0], right[0]) + (dot(left[0], right[1]) + dot(left[1], right[0]))
+    count = left.shape[0] // 2
+    both = dot(left, right[0])
+    return both[:count] + (both[count:] + dot(left[:count], right[1]))
 
 
 def from_left(row):
@@ -98,20 +100,18 @@
         copy.wait()
 
 
-def prepare_kernel(win_hbm, wout_hbm, bias_hbm, lat_hbm, in_hi, in_lo, out_hi, out_lo, wide_bias_ref, wide_lat_ref,
+def prepare_kernel(win_hbm, wout_hbm, bias_hbm, lat_hbm, in_ref, out_ref, wide_bias_ref, wide_lat_ref,
                    win_ref, wout_ref, bias_ref, lat_ref, arrived):
     fetch(((win_hbm, win_ref), (wout_hbm, wout_ref), (bias_hbm, bias_ref), (lat_hbm, lat_ref)), arrived)
     outer, width = wout_ref.shape
     hidden = width // 9
-    high, low = split(win_ref[...].T)
-    in_hi[...] = high
-    in_lo[...] = low
+    in_ref[:hidden, :], in_ref[hidden:, :] = split(win_ref[...].T)
     for a in range(3):
         for b in range(3):
             tap = 3 * a + b
             high, low = split(wout_ref[:, tap * hidden : (tap + 1) * hidden])
-            out_hi[b * outer : (b + 1) * outer, a * hidden : (a + 1) * hidden] = high
-            out_lo[b * outer : (b + 1) * outer, a * hidden : (a + 1) * hidden] = low
+            out_ref[b * outer : (b + 1) * outer, a * hidden : (a + 1) * hidden] = high
+            out_ref[(3 + b) * outer : (4 + b) * outer, a * hidden : (a + 1) * hidden] = low
     wide_bias_ref[...] = jnp.broadcast_to(bias_ref[...], wide_bias_ref.shape[::-1]).T
     for row in range(2):
         one = jnp.broadcast_to(lat_ref[:, row : row + 1], (8, wide_lat_ref.shape[1]))
@@ -122,7 +122,7 @@
     taps_in, hidden = weight_in.shape
     outer = weight_out.shape[0]
     arrays = (weight_in, weight_out, bias, lat_weight)
-    shapes = [(hidden, taps_in)] * 2 + [(3 * outer, 3 * hidden)] * 2
+    shapes = [(2 * hidden, taps_in), (6 * outer, 3 * hidden)]
     return pl.pallas_call(
         prepare_kernel,
         out_shape=[jax.ShapeDtypeStruct(shape, bf16) for shape in shapes]
@@ -134,7 +134,7 @@
     )(*(pltpu.with_memory_space_constraint(array, pltpu.HBM) for array in arrays))
 
 
-def prepare_back_kernel(win_hbm, wout_hbm, before_ref, outb_hi, outb_lo, inb_hi, inb_lo, slope_ref,
+def prepare_back_kernel(win_hbm, wout_hbm, before_ref, outb_ref, inb_ref, slope_ref,
                         stack, win_ref, wout_ref, arrived):
     pairs = ((win_hbm, win_ref), (wout_hbm, wout_ref))
     copies = [pltpu.make_async_copy(*pair, arrived.at[i]) for i, pair in enumerate(pairs)]
@@ -154,11 +154,9 @@
             stack[(8 - tap) * outer : (9 - tap) * outer, :] = wout_ref[:, tap * hidden : (tap + 1) * hidden]
             high, low = split(win_ref[tap * inner : (tap + 1) * inner, :])
             j, k = 2 - a, 2 - b
-            inb_hi[k * inner : (k + 1) * inner, j * hidden : (j + 1) * hidden] = high
-            inb_lo[k * inner : (k + 1) * inner, j * hidden : (j + 1) * hidden] = low
-    high, low = split(stack[...].T)
-    outb_hi[...] = high
-    outb_lo[...] = low
+            inb_ref[k * inner : (k + 1) * inner, j * hidden : (j + 1) * hidden] = high
+            inb_ref[(3 + k) * inner : (4 + k) * inner, j * hidden : (j + 1) * hidden] = low
+    outb_ref[:hidden, :], outb_ref[hidden:, :] = split(stack[...].T)
 
 
 def prepare_back(weight_in, weight_out, before):
@@ -166,7 +164,7 @@
     outer = weight_out.shape[0]
     inner = taps_in // 9
     arrays = (weight_in, weight_out)
-    shapes = [(hidden, 9 * outer)] * 2 + [(3 * inner, 3 * hidden)] * 2
+    shapes = [(2 * hidden, 9 * outer), (6 * inner, 3 * hidden)]
     hbm = pl.BlockSpec(memory_space=pltpu.HBM)
     return pl.pallas_call(
         prepare_back_kernel,
@@ -191,14 +189,14 @@
 
 
 def forward_kernel(own_ref, near_ref, across_ref, far_across_ref, far_near_ref, bias_ref,
-                   in_hi, in_lo, out_hi, out_lo, before_ref, fields_ref, wide_hi, wide_lo, hid_hi, hid_lo):
+                   in_ref, out_ref, before_ref, fields_ref, wide_hi, wide_lo, hid_hi, hid_lo):
     channels, width = own_ref.shape[1:]
-    hidden = in_hi.shape[0]
+    hidden = in_ref.shape[0] // 2
     even = is_even()
     wide = (wide_hi, wide_lo)
     hid = (hid_hi, hid_lo)
-    w_in = (in_hi[...], in_lo[...])
-    w_out = (out_hi[...], out_lo[...])
+    w_in = in_ref[...]
+    w_out = out_ref[...]
     bias = jnp.concatenate([bias_ref[...]] * 2, axis=1)
 
     def initial(index):
@@ -244,11 +242,11 @@
 
 def forward(own, near, across, far_across, far_near, bias, w_in, w_out):
     channels, width = own.shape[1:]
-    hidden = w_in[0].shape[0]
+    hidden = w_in.shape[0] // 2
     vmem = pl.BlockSpec(memory_space=pltpu.VMEM)
     return pl.pallas_call(
         forward_kernel,
-        in_specs=[vmem] * 10,
+        in_specs=[vmem] * 8,
         out_shape=[
             jax.ShapeDtypeStruct((2, 2, hidden, 2 * width), f32),
             jax.ShapeDtypeStruct((4 * channels, width), f32),
@@ -257,7 +255,7 @@
         + [pltpu.VMEM((8 * hidden, 2 * width), bf16)] * 2,
         compiler_params=params,
         name="forward",
-    )(own, near, across, far_across, far_near, bias, *w_in, *w_out)
+    )(own, near, across, far_across, far_near, bias, w_in, w_out)
 
 
 def crps_kernel(weight_ref, fields_ref, targets_ref, out_ref):
@@ -304,7 +302,7 @@
     )(weights, fields, targets)
 
 
-def collect_kernel(grads_ref, first_ref, second_ref):
+def collect_kernel(grads_ref, first_ref, second_ref, known_ref):
     chunks, height, width = grads_ref.shape
     height = height - 8
     half = chunks // 2
@@ -316,7 +314,9 @@
         second_ref[chunk * height : (chunk + 1) * height, :] = grads_ref[half + chunk, :height, :]
     known = jnp.broadcast_to(jnp.sum(total, axis=0, keepdims=True), (slab_count, width))
     slab = lax.broadcasted_iota(jnp.int32, known.shape, 0)
-    second_ref[half * height :, :] = jnp.where(slab == lax.axis_index(LAT), known, 0.0)
+    known = jnp.where(slab == lax.axis_index(LAT), known, 0.0)
+    second_ref[half * height :, :] = known
+    known_ref[...] = known
 
 
 def collect(grads):
@@ -327,6 +327,7 @@
         out_shape=[
             jax.ShapeDtypeStruct((count, width), f32),
             jax.ShapeDtypeStruct((count + slab_count, width), f32),
+            jax.ShapeDtypeStruct((slab_count, width), f32),
         ],
         compiler_params=params,
         name="collect",
@@ -340,33 +341,59 @@
     return result
 
 
-def merge_kernel(own_ref, near_ref, across_ref, *rest):
-    count = own_ref.shape[0] - slab_count
-    tables = [ref[count:, :] for ref in (own_ref, near_ref, across_ref)]
-    rest[-1][...] = merged(*tables, *(ref[...] for ref in rest[:-1]))
-
-
-def merge(own, near, across, *far):
+def table_of(*refs):
+    return merged(*(ref[ref.shape[0] - slab_count :, :] for ref in refs))
+
+
+def merge_kernel(*refs):
+    refs[-1][...] = table_of(*refs[:-1])
+
+
+def merge(*messages):
     return pl.pallas_call(
         merge_kernel,
-        out_shape=jax.ShapeDtypeStruct((slab_count, own.shape[1]), f32),
+        out_shape=jax.ShapeDtypeStruct((slab_count, messages[0].shape[1]), f32),
         compiler_params=params,
         name="merge",
-    )(own, near, across, *far)
-
-
-def backward_kernel(step, own_ref, near_ref, across_ref, slope_ref, outb_hi, outb_lo, inb_hi, inb_lo,
+    )(*messages)
+
+
+def finish_kernel(count, gradient_ref, known_ref, opposite_ref, out_hbm, loss_ref, done):
+    copy = pltpu.make_async_copy(gradient_ref, out_hbm, done)
+    copy.start()
+    total = jnp.sum(table_of(known_ref, opposite_ref), axis=0, keepdims=True)
+    loss_ref[...] = jnp.sum(total, axis=1, keepdims=True) / count
+    copy.wait()
+
+
+def finish(gradient, known, opposite, count):
+    vmem = pl.BlockSpec(memory_space=pltpu.VMEM)
+    return pl.pallas_call(
+        functools.partial(finish_kernel, count),
+        out_shape=[
+            jax.ShapeDtypeStruct(gradient.shape, f32),
+            jax.ShapeDtypeStruct((1, 1), f32),
+        ],
+        in_specs=[vmem] * 3,
+        out_specs=[pl.BlockSpec(memory_space=pltpu.HBM), vmem],
+        scratch_shapes=[pltpu.SemaphoreType.DMA(())],
+        compiler_params=params,
+        name="finish",
+    )(gradient, known, opposite)
+
+
+def backward_kernel(step, own_ref, near_ref, across_ref, slope_ref, outb_ref, inb_ref,
                     *rest):
-    added, known_ref = rest[:-5][:1], rest[:-5][1:]
+    added, far_ref = rest[:-5][:1], rest[:-5][1:]
     out_ref, wide_hi, wide_lo, hid_hi, hid_lo = rest[-5:]
     width = own_ref.shape[1]
     channels = (own_ref.shape[0] - slab_count) // 2
-    hidden = outb_hi.shape[0]
+    hidden = outb_ref.shape[0] // 2
     even = is_even()
     wide = (wide_hi, wide_lo)
     hid = (hid_hi, hid_lo)
-    w_out = (outb_hi[...], outb_lo[...])
-    w_in = (inb_hi[...], inb_lo[...])
+    w_out = outb_ref[...]
+    w_in = inb_ref[...]
 
     def take(ref, row):
         return ref[row * channels : (row + 1) * channels, :]
@@ -393,25 +420,24 @@
         for extra in added:
             total = total + take(extra, row)
         out_ref[row * channels : (row + 1) * channels, :] = total
-    if known_ref:
-        last = 2 * channels
-        out_ref[last:, :] = known_ref[0][...]
+    if far_ref:
+        out_ref[2 * channels :, :] = table_of(own_ref, near_ref, across_ref, *far_ref)
 
 
 def backward(step, own, near, across, slopes, w_out, w_in, *added):
     count, width = own.shape
     channels = (count - slab_count) // 2
-    hidden = w_out[0].shape[0]
+    hidden = w_out.shape[0] // 2
     vmem = pl.BlockSpec(memory_space=pltpu.VMEM)
     return pl.pallas_call(
         functools.partial(backward_kernel, step),
-        in_specs=[vmem] * (8 + len(added)),
+        in_specs=[vmem] * (6 + len(added)),
         out_shape=jax.ShapeDtypeStruct((count if step else 2 * channels, width), f32),
         scratch_shapes=[pltpu.VMEM((18 * channels, 2 * width), bf16)] * 2
         + [pltpu.VMEM((4 * hidden, 2 * width), bf16)] * 2,
         compiler_params=params,
         name="backward",
-    )(own, near, across, slopes, *w_out, *w_in, *added)
+    )(own, near, across, slopes, w_out, w_in, *added)
 
 
 def on_device(initial_states, targets, lat_weight, weight_in, weight_out, hidden_bias):
@@ -430,32 +456,34 @@
     crossed, beside = lax.optimization_barrier((crossed, beside))
     far_beside = lax.ppermute(crossed, LAT, near)
     before, fields = forward(
-        own, beside, crossed, far_crossed, far_beside, ready[4], ready[:2], ready[2:4]
+        own, beside, crossed, far_crossed, far_beside, ready[2], ready[0], ready[1]
     )
     height = steps * slab_rows * channels // members
     chunks = lax.all_to_all(
         fields.reshape(members, height, width), MEMBER, split_axis=0, concat_axis=0, tiled=True
     )
-    grads = crps(ready[5], chunks, targets.reshape(members, height, width))
+    grads = crps(ready[3], chunks, targets.reshape(members, height, width))
     grads = lax.all_to_all(grads, MEMBER, split_axis=0, concat_axis=0, tiled=True)
     grads, before = lax.optimization_barrier((grads, before))
-    *back, slopes = prepare_back(weight_in.T, weight_out, before)
-    w_out_back, w_in_back = back[:2], back[2:]
-    first_grads, message = collect(grads)
-
+    w_out_back, w_in_back, slopes = prepare_back(weight_in.T, weight_out, before)
+    first_grads, message, known = collect(grads)
+
+    beside = lax.ppermute(message, LAT, near)
+    crossed = lax.ppermute(message, LAT, across)
+    far = lax.ppermute(known, LAT, [(i, i ^ 4) for i in range(slabs)])
+    beside, crossed, far, slopes = lax.optimization_barrier((beside, crossed, far, slopes))
+    message = backward(
+        1, message, beside, crossed, slopes, w_out_back, w_in_back, first_grads, far
+    )
     beside = lax.ppermute(message, LAT, near)
     crossed = lax.ppermute(message, LAT, across)
     known = merge(message, beside, crossed)
-    far = lax.ppermute(known, LAT, [(i, i ^ 4) for i in range(slabs)])
-    message = backward(1, message, beside, crossed, slopes, w_out_back, w_in_back, first_grads, known)
-    message, far = lax.optimization_barrier((message, far))
-    beside = lax.ppermute(message, LAT, near)
-    crossed = lax.ppermute(message, LAT, across)
-    known = merge(message, beside, crossed, far)
     gradient = backward(0, message, beside, crossed, slopes, w_out_back, w_in_back)
     opposite = lax.ppermute(known, LAT, [(i, i ^ 8) for i in range(slabs)])
-    total = jnp.sum(jnp.where(known != 0.0, known, opposite))
-    loss = total / (members * steps * rows * channels * width)
+    gradient, loss = finish(
+        gradient, known, opposite, members * steps * rows * channels * width
+    )
+    loss = loss.reshape(())
     return gradient.reshape(initial_states.shape), loss
 
 

time: 68.4 us -> 65.1 us (0.952)
  waiting for transfers between devices: 16.8 us -> 12.1 us
  starting transfers between devices: 8.6 us -> 12.5 us
  between operations: 2.47 us -> 0.72 us
    ppermute x2, waiting for transfers between devices: 9.64 us -> 4.87 us  [on_device(): crossed = lax.ppermute(message, LAT, across)]
    ppermute x2, starting transfers between devices: 0.14 us -> 3.12 us  [on_device(): crossed = lax.ppermute(message, LAT, across)]
    ppermute x2, waiting for transfers between devices: 2.42 us -> 0.21 us  [on_device(): beside = lax.ppermute(message, LAT, near)]
    ppermute x1, waiting for transfers between devices: 1.55 us -> 3.48 us  [on_device(): far = lax.ppermute(known, LAT, [(i, i ^ 4) for i in range(slabs)])]
    pallas_call x1 -> x2, Pallas kernels: 4.65 us -> 5.69 us  [the longest x1 4.54 us: forward(): pl.pallas_call(forward_kernel, in_specs=[vmem] * 8, out_shape=[jax.ShapeD...]
    pallas_call x2, Pallas kernels: 4.49 us -> 3.71 us  [backward(): pl.pallas_call(functools.partial(backward_kernel, step), in_specs=[vmem]...]
    ppermute x1, waiting for transfers between devices: 0.07 us -> 0.78 us  [on_device(): opposite = lax.ppermute(known, LAT, [(i, i ^ 8) for i in range(slabs)])]
  transfers between devices with their start and end apart: 10 -> 10, of which waited for: 8 -> 6; matrix products, arithmetic and copies ran while one was open for 0% -> 0% of each run, Pallas kernels for 12% -> 8%
where the time goes in v4:
time: 65.1 us; the launch traced here: 64.8 us
  blocking collectives  26.4 us (41%)
  Pallas kernels  13.1 us (20%)
  starting transfers between devices  12.5 us (19%)
  waiting for transfers between devices  12.1 us (19%)
  between operations  0.72 us (1%)
    all_to_all x1, blocking collectives, on_device(): lax.all_to_all(fields.reshape(members, height, width), MEMBER, split_axis...  15.5 us
    all_to_all x1, blocking collectives, on_device(): lax.all_to_all(grads, MEMBER, split_axis=0, concat_axis=0, tiled=True)  10.9 us
    ppermute x2, waiting for transfers between devices, on_device(): crossed = lax.ppermute(message, LAT, across)  4.87 us
    pallas_call x1, Pallas kernels, forward(): pl.pallas_call(forward_kernel, in_specs=[vmem] * 8, out_shape=[jax.ShapeD...  4.54 us
    ppermute x1, starting transfers between devices, on_device(): crossed = lax.ppermute(own, LAT, across)  4.3 us
    ppermute x1, starting transfers between devices, on_device(): far_crossed = lax.ppermute(beside, LAT, across)  3.81 us
    pallas_call x2, Pallas kernels, backward(): pl.pallas_call(functools.partial(backward_kernel, step), in_specs=[vmem]...  3.71 us
    ppermute x1, waiting for transfers between devices, on_device(): far = lax.ppermute(known, LAT, [(i, i ^ 4) for i in range(slabs)])  3.48 us
  transfers between devices with their start and end apart: 10, of which 6 were waited for; matrix products, arithmetic and copies ran while one was open for 0% of the time, Pallas kernels for 8%

profile of v4, /device:TPU:0, one launch (start us, length us, event | category | flops | bytes accessed | tf_op | source)
XLA Modules:
  0.0 64.8 jit_solution(11449835043085573618)
XLA Ops:
  0.6 0.1 collective-permute-start.1
  0.7 4.3 %collective-permute-start = (f32[2,80,128]{2,1,0:T(8,128)}, f32[2,80,128]{2,1,0:T(8,128)S(1)}, u32[]{:S(2)}, u32[]{:S(2)}) collective-permute-start(f32[2,80,128]{2,1,0:T(8,128)} %bitcast.11), channel_id=1, source_target_pairs={{0,15},{1,2},{2,1},{3,4},{4,3},{5,6},{6,5},{7,8},{8,7},{9,10},{10,... | collective-permute-start | bytes 245768 | tf_op jit(solution)/shard_map/ppermute | solution.py:453
  5.0 0.0 collective-permute-done.1.near_ref
  5.0 2.4 %collective-permute-done.across_ref = f32[2,80,128]{2,1,0:T(8,128)S(1)} collective-permute-done((f32[2,80,128]{2,1,0:T(8,128)}, f32[2,80,128]{2,1,0:T(8,128)S(1)}, u32[]{:S(2)}, u32[]{:S(2)}) %collective-permute-start) | collective-permute-done | bytes 81952 | tf_op jit(solution)/shard_map/ppermute | solution.py:453
  7.4 0.0 collective-permute-start.3
  7.4 3.8 %collective-permute-start.2 = (f32[2,80,128]{2,1,0:T(8,128)S(1)}, f32[2,80,128]{2,1,0:T(8,128)S(1)}, u32[]{:S(2)}, u32[]{:S(2)}) collective-permute-start(f32[2,80,128]{2,1,0:T(8,128)S(1)} %collective-permute-done.1.near_ref), channel_id=1, source_target_pairs={{0,15},{1,2},{2,1},{3,4},{4,3},{5,6},{6,5},{7,8},{8,7},{9,10},{10,... | collective-permute-start | bytes 245768 | tf_op jit(solution)/shard_map/ppermute | solution.py:454
  11.2 0.0 copy-start.1
  11.2 1.8 %prepare.1 = (bf16[512,720]{1,0:T(8,128)(2,1)S(1)}, bf16[480,768]{1,0:T(8,128)(2,1)S(1)}, f32[256,128]{1,0:T(8,128)S(1)}, f32[16,128]{1,0:T(8,128)S(1)}) custom-call(f32[720,256]{1,0:T(8,128)} %bitcast.13, f32[80,2304]{1,0:T(8,128)} %wout_hbm.3, f32[1,256]{1,0:T(1,128)} %bitcast.15, f32[1,2]{1,0:T(1,128)} %bitcast.16), custom_call_target="tpu_custom_call" | custom-call | tf_op jit(solution)/shard_map/prepare/pallas_call | solution.py:126
  13.0 0.0 collective-permute-done.3.far_near_ref
  13.0 0.4 collective-permute-done.2.far_across_ref
  13.4 0.0 copy-done.1
  13.4 4.5 %forward.1 = (f32[2,2,256,256]{3,2,1,0:T(8,128)S(1)}, f32[320,128]{1,0:T(8,128)S(1)}) custom-call(f32[2,80,128]{2,1,0:T(8,128)S(1)} %bitcast.12, f32[2,80,128]{2,1,0:T(8,128)S(1)} %collective-permute-done.1.near_ref, f32[2,80,128]{2,1,0:T(8,128)S(1)} %collective-permute-done.across_ref, f32[2,80,128]{2,1,0:T(8,128)S(1)} %collective-permute-done.2.far_across_ref, ...), custom_call_target="tpu_custom_call" | custom-call | tf_op jit(solution)/shard_map/forward/pallas_call | solution.py:247
  17.9 0.0 copy-start
  17.9 15.5 %all_to_all.10.fields_ref = f32[8,40,128]{2,1,0:T(8,128)S(1)} all-to-all(f32[8,40,128]{2,1,0:T(8,128)S(1)} %bitcast.9), channel_id=1, replica_groups=mesh['member_0'=4,'member_1'=2,'lat_0'=2,'lat_1'=4,'lat_2'=2] {'member_0..., dimensions={0} | all-to-all | bytes 327680 | tf_op jit(solution)/shard_map/all_to_all | solution.py:462
  33.4 0.0 copy-done
  33.4 0.2 crps.1
  33.6 10.9 %all_to_all.11.grads_ref = f32[8,48,128]{2,1,0:T(8,128)S(1)} all-to-all(f32[8,48,128]{2,1,0:T(8,128)S(1)} %crps.1), channel_id=1, replica_groups=mesh['member_0'=4,'member_1'=2,'lat_0'=2,'lat_1'=4,'lat_2'=2] {'member_0..., dimensions={0} | all-to-all | bytes 393216 | tf_op jit(solution)/shard_map/all_to_all | solution.py:466
  44.6 0.1 collective-permute-start.4
  44.7 2.0 %collective-permute-start.5 = (f32[176,128]{1,0:T(8,128)S(1)}, f32[176,128]{1,0:T(8,128)S(1)}, u32[]{:S(2)}, u32[]{:S(2)}) collective-permute-start(f32[176,128]{1,0:T(8,128)S(1)} %get-tuple-element.33.own_ref), channel_id=1, source_target_pairs={{0,15},{1,2},{2,1},{3,4},{4,3},{5,6},{6,5},{7,8},{8,7},{9,10},{10,... | collective-permute-start | bytes 270344 | tf_op jit(solution)/shard_map/ppermute | solution.py:472
  46.7 0.0 collective-permute-start.6
  46.7 1.7 %prepare_back.1 = (bf16[512,720]{1,0:T(8,128)(2,1)S(1)}, bf16[480,768]{1,0:T(8,128)(2,1)S(1)}, f32[2,2,256,256]{3,2,1,0:T(8,128)S(1)}) custom-call(f32[720,256]{1,0:T(8,128)} %bitcast.14, f32[80,2304]{1,0:T(8,128)} %wout_hbm.3, f32[2,2,256,256]{3,2,1,0:T(8,128)S(1)} %get-tuple-element.35.before_ref), custom_call_target="tpu_custom_call" | custom-call | tf_op jit(solution)/shard_map/prepare_back/pallas_call | solution.py:169
  48.4 3.5 %collective-permute-done.6.rest_1_ = f32[16,128]{1,0:T(8,128)S(1)} collective-permute-done((f32[16,128]{1,0:T(8,128)S(1)}, f32[16,128]{1,0:T(8,128)S(1)}, u32[]{:S(2)}, u32[]{:S(2)}) %collective-permute-start.6) | collective-permute-done | bytes 8224 | tf_op jit(solution)/shard_map/ppermute | solution.py:473
  51.9 0.0 collective-permute-done.4.near_ref
  51.9 0.0 collective-permute-done.5.across_ref
  51.9 1.9 %backward.2.own_ref.refs_0_ = f32[176,128]{1,0:T(8,128)S(1)} custom-call(f32[176,128]{1,0:T(8,128)S(1)} %get-tuple-element.33.own_ref, f32[176,128]{1,0:T(8,128)S(1)} %collective-permute-done.4.near_ref, f32[176,128]{1,0:T(8,128)S(1)} %collective-permute-done.5.across_ref, f32[2,2,256,256]{3,2,1,0:T(8,128)S(1)} %get-tuple-element.39.slope_ref, ...), custom_call_target="tpu_custom_call" | custom-call | tf_op jit(solution)/shard_map/backward/pallas_call | solution.py:432
  53.8 0.1 collective-permute-start.7
  53.9 1.1 %collective-permute-start.8 = (f32[176,128]{1,0:T(8,128)S(1)}, f32[176,128]{1,0:T(8,128)S(1)}, u32[]{:S(2)}, u32[]{:S(2)}) collective-permute-start(f32[176,128]{1,0:T(8,128)S(1)} %backward.2.own_ref.refs_0_), channel_id=1, source_target_pairs={{0,15},{1,2},{2,1},{3,4},{4,3},{5,6},{6,5},{7,8},{8,7},{9,10},{10,... | collective-permute-start | bytes 270344 | tf_op jit(solution)/shard_map/ppermute | solution.py:479
  54.9 0.2 collective-permute-done.7.near_ref.refs_1_
  55.1 4.9 %collective-permute-done.8.across_ref.refs_2_ = f32[176,128]{1,0:T(8,128)S(1)} collective-permute-done((f32[176,128]{1,0:T(8,128)S(1)}, f32[176,128]{1,0:T(8,128)S(1)}, u32[]{:S(2)}, u32[]{:S(2)}) %collective-permute-start.8) | collective-permute-done | bytes 90144 | tf_op jit(solution)/shard_map/ppermute | solution.py:479
  60.0 1.0 %collective-permute-start.9 = (f32[16,128]{1,0:T(8,128)S(1)}, f32[16,128]{1,0:T(8,128)S(1)}, u32[]{:S(2)}, u32[]{:S(2)}) collective-permute-start(f32[16,128]{1,0:T(8,128)S(1)} %merge.1.known_ref), channel_id=1, source_target_pairs={{0,8},{1,9},{2,10},{3,11},{4,12},{5,13},{6,14},{7,15},{8,0},{9,1},... | collective-permute-start | bytes 24584 | tf_op jit(solution)/shard_map/ppermute | solution.py:482
  61.0 1.9 %backward.3.gradient_ref = f32[160,128]{1,0:T(8,128)S(1)} custom-call(f32[176,128]{1,0:T(8,128)S(1)} %backward.2.own_ref.refs_0_, f32[176,128]{1,0:T(8,128)S(1)} %collective-permute-done.7.near_ref.refs_1_, f32[176,128]{1,0:T(8,128)S(1)} %collective-permute-done.8.across_ref.refs_2_, f32[2,2,256,256]{3,2,1,0:T(8,128)S(1)} %get-tuple-element.39.slope_ref, ...), custom_call_target="tpu_custom_call" | custom-call | tf_op jit(solution)/shard_map/backward/pallas_call | solution.py:432
  62.9 0.8 %collective-permute-done.9.opposite_ref = f32[16,128]{1,0:T(8,128)S(1)} collective-permute-done((f32[16,128]{1,0:T(8,128)S(1)}, f32[16,128]{1,0:T(8,128)S(1)}, u32[]{:S(2)}, u32[]{:S(2)}) %collective-permute-start.9) | collective-permute-done | bytes 8224 | tf_op jit(solution)/shard_map/ppermute | solution.py:482
  63.7 1.2 %finish.1 = (f32[160,128]{1,0:T(8,128)}, f32[1,1]{1,0:T(1,128)}) custom-call(f32[160,128]{1,0:T(8,128)S(1)} %backward.3.gradient_ref, f32[16,128]{1,0:T(8,128)S(1)} %merge.1.known_ref, f32[16,128]{1,0:T(8,128)S(1)} %collective-permute-done.9.opposite_ref), custom_call_target="tpu_custom_call" | custom-call | tf_op jit(solution)/shard_map/finish/pallas_call | solution.py:371
  (2 shorter events, 0.0 us)
Async XLA Ops:
  0.6 4.4 %collective-permute-start.1 = (f32[2,80,128]{2,1,0:T(8,128)}, f32[2,80,128]{2,1,0:T(8,128)S(1)}, u32[]{:S(2)}, u32[]{:S(2)}) collective-permute-start(f32[2,80,128]{2,1,0:T(8,128)} %bitcast.10), channel_id=1, source_target_pairs={{0,1},{1,0},{2,3},{3,2},{4,5},{5,4},{6,7},{7,6},{8,9},{9,8},{10,11... | collective-permute-start | bytes 245768 | tf_op jit(solution)/shard_map/ppermute | solution.py:452
  0.7 6.7 %collective-permute-start = (f32[2,80,128]{2,1,0:T(8,128)}, f32[2,80,128]{2,1,0:T(8,128)S(1)}, u32[]{:S(2)}, u32[]{:S(2)}) collective-permute-start(f32[2,80,128]{2,1,0:T(8,128)} %bitcast.11), channel_id=1, source_target_pairs={{0,15},{1,2},{2,1},{3,4},{4,3},{5,6},{6,5},{7,8},{8,7},{9,10},{10,... | collective-permute-start | bytes 245768 | tf_op jit(solution)/shard_map/ppermute | solution.py:453
  7.4 5.6 %collective-permute-start.3 = (f32[2,80,128]{2,1,0:T(8,128)S(1)}, f32[2,80,128]{2,1,0:T(8,128)S(1)}, u32[]{:S(2)}, u32[]{:S(2)}) collective-permute-start(f32[2,80,128]{2,1,0:T(8,128)S(1)} %collective-permute-done.across_ref), channel_id=1, source_target_pairs={{0,1},{1,0},{2,3},{3,2},{4,5},{5,4},{6,7},{7,6},{8,9},{9,8},{10,11... | collective-permute-start | bytes 245768 | tf_op jit(solution)/shard_map/ppermute | solution.py:457
  7.4 6.0 %collective-permute-start.2 = (f32[2,80,128]{2,1,0:T(8,128)S(1)}, f32[2,80,128]{2,1,0:T(8,128)S(1)}, u32[]{:S(2)}, u32[]{:S(2)}) collective-permute-start(f32[2,80,128]{2,1,0:T(8,128)S(1)} %collective-permute-done.1.near_ref), channel_id=1, source_target_pairs={{0,15},{1,2},{2,1},{3,4},{4,3},{5,6},{6,5},{7,8},{8,7},{9,10},{10,... | collective-permute-start | bytes 245768 | tf_op jit(solution)/shard_map/ppermute | solution.py:454
  11.2 2.2 %copy-start.1 = (f32[1,2,80,128]{3,2,1,0:T(8,128)S(1)}, f32[1,2,80,128]{3,2,1,0:T(8,128)}, u32[]{:S(2)}) copy-start(f32[1,2,80,128]{3,2,1,0:T(8,128)} %param.6) | copy-start | bytes 245764
  17.9 15.5 %copy-start = (f32[2,2,80,128]{3,2,1,0:T(8,128)S(1)}, f32[2,2,80,128]{3,2,1,0:T(8,128)}, u32[]{:S(2)}) copy-start(f32[2,2,80,128]{3,2,1,0:T(8,128)} %param.7) | copy-start | bytes 491524
  44.6 7.3 %collective-permute-start.4 = (f32[176,128]{1,0:T(8,128)S(1)}, f32[176,128]{1,0:T(8,128)S(1)}, u32[]{:S(2)}, u32[]{:S(2)}) collective-permute-start(f32[176,128]{1,0:T(8,128)S(1)} %get-tuple-element.33.own_ref), channel_id=1, source_target_pairs={{0,1},{1,0},{2,3},{3,2},{4,5},{5,4},{6,7},{7,6},{8,9},{9,8},{10,11... | collective-permute-start | bytes 270344 | tf_op jit(solution)/shard_map/ppermute | solution.py:471
  44.7 7.2 %collective-permute-start.5 = (f32[176,128]{1,0:T(8,128)S(1)}, f32[176,128]{1,0:T(8,128)S(1)}, u32[]{:S(2)}, u32[]{:S(2)}) collective-permute-start(f32[176,128]{1,0:T(8,128)S(1)} %get-tuple-element.33.own_ref), channel_id=1, source_target_pairs={{0,15},{1,2},{2,1},{3,4},{4,3},{5,6},{6,5},{7,8},{8,7},{9,10},{10,... | collective-permute-start | bytes 270344 | tf_op jit(solution)/shard_map/ppermute | solution.py:472
  46.7 5.2 %collective-permute-start.6 = (f32[16,128]{1,0:T(8,128)S(1)}, f32[16,128]{1,0:T(8,128)S(1)}, u32[]{:S(2)}, u32[]{:S(2)}) collective-permute-start(f32[16,128]{1,0:T(8,128)S(1)} %get-tuple-element.34), channel_id=1, source_target_pairs={{0,4},{1,5},{2,6},{3,7},{4,0},{5,1},{6,2},{7,3},{8,12},{9,13},{10,... | collective-permute-start | bytes 24584 | tf_op jit(solution)/shard_map/ppermute | solution.py:473
  53.8 1.4 %collective-permute-start.7 = (f32[176,128]{1,0:T(8,128)S(1)}, f32[176,128]{1,0:T(8,128)S(1)}, u32[]{:S(2)}, u32[]{:S(2)}) collective-permute-start(f32[176,128]{1,0:T(8,128)S(1)} %backward.2.own_ref.refs_0_), channel_id=1, source_target_pairs={{0,1},{1,0},{2,3},{3,2},{4,5},{5,4},{6,7},{7,6},{8,9},{9,8},{10,11... | collective-permute-start | bytes 270344 | tf_op jit(solution)/shard_map/ppermute | solution.py:478
  53.9 6.1 %collective-permute-start.8 = (f32[176,128]{1,0:T(8,128)S(1)}, f32[176,128]{1,0:T(8,128)S(1)}, u32[]{:S(2)}, u32[]{:S(2)}) collective-permute-start(f32[176,128]{1,0:T(8,128)S(1)} %backward.2.own_ref.refs_0_), channel_id=1, source_target_pairs={{0,15},{1,2},{2,1},{3,4},{4,3},{5,6},{6,5},{7,8},{8,7},{9,10},{10,... | collective-permute-start | bytes 270344 | tf_op jit(solution)/shard_map/ppermute | solution.py:479
  60.0 3.7 %collective-permute-start.9 = (f32[16,128]{1,0:T(8,128)S(1)}, f32[16,128]{1,0:T(8,128)S(1)}, u32[]{:S(2)}, u32[]{:S(2)}) collective-permute-start(f32[16,128]{1,0:T(8,128)S(1)} %merge.1.known_ref), channel_id=1, source_target_pairs={{0,8},{1,9},{2,10},{3,11},{4,12},{5,13},{6,14},{7,15},{8,0},{9,1},... | collective-permute-start | bytes 24584 | tf_op jit(solution)/shard_map/ppermute | solution.py:482

commit v5 on v4

--- a/solution.py
+++ b/solution.py
@@ -134,15 +134,15 @@
     )(*(pltpu.with_memory_space_constraint(array, pltpu.HBM) for array in arrays))
 
 
-def prepare_back_kernel(win_hbm, wout_hbm, before_ref, outb_ref, inb_ref, slope_ref,
+def prepare_back_kernel(win_hbm, wout_hbm, first_ref, second_ref, outb_ref, inb_ref, slope_ref,
                         stack, win_ref, wout_ref, arrived):
     pairs = ((win_hbm, win_ref), (wout_hbm, wout_ref))
     copies = [pltpu.make_async_copy(*pair, arrived.at[i]) for i, pair in enumerate(pairs)]
     for copy in copies:
         copy.start()
-    for step in range(2):
+    for step, before_ref in enumerate((first_ref, second_ref)):
         for pair in range(2):
-            slope_ref[step, pair] = gelu_slope(before_ref[step, pair])
+            slope_ref[step, pair] = gelu_slope(before_ref[pair])
     for copy in copies:
         copy.wait()
     outer, width = wout_ref.shape
@@ -159,7 +159,7 @@
     outb_ref[:hidden, :], outb_ref[hidden:, :] = split(stack[...].T)
 
 
-def prepare_back(weight_in, weight_out, before):
+def prepare_back(weight_in, weight_out, first, second):
     taps_in, hidden = weight_in.shape
     outer = weight_out.shape[0]
     inner = taps_in // 9
@@ -169,14 +169,14 @@
     return pl.pallas_call(
         prepare_back_kernel,
         out_shape=[jax.ShapeDtypeStruct(shape, bf16) for shape in shapes]
-        + [jax.ShapeDtypeStruct(before.shape, f32)],
-        in_specs=[hbm, hbm, pl.BlockSpec(memory_space=pltpu.VMEM)],
+        + [jax.ShapeDtypeStruct((2, *first.shape), f32)],
+        in_specs=[hbm, hbm] + [pl.BlockSpec(memory_space=pltpu.VMEM)] * 2,
         scratch_shapes=[pltpu.VMEM((9 * outer, hidden), f32)]
         + [pltpu.VMEM(array.shape, f32) for array in arrays]
         + [pltpu.SemaphoreType.DMA((2,))],
         compiler_params=params,
         name="prepare_back",
-    )(*(pltpu.with_memory_space_constraint(array, pltpu.HBM) for array in arrays), before)
+    )(*(pltpu.with_memory_space_constraint(array, pltpu.HBM) for array in arrays), first, second)
 
 
 def inside(row):
@@ -188,74 +188,122 @@
     return lax.rem(lax.axis_index(LAT), 2) == 0
 
 
-def forward_kernel(own_ref, near_ref, across_ref, far_across_ref, far_near_ref, bias_ref,
-                   in_ref, out_ref, before_ref, fields_ref, wide_hi, wide_lo, hid_hi, hid_lo):
+def either(first, second):
+    return lambda row: jnp.where(is_even(), first[row], second[row])
+
+
+def activate(before, first, hid, index, hidden, width):
+    active = gelu(before)
+    for half in range(2):
+        row = active[:, half * width : (half + 1) * width]
+        row = jnp.where(inside(first + half), row, 0.0)
+        put_twice(hid, index + half, hidden, 0, split(row))
+
+
+def inner_kernel(own_ref, near_ref, across_ref, bias_ref, in_ref, out_ref, before_ref, field_ref, hid_hi, hid_lo,
+                 wide_hi, wide_lo):
     channels, width = own_ref.shape[1:]
     hidden = in_ref.shape[0] // 2
-    even = is_even()
     wide = (wide_hi, wide_lo)
     hid = (hid_hi, hid_lo)
+    bias = jnp.concatenate([bias_ref[...]] * 2, axis=1)
+    slabs = (either(across_ref, near_ref), lambda row: own_ref[row], either(near_ref, across_ref))
+    for index in range(6):
+        row = slabs[index // 2](index % 2)
+        if index // 2 != 1:
+            row = jnp.where(inside(index - 2), row, 0.0)
+        put_windows(wide, index, row)
+    w_in = in_ref[...]
+    for pair in (0, 2):
+        before = to_channels(w_in, wide, pair, channels) + bias
+        before_ref[pair // 2] = before
+        activate(before, pair - 1, hid, pair, hidden, width)
+    moved = from_channels(out_ref[...], hid, 0, hidden, channels)
+    for row in range(2):
+        field_ref[row * channels : (row + 1) * channels, :] = own_ref[row] + moved[row]
+
+
+def inner(own, near, across, bias, w_in, w_out):
+    channels, width = own.shape[1:]
+    hidden = w_in.shape[0] // 2
+    return pl.pallas_call(
+        inner_kernel,
+        out_shape=[
+            jax.ShapeDtypeStruct((2, hidden, 2 * width), f32),
+            jax.ShapeDtypeStruct((2 * channels, width), f32),
+        ]
+        + [jax.ShapeDtypeStruct((4 * hidden, 2 * width), bf16)] * 2,
+        scratch_shapes=[pltpu.VMEM((18 * channels, 2 * width), bf16)] * 2,
+        compiler_params=params,
+        name="inner",
+    )(own, near, across, bias, w_in, w_out)
+
+
+def outer_kernel(near_ref, across_ref, far_across_ref, far_near_ref, field_ref, hid_hi, hid_lo, bias_ref, in_ref,
+                 out_ref, before_ref, fields_ref, wide_hi, wide_lo, side_hi, side_lo):
+    channels, width = near_ref.shape[1:]
+    hidden = in_ref.shape[0] // 2
+    wide = (wide_hi, wide_lo)
+    side = (side_hi, side_lo)
+    bias = jnp.concatenate([bias_ref[...]] * 2, axis=1)
     w_in = in_ref[...]
     w_out = out_ref[...]
-    bias = jnp.concatenate([bias_ref[...]] * 2, axis=1)
-
-    def initial(index):
-        slab, row = index // 2, index % 2
-        if slab == 2:
-            return own_ref[row]
-        first, second = {
-            0: (far_across_ref, far_near_ref),
-            1: (across_ref, near_ref),
-            3: (near_ref, across_ref),
-            4: (far_near_ref, far_across_ref),
-        }[slab]
-        value = jnp.where(even, first[row], second[row])
-        return jnp.where(inside(index - 4), value, 0.0)
-
-    def advance(field, first, count, keep, step):
-        for index in range(count):
-            put_windows(wide, index, field(index))
-        for pair in range(0, count - 2, 2):
-            before = to_channels(w_in, wide, pair, channels) + bias
-            if pair in keep:
-                before_ref[step, keep.index(pair)] = before
-            active = gelu(before)
-            for half in range(2):
-                row = active[:, half * width : (half + 1) * width]
-                row = jnp.where(inside(first + 1 + pair + half), row, 0.0)
-                put_twice(hid, pair + half, hidden, 0, split(row))
-        result = []
-        for pair in range(0, count - 4, 2):
-            moved = from_channels(w_out, hid, pair, hidden, channels)
-            for half in range(2):
-                row = field(pair + 2 + half) + moved[half]
-                result.append(jnp.where(inside(first + 2 + pair + half), row, 0.0))
-        return result
-
-    first = advance(initial, -4, 10, (2, 4), 0)
-    for half in range(2):
-        fields_ref[half * channels : (half + 1) * channels, :] = first[2 + half]
-    second = advance(lambda index: first[index], -2, 6, (0, 2), 1)
-    for half in range(2):
-        fields_ref[(2 + half) * channels : (3 + half) * channels, :] = second[half]
-
-
-def forward(own, near, across, far_across, far_near, bias, w_in, w_out):
-    channels, width = own.shape[1:]
+    fields = [None, None] + [field_ref[row * channels : (row + 1) * channels, :] for row in range(2)] + [None, None]
+    count = 2 * hidden
+    for after in range(2):
+        if after:
+            slabs = (either(near_ref, across_ref), either(far_near_ref, far_across_ref))
+        else:
+            slabs = (either(far_across_ref, far_near_ref), either(across_ref, near_ref))
+        first = 2 if after else -4
+        base = 4 * after
+        rows = []
+        for index in range(4):
+            row = jnp.where(inside(first + index), slabs[index // 2](index % 2), 0.0)
+            rows.append(row)
+            put_windows(wide, base + index, row)
+        before = to_channels(w_in, wide, base, channels) + bias
+        if after:
+            for ref, known in zip(side, (hid_hi, hid_lo)):
+                ref[4 * hidden : 5 * hidden, :] = known[count : count + hidden, :]
+                ref[5 * hidden : 6 * hidden, :width] = known[count : count + hidden, width:]
+            activate(before, 3, side, 6, hidden, width)
+        else:
+            for ref, known in zip(side, (hid_hi, hid_lo)):
+                ref[count : count + hidden, :] = known[:hidden, :]
+                ref[hidden:count, width:] = known[:hidden, :width]
+            activate(before, -3, side, 0, hidden, width)
+        moved = from_channels(w_out, side, base, hidden, channels)
+        for row in range(2):
+            at = 4 * after + row
+            value = rows[(0 if after else 2) + row] + moved[row]
+            fields[at] = jnp.where(inside(at - 2), value, 0.0)
+    for index in range(6):
+        put_windows(wide, index, fields[index])
+    for pair in (0, 2):
+        before = to_channels(w_in, wide, pair, channels) + bias
+        before_ref[pair // 2] = before
+        activate(before, pair - 1, side, pair, hidden, width)
+    moved = from_channels(w_out, side, 0, hidden, channels)
+    for row in range(2):
+        fields_ref[row * channels : (row + 1) * channels, :] = fields[2 + row]
+        fields_ref[(2 + row) * channels : (3 + row) * channels, :] = fields[2 + row] + moved[row]
+
+
+def outer(near, across, far_across, far_near, field, hid, bias, w_in, w_out):
+    channels, width = near.shape[1:]
     hidden = w_in.shape[0] // 2
-    vmem = pl.BlockSpec(memory_space=pltpu.VMEM)
-    return pl.pallas_call(
-        forward_kernel,
-        in_specs=[vmem] * 8,
+    return pl.pallas_call(
+        outer_kernel,
         out_shape=[
-            jax.ShapeDtypeStruct((2, 2, hidden, 2 * width), f32),
+            jax.ShapeDtypeStruct((2, hidden, 2 * width), f32),
             jax.ShapeDtypeStruct((4 * channels, width), f32),
         ],
-        scratch_shapes=[pltpu.VMEM((30 * channels, 2 * width), bf16)] * 2
+        scratch_shapes=[pltpu.VMEM((24 * channels, 2 * width), bf16)] * 2
         + [pltpu.VMEM((8 * hidden, 2 * width), bf16)] * 2,
         compiler_params=params,
-        name="forward",
-    )(own, near, across, far_across, far_near, bias, w_in, w_out)
+        name="outer",
+    )(near, across, far_across, far_near, field, *hid, bias, w_in, w_out)
 
 
 def crps_kernel(weight_ref, fields_ref, targets_ref, out_ref):
@@ -358,12 +406,15 @@
     )(*messages)
 
 
-def finish_kernel(count, gradient_ref, known_ref, opposite_ref, out_hbm, loss_ref, done):
-    copy = pltpu.make_async_copy(gradient_ref, out_hbm, done)
+def finish_kernel(count, gradient_ref, known_ref, opposite_ref, out_hbm, loss_hbm, loss_ref, done):
+    copy = pltpu.make_async_copy(gradient_ref, out_hbm, done.at[0])
     copy.start()
     total = jnp.sum(table_of(known_ref, opposite_ref), axis=0, keepdims=True)
     loss_ref[...] = jnp.sum(total, axis=1, keepdims=True) / count
+    second = pltpu.make_async_copy(loss_ref, loss_hbm, done.at[1])
+    second.start()
     copy.wait()
+    second.wait()
 
 
 def finish(gradient, known, opposite, count):
@@ -375,69 +426,90 @@
             jax.ShapeDtypeStruct((1, 1), f32),
         ],
         in_specs=[vmem] * 3,
-        out_specs=[pl.BlockSpec(memory_space=pltpu.HBM), vmem],
-        scratch_shapes=[pltpu.SemaphoreType.DMA(())],
+        out_specs=[pl.BlockSpec(memory_space=pltpu.HBM)] * 2,
+        scratch_shapes=[pltpu.VMEM((1, 1), f32), pltpu.SemaphoreType.DMA((2,))],
         compiler_params=params,
         name="finish",
     )(gradient, known, opposite)
 
 
-def backward_kernel(step, own_ref, near_ref, across_ref, slope_ref, outb_ref, inb_ref,
-                    *rest):
-    added, far_ref = rest[:-5][:1], rest[:-5][1:]
-    out_ref, wide_hi, wide_lo, hid_hi, hid_lo = rest[-5:]
+def hidden_grads(step, near_side, beside_ref, own_ref, slope_ref, weight_ref, wide):
     width = own_ref.shape[1]
     channels = (own_ref.shape[0] - slab_count) // 2
-    hidden = outb_ref.shape[0] // 2
     even = is_even()
-    wide = (wide_hi, wide_lo)
-    hid = (hid_hi, hid_lo)
-    w_out = outb_ref[...]
-    w_in = inb_ref[...]
+    below = even if near_side else jnp.logical_not(even)
 
     def take(ref, row):
         return ref[row * channels : (row + 1) * channels, :]
 
-    def put_beside(index, first, second, row):
-        value = jnp.where(even, take(first, row), take(second, row))
-        value = jnp.where(inside(index - 2), value, 0.0)
-        put_windows(wide, index, value)
-
-    for row in range(2):
-        put_windows(wide, 2 + row, take(own_ref, row))
-    for row in range(2):
-        put_beside(row, across_ref, near_ref, row)
-        put_beside(4 + row, near_ref, across_ref, row)
-    for pair in (0, 2):
-        grads = to_channels(w_out, wide, pair, channels) * slope_ref[step, pair // 2]
-        for half in range(2):
-            row = grads[:, half * width : (half + 1) * width]
-            row = jnp.where(inside(pair + half - 1), row, 0.0)
-            put_twice(hid, pair + half, hidden, 0, split(row))
-    moved = from_channels(w_in, hid, 0, hidden, channels)
-    for row in range(2):
-        total = take(own_ref, row) + moved[row]
-        for extra in added:
-            total = total + take(extra, row)
-        out_ref[row * channels : (row + 1) * channels, :] = total
-    if far_ref:
-        out_ref[2 * channels :, :] = table_of(own_ref, near_ref, across_ref, *far_ref)
-
-
-def backward(step, own, near, across, slopes, w_out, w_in, *added):
+    first = jnp.where(below, 0, -2)
+    for index in range(4):
+        own, beside = take(own_ref, index % 2), take(beside_ref, index % 2)
+        row = jnp.where(below, own, beside) if index < 2 else jnp.where(below, beside, own)
+        put_windows(wide, index, jnp.where(inside(first + index), row, 0.0))
+    grads = to_channels(weight_ref[...], wide, 0, channels) * slope_ref[step, jnp.where(below, 1, 0)]
+    rows = []
+    for half in range(2):
+        row = grads[:, half * width : (half + 1) * width]
+        rows.append(split(jnp.where(inside(first + 1 + half), row, 0.0)))
+    return rows
+
+
+def backward_near_kernel(step, own_ref, near_ref, slope_ref, outb_ref, high_ref, low_ref, wide_hi, wide_lo):
+    rows = hidden_grads(step, True, near_ref, own_ref, slope_ref, outb_ref, (wide_hi, wide_lo))
+    for half in range(2):
+        high_ref[half], low_ref[half] = rows[half]
+
+
+def backward_near(step, own, near, slopes, w_out):
     count, width = own.shape
     channels = (count - slab_count) // 2
     hidden = w_out.shape[0] // 2
-    vmem = pl.BlockSpec(memory_space=pltpu.VMEM)
+    return pl.pallas_call(
+        functools.partial(backward_near_kernel, step),
+        out_shape=[jax.ShapeDtypeStruct((2, hidden, width), bf16)] * 2,
+        scratch_shapes=[pltpu.VMEM((12 * channels, 2 * width), bf16)] * 2,
+        compiler_params=params,
+        name="backward_near",
+    )(own, near, slopes, w_out)
+
+
+def backward_kernel(step, own_ref, across_ref, slope_ref, high_ref, low_ref, outb_ref, inb_ref, *rest):
+    added, tables = rest[:-5][:1], rest[:-5][1:]
+    out_ref, wide_hi, wide_lo, hid_hi, hid_lo = rest[-5:]
+    channels = (own_ref.shape[0] - slab_count) // 2
+    hidden = outb_ref.shape[0] // 2
+    hid = (hid_hi, hid_lo)
+    even = is_even()
+    rows = hidden_grads(step, False, across_ref, own_ref, slope_ref, outb_ref, (wide_hi, wide_lo))
+    for half in range(2):
+        known = (high_ref[half], low_ref[half])
+        pairs = list(zip(rows[half], known))
+        put_twice(hid, half, hidden, 0, [jnp.where(even, far, close) for far, close in pairs])
+        put_twice(hid, 2 + half, hidden, 0, [jnp.where(even, close, far) for far, close in pairs])
+    moved = from_channels(inb_ref[...], hid, 0, hidden, channels)
+    for row in range(2):
+        part = slice(row * channels, (row + 1) * channels)
+        total = own_ref[part, :] + moved[row]
+        for extra in added:
+            total = total + extra[part, :]
+        out_ref[part, :] = total
+    if tables:
+        out_ref[2 * channels :, :] = table_of(own_ref, across_ref, *tables)
+
+
+def backward(step, own, across, slopes, close, w_out, w_in, *added):
+    count, width = own.shape
+    channels = (count - slab_count) // 2
+    hidden = w_out.shape[0] // 2
     return pl.pallas_call(
         functools.partial(backward_kernel, step),
-        in_specs=[vmem] * (6 + len(added)),
         out_shape=jax.ShapeDtypeStruct((count if step else 2 * channels, width), f32),
-        scratch_shapes=[pltpu.VMEM((18 * channels, 2 * width), bf16)] * 2
+        scratch_shapes=[pltpu.VMEM((12 * channels, 2 * width), bf16)] * 2
         + [pltpu.VMEM((4 * hidden, 2 * width), bf16)] * 2,
         compiler_params=params,
         name="backward",
-    )(own, near, across, slopes, w_out, w_in, *added)
+    )(own, across, slopes, *close, w_out, w_in, *added)
 
 
 def on_device(initial_states, targets, lat_weight, weight_in, weight_out, hidden_bias):
@@ -451,34 +523,39 @@
     own = initial_states[0]
     beside = lax.ppermute(own, LAT, near)
     crossed = lax.ppermute(own, LAT, across)
+    ready = prepare(weight_in.T, weight_out, hidden_bias[None, :], lat_weight[None, :], width)
+    crossed, beside, ready = lax.optimization_barrier((crossed, beside, ready))
     far_crossed = lax.ppermute(beside, LAT, across)
-    ready = prepare(weight_in.T, weight_out, hidden_bias[None, :], lat_weight[None, :], width)
-    crossed, beside = lax.optimization_barrier((crossed, beside))
     far_beside = lax.ppermute(crossed, LAT, near)
-    before, fields = forward(
-        own, beside, crossed, far_crossed, far_beside, ready[2], ready[0], ready[1]
+    w_in, w_out, bias, lat_weights = ready
+    before_first, field, *hid = inner(own, beside, crossed, bias, w_in, w_out)
+    before_second, fields = outer(
+        beside, crossed, far_crossed, far_beside, field, hid, bias, w_in, w_out
     )
     height = steps * slab_rows * channels // members
     chunks = lax.all_to_all(
         fields.reshape(members, height, width), MEMBER, split_axis=0, concat_axis=0, tiled=True
     )
-    grads = crps(ready[3], chunks, targets.reshape(members, height, width))
+    grads = crps(lat_weights, chunks, targets.reshape(members, height, width))
     grads = lax.all_to_all(grads, MEMBER, split_axis=0, concat_axis=0, tiled=True)
-    grads, before = lax.optimization_barrier((grads, before))
-    w_out_back, w_in_back, slopes = prepare_back(weight_in.T, weight_out, before)
+    grads, before_first = lax.optimization_barrier((grads, before_first))
+    back = prepare_back(weight_in.T, weight_out, before_first, before_second)
+    w_out_back, w_in_back, slopes = back
     first_grads, message, known = collect(grads)
 
     beside = lax.ppermute(message, LAT, near)
     crossed = lax.ppermute(message, LAT, across)
     far = lax.ppermute(known, LAT, [(i, i ^ 4) for i in range(slabs)])
-    beside, crossed, far, slopes = lax.optimization_barrier((beside, crossed, far, slopes))
+    close = backward_near(1, message, beside, slopes, w_out_back)
     message = backward(
-        1, message, beside, crossed, slopes, w_out_back, w_in_back, first_grads, far
+        1, message, crossed, slopes, close, w_out_back, w_in_back, first_grads, beside, far
     )
     beside = lax.ppermute(message, LAT, near)
     crossed = lax.ppermute(message, LAT, across)
+    close = backward_near(0, message, beside, slopes, w_out_back)
+    crossed, close = lax.optimization_barrier((crossed, close))
     known = merge(message, beside, crossed)
-    gradient = backward(0, message, beside, crossed, slopes, w_out_back, w_in_back)
+    gradient = backward(0, message, crossed, slopes, close, w_out_back, w_in_back)
     opposite = lax.ppermute(known, LAT, [(i, i ^ 8) for i in range(slabs)])
     gradient, loss = finish(
         gradient, known, opposite, members * steps * rows * channels * width

time: 65.1 us -> 63.1 us (0.969)
  waiting for transfers between devices: 12.1 us -> 7.91 us
  Pallas kernels: 13.1 us -> 15.2 us
    pallas_call x3 -> x6, Pallas kernels: 8.25 us -> 10.9 us  [the longest x1 4.3 us: outer(): pl.pallas_call(outer_kernel, out_shape=[jax.ShapeDtypeStruct((2, hidden,...]
    ppermute x1, waiting for transfers between devices: 2.37 us -> 0.59 us  [on_device(): crossed = lax.ppermute(own, LAT, across)]
    ppermute x1, starting transfers between devices: 1.01 us -> 1.83 us  [on_device(): opposite = lax.ppermute(known, LAT, [(i, i ^ 8) for i in range(slabs)])]
    ppermute x2, starting transfers between devices: 3.12 us -> 2.37 us  [on_device(): crossed = lax.ppermute(message, LAT, across)]
    ppermute x2, waiting for transfers between devices: 4.87 us -> 4.12 us  [on_device(): crossed = lax.ppermute(message, LAT, across)]
    ppermute x1, waiting for transfers between devices: 0.78 us -> 0.11 us  [on_device(): opposite = lax.ppermute(known, LAT, [(i, i ^ 8) for i in range(slabs)])]
  transfers between devices with their start and end apart: 10 -> 10, of which waited for: 6 -> 6; matrix products, arithmetic and copies ran while one was open for 0% -> 0% of each run, Pallas kernels for 8% -> 13%
where the time goes in v5:
time: 63.1 us; the launch traced here: 62.8 us
  blocking collectives  26.4 us (42%)
  Pallas kernels  15.2 us (24%)
  starting transfers between devices  12.6 us (20%)
  waiting for transfers between devices  7.91 us (13%)
  between operations  0.75 us (1%)
    all_to_all x1, blocking collectives, on_device(): lax.all_to_all(fields.reshape(members, height, width), MEMBER, split_axis...  15.7 us
    all_to_all x1, blocking collectives, on_device(): lax.all_to_all(grads, MEMBER, split_axis=0, concat_axis=0, tiled=True)  10.7 us
    pallas_call x1, Pallas kernels, outer(): pl.pallas_call(outer_kernel, out_shape=[jax.ShapeDtypeStruct((2, hidden,...  4.3 us
    ppermute x1, starting transfers between devices, on_device(): crossed = lax.ppermute(own, LAT, across)  4.3 us
    ppermute x2, waiting for transfers between devices, on_device(): crossed = lax.ppermute(message, LAT, across)  4.12 us
    ppermute x1, starting transfers between devices, on_device(): far_crossed = lax.ppermute(beside, LAT, across)  3.81 us
    pallas_call x2, Pallas kernels, backward(): pl.pallas_call(functools.partial(backward_kernel, step), out_shape=jax.Sh...  3.4 us
    ppermute x1, waiting for transfers between devices, on_device(): far = lax.ppermute(known, LAT, [(i, i ^ 4) for i in range(slabs)])  2.83 us
  transfers between devices with their start and end apart: 10, of which 6 were waited for; matrix products, arithmetic and copies ran while one was open for 0% of the time, Pallas kernels for 13%

profile of v5, /device:TPU:0, one launch (start us, length us, event | category | flops | bytes accessed | tf_op | source)
XLA Modules:
  0.0 62.8 jit_solution(8404748272431136336)
XLA Ops:
  0.6 0.1 collective-permute-start.1
  0.7 4.3 %collective-permute-start = (f32[2,80,128]{2,1,0:T(8,128)}, f32[2,80,128]{2,1,0:T(8,128)S(1)}, u32[]{:S(2)}, u32[]{:S(2)}) collective-permute-start(f32[2,80,128]{2,1,0:T(8,128)} %bitcast.11), channel_id=1, source_target_pairs={{0,15},{1,2},{2,1},{3,4},{4,3},{5,6},{6,5},{7,8},{8,7},{9,10},{10,... | collective-permute-start | bytes 245768 | tf_op jit(solution)/shard_map/ppermute | solution.py:525
  5.0 0.0 copy-start.1
  5.0 1.8 %prepare.1 = (bf16[512,720]{1,0:T(8,128)(2,1)S(1)}, bf16[480,768]{1,0:T(8,128)(2,1)S(1)}, f32[256,128]{1,0:T(8,128)S(1)}, f32[16,128]{1,0:T(8,128)S(1)}) custom-call(f32[720,256]{1,0:T(8,128)} %bitcast.13, f32[80,2304]{1,0:T(8,128)} %wout_hbm.3, f32[1,256]{1,0:T(1,128)} %bitcast.15, f32[1,2]{1,0:T(1,128)} %bitcast.16), custom_call_target="tpu_custom_call" | custom-call | tf_op jit(solution)/shard_map/prepare/pallas_call | solution.py:126
  6.8 0.0 collective-permute-done.1.near_ref
  6.8 0.6 collective-permute-done.across_ref
  7.4 3.8 %collective-permute-start.2 = (f32[2,80,128]{2,1,0:T(8,128)S(1)}, f32[2,80,128]{2,1,0:T(8,128)S(1)}, u32[]{:S(2)}, u32[]{:S(2)}) collective-permute-start(f32[2,80,128]{2,1,0:T(8,128)S(1)} %collective-permute-done.1.near_ref), channel_id=1, source_target_pairs={{0,15},{1,2},{2,1},{3,4},{4,3},{5,6},{6,5},{7,8},{8,7},{9,10},{10,... | collective-permute-start | bytes 245768 | tf_op jit(solution)/shard_map/ppermute | solution.py:528
  11.2 0.0 collective-permute-start.3
  11.2 0.0 copy-done.1
  11.2 1.9 %inner.1 = (f32[2,256,256]{2,1,0:T(8,128)S(1)}, f32[160,128]{1,0:T(8,128)S(1)}, bf16[1024,256]{1,0:T(8,128)(2,1)S(1)}, bf16[1024,256]{1,0:T(8,128)(2,1)S(1)}) custom-call(f32[2,80,128]{2,1,0:T(8,128)S(1)} %bitcast.12, f32[2,80,128]{2,1,0:T(8,128)S(1)} %collective-permute-done.1.near_ref, f32[2,80,128]{2,1,0:T(8,128)S(1)} %collective-permute-done.across_ref, ...), custom_call_target="tpu_custom_call" | custom-call | tf_op jit(solution)/shard_map/inner/pallas_call | solution.py:229
  13.1 0.2 collective-permute-done.2.far_across_ref
  13.4 0.0 collective-permute-done.3.far_near_ref
  13.4 4.3 %outer.1 = (f32[2,256,256]{2,1,0:T(8,128)S(1)}, f32[320,128]{1,0:T(8,128)S(1)}) custom-call(f32[2,80,128]{2,1,0:T(8,128)S(1)} %collective-permute-done.1.near_ref, f32[2,80,128]{2,1,0:T(8,128)S(1)} %collective-permute-done.across_ref, f32[2,80,128]{2,1,0:T(8,128)S(1)} %collective-permute-done.2.far_across_ref, ...), custom_call_target="tpu_custom_call" | custom-call | tf_op jit(solution)/shard_map/outer/pallas_call | solution.py:296
  17.7 0.0 copy-start
  17.7 15.7 %all_to_all.10.fields_ref = f32[8,40,128]{2,1,0:T(8,128)S(1)} all-to-all(f32[8,40,128]{2,1,0:T(8,128)S(1)} %bitcast.9), channel_id=1, replica_groups=mesh['member_0'=4,'member_1'=2,'lat_0'=2,'lat_1'=4,'lat_2'=2] {'member_0..., dimensions={0} | all-to-all | bytes 327680 | tf_op jit(solution)/shard_map/all_to_all | solution.py:536
  33.4 0.0 copy-done
  33.4 0.2 crps.1
  33.6 10.7 %all_to_all.11.grads_ref = f32[8,48,128]{2,1,0:T(8,128)S(1)} all-to-all(f32[8,48,128]{2,1,0:T(8,128)S(1)} %crps.1), channel_id=1, replica_groups=mesh['member_0'=4,'member_1'=2,'lat_0'=2,'lat_1'=4,'lat_2'=2] {'member_0..., dimensions={0} | all-to-all | bytes 393216 | tf_op jit(solution)/shard_map/all_to_all | solution.py:540
  44.4 0.1 collective-permute-start.5
  44.5 0.5 collective-permute-start.4
  44.9 0.0 collective-permute-start.6
  44.9 1.7 %prepare_back.1 = (bf16[512,720]{1,0:T(8,128)(2,1)S(1)}, bf16[480,768]{1,0:T(8,128)(2,1)S(1)}, f32[2,2,256,256]{3,2,1,0:T(8,128)S(1)}) custom-call(f32[720,256]{1,0:T(8,128)} %bitcast.14, f32[80,2304]{1,0:T(8,128)} %wout_hbm.3, f32[2,256,256]{2,1,0:T(8,128)S(1)} %get-tuple-element.52.first_ref, f32[2,256,256]{2,1,0:T(8,128)S(1)} %get-tuple-element.53.second_ref), custom_call_target="tpu_custom_call" | custom-call | tf_op jit(solution)/shard_map/prepare_back/pallas_call | solution.py:169
  46.6 0.0 collective-permute-done.5.near_ref.rest_1_
  46.6 0.6 %backward_near.2 = (bf16[2,256,128]{2,1,0:T(8,128)(2,1)S(1)}, bf16[2,256,128]{2,1,0:T(8,128)(2,1)S(1)}) custom-call(f32[176,128]{1,0:T(8,128)S(1)} %get-tuple-element.51.own_ref, f32[176,128]{1,0:T(8,128)S(1)} %collective-permute-done.5.near_ref.rest_1_, f32[2,2,256,256]{3,2,1,0:T(8,128)S(1)} %get-tuple-element.54.slope_ref, ...), custom_call_target="tpu_custom_call" | custom-call | tf_op jit(solution)/shard_map/backward_near/pallas_call | solution.py:468
  47.3 2.8 %collective-permute-done.6.rest_2_ = f32[16,128]{1,0:T(8,128)S(1)} collective-permute-done((f32[16,128]{1,0:T(8,128)S(1)}, f32[16,128]{1,0:T(8,128)S(1)}, u32[]{:S(2)}, u32[]{:S(2)}) %collective-permute-start.6) | collective-permute-done | bytes 8224 | tf_op jit(solution)/shard_map/ppermute | solution.py:548
  50.1 0.5 collective-permute-done.4.across_ref
  50.6 1.7 %backward.2.own_ref.refs_0_ = f32[176,128]{1,0:T(8,128)S(1)} custom-call(f32[176,128]{1,0:T(8,128)S(1)} %get-tuple-element.51.own_ref, f32[176,128]{1,0:T(8,128)S(1)} %collective-permute-done.4.across_ref, f32[2,2,256,256]{3,2,1,0:T(8,128)S(1)} %get-tuple-element.54.slope_ref, bf16[2,256,128]{2,1,0:T(8,128)(2,1)S(1)} %get-tuple-element.56.high_ref, ...), custom_call_target="tpu_custom_call" | custom-call | tf_op jit(solution)/shard_map/backward/pallas_call | solution.py:505
  52.3 0.1 collective-permute-start.8
  52.4 1.9 %collective-permute-start.7 = (f32[176,128]{1,0:T(8,128)S(1)}, f32[176,128]{1,0:T(8,128)S(1)}, u32[]{:S(2)}, u32[]{:S(2)}) collective-permute-start(f32[176,128]{1,0:T(8,128)S(1)} %backward.2.own_ref.refs_0_), channel_id=1, source_target_pairs={{0,15},{1,2},{2,1},{3,4},{4,3},{5,6},{6,5},{7,8},{8,7},{9,10},{10,... | collective-permute-start | bytes 270344 | tf_op jit(solution)/shard_map/ppermute | solution.py:554
  54.3 0.0 collective-permute-done.8.near_ref.refs_1_
  54.3 0.6 backward_near.3
  54.9 3.6 %collective-permute-done.7.across_ref.refs_2_ = f32[176,128]{1,0:T(8,128)S(1)} collective-permute-done((f32[176,128]{1,0:T(8,128)S(1)}, f32[176,128]{1,0:T(8,128)S(1)}, u32[]{:S(2)}, u32[]{:S(2)}) %collective-permute-start.7) | collective-permute-done | bytes 90144 | tf_op jit(solution)/shard_map/ppermute | solution.py:554
  58.5 1.8 %collective-permute-start.9 = (f32[16,128]{1,0:T(8,128)S(1)}, f32[16,128]{1,0:T(8,128)S(1)}, u32[]{:S(2)}, u32[]{:S(2)}) collective-permute-start(f32[16,128]{1,0:T(8,128)S(1)} %merge.1.known_ref), channel_id=1, source_target_pairs={{0,8},{1,9},{2,10},{3,11},{4,12},{5,13},{6,14},{7,15},{8,0},{9,1},... | collective-permute-start | bytes 24584 | tf_op jit(solution)/shard_map/ppermute | solution.py:559
  60.4 1.7 %backward.3.gradient_ref = f32[160,128]{1,0:T(8,128)S(1)} custom-call(f32[176,128]{1,0:T(8,128)S(1)} %backward.2.own_ref.refs_0_, f32[176,128]{1,0:T(8,128)S(1)} %collective-permute-done.7.across_ref.refs_2_, f32[2,2,256,256]{3,2,1,0:T(8,128)S(1)} %get-tuple-element.54.slope_ref, bf16[2,256,128]{2,1,0:T(8,128)(2,1)S(1)} %get-tuple-element.64.high_ref, ...), custom_call_target="tpu_custom_call" | custom-call | tf_op jit(solution)/shard_map/backward/pallas_call | solution.py:505
  62.1 0.1 collective-permute-done.9.opposite_ref
  62.2 0.7 %finish.1 = (f32[160,128]{1,0:T(8,128)}, f32[1,1]{1,0:T(1,128)}) custom-call(f32[160,128]{1,0:T(8,128)S(1)} %backward.3.gradient_ref, f32[16,128]{1,0:T(8,128)S(1)} %merge.1.known_ref, f32[16,128]{1,0:T(8,128)S(1)} %collective-permute-done.9.opposite_ref), custom_call_target="tpu_custom_call" | custom-call | tf_op jit(solution)/shard_map/finish/pallas_call | solution.py:422
  (2 shorter events, 0.0 us)
Async XLA Ops:
  0.6 6.2 %collective-permute-start.1 = (f32[2,80,128]{2,1,0:T(8,128)}, f32[2,80,128]{2,1,0:T(8,128)S(1)}, u32[]{:S(2)}, u32[]{:S(2)}) collective-permute-start(f32[2,80,128]{2,1,0:T(8,128)} %bitcast.10), channel_id=1, source_target_pairs={{0,1},{1,0},{2,3},{3,2},{4,5},{5,4},{6,7},{7,6},{8,9},{9,8},{10,11... | collective-permute-start | bytes 245768 | tf_op jit(solution)/shard_map/ppermute | solution.py:524
  0.7 6.7 %collective-permute-start = (f32[2,80,128]{2,1,0:T(8,128)}, f32[2,80,128]{2,1,0:T(8,128)S(1)}, u32[]{:S(2)}, u32[]{:S(2)}) collective-permute-start(f32[2,80,128]{2,1,0:T(8,128)} %bitcast.11), channel_id=1, source_target_pairs={{0,15},{1,2},{2,1},{3,4},{4,3},{5,6},{6,5},{7,8},{8,7},{9,10},{10,... | collective-permute-start | bytes 245768 | tf_op jit(solution)/shard_map/ppermute | solution.py:525
  5.0 6.2 %copy-start.1 = (f32[1,2,80,128]{3,2,1,0:T(8,128)S(1)}, f32[1,2,80,128]{3,2,1,0:T(8,128)}, u32[]{:S(2)}) copy-start(f32[1,2,80,128]{3,2,1,0:T(8,128)} %param.6) | copy-start | bytes 245764
  7.4 6.0 %collective-permute-start.2 = (f32[2,80,128]{2,1,0:T(8,128)S(1)}, f32[2,80,128]{2,1,0:T(8,128)S(1)}, u32[]{:S(2)}, u32[]{:S(2)}) collective-permute-start(f32[2,80,128]{2,1,0:T(8,128)S(1)} %collective-permute-done.1.near_ref), channel_id=1, source_target_pairs={{0,15},{1,2},{2,1},{3,4},{4,3},{5,6},{6,5},{7,8},{8,7},{9,10},{10,... | collective-permute-start | bytes 245768 | tf_op jit(solution)/shard_map/ppermute | solution.py:528
  11.2 2.2 %collective-permute-start.3 = (f32[2,80,128]{2,1,0:T(8,128)S(1)}, f32[2,80,128]{2,1,0:T(8,128)S(1)}, u32[]{:S(2)}, u32[]{:S(2)}) collective-permute-start(f32[2,80,128]{2,1,0:T(8,128)S(1)} %collective-permute-done.across_ref), channel_id=1, source_target_pairs={{0,1},{1,0},{2,3},{3,2},{4,5},{5,4},{6,7},{7,6},{8,9},{9,8},{10,11... | collective-permute-start | bytes 245768 | tf_op jit(solution)/shard_map/ppermute | solution.py:529
  17.7 15.7 %copy-start = (f32[2,2,80,128]{3,2,1,0:T(8,128)S(1)}, f32[2,2,80,128]{3,2,1,0:T(8,128)}, u32[]{:S(2)}) copy-start(f32[2,2,80,128]{3,2,1,0:T(8,128)} %param.7) | copy-start | bytes 491524
  44.4 2.2 %collective-permute-start.5 = (f32[176,128]{1,0:T(8,128)S(1)}, f32[176,128]{1,0:T(8,128)S(1)}, u32[]{:S(2)}, u32[]{:S(2)}) collective-permute-start(f32[176,128]{1,0:T(8,128)S(1)} %get-tuple-element.51.own_ref), channel_id=1, source_target_pairs={{0,1},{1,0},{2,3},{3,2},{4,5},{5,4},{6,7},{7,6},{8,9},{9,8},{10,11... | collective-permute-start | bytes 270344 | tf_op jit(solution)/shard_map/ppermute | solution.py:546
  44.5 6.1 %collective-permute-start.4 = (f32[176,128]{1,0:T(8,128)S(1)}, f32[176,128]{1,0:T(8,128)S(1)}, u32[]{:S(2)}, u32[]{:S(2)}) collective-permute-start(f32[176,128]{1,0:T(8,128)S(1)} %get-tuple-element.51.own_ref), channel_id=1, source_target_pairs={{0,15},{1,2},{2,1},{3,4},{4,3},{5,6},{6,5},{7,8},{8,7},{9,10},{10,... | collective-permute-start | bytes 270344 | tf_op jit(solution)/shard_map/ppermute | solution.py:547
  44.9 5.2 %collective-permute-start.6 = (f32[16,128]{1,0:T(8,128)S(1)}, f32[16,128]{1,0:T(8,128)S(1)}, u32[]{:S(2)}, u32[]{:S(2)}) collective-permute-start(f32[16,128]{1,0:T(8,128)S(1)} %get-tuple-element.60), channel_id=1, source_target_pairs={{0,4},{1,5},{2,6},{3,7},{4,0},{5,1},{6,2},{7,3},{8,12},{9,13},{10,... | collective-permute-start | bytes 24584 | tf_op jit(solution)/shard_map/ppermute | solution.py:548
  52.3 2.0 %collective-permute-start.8 = (f32[176,128]{1,0:T(8,128)S(1)}, f32[176,128]{1,0:T(8,128)S(1)}, u32[]{:S(2)}, u32[]{:S(2)}) collective-permute-start(f32[176,128]{1,0:T(8,128)S(1)} %backward.2.own_ref.refs_0_), channel_id=1, source_target_pairs={{0,1},{1,0},{2,3},{3,2},{4,5},{5,4},{6,7},{7,6},{8,9},{9,8},{10,11... | collective-permute-start | bytes 270344 | tf_op jit(solution)/shard_map/ppermute | solution.py:553
  52.4 6.1 %collective-permute-start.7 = (f32[176,128]{1,0:T(8,128)S(1)}, f32[176,128]{1,0:T(8,128)S(1)}, u32[]{:S(2)}, u32[]{:S(2)}) collective-permute-start(f32[176,128]{1,0:T(8,128)S(1)} %backward.2.own_ref.refs_0_), channel_id=1, source_target_pairs={{0,15},{1,2},{2,1},{3,4},{4,3},{5,6},{6,5},{7,8},{8,7},{9,10},{10,... | collective-permute-start | bytes 270344 | tf_op jit(solution)/shard_map/ppermute | solution.py:554
  58.5 3.7 %collective-permute-start.9 = (f32[16,128]{1,0:T(8,128)S(1)}, f32[16,128]{1,0:T(8,128)S(1)}, u32[]{:S(2)}, u32[]{:S(2)}) collective-permute-start(f32[16,128]{1,0:T(8,128)S(1)} %merge.1.known_ref), channel_id=1, source_target_pairs={{0,8},{1,9},{2,10},{3,11},{4,12},{5,13},{6,14},{7,15},{8,0},{9,1},... | collective-permute-start | bytes 24584 | tf_op jit(solution)/shard_map/ppermute | solution.py:559

commit v6 on v5

--- a/solution.py
+++ b/solution.py
@@ -43,33 +43,28 @@
     return jnp.where(lane == row.shape[1] - 1, 0.0, pltpu.roll(row, row.shape[1] - 1, 1))
 
 
-def put_twice(refs, index, height, part, values):
-    width = values[0].shape[1]
-    size = values[0].shape[0]
+def put(refs, start, values):
     for ref, value in zip(refs, values):
-        base = index * height + part * size
-        if base + size <= ref.shape[0]:
-            ref[base : base + size, :width] = value
-        if index:
-            ref[base - height : base - height + size, width:] = value
+        ref[start : start + value.shape[0], :] = value
 
 
 def put_windows(refs, index, row):
-    height = 3 * row.shape[0]
+    channels = row.shape[0]
     for part, shifted in enumerate((from_left(row), row, from_right(row))):
-        put_twice(refs, index, height, part, split(shifted))
-
-
-def read(refs, start, size):
-    return tuple(ref[start : start + size, :] for ref in refs)
+        put(refs, (3 * index + part) * channels, split(shifted))
+
+
+def read(refs, start, size, height):
+    parts = [(ref[start : start + size, :], ref[start + height : start + height + size, :]) for ref in refs]
+    return tuple(jnp.concatenate(part, axis=1) for part in parts)
 
 
 def to_channels(weights, windows, pair, channels):
-    return product(weights, read(windows, pair * 3 * channels, 9 * channels))
+    return product(weights, read(windows, pair * 3 * channels, 9 * channels, 3 * channels))
 
 
 def from_channels(weights, hidden, pair, channels, outer):
-    mixed = product(weights, read(hidden, pair * channels, 3 * channels))
+    mixed = product(weights, read(hidden, pair * channels, 3 * channels, channels))
     width = mixed.shape[1] // 2
     rows = []
     for half in range(2):
@@ -82,8 +77,10 @@
     return rows
 
 
-def gelu(x):
-    return 0.5 * x * (1.0 + jnp.tanh(gelu_scale * (x + gelu_cubic * x * x * x)))
+def gelu(x, half):
+    t = jnp.tanh(x * (gelu_scale + (gelu_scale * gelu_cubic) * (x * x)))
+    h = half * x
+    return h + h * t
 
 
 def gelu_slope(x):
@@ -142,7 +139,15 @@
         copy.start()
     for step, before_ref in enumerate((first_ref, second_ref)):
         for pair in range(2):
-            slope_ref[step, pair] = gelu_slope(before_ref[pair])
+            slope = gelu_slope(before_ref[pair])
+            width = slope.shape[1] // 2
+            for half in range(2):
+                part = slope[:, half * width : (half + 1) * width]
+                if pair != half:
+                    slope_ref[step, pair, :, half * width : (half + 1) * width] = part
+                else:
+                    part = jnp.where(inside(3 * pair - 1), part, 0.0)
+                    slope_ref[step, pair, :, half * width : (half + 1) * width] = part
     for copy in copies:
         copy.wait()
     outer, width = wout_ref.shape
@@ -193,11 +198,11 @@
 
 
 def activate(before, first, hid, index, hidden, width):
-    active = gelu(before)
     for half in range(2):
-        row = active[:, half * width : (half + 1) * width]
-        row = jnp.where(inside(first + half), row, 0.0)
-        put_twice(hid, index + half, hidden, 0, split(row))
+        row = first + half
+        scale = 0.5 if row in (0, 1) else jnp.where(inside(row), 0.5, 0.0)
+        active = gelu(before[:, half * width : (half + 1) * width], scale)
+        put(hid, (index + half) * hidden, split(active))
 
 
 def inner_kernel(own_ref, near_ref, across_ref, bias_ref, in_ref, out_ref, before_ref, field_ref, hid_hi, hid_lo,
@@ -213,9 +218,8 @@
         if index // 2 != 1:
             row = jnp.where(inside(index - 2), row, 0.0)
         put_windows(wide, index, row)
-    w_in = in_ref[...]
     for pair in (0, 2):
-        before = to_channels(w_in, wide, pair, channels) + bias
+        before = to_channels(in_ref[...], wide, pair, channels) + bias
         before_ref[pair // 2] = before
         activate(before, pair - 1, hid, pair, hidden, width)
     moved = from_channels(out_ref[...], hid, 0, hidden, channels)
@@ -232,8 +236,8 @@
             jax.ShapeDtypeStruct((2, hidden, 2 * width), f32),
             jax.ShapeDtypeStruct((2 * channels, width), f32),
         ]
-        + [jax.ShapeDtypeStruct((4 * hidden, 2 * width), bf16)] * 2,
-        scratch_shapes=[pltpu.VMEM((18 * channels, 2 * width), bf16)] * 2,
+        + [jax.ShapeDtypeStruct((4 * hidden, width), bf16)] * 2,
+        scratch_shapes=[pltpu.VMEM((18 * channels, width), bf16)] * 2,
         compiler_params=params,
         name="inner",
     )(own, near, across, bias, w_in, w_out)
@@ -246,45 +250,37 @@
     wide = (wide_hi, wide_lo)
     side = (side_hi, side_lo)
     bias = jnp.concatenate([bias_ref[...]] * 2, axis=1)
-    w_in = in_ref[...]
-    w_out = out_ref[...]
     fields = [None, None] + [field_ref[row * channels : (row + 1) * channels, :] for row in range(2)] + [None, None]
-    count = 2 * hidden
-    for after in range(2):
-        if after:
-            slabs = (either(near_ref, across_ref), either(far_near_ref, far_across_ref))
-        else:
-            slabs = (either(far_across_ref, far_near_ref), either(across_ref, near_ref))
-        first = 2 if after else -4
-        base = 4 * after
-        rows = []
+    sides = (
+        (-4, (either(far_across_ref, far_near_ref), either(across_ref, near_ref))),
+        (2, (either(near_ref, across_ref), either(far_near_ref, far_across_ref))),
+    )
+    rows = []
+    for after, (first, slabs) in enumerate(sides):
         for index in range(4):
             row = jnp.where(inside(first + index), slabs[index // 2](index % 2), 0.0)
             rows.append(row)
-            put_windows(wide, base + index, row)
-        before = to_channels(w_in, wide, base, channels) + bias
-        if after:
-            for ref, known in zip(side, (hid_hi, hid_lo)):
-                ref[4 * hidden : 5 * hidden, :] = known[count : count + hidden, :]
-                ref[5 * hidden : 6 * hidden, :width] = known[count : count + hidden, width:]
-            activate(before, 3, side, 6, hidden, width)
-        else:
-            for ref, known in zip(side, (hid_hi, hid_lo)):
-                ref[count : count + hidden, :] = known[:hidden, :]
-                ref[hidden:count, width:] = known[:hidden, :width]
-            activate(before, -3, side, 0, hidden, width)
-        moved = from_channels(w_out, side, base, hidden, channels)
+            put_windows(wide, 4 * after + index, row)
+        for ref, known in zip(side, (hid_hi, hid_lo)):
+            ref[(2 + 2 * after) * hidden : (4 + 2 * after) * hidden, :] = known[
+                2 * after * hidden : 2 * (after + 1) * hidden, :
+            ]
+    before = [to_channels(in_ref[...], wide, 4 * after, channels) + bias for after in range(2)]
+    activate(before[0], -3, side, 0, hidden, width)
+    activate(before[1], 3, side, 6, hidden, width)
+    for after in range(2):
+        moved = from_channels(out_ref[...], side, 4 * after, hidden, channels)
         for row in range(2):
             at = 4 * after + row
-            value = rows[(0 if after else 2) + row] + moved[row]
+            value = rows[2 + 2 * after + row] + moved[row]
             fields[at] = jnp.where(inside(at - 2), value, 0.0)
     for index in range(6):
         put_windows(wide, index, fields[index])
     for pair in (0, 2):
-        before = to_channels(w_in, wide, pair, channels) + bias
+        before = to_channels(in_ref[...], wide, pair, channels) + bias
         before_ref[pair // 2] = before
         activate(before, pair - 1, side, pair, hidden, width)
-    moved = from_channels(w_out, side, 0, hidden, channels)
+    moved = from_channels(out_ref[...], side, 0, hidden, channels)
     for row in range(2):
         fields_ref[row * channels : (row + 1) * channels, :] = fields[2 + row]
         fields_ref[(2 + row) * channels : (3 + row) * channels, :] = fields[2 + row] + moved[row]
@@ -299,8 +295,8 @@
             jax.ShapeDtypeStruct((2, hidden, 2 * width), f32),
             jax.ShapeDtypeStruct((4 * channels, width), f32),
         ],
-        scratch_shapes=[pltpu.VMEM((24 * channels, 2 * width), bf16)] * 2
-        + [pltpu.VMEM((8 * hidden, 2 * width), bf16)] * 2,
+        scratch_shapes=[pltpu.VMEM((24 * channels, width), bf16)] * 2
+        + [pltpu.VMEM((8 * hidden, width), bf16)] * 2,
         compiler_params=params,
         name="outer",
     )(near, across, far_across, far_near, field, *hid, bias, w_in, w_out)
@@ -451,43 +447,43 @@
     rows = []
     for half in range(2):
         row = grads[:, half * width : (half + 1) * width]
-        rows.append(split(jnp.where(inside(first + 1 + half), row, 0.0)))
+        rows.append(split(row))
     return rows
 
 
-def backward_near_kernel(step, own_ref, near_ref, slope_ref, outb_ref, high_ref, low_ref, wide_hi, wide_lo):
-    rows = hidden_grads(step, True, near_ref, own_ref, slope_ref, outb_ref, (wide_hi, wide_lo))
+def backward_side_kernel(step, near_side, own_ref, beside_ref, slope_ref, outb_ref, high_ref, low_ref, wide_hi,
+                         wide_lo):
+    rows = hidden_grads(step, near_side, beside_ref, own_ref, slope_ref, outb_ref, (wide_hi, wide_lo))
     for half in range(2):
         high_ref[half], low_ref[half] = rows[half]
 
 
-def backward_near(step, own, near, slopes, w_out):
+def backward_side(step, near_side, own, beside, slopes, w_out):
     count, width = own.shape
     channels = (count - slab_count) // 2
     hidden = w_out.shape[0] // 2
     return pl.pallas_call(
-        functools.partial(backward_near_kernel, step),
+        functools.partial(backward_side_kernel, step, near_side),
         out_shape=[jax.ShapeDtypeStruct((2, hidden, width), bf16)] * 2,
-        scratch_shapes=[pltpu.VMEM((12 * channels, 2 * width), bf16)] * 2,
-        compiler_params=params,
-        name="backward_near",
-    )(own, near, slopes, w_out)
-
-
-def backward_kernel(step, own_ref, across_ref, slope_ref, high_ref, low_ref, outb_ref, inb_ref, *rest):
-    added, tables = rest[:-5][:1], rest[:-5][1:]
-    out_ref, wide_hi, wide_lo, hid_hi, hid_lo = rest[-5:]
+        scratch_shapes=[pltpu.VMEM((12 * channels, width), bf16)] * 2,
+        compiler_params=params,
+        name="backward_near" if near_side else "backward_across",
+    )(own, beside, slopes, w_out)
+
+
+def join_kernel(own_ref, close_hi, close_lo, far_hi, far_lo, inb_ref, *rest):
+    added, tables = rest[:-3][:1], rest[:-3][1:]
+    out_ref, hid_hi, hid_lo = rest[-3:]
     channels = (own_ref.shape[0] - slab_count) // 2
-    hidden = outb_ref.shape[0] // 2
-    hid = (hid_hi, hid_lo)
+    hidden = close_hi.shape[1]
     even = is_even()
-    rows = hidden_grads(step, False, across_ref, own_ref, slope_ref, outb_ref, (wide_hi, wide_lo))
     for half in range(2):
-        known = (high_ref[half], low_ref[half])
-        pairs = list(zip(rows[half], known))
-        put_twice(hid, half, hidden, 0, [jnp.where(even, far, close) for far, close in pairs])
-        put_twice(hid, 2 + half, hidden, 0, [jnp.where(even, close, far) for far, close in pairs])
-    moved = from_channels(inb_ref[...], hid, 0, hidden, channels)
+        far = pl.multiple_of(jnp.where(even, half, 2 + half) * hidden, hidden)
+        close = pl.multiple_of(jnp.where(even, 2 + half, half) * hidden, hidden)
+        for ref, far_ref, close_ref in ((hid_hi, far_hi, close_hi), (hid_lo, far_lo, close_lo)):
+            ref[pl.ds(far, hidden), :] = far_ref[half]
+            ref[pl.ds(close, hidden), :] = close_ref[half]
+    moved = from_channels(inb_ref[...], (hid_hi, hid_lo), 0, hidden, channels)
     for row in range(2):
         part = slice(row * channels, (row + 1) * channels)
         total = own_ref[part, :] + moved[row]
@@ -495,21 +491,20 @@
             total = total + extra[part, :]
         out_ref[part, :] = total
     if tables:
-        out_ref[2 * channels :, :] = table_of(own_ref, across_ref, *tables)
-
-
-def backward(step, own, across, slopes, close, w_out, w_in, *added):
+        out_ref[2 * channels :, :] = table_of(own_ref, *tables)
+
+
+def join(own, close, far, w_in, *added):
     count, width = own.shape
     channels = (count - slab_count) // 2
-    hidden = w_out.shape[0] // 2
-    return pl.pallas_call(
-        functools.partial(backward_kernel, step),
-        out_shape=jax.ShapeDtypeStruct((count if step else 2 * channels, width), f32),
-        scratch_shapes=[pltpu.VMEM((12 * channels, 2 * width), bf16)] * 2
-        + [pltpu.VMEM((4 * hidden, 2 * width), bf16)] * 2,
-        compiler_params=params,
-        name="backward",
-    )(own, across, slopes, *close, w_out, w_in, *added)
+    hidden = close[0].shape[1]
+    return pl.pallas_call(
+        join_kernel,
+        out_shape=jax.ShapeDtypeStruct((count if added else 2 * channels, width), f32),
+        scratch_shapes=[pltpu.VMEM((4 * hidden, width), bf16)] * 2,
+        compiler_params=params,
+        name="join",
+    )(own, *close, *far, w_in, *added)
 
 
 def on_device(initial_states, targets, lat_weight, weight_in, weight_out, hidden_bias):
@@ -538,7 +533,6 @@
     )
     grads = crps(lat_weights, chunks, targets.reshape(members, height, width))
     grads = lax.all_to_all(grads, MEMBER, split_axis=0, concat_axis=0, tiled=True)
-    grads, before_first = lax.optimization_barrier((grads, before_first))
     back = prepare_back(weight_in.T, weight_out, before_first, before_second)
     w_out_back, w_in_back, slopes = back
     first_grads, message, known = collect(grads)
@@ -546,16 +540,17 @@
     beside = lax.ppermute(message, LAT, near)
     crossed = lax.ppermute(message, LAT, across)
     far = lax.ppermute(known, LAT, [(i, i ^ 4) for i in range(slabs)])
-    close = backward_near(1, message, beside, slopes, w_out_back)
-    message = backward(
-        1, message, crossed, slopes, close, w_out_back, w_in_back, first_grads, beside, far
-    )
+    close = backward_side(1, True, message, beside, slopes, w_out_back)
+    crossed, close = lax.optimization_barrier((crossed, close))
+    distant = backward_side(1, False, message, crossed, slopes, w_out_back)
+    message = join(message, close, distant, w_in_back, first_grads, beside, crossed, far)
     beside = lax.ppermute(message, LAT, near)
     crossed = lax.ppermute(message, LAT, across)
-    close = backward_near(0, message, beside, slopes, w_out_back)
+    close = backward_side(0, True, message, beside, slopes, w_out_back)
     crossed, close = lax.optimization_barrier((crossed, close))
     known = merge(message, beside, crossed)
-    gradient = backward(0, message, crossed, slopes, close, w_out_back, w_in_back)
+    distant = backward_side(0, False, message, crossed, slopes, w_out_back)
+    gradient = join(message, close, distant, w_in_back)
     opposite = lax.ppermute(known, LAT, [(i, i ^ 8) for i in range(slabs)])
     gradient, loss = finish(
         gradient, known, opposite, members * steps * rows * channels * width

time: 63.1 us -> 61.7 us (0.978)
  starting transfers between devices: 12.6 us -> 10.3 us
  waiting for transfers between devices: 7.91 us -> 10.1 us
  Pallas kernels: 15.2 us -> 13.4 us
    ppermute x2, waiting for transfers between devices: 4.12 us -> 7.6 us  [on_device(): crossed = lax.ppermute(message, LAT, across)]
    ppermute x1, waiting for transfers between devices: 2.83 us -> 0.01 us  [on_device(): far = lax.ppermute(known, LAT, [(i, i ^ 4) for i in range(slabs)])]
    ppermute x1, waiting for transfers between devices: 0.11 us -> 1.34 us  [on_device(): opposite = lax.ppermute(known, LAT, [(i, i ^ 8) for i in range(slabs)])]
    pallas_call x4 -> x6, Pallas kernels: 4.65 us -> 3.64 us  [the longest x4 2.49 us: backward_side(): pl.pallas_call(functools.partial(backward_side_kernel, step, near_side),...]
    pallas_call x1, Pallas kernels: 4.3 us -> 3.5 us  [outer(): pl.pallas_call(outer_kernel, out_shape=[jax.ShapeDtypeStruct((2, hidden,...]
    ppermute x1, starting transfers between devices: 1.83 us -> 1.1 us  [on_device(): opposite = lax.ppermute(known, LAT, [(i, i ^ 8) for i in range(slabs)])]
    ppermute x2, starting transfers between devices: 2.37 us -> 1.7 us  [on_device(): crossed = lax.ppermute(message, LAT, across)]
  transfers between devices with their start and end apart: 10 -> 10, of which waited for: 6 -> 5; matrix products, arithmetic and copies ran while one was open for 0% -> 0% of each run, Pallas kernels for 13% -> 14%
where the time goes in v6:
time: 61.7 us; the launch traced here: 61.4 us
  blocking collectives  26.8 us (43%)
  Pallas kernels  13.4 us (22%)
  starting transfers between devices  10.3 us (17%)
  waiting for transfers between devices  10.1 us (16%)
  between operations  0.76 us (1%)
    all_to_all x1, blocking collectives, on_device(): lax.all_to_all(fields.reshape(members, height, width), MEMBER, split_axis...  15.8 us
    all_to_all x1, blocking collectives, on_device(): lax.all_to_all(grads, MEMBER, split_axis=0, concat_axis=0, tiled=True)  10.9 us
    ppermute x2, waiting for transfers between devices, on_device(): crossed = lax.ppermute(message, LAT, across)  7.6 us
    ppermute x1, starting transfers between devices, on_device(): crossed = lax.ppermute(own, LAT, across)  3.71 us
    ppermute x1, starting transfers between devices, on_device(): far_crossed = lax.ppermute(beside, LAT, across)  3.64 us
    pallas_call x1, Pallas kernels, outer(): pl.pallas_call(outer_kernel, out_shape=[jax.ShapeDtypeStruct((2, hidden,...  3.5 us
    pallas_call x4, Pallas kernels, backward_side(): pl.pallas_call(functools.partial(backward_side_kernel, step, near_side),...  2.49 us
    pallas_call x1, Pallas kernels, inner(): pl.pallas_call(inner_kernel, out_shape=[jax.ShapeDtypeStruct((2, hidden,...  1.9 us
  transfers between devices with their start and end apart: 10, of which 5 were waited for; matrix products, arithmetic and copies ran while one was open for 0% of the time, Pallas kernels for 14%

profile of v6, /device:TPU:0, one launch (start us, length us, event | category | flops | bytes accessed | tf_op | source)
XLA Modules:
  0.0 61.4 jit_solution(4274208810160976916)
XLA Ops:
  0.6 3.7 %collective-permute-start = (f32[2,80,128]{2,1,0:T(8,128)}, f32[2,80,128]{2,1,0:T(8,128)S(1)}, u32[]{:S(2)}, u32[]{:S(2)}) collective-permute-start(f32[2,80,128]{2,1,0:T(8,128)} %bitcast.10), channel_id=1, source_target_pairs={{0,15},{1,2},{2,1},{3,4},{4,3},{5,6},{6,5},{7,8},{8,7},{9,10},{10,... | collective-permute-start | bytes 245768 | tf_op jit(solution)/shard_map/ppermute | solution.py:520
  4.3 0.0 collective-permute-start.1
  4.3 0.0 copy-start.1
  4.3 1.8 %prepare.1 = (bf16[512,720]{1,0:T(8,128)(2,1)S(1)}, bf16[480,768]{1,0:T(8,128)(2,1)S(1)}, f32[256,128]{1,0:T(8,128)S(1)}, f32[16,128]{1,0:T(8,128)S(1)}) custom-call(f32[720,256]{1,0:T(8,128)} %bitcast.13, f32[80,2304]{1,0:T(8,128)} %wout_hbm.3, f32[1,256]{1,0:T(1,128)} %bitcast.15, f32[1,2]{1,0:T(1,128)} %bitcast.16), custom_call_target="tpu_custom_call" | custom-call | tf_op jit(solution)/shard_map/prepare/pallas_call | solution.py:123
  6.1 0.8 %collective-permute-done.across_ref = f32[2,80,128]{2,1,0:T(8,128)S(1)} collective-permute-done((f32[2,80,128]{2,1,0:T(8,128)}, f32[2,80,128]{2,1,0:T(8,128)S(1)}, u32[]{:S(2)}, u32[]{:S(2)}) %collective-permute-start) | collective-permute-done | bytes 81952 | tf_op jit(solution)/shard_map/ppermute | solution.py:520
  6.9 0.0 collective-permute-done.1.near_ref
  6.9 3.6 %collective-permute-start.2 = (f32[2,80,128]{2,1,0:T(8,128)S(1)}, f32[2,80,128]{2,1,0:T(8,128)S(1)}, u32[]{:S(2)}, u32[]{:S(2)}) collective-permute-start(f32[2,80,128]{2,1,0:T(8,128)S(1)} %collective-permute-done.1.near_ref), channel_id=1, source_target_pairs={{0,15},{1,2},{2,1},{3,4},{4,3},{5,6},{6,5},{7,8},{8,7},{9,10},{10,... | collective-permute-start | bytes 245768 | tf_op jit(solution)/shard_map/ppermute | solution.py:523
  10.5 0.0 collective-permute-start.3
  10.5 0.0 copy-done.1
  10.5 1.9 %inner.1 = (f32[2,256,256]{2,1,0:T(8,128)S(1)}, f32[160,128]{1,0:T(8,128)S(1)}, bf16[1024,128]{1,0:T(8,128)(2,1)S(1)}, bf16[1024,128]{1,0:T(8,128)(2,1)S(1)}) custom-call(f32[2,80,128]{2,1,0:T(8,128)S(1)} %bitcast.12, f32[2,80,128]{2,1,0:T(8,128)S(1)} %collective-permute-done.1.near_ref, f32[2,80,128]{2,1,0:T(8,128)S(1)} %collective-permute-done.across_ref, ...), custom_call_target="tpu_custom_call" | custom-call | tf_op jit(solution)/shard_map/inner/pallas_call | solution.py:233
  12.4 0.4 collective-permute-done.2.far_across_ref
  12.9 0.0 collective-permute-done.3.far_near_ref
  12.9 3.5 %outer.1 = (f32[2,256,256]{2,1,0:T(8,128)S(1)}, f32[320,128]{1,0:T(8,128)S(1)}) custom-call(f32[2,80,128]{2,1,0:T(8,128)S(1)} %collective-permute-done.1.near_ref, f32[2,80,128]{2,1,0:T(8,128)S(1)} %collective-permute-done.across_ref, f32[2,80,128]{2,1,0:T(8,128)S(1)} %collective-permute-done.2.far_across_ref, ...), custom_call_target="tpu_custom_call" | custom-call | tf_op jit(solution)/shard_map/outer/pallas_call | solution.py:292
  16.4 0.0 copy-start
  16.4 15.8 %all_to_all.10.fields_ref = f32[8,40,128]{2,1,0:T(8,128)S(1)} all-to-all(f32[8,40,128]{2,1,0:T(8,128)S(1)} %bitcast.9), channel_id=1, replica_groups=mesh['member_0'=4,'member_1'=2,'lat_0'=2,'lat_1'=4,'lat_2'=2] {'member_0..., dimensions={0} | all-to-all | bytes 327680 | tf_op jit(solution)/shard_map/all_to_all | solution.py:531
  32.2 0.0 copy-done
  32.2 0.2 crps.1
  32.5 10.9 %all_to_all.11.grads_ref = f32[8,48,128]{2,1,0:T(8,128)S(1)} all-to-all(f32[8,48,128]{2,1,0:T(8,128)S(1)} %crps.1), channel_id=1, replica_groups=mesh['member_0'=4,'member_1'=2,'lat_0'=2,'lat_1'=4,'lat_2'=2] {'member_0..., dimensions={0} | all-to-all | bytes 393216 | tf_op jit(solution)/shard_map/all_to_all | solution.py:535
  43.4 0.1 collective-permute-start.5
  43.5 0.2 collective-permute-start.4
  43.7 0.0 collective-permute-start.6
  43.7 1.7 %prepare_back.1 = (bf16[512,720]{1,0:T(8,128)(2,1)S(1)}, bf16[480,768]{1,0:T(8,128)(2,1)S(1)}, f32[2,2,256,256]{3,2,1,0:T(8,128)S(1)}) custom-call(f32[720,256]{1,0:T(8,128)} %bitcast.14, f32[80,2304]{1,0:T(8,128)} %wout_hbm.3, f32[2,256,256]{2,1,0:T(8,128)S(1)} %get-tuple-element.55.first_ref, f32[2,256,256]{2,1,0:T(8,128)S(1)} %get-tuple-element.56.second_ref), custom_call_target="tpu_custom_call" | custom-call | tf_op jit(solution)/shard_map/prepare_back/pallas_call | solution.py:174
  45.4 0.0 collective-permute-done.5.beside_ref.rest_1_
  45.4 0.6 %backward_near.2 = (bf16[2,256,128]{2,1,0:T(8,128)(2,1)S(1)}, bf16[2,256,128]{2,1,0:T(8,128)(2,1)S(1)}) custom-call(f32[176,128]{1,0:T(8,128)S(1)} %get-tuple-element.54.own_ref, f32[176,128]{1,0:T(8,128)S(1)} %collective-permute-done.5.beside_ref.rest_1_, f32[2,2,256,256]{3,2,1,0:T(8,128)S(1)} %get-tuple-element.57.slope_ref, ...), custom_call_target="tpu_custom_call" | custom-call | tf_op jit(solution)/shard_map/backward_near/pallas_call | solution.py:465
  46.0 3.6 %collective-permute-done.4.beside_ref.rest_2_ = f32[176,128]{1,0:T(8,128)S(1)} collective-permute-done((f32[176,128]{1,0:T(8,128)S(1)}, f32[176,128]{1,0:T(8,128)S(1)}, u32[]{:S(2)}, u32[]{:S(2)}) %collective-permute-start.4) | collective-permute-done | bytes 90144 | tf_op jit(solution)/shard_map/ppermute | solution.py:541
  49.7 0.6 %backward_across.2 = (bf16[2,256,128]{2,1,0:T(8,128)(2,1)S(1)}, bf16[2,256,128]{2,1,0:T(8,128)(2,1)S(1)}) custom-call(f32[176,128]{1,0:T(8,128)S(1)} %get-tuple-element.54.own_ref, f32[176,128]{1,0:T(8,128)S(1)} %collective-permute-done.4.beside_ref.rest_2_, f32[2,2,256,256]{3,2,1,0:T(8,128)S(1)} %get-tuple-element.57.slope_ref, ...), custom_call_target="tpu_custom_call" | custom-call | tf_op jit(solution)/shard_map/backward_across/pallas_call | solution.py:465
  50.3 0.0 collective-permute-done.6.rest_3_
  50.3 0.6 join.2.own_ref.refs_0_
  50.9 0.1 collective-permute-start.8
  51.0 1.5 %collective-permute-start.7 = (f32[176,128]{1,0:T(8,128)S(1)}, f32[176,128]{1,0:T(8,128)S(1)}, u32[]{:S(2)}, u32[]{:S(2)}) collective-permute-start(f32[176,128]{1,0:T(8,128)S(1)} %join.2.own_ref.refs_0_), channel_id=1, source_target_pairs={{0,15},{1,2},{2,1},{3,4},{4,3},{5,6},{6,5},{7,8},{8,7},{9,10},{10,... | collective-permute-start | bytes 270344 | tf_op jit(solution)/shard_map/ppermute | solution.py:548
  52.5 0.0 collective-permute-done.8.beside_ref.refs_1_
  52.5 0.6 %backward_near.3 = (bf16[2,256,128]{2,1,0:T(8,128)(2,1)S(1)}, bf16[2,256,128]{2,1,0:T(8,128)(2,1)S(1)}) custom-call(f32[176,128]{1,0:T(8,128)S(1)} %join.2.own_ref.refs_0_, f32[176,128]{1,0:T(8,128)S(1)} %collective-permute-done.8.beside_ref.refs_1_, f32[2,2,256,256]{3,2,1,0:T(8,128)S(1)} %get-tuple-element.57.slope_ref, ...), custom_call_target="tpu_custom_call" | custom-call | tf_op jit(solution)/shard_map/backward_near/pallas_call | solution.py:465
  53.2 4.0 %collective-permute-done.7.beside_ref.refs_2_ = f32[176,128]{1,0:T(8,128)S(1)} collective-permute-done((f32[176,128]{1,0:T(8,128)S(1)}, f32[176,128]{1,0:T(8,128)S(1)}, u32[]{:S(2)}, u32[]{:S(2)}) %collective-permute-start.7) | collective-permute-done | bytes 90144 | tf_op jit(solution)/shard_map/ppermute | solution.py:548
  57.1 1.1 %collective-permute-start.9 = (f32[16,128]{1,0:T(8,128)S(1)}, f32[16,128]{1,0:T(8,128)S(1)}, u32[]{:S(2)}, u32[]{:S(2)}) collective-permute-start(f32[16,128]{1,0:T(8,128)S(1)} %merge.1.known_ref), channel_id=1, source_target_pairs={{0,8},{1,9},{2,10},{3,11},{4,12},{5,13},{6,14},{7,15},{8,0},{9,1},... | collective-permute-start | bytes 24584 | tf_op jit(solution)/shard_map/ppermute | solution.py:554
  58.2 0.6 %backward_across.3 = (bf16[2,256,128]{2,1,0:T(8,128)(2,1)S(1)}, bf16[2,256,128]{2,1,0:T(8,128)(2,1)S(1)}) custom-call(f32[176,128]{1,0:T(8,128)S(1)} %join.2.own_ref.refs_0_, f32[176,128]{1,0:T(8,128)S(1)} %collective-permute-done.7.beside_ref.refs_2_, f32[2,2,256,256]{3,2,1,0:T(8,128)S(1)} %get-tuple-element.57.slope_ref, ...), custom_call_target="tpu_custom_call" | custom-call | tf_op jit(solution)/shard_map/backward_across/pallas_call | solution.py:465
  58.9 0.6 join.3.gradient_ref
  59.4 1.3 %collective-permute-done.9.opposite_ref = f32[16,128]{1,0:T(8,128)S(1)} collective-permute-done((f32[16,128]{1,0:T(8,128)S(1)}, f32[16,128]{1,0:T(8,128)S(1)}, u32[]{:S(2)}, u32[]{:S(2)}) %collective-permute-start.9) | collective-permute-done | bytes 8224 | tf_op jit(solution)/shard_map/ppermute | solution.py:554
  60.8 0.7 %finish.1 = (f32[160,128]{1,0:T(8,128)}, f32[1,1]{1,0:T(1,128)}) custom-call(f32[160,128]{1,0:T(8,128)S(1)} %join.3.gradient_ref, f32[16,128]{1,0:T(8,128)S(1)} %merge.1.known_ref, f32[16,128]{1,0:T(8,128)S(1)} %collective-permute-done.9.opposite_ref), custom_call_target="tpu_custom_call" | custom-call | tf_op jit(solution)/shard_map/finish/pallas_call | solution.py:418
  (2 shorter events, 0.0 us)
Async XLA Ops:
  0.6 6.3 %collective-permute-start = (f32[2,80,128]{2,1,0:T(8,128)}, f32[2,80,128]{2,1,0:T(8,128)S(1)}, u32[]{:S(2)}, u32[]{:S(2)}) collective-permute-start(f32[2,80,128]{2,1,0:T(8,128)} %bitcast.10), channel_id=1, source_target_pairs={{0,15},{1,2},{2,1},{3,4},{4,3},{5,6},{6,5},{7,8},{8,7},{9,10},{10,... | collective-permute-start | bytes 245768 | tf_op jit(solution)/shard_map/ppermute | solution.py:520
  4.3 2.6 %collective-permute-start.1 = (f32[2,80,128]{2,1,0:T(8,128)}, f32[2,80,128]{2,1,0:T(8,128)S(1)}, u32[]{:S(2)}, u32[]{:S(2)}) collective-permute-start(f32[2,80,128]{2,1,0:T(8,128)} %bitcast.11), channel_id=1, source_target_pairs={{0,1},{1,0},{2,3},{3,2},{4,5},{5,4},{6,7},{7,6},{8,9},{9,8},{10,11... | collective-permute-start | bytes 245768 | tf_op jit(solution)/shard_map/ppermute | solution.py:519
  4.3 6.2 %copy-start.1 = (f32[1,2,80,128]{3,2,1,0:T(8,128)S(1)}, f32[1,2,80,128]{3,2,1,0:T(8,128)}, u32[]{:S(2)}) copy-start(f32[1,2,80,128]{3,2,1,0:T(8,128)} %param.6) | copy-start | bytes 245764
  6.9 6.0 %collective-permute-start.2 = (f32[2,80,128]{2,1,0:T(8,128)S(1)}, f32[2,80,128]{2,1,0:T(8,128)S(1)}, u32[]{:S(2)}, u32[]{:S(2)}) collective-permute-start(f32[2,80,128]{2,1,0:T(8,128)S(1)} %collective-permute-done.1.near_ref), channel_id=1, source_target_pairs={{0,15},{1,2},{2,1},{3,4},{4,3},{5,6},{6,5},{7,8},{8,7},{9,10},{10,... | collective-permute-start | bytes 245768 | tf_op jit(solution)/shard_map/ppermute | solution.py:523
  10.5 2.3 %collective-permute-start.3 = (f32[2,80,128]{2,1,0:T(8,128)S(1)}, f32[2,80,128]{2,1,0:T(8,128)S(1)}, u32[]{:S(2)}, u32[]{:S(2)}) collective-permute-start(f32[2,80,128]{2,1,0:T(8,128)S(1)} %collective-permute-done.across_ref), channel_id=1, source_target_pairs={{0,1},{1,0},{2,3},{3,2},{4,5},{5,4},{6,7},{7,6},{8,9},{9,8},{10,11... | collective-permute-start | bytes 245768 | tf_op jit(solution)/shard_map/ppermute | solution.py:524
  16.4 15.9 %copy-start = (f32[2,2,80,128]{3,2,1,0:T(8,128)S(1)}, f32[2,2,80,128]{3,2,1,0:T(8,128)}, u32[]{:S(2)}) copy-start(f32[2,2,80,128]{3,2,1,0:T(8,128)} %param.7) | copy-start | bytes 491524
  43.4 2.0 %collective-permute-start.5 = (f32[176,128]{1,0:T(8,128)S(1)}, f32[176,128]{1,0:T(8,128)S(1)}, u32[]{:S(2)}, u32[]{:S(2)}) collective-permute-start(f32[176,128]{1,0:T(8,128)S(1)} %get-tuple-element.54.own_ref), channel_id=1, source_target_pairs={{0,1},{1,0},{2,3},{3,2},{4,5},{5,4},{6,7},{7,6},{8,9},{9,8},{10,11... | collective-permute-start | bytes 270344 | tf_op jit(solution)/shard_map/ppermute | solution.py:540
  43.5 6.1 %collective-permute-start.4 = (f32[176,128]{1,0:T(8,128)S(1)}, f32[176,128]{1,0:T(8,128)S(1)}, u32[]{:S(2)}, u32[]{:S(2)}) collective-permute-start(f32[176,128]{1,0:T(8,128)S(1)} %get-tuple-element.54.own_ref), channel_id=1, source_target_pairs={{0,15},{1,2},{2,1},{3,4},{4,3},{5,6},{6,5},{7,8},{8,7},{9,10},{10,... | collective-permute-start | bytes 270344 | tf_op jit(solution)/shard_map/ppermute | solution.py:541
  43.7 6.6 %collective-permute-start.6 = (f32[16,128]{1,0:T(8,128)S(1)}, f32[16,128]{1,0:T(8,128)S(1)}, u32[]{:S(2)}, u32[]{:S(2)}) collective-permute-start(f32[16,128]{1,0:T(8,128)S(1)} %get-tuple-element.68), channel_id=1, source_target_pairs={{0,4},{1,5},{2,6},{3,7},{4,0},{5,1},{6,2},{7,3},{8,12},{9,13},{10,... | collective-permute-start | bytes 24584 | tf_op jit(solution)/shard_map/ppermute | solution.py:542
  50.9 1.6 %collective-permute-start.8 = (f32[176,128]{1,0:T(8,128)S(1)}, f32[176,128]{1,0:T(8,128)S(1)}, u32[]{:S(2)}, u32[]{:S(2)}) collective-permute-start(f32[176,128]{1,0:T(8,128)S(1)} %join.2.own_ref.refs_0_), channel_id=1, source_target_pairs={{0,1},{1,0},{2,3},{3,2},{4,5},{5,4},{6,7},{7,6},{8,9},{9,8},{10,11... | collective-permute-start | bytes 270344 | tf_op jit(solution)/shard_map/ppermute | solution.py:547
  51.0 6.1 %collective-permute-start.7 = (f32[176,128]{1,0:T(8,128)S(1)}, f32[176,128]{1,0:T(8,128)S(1)}, u32[]{:S(2)}, u32[]{:S(2)}) collective-permute-start(f32[176,128]{1,0:T(8,128)S(1)} %join.2.own_ref.refs_0_), channel_id=1, source_target_pairs={{0,15},{1,2},{2,1},{3,4},{4,3},{5,6},{6,5},{7,8},{8,7},{9,10},{10,... | collective-permute-start | bytes 270344 | tf_op jit(solution)/shard_map/ppermute | solution.py:548
  57.1 3.7 %collective-permute-start.9 = (f32[16,128]{1,0:T(8,128)S(1)}, f32[16,128]{1,0:T(8,128)S(1)}, u32[]{:S(2)}, u32[]{:S(2)}) collective-permute-start(f32[16,128]{1,0:T(8,128)S(1)} %merge.1.known_ref), channel_id=1, source_target_pairs={{0,8},{1,9},{2,10},{3,11},{4,12},{5,13},{6,14},{7,15},{8,0},{9,1},... | collective-permute-start | bytes 24584 | tf_op jit(solution)/shard_map/ppermute | solution.py:554

commit v7 on v6

--- a/solution.py
+++ b/solution.py
@@ -389,46 +389,6 @@
     return merged(*(ref[ref.shape[0] - slab_count :, :] for ref in refs))
 
 
-def merge_kernel(*refs):
-    refs[-1][...] = table_of(*refs[:-1])
-
-
-def merge(*messages):
-    return pl.pallas_call(
-        merge_kernel,
-        out_shape=jax.ShapeDtypeStruct((slab_count, messages[0].shape[1]), f32),
-        compiler_params=params,
-        name="merge",
-    )(*messages)
-
-
-def finish_kernel(count, gradient_ref, known_ref, opposite_ref, out_hbm, loss_hbm, loss_ref, done):
-    copy = pltpu.make_async_copy(gradient_ref, out_hbm, done.at[0])
-    copy.start()
-    total = jnp.sum(table_of(known_ref, opposite_ref), axis=0, keepdims=True)
-    loss_ref[...] = jnp.sum(total, axis=1, keepdims=True) / count
-    second = pltpu.make_async_copy(loss_ref, loss_hbm, done.at[1])
-    second.start()
-    copy.wait()
-    second.wait()
-
-
-def finish(gradient, known, opposite, count):
-    vmem = pl.BlockSpec(memory_space=pltpu.VMEM)
-    return pl.pallas_call(
-        functools.partial(finish_kernel, count),
-        out_shape=[
-            jax.ShapeDtypeStruct(gradient.shape, f32),
-            jax.ShapeDtypeStruct((1, 1), f32),
-        ],
-        in_specs=[vmem] * 3,
-        out_specs=[pl.BlockSpec(memory_space=pltpu.HBM)] * 2,
-        scratch_shapes=[pltpu.VMEM((1, 1), f32), pltpu.SemaphoreType.DMA((2,))],
-        compiler_params=params,
-        name="finish",
-    )(gradient, known, opposite)
-
-
 def hidden_grads(step, near_side, beside_ref, own_ref, slope_ref, weight_ref, wide):
     width = own_ref.shape[1]
     channels = (own_ref.shape[0] - slab_count) // 2
@@ -471,40 +431,80 @@
     )(own, beside, slopes, w_out)
 
 
-def join_kernel(own_ref, close_hi, close_lo, far_hi, far_lo, inb_ref, *rest):
-    added, tables = rest[:-3][:1], rest[:-3][1:]
-    out_ref, hid_hi, hid_lo = rest[-3:]
-    channels = (own_ref.shape[0] - slab_count) // 2
-    hidden = close_hi.shape[1]
+def gather_hidden(hid, close, far):
+    hidden = close[0].shape[1]
     even = is_even()
     for half in range(2):
-        far = pl.multiple_of(jnp.where(even, half, 2 + half) * hidden, hidden)
-        close = pl.multiple_of(jnp.where(even, 2 + half, half) * hidden, hidden)
-        for ref, far_ref, close_ref in ((hid_hi, far_hi, close_hi), (hid_lo, far_lo, close_lo)):
-            ref[pl.ds(far, hidden), :] = far_ref[half]
-            ref[pl.ds(close, hidden), :] = close_ref[half]
-    moved = from_channels(inb_ref[...], (hid_hi, hid_lo), 0, hidden, channels)
+        far_at = pl.multiple_of(jnp.where(even, half, 2 + half) * hidden, hidden)
+        close_at = pl.multiple_of(jnp.where(even, 2 + half, half) * hidden, hidden)
+        for ref, far_ref, close_ref in zip(hid, far, close):
+            ref[pl.ds(far_at, hidden), :] = far_ref[half]
+            ref[pl.ds(close_at, hidden), :] = close_ref[half]
+
+
+def join_kernel(own_ref, close_hi, close_lo, far_hi, far_lo, inb_ref, added_ref, *rest):
+    *tables, out_ref, known_ref, hid_hi, hid_lo = rest
+    channels = (own_ref.shape[0] - slab_count) // 2
+    gather_hidden((hid_hi, hid_lo), (close_hi, close_lo), (far_hi, far_lo))
+    moved = from_channels(inb_ref[...], (hid_hi, hid_lo), 0, close_hi.shape[1], channels)
     for row in range(2):
         part = slice(row * channels, (row + 1) * channels)
-        total = own_ref[part, :] + moved[row]
-        for extra in added:
-            total = total + extra[part, :]
-        out_ref[part, :] = total
-    if tables:
-        out_ref[2 * channels :, :] = table_of(own_ref, *tables)
-
-
-def join(own, close, far, w_in, *added):
-    count, width = own.shape
-    channels = (count - slab_count) // 2
-    hidden = close[0].shape[1]
+        out_ref[part, :] = own_ref[part, :] + moved[row] + added_ref[part, :]
+    known = table_of(own_ref, *tables)
+    out_ref[2 * channels :, :] = known
+    known_ref[...] = known
+
+
+def join(own, close, far, w_in, added, *tables):
+    hidden, width = close[0].shape[1:]
     return pl.pallas_call(
         join_kernel,
-        out_shape=jax.ShapeDtypeStruct((count if added else 2 * channels, width), f32),
+        out_shape=[
+            jax.ShapeDtypeStruct(own.shape, f32),
+            jax.ShapeDtypeStruct((slab_count, width), f32),
+        ],
         scratch_shapes=[pltpu.VMEM((4 * hidden, width), bf16)] * 2,
         compiler_params=params,
         name="join",
-    )(own, *close, *far, w_in, *added)
+    )(own, *close, *far, w_in, added, *tables)
+
+
+def finish_kernel(count, own_ref, close_hi, close_lo, far_hi, far_lo, inb_ref, *rest):
+    *tables, out_hbm, loss_hbm, out_ref, loss_ref, hid_hi, hid_lo, done = rest
+    channels = (own_ref.shape[0] - slab_count) // 2
+    total = jnp.sum(table_of(own_ref, *tables), axis=0, keepdims=True)
+    loss_ref[...] = jnp.sum(total, axis=1, keepdims=True) / count
+    copies = [pltpu.make_async_copy(loss_ref, loss_hbm, done.at[0])]
+    copies[0].start()
+    gather_hidden((hid_hi, hid_lo), (close_hi, close_lo), (far_hi, far_lo))
+    moved = from_channels(inb_ref[...], (hid_hi, hid_lo), 0, close_hi.shape[1], channels)
+    for row in range(2):
+        part = pl.ds(row * channels, channels)
+        out_ref[part, :] = own_ref[part, :] + moved[row]
+        copies.append(pltpu.make_async_copy(out_ref.at[part, :], out_hbm.at[part, :], done.at[1 + row]))
+        copies[-1].start()
+    for copy in copies:
+        copy.wait()
+
+
+def finish(count, own, close, far, w_in, *tables):
+    hidden, width = close[0].shape[1:]
+    lines = own.shape[0] - slab_count
+    vmem = pl.BlockSpec(memory_space=pltpu.VMEM)
+    return pl.pallas_call(
+        functools.partial(finish_kernel, count),
+        out_shape=[
+            jax.ShapeDtypeStruct((lines, width), f32),
+            jax.ShapeDtypeStruct((1, 1), f32),
+        ],
+        in_specs=[vmem] * (6 + len(tables)),
+        out_specs=[pl.BlockSpec(memory_space=pltpu.HBM)] * 2,
+        scratch_shapes=[pltpu.VMEM((lines, width), f32), pltpu.VMEM((1, 1), f32)]
+        + [pltpu.VMEM((4 * hidden, width), bf16)] * 2
+        + [pltpu.SemaphoreType.DMA((3,))],
+        compiler_params=params,
+        name="finish",
+    )(own, *close, *far, w_in, *tables)
 
 
 def on_device(initial_states, targets, lat_weight, weight_in, weight_out, hidden_bias):
@@ -539,21 +539,25 @@
 
     beside = lax.ppermute(message, LAT, near)
     crossed = lax.ppermute(message, LAT, across)
-    far = lax.ppermute(known, LAT, [(i, i ^ 4) for i in range(slabs)])
+    opposite = [(i, i ^ 8) for i in range(slabs)]
+    ahead = [(i, (i + 5 if i % 2 == 0 else i - 5) % slabs) for i in range(slabs)]
+    behind = [(i, (i - 5 if i % 2 == 0 else i + 5) % slabs) for i in range(slabs)]
+    distant_tables = [lax.ppermute(known, LAT, pairs) for pairs in (ahead, behind)]
     close = backward_side(1, True, message, beside, slopes, w_out_back)
     crossed, close = lax.optimization_barrier((crossed, close))
     distant = backward_side(1, False, message, crossed, slopes, w_out_back)
-    message = join(message, close, distant, w_in_back, first_grads, beside, crossed, far)
+    message, known = join(
+        message, close, distant, w_in_back, first_grads, beside, crossed, *distant_tables
+    )
     beside = lax.ppermute(message, LAT, near)
     crossed = lax.ppermute(message, LAT, across)
+    distant_tables = [lax.ppermute(known, LAT, pairs) for pairs in (opposite,)]
     close = backward_side(0, True, message, beside, slopes, w_out_back)
     crossed, close = lax.optimization_barrier((crossed, close))
-    known = merge(message, beside, crossed)
     distant = backward_side(0, False, message, crossed, slopes, w_out_back)
-    gradient = join(message, close, distant, w_in_back)
-    opposite = lax.ppermute(known, LAT, [(i, i ^ 8) for i in range(slabs)])
+    count = members * steps * rows * channels * width
     gradient, loss = finish(
-        gradient, known, opposite, members * steps * rows * channels * width
+        count, message, close, distant, w_in_back, beside, crossed, *distant_tables
     )
     loss = loss.reshape(())
     return gradient.reshape(initial_states.shape), loss

time: 61.7 us -> 59.6 us (0.966)
  waiting for transfers between devices: 10.1 us -> 5.37 us
  starting transfers between devices: 10.3 us -> 13 us
    ppermute x2, waiting for transfers between devices: 7.6 us -> 4.16 us  [on_device(): crossed = lax.ppermute(message, LAT, across)]
    ppermute x2 -> x3, starting transfers between devices: 1.12 us -> 3.37 us  [the longest x2 2.36 us: on_device(): lax.ppermute(known, LAT, pairs)]
    ppermute x2 -> x3, waiting for transfers between devices: 1.34 us -> 0.01 us  [the longest x2 0.01 us: on_device(): lax.ppermute(known, LAT, pairs)]
  transfers between devices with their start and end apart: 10 -> 11, of which waited for: 5 -> 4; matrix products, arithmetic and copies ran while one was open for 0% -> 0% of each run, Pallas kernels for 14% -> 13%
where the time goes in v7:
time: 59.6 us; the launch traced here: 59.3 us
  blocking collectives  26.8 us (45%)
  Pallas kernels  13.4 us (22%)
  starting transfers between devices  13 us (22%)
  waiting for transfers between devices  5.37 us (9%)
  between operations  0.77 us (1%)
    all_to_all x1, blocking collectives, on_device(): lax.all_to_all(fields.reshape(members, height, width), MEMBER, split_axis...  15.8 us
    all_to_all x1, blocking collectives, on_device(): lax.all_to_all(grads, MEMBER, split_axis=0, concat_axis=0, tiled=True)  10.9 us
    ppermute x2, waiting for transfers between devices, on_device(): crossed = lax.ppermute(message, LAT, across)  4.16 us
    ppermute x1, starting transfers between devices, on_device(): crossed = lax.ppermute(own, LAT, across)  3.71 us
    ppermute x1, starting transfers between devices, on_device(): far_crossed = lax.ppermute(beside, LAT, across)  3.64 us
    pallas_call x1, Pallas kernels, outer(): pl.pallas_call(outer_kernel, out_shape=[jax.ShapeDtypeStruct((2, hidden,...  3.5 us
    pallas_call x4, Pallas kernels, backward_side(): pl.pallas_call(functools.partial(backward_side_kernel, step, near_side),...  2.49 us
    ppermute x2, starting transfers between devices, on_device(): lax.ppermute(known, LAT, pairs)  2.36 us
  transfers between devices with their start and end apart: 11, of which 4 were waited for; matrix products, arithmetic and copies ran while one was open for 0% of the time, Pallas kernels for 13%

profile of v7, /device:TPU:0, one launch (start us, length us, event | category | flops | bytes accessed | tf_op | source)
XLA Modules:
  0.0 59.3 jit_solution(6437681605821554063)
XLA Ops:
  0.6 3.7 %collective-permute-start = (f32[2,80,128]{2,1,0:T(8,128)}, f32[2,80,128]{2,1,0:T(8,128)S(1)}, u32[]{:S(2)}, u32[]{:S(2)}) collective-permute-start(f32[2,80,128]{2,1,0:T(8,128)} %bitcast.10), channel_id=1, source_target_pairs={{0,15},{1,2},{2,1},{3,4},{4,3},{5,6},{6,5},{7,8},{8,7},{9,10},{10,... | collective-permute-start | bytes 245768 | tf_op jit(solution)/shard_map/ppermute | solution.py:520
  4.3 0.0 collective-permute-start.1
  4.3 0.0 copy-start.1
  4.3 1.8 %prepare.1 = (bf16[512,720]{1,0:T(8,128)(2,1)S(1)}, bf16[480,768]{1,0:T(8,128)(2,1)S(1)}, f32[256,128]{1,0:T(8,128)S(1)}, f32[16,128]{1,0:T(8,128)S(1)}) custom-call(f32[720,256]{1,0:T(8,128)} %bitcast.13, f32[80,2304]{1,0:T(8,128)} %wout_hbm.3, f32[1,256]{1,0:T(1,128)} %bitcast.15, f32[1,2]{1,0:T(1,128)} %bitcast.16), custom_call_target="tpu_custom_call" | custom-call | tf_op jit(solution)/shard_map/prepare/pallas_call | solution.py:123
  6.1 0.8 %collective-permute-done.across_ref = f32[2,80,128]{2,1,0:T(8,128)S(1)} collective-permute-done((f32[2,80,128]{2,1,0:T(8,128)}, f32[2,80,128]{2,1,0:T(8,128)S(1)}, u32[]{:S(2)}, u32[]{:S(2)}) %collective-permute-start) | collective-permute-done | bytes 81952 | tf_op jit(solution)/shard_map/ppermute | solution.py:520
  6.9 0.0 collective-permute-done.1.near_ref
  6.9 3.6 %collective-permute-start.2 = (f32[2,80,128]{2,1,0:T(8,128)S(1)}, f32[2,80,128]{2,1,0:T(8,128)S(1)}, u32[]{:S(2)}, u32[]{:S(2)}) collective-permute-start(f32[2,80,128]{2,1,0:T(8,128)S(1)} %collective-permute-done.1.near_ref), channel_id=1, source_target_pairs={{0,15},{1,2},{2,1},{3,4},{4,3},{5,6},{6,5},{7,8},{8,7},{9,10},{10,... | collective-permute-start | bytes 245768 | tf_op jit(solution)/shard_map/ppermute | solution.py:523
  10.5 0.0 collective-permute-start.3
  10.5 0.0 copy-done.1
  10.5 1.9 %inner.1 = (f32[2,256,256]{2,1,0:T(8,128)S(1)}, f32[160,128]{1,0:T(8,128)S(1)}, bf16[1024,128]{1,0:T(8,128)(2,1)S(1)}, bf16[1024,128]{1,0:T(8,128)(2,1)S(1)}) custom-call(f32[2,80,128]{2,1,0:T(8,128)S(1)} %bitcast.12, f32[2,80,128]{2,1,0:T(8,128)S(1)} %collective-permute-done.1.near_ref, f32[2,80,128]{2,1,0:T(8,128)S(1)} %collective-permute-done.across_ref, ...), custom_call_target="tpu_custom_call" | custom-call | tf_op jit(solution)/shard_map/inner/pallas_call | solution.py:233
  12.4 0.4 collective-permute-done.2.far_across_ref
  12.9 0.0 collective-permute-done.3.far_near_ref
  12.9 3.5 %outer.1 = (f32[2,256,256]{2,1,0:T(8,128)S(1)}, f32[320,128]{1,0:T(8,128)S(1)}) custom-call(f32[2,80,128]{2,1,0:T(8,128)S(1)} %collective-permute-done.1.near_ref, f32[2,80,128]{2,1,0:T(8,128)S(1)} %collective-permute-done.across_ref, f32[2,80,128]{2,1,0:T(8,128)S(1)} %collective-permute-done.2.far_across_ref, ...), custom_call_target="tpu_custom_call" | custom-call | tf_op jit(solution)/shard_map/outer/pallas_call | solution.py:292
  16.4 0.0 copy-start
  16.4 15.8 %all_to_all.10.fields_ref = f32[8,40,128]{2,1,0:T(8,128)S(1)} all-to-all(f32[8,40,128]{2,1,0:T(8,128)S(1)} %bitcast.9), channel_id=1, replica_groups=mesh['member_0'=4,'member_1'=2,'lat_0'=2,'lat_1'=4,'lat_2'=2] {'member_0..., dimensions={0} | all-to-all | bytes 327680 | tf_op jit(solution)/shard_map/all_to_all | solution.py:531
  32.2 0.0 copy-done
  32.2 0.2 crps.1
  32.5 10.9 %all_to_all.11.grads_ref = f32[8,48,128]{2,1,0:T(8,128)S(1)} all-to-all(f32[8,48,128]{2,1,0:T(8,128)S(1)} %crps.1), channel_id=1, replica_groups=mesh['member_0'=4,'member_1'=2,'lat_0'=2,'lat_1'=4,'lat_2'=2] {'member_0..., dimensions={0} | all-to-all | bytes 393216 | tf_op jit(solution)/shard_map/all_to_all | solution.py:535
  43.4 0.1 collective-permute-start.5
  43.5 0.2 collective-permute-start.4
  43.7 2.0 %collective-permute-start.6 = (f32[16,128]{1,0:T(8,128)S(1)}, f32[16,128]{1,0:T(8,128)S(1)}, u32[]{:S(2)}, u32[]{:S(2)}) collective-permute-start(f32[16,128]{1,0:T(8,128)S(1)} %get-tuple-element.70), channel_id=1, source_target_pairs={{0,5},{1,12},{2,7},{3,14},{4,9},{5,0},{6,11},{7,2},{8,13},{9,4},{1... | collective-permute-start | bytes 24584 | tf_op jit(solution)/shard_map/ppermute | solution.py:545
  45.7 0.4 collective-permute-start.7
  46.1 1.7 %prepare_back.1 = (bf16[512,720]{1,0:T(8,128)(2,1)S(1)}, bf16[480,768]{1,0:T(8,128)(2,1)S(1)}, f32[2,2,256,256]{3,2,1,0:T(8,128)S(1)}) custom-call(f32[720,256]{1,0:T(8,128)} %bitcast.14, f32[80,2304]{1,0:T(8,128)} %wout_hbm.3, f32[2,256,256]{2,1,0:T(8,128)S(1)} %get-tuple-element.57.first_ref, f32[2,256,256]{2,1,0:T(8,128)S(1)} %get-tuple-element.58.second_ref), custom_call_target="tpu_custom_call" | custom-call | tf_op jit(solution)/shard_map/prepare_back/pallas_call | solution.py:174
  47.7 0.0 collective-permute-done.5.beside_ref.rest_0_
  47.7 0.6 %backward_near.2 = (bf16[2,256,128]{2,1,0:T(8,128)(2,1)S(1)}, bf16[2,256,128]{2,1,0:T(8,128)(2,1)S(1)}) custom-call(f32[176,128]{1,0:T(8,128)S(1)} %get-tuple-element.56.own_ref, f32[176,128]{1,0:T(8,128)S(1)} %collective-permute-done.5.beside_ref.rest_0_, f32[2,2,256,256]{3,2,1,0:T(8,128)S(1)} %get-tuple-element.59.slope_ref, ...), custom_call_target="tpu_custom_call" | custom-call | tf_op jit(solution)/shard_map/backward_near/pallas_call | solution.py:425
  48.4 1.6 %collective-permute-done.4.beside_ref.rest_1_ = f32[176,128]{1,0:T(8,128)S(1)} collective-permute-done((f32[176,128]{1,0:T(8,128)S(1)}, f32[176,128]{1,0:T(8,128)S(1)}, u32[]{:S(2)}, u32[]{:S(2)}) %collective-permute-start.4) | collective-permute-done | bytes 90144 | tf_op jit(solution)/shard_map/ppermute | solution.py:541
  49.9 0.6 %backward_across.2 = (bf16[2,256,128]{2,1,0:T(8,128)(2,1)S(1)}, bf16[2,256,128]{2,1,0:T(8,128)(2,1)S(1)}) custom-call(f32[176,128]{1,0:T(8,128)S(1)} %get-tuple-element.56.own_ref, f32[176,128]{1,0:T(8,128)S(1)} %collective-permute-done.4.beside_ref.rest_1_, f32[2,2,256,256]{3,2,1,0:T(8,128)S(1)} %get-tuple-element.59.slope_ref, ...), custom_call_target="tpu_custom_call" | custom-call | tf_op jit(solution)/shard_map/backward_across/pallas_call | solution.py:425
  50.6 0.0 collective-permute-done.6.rest_2_
  50.6 0.0 collective-permute-done.7.rest_3_
  50.6 0.6 join.1
  51.2 0.1 collective-permute-start.9
  51.3 2.0 %collective-permute-start.8 = (f32[176,128]{1,0:T(8,128)S(1)}, f32[176,128]{1,0:T(8,128)S(1)}, u32[]{:S(2)}, u32[]{:S(2)}) collective-permute-start(f32[176,128]{1,0:T(8,128)S(1)} %get-tuple-element.71.own_ref), channel_id=1, source_target_pairs={{0,15},{1,2},{2,1},{3,4},{4,3},{5,6},{6,5},{7,8},{8,7},{9,10},{10,... | collective-permute-start | bytes 270344 | tf_op jit(solution)/shard_map/ppermute | solution.py:553
  53.2 1.0 %collective-permute-start.10 = (f32[16,128]{1,0:T(8,128)S(1)}, f32[16,128]{1,0:T(8,128)S(1)}, u32[]{:S(2)}, u32[]{:S(2)}) collective-permute-start(f32[16,128]{1,0:T(8,128)S(1)} %get-tuple-element.79), channel_id=1, source_target_pairs={{0,8},{1,9},{2,10},{3,11},{4,12},{5,13},{6,14},{7,15},{8,0},{9,1},... | collective-permute-start | bytes 24584 | tf_op jit(solution)/shard_map/ppermute | solution.py:554
  54.2 0.0 collective-permute-done.9.beside_ref.rest_0_
  54.2 0.6 %backward_near.3 = (bf16[2,256,128]{2,1,0:T(8,128)(2,1)S(1)}, bf16[2,256,128]{2,1,0:T(8,128)(2,1)S(1)}) custom-call(f32[176,128]{1,0:T(8,128)S(1)} %get-tuple-element.71.own_ref, f32[176,128]{1,0:T(8,128)S(1)} %collective-permute-done.9.beside_ref.rest_0_, f32[2,2,256,256]{3,2,1,0:T(8,128)S(1)} %get-tuple-element.59.slope_ref, ...), custom_call_target="tpu_custom_call" | custom-call | tf_op jit(solution)/shard_map/backward_near/pallas_call | solution.py:425
  54.9 2.6 %collective-permute-done.8.beside_ref.rest_1_ = f32[176,128]{1,0:T(8,128)S(1)} collective-permute-done((f32[176,128]{1,0:T(8,128)S(1)}, f32[176,128]{1,0:T(8,128)S(1)}, u32[]{:S(2)}, u32[]{:S(2)}) %collective-permute-start.8) | collective-permute-done | bytes 90144 | tf_op jit(solution)/shard_map/ppermute | solution.py:553
  57.5 0.6 %backward_across.3 = (bf16[2,256,128]{2,1,0:T(8,128)(2,1)S(1)}, bf16[2,256,128]{2,1,0:T(8,128)(2,1)S(1)}) custom-call(f32[176,128]{1,0:T(8,128)S(1)} %get-tuple-element.71.own_ref, f32[176,128]{1,0:T(8,128)S(1)} %collective-permute-done.8.beside_ref.rest_1_, f32[2,2,256,256]{3,2,1,0:T(8,128)S(1)} %get-tuple-element.59.slope_ref, ...), custom_call_target="tpu_custom_call" | custom-call | tf_op jit(solution)/shard_map/backward_across/pallas_call | solution.py:425
  58.1 0.0 collective-permute-done.10.rest_2_
  58.1 1.2 %finish.1 = (f32[160,128]{1,0:T(8,128)}, f32[1,1]{1,0:T(1,128)}) custom-call(f32[176,128]{1,0:T(8,128)S(1)} %get-tuple-element.71.own_ref, bf16[2,256,128]{2,1,0:T(8,128)(2,1)S(1)} %get-tuple-element.74.close_hi, bf16[2,256,128]{2,1,0:T(8,128)(2,1)S(1)} %get-tuple-element.75.close_lo, bf16[2,256,128]{2,1,0:T(8,128)(2,1)S(1)} %get-tuple-element.77.far_hi, ...), custom_call_target="tpu_custom_call" | custom-call | tf_op jit(solution)/shard_map/finish/pallas_call | solution.py:494
  (1 shorter events, 0.0 us)
Async XLA Ops:
  0.6 6.3 %collective-permute-start = (f32[2,80,128]{2,1,0:T(8,128)}, f32[2,80,128]{2,1,0:T(8,128)S(1)}, u32[]{:S(2)}, u32[]{:S(2)}) collective-permute-start(f32[2,80,128]{2,1,0:T(8,128)} %bitcast.10), channel_id=1, source_target_pairs={{0,15},{1,2},{2,1},{3,4},{4,3},{5,6},{6,5},{7,8},{8,7},{9,10},{10,... | collective-permute-start | bytes 245768 | tf_op jit(solution)/shard_map/ppermute | solution.py:520
  4.3 2.6 %collective-permute-start.1 = (f32[2,80,128]{2,1,0:T(8,128)}, f32[2,80,128]{2,1,0:T(8,128)S(1)}, u32[]{:S(2)}, u32[]{:S(2)}) collective-permute-start(f32[2,80,128]{2,1,0:T(8,128)} %bitcast.11), channel_id=1, source_target_pairs={{0,1},{1,0},{2,3},{3,2},{4,5},{5,4},{6,7},{7,6},{8,9},{9,8},{10,11... | collective-permute-start | bytes 245768 | tf_op jit(solution)/shard_map/ppermute | solution.py:519
  4.3 6.2 %copy-start.1 = (f32[1,2,80,128]{3,2,1,0:T(8,128)S(1)}, f32[1,2,80,128]{3,2,1,0:T(8,128)}, u32[]{:S(2)}) copy-start(f32[1,2,80,128]{3,2,1,0:T(8,128)} %param.6) | copy-start | bytes 245764
  6.9 6.0 %collective-permute-start.2 = (f32[2,80,128]{2,1,0:T(8,128)S(1)}, f32[2,80,128]{2,1,0:T(8,128)S(1)}, u32[]{:S(2)}, u32[]{:S(2)}) collective-permute-start(f32[2,80,128]{2,1,0:T(8,128)S(1)} %collective-permute-done.1.near_ref), channel_id=1, source_target_pairs={{0,15},{1,2},{2,1},{3,4},{4,3},{5,6},{6,5},{7,8},{8,7},{9,10},{10,... | collective-permute-start | bytes 245768 | tf_op jit(solution)/shard_map/ppermute | solution.py:523
  10.5 2.3 %collective-permute-start.3 = (f32[2,80,128]{2,1,0:T(8,128)S(1)}, f32[2,80,128]{2,1,0:T(8,128)S(1)}, u32[]{:S(2)}, u32[]{:S(2)}) collective-permute-start(f32[2,80,128]{2,1,0:T(8,128)S(1)} %collective-permute-done.across_ref), channel_id=1, source_target_pairs={{0,1},{1,0},{2,3},{3,2},{4,5},{5,4},{6,7},{7,6},{8,9},{9,8},{10,11... | collective-permute-start | bytes 245768 | tf_op jit(solution)/shard_map/ppermute | solution.py:524
  16.4 15.9 %copy-start = (f32[2,2,80,128]{3,2,1,0:T(8,128)S(1)}, f32[2,2,80,128]{3,2,1,0:T(8,128)}, u32[]{:S(2)}) copy-start(f32[2,2,80,128]{3,2,1,0:T(8,128)} %param.7) | copy-start | bytes 491524
  43.4 4.3 %collective-permute-start.5 = (f32[176,128]{1,0:T(8,128)S(1)}, f32[176,128]{1,0:T(8,128)S(1)}, u32[]{:S(2)}, u32[]{:S(2)}) collective-permute-start(f32[176,128]{1,0:T(8,128)S(1)} %get-tuple-element.56.own_ref), channel_id=1, source_target_pairs={{0,1},{1,0},{2,3},{3,2},{4,5},{5,4},{6,7},{7,6},{8,9},{9,8},{10,11... | collective-permute-start | bytes 270344 | tf_op jit(solution)/shard_map/ppermute | solution.py:540
  43.5 6.4 %collective-permute-start.4 = (f32[176,128]{1,0:T(8,128)S(1)}, f32[176,128]{1,0:T(8,128)S(1)}, u32[]{:S(2)}, u32[]{:S(2)}) collective-permute-start(f32[176,128]{1,0:T(8,128)S(1)} %get-tuple-element.56.own_ref), channel_id=1, source_target_pairs={{0,15},{1,2},{2,1},{3,4},{4,3},{5,6},{6,5},{7,8},{8,7},{9,10},{10,... | collective-permute-start | bytes 270344 | tf_op jit(solution)/shard_map/ppermute | solution.py:541
  43.7 6.9 %collective-permute-start.6 = (f32[16,128]{1,0:T(8,128)S(1)}, f32[16,128]{1,0:T(8,128)S(1)}, u32[]{:S(2)}, u32[]{:S(2)}) collective-permute-start(f32[16,128]{1,0:T(8,128)S(1)} %get-tuple-element.70), channel_id=1, source_target_pairs={{0,5},{1,12},{2,7},{3,14},{4,9},{5,0},{6,11},{7,2},{8,13},{9,4},{1... | collective-permute-start | bytes 24584 | tf_op jit(solution)/shard_map/ppermute | solution.py:545
  45.7 4.9 %collective-permute-start.7 = (f32[16,128]{1,0:T(8,128)S(1)}, f32[16,128]{1,0:T(8,128)S(1)}, u32[]{:S(2)}, u32[]{:S(2)}) collective-permute-start(f32[16,128]{1,0:T(8,128)S(1)} %get-tuple-element.70), channel_id=1, source_target_pairs={{0,11},{1,6},{2,13},{3,8},{4,15},{5,10},{6,1},{7,12},{8,3},{9,14},... | collective-permute-start | bytes 24584 | tf_op jit(solution)/shard_map/ppermute | solution.py:545
  51.2 3.1 %collective-permute-start.9 = (f32[176,128]{1,0:T(8,128)S(1)}, f32[176,128]{1,0:T(8,128)S(1)}, u32[]{:S(2)}, u32[]{:S(2)}) collective-permute-start(f32[176,128]{1,0:T(8,128)S(1)} %get-tuple-element.71.own_ref), channel_id=1, source_target_pairs={{0,1},{1,0},{2,3},{3,2},{4,5},{5,4},{6,7},{7,6},{8,9},{9,8},{10,11... | collective-permute-start | bytes 270344 | tf_op jit(solution)/shard_map/ppermute | solution.py:552
  51.3 6.2 %collective-permute-start.8 = (f32[176,128]{1,0:T(8,128)S(1)}, f32[176,128]{1,0:T(8,128)S(1)}, u32[]{:S(2)}, u32[]{:S(2)}) collective-permute-start(f32[176,128]{1,0:T(8,128)S(1)} %get-tuple-element.71.own_ref), channel_id=1, source_target_pairs={{0,15},{1,2},{2,1},{3,4},{4,3},{5,6},{6,5},{7,8},{8,7},{9,10},{10,... | collective-permute-start | bytes 270344 | tf_op jit(solution)/shard_map/ppermute | solution.py:553
  53.2 4.9 %collective-permute-start.10 = (f32[16,128]{1,0:T(8,128)S(1)}, f32[16,128]{1,0:T(8,128)S(1)}, u32[]{:S(2)}, u32[]{:S(2)}) collective-permute-start(f32[16,128]{1,0:T(8,128)S(1)} %get-tuple-element.79), channel_id=1, source_target_pairs={{0,8},{1,9},{2,10},{3,11},{4,12},{5,13},{6,14},{7,15},{8,0},{9,1},... | collective-permute-start | bytes 24584 | tf_op jit(solution)/shard_map/ppermute | solution.py:554

commit v8 on v7

--- a/solution.py
+++ b/solution.py
@@ -123,33 +123,27 @@
     return pl.pallas_call(
         prepare_kernel,
         out_shape=[jax.ShapeDtypeStruct(shape, bf16) for shape in shapes]
-        + [jax.ShapeDtypeStruct((hidden, width), f32), jax.ShapeDtypeStruct((16, width), f32)],
+        + [jax.ShapeDtypeStruct((hidden, width), f32), jax.ShapeDtypeStruct((16, width), f32)]
+        + [jax.ShapeDtypeStruct(array.shape, f32) for array in arrays[:2]],
         in_specs=[pl.BlockSpec(memory_space=pltpu.HBM)] * 4,
-        scratch_shapes=[pltpu.VMEM(array.shape, f32) for array in arrays] + [pltpu.SemaphoreType.DMA((4,))],
+        scratch_shapes=[pltpu.VMEM(array.shape, f32) for array in arrays[2:]] + [pltpu.SemaphoreType.DMA((4,))],
         compiler_params=params,
         name="prepare",
     )(*(pltpu.with_memory_space_constraint(array, pltpu.HBM) for array in arrays))
 
 
-def prepare_back_kernel(win_hbm, wout_hbm, first_ref, second_ref, outb_ref, inb_ref, slope_ref,
-                        stack, win_ref, wout_ref, arrived):
-    pairs = ((win_hbm, win_ref), (wout_hbm, wout_ref))
-    copies = [pltpu.make_async_copy(*pair, arrived.at[i]) for i, pair in enumerate(pairs)]
-    for copy in copies:
-        copy.start()
-    for step, before_ref in enumerate((first_ref, second_ref)):
-        for pair in range(2):
-            slope = gelu_slope(before_ref[pair])
+def prepare_back_kernel(win_ref, wout_ref, *rest):
+    before_refs, (outb_ref, inb_ref, slope_ref, stack) = rest[:4], rest[4:]
+    for side in range(2):
+        below = is_even() if side == 0 else jnp.logical_not(is_even())
+        first = jnp.where(below, 0, -2)
+        for step, before_ref in enumerate(before_refs[side::2]):
+            slope = gelu_slope(before_ref[...])
             width = slope.shape[1] // 2
             for half in range(2):
                 part = slope[:, half * width : (half + 1) * width]
-                if pair != half:
-                    slope_ref[step, pair, :, half * width : (half + 1) * width] = part
-                else:
-                    part = jnp.where(inside(3 * pair - 1), part, 0.0)
-                    slope_ref[step, pair, :, half * width : (half + 1) * width] = part
-    for copy in copies:
-        copy.wait()
+                part = jnp.where(inside(first + 1 + half), part, 0.0)
+                slope_ref[step, side, :, half * width : (half + 1) * width] = part
     outer, width = wout_ref.shape
     hidden = width // 9
     inner = win_ref.shape[0] // 9
@@ -164,24 +158,19 @@
     outb_ref[:hidden, :], outb_ref[hidden:, :] = split(stack[...].T)
 
 
-def prepare_back(weight_in, weight_out, first, second):
+def prepare_back(weight_in, weight_out, *before):
     taps_in, hidden = weight_in.shape
     outer = weight_out.shape[0]
     inner = taps_in // 9
-    arrays = (weight_in, weight_out)
     shapes = [(2 * hidden, 9 * outer), (6 * inner, 3 * hidden)]
-    hbm = pl.BlockSpec(memory_space=pltpu.HBM)
     return pl.pallas_call(
         prepare_back_kernel,
         out_shape=[jax.ShapeDtypeStruct(shape, bf16) for shape in shapes]
-        + [jax.ShapeDtypeStruct((2, *first.shape), f32)],
-        in_specs=[hbm, hbm] + [pl.BlockSpec(memory_space=pltpu.VMEM)] * 2,
-        scratch_shapes=[pltpu.VMEM((9 * outer, hidden), f32)]
-        + [pltpu.VMEM(array.shape, f32) for array in arrays]
-        + [pltpu.SemaphoreType.DMA((2,))],
+        + [jax.ShapeDtypeStruct((2, 2, *before[0].shape), f32)],
+        scratch_shapes=[pltpu.VMEM((9 * outer, hidden), f32)],
         compiler_params=params,
         name="prepare_back",
-    )(*(pltpu.with_memory_space_constraint(array, pltpu.HBM) for array in arrays), first, second)
+    )(weight_in, weight_out, *before)
 
 
 def inside(row):
@@ -193,113 +182,63 @@
     return lax.rem(lax.axis_index(LAT), 2) == 0
 
 
-def either(first, second):
-    return lambda row: jnp.where(is_even(), first[row], second[row])
-
-
-def activate(before, first, hid, index, hidden, width):
+def side_windows(near_side, own, beside, wide):
+    even = is_even()
+    below = even if near_side else jnp.logical_not(even)
+    first = jnp.where(below, 0, -2)
+    for index in range(4):
+        mine, other = own(index % 2), beside(index % 2)
+        row = jnp.where(below, mine, other) if index < 2 else jnp.where(below, other, mine)
+        put_windows(wide, index, jnp.where(inside(first + index), row, 0.0))
+    return first
+
+
+def forward_side_kernel(near_side, own_ref, beside_ref, bias_ref, in_ref, before_ref, high_ref, low_ref, wide_hi,
+                        wide_lo):
+    channels, width = own_ref.shape[1:]
+    wide = (wide_hi, wide_lo)
+    first = side_windows(near_side, lambda row: own_ref[row], lambda row: beside_ref[row], wide)
+    before = to_channels(in_ref[...], wide, 0, channels) + jnp.concatenate([bias_ref[...]] * 2, axis=1)
+    before_ref[...] = before
     for half in range(2):
-        row = first + half
-        scale = 0.5 if row in (0, 1) else jnp.where(inside(row), 0.5, 0.0)
+        scale = jnp.where(inside(first + 1 + half), 0.5, 0.0)
         active = gelu(before[:, half * width : (half + 1) * width], scale)
-        put(hid, (index + half) * hidden, split(active))
-
-
-def inner_kernel(own_ref, near_ref, across_ref, bias_ref, in_ref, out_ref, before_ref, field_ref, hid_hi, hid_lo,
-                 wide_hi, wide_lo):
-    channels, width = own_ref.shape[1:]
-    hidden = in_ref.shape[0] // 2
-    wide = (wide_hi, wide_lo)
-    hid = (hid_hi, hid_lo)
-    bias = jnp.concatenate([bias_ref[...]] * 2, axis=1)
-    slabs = (either(across_ref, near_ref), lambda row: own_ref[row], either(near_ref, across_ref))
-    for index in range(6):
-        row = slabs[index // 2](index % 2)
-        if index // 2 != 1:
-            row = jnp.where(inside(index - 2), row, 0.0)
-        put_windows(wide, index, row)
-    for pair in (0, 2):
-        before = to_channels(in_ref[...], wide, pair, channels) + bias
-        before_ref[pair // 2] = before
-        activate(before, pair - 1, hid, pair, hidden, width)
-    moved = from_channels(out_ref[...], hid, 0, hidden, channels)
-    for row in range(2):
-        field_ref[row * channels : (row + 1) * channels, :] = own_ref[row] + moved[row]
-
-
-def inner(own, near, across, bias, w_in, w_out):
+        high_ref[half], low_ref[half] = split(active)
+
+
+def forward_side(near_side, own, beside, bias, w_in):
     channels, width = own.shape[1:]
     hidden = w_in.shape[0] // 2
     return pl.pallas_call(
-        inner_kernel,
-        out_shape=[
-            jax.ShapeDtypeStruct((2, hidden, 2 * width), f32),
-            jax.ShapeDtypeStruct((2 * channels, width), f32),
-        ]
-        + [jax.ShapeDtypeStruct((4 * hidden, width), bf16)] * 2,
-        scratch_shapes=[pltpu.VMEM((18 * channels, width), bf16)] * 2,
-        compiler_params=params,
-        name="inner",
-    )(own, near, across, bias, w_in, w_out)
-
-
-def outer_kernel(near_ref, across_ref, far_across_ref, far_near_ref, field_ref, hid_hi, hid_lo, bias_ref, in_ref,
-                 out_ref, before_ref, fields_ref, wide_hi, wide_lo, side_hi, side_lo):
-    channels, width = near_ref.shape[1:]
-    hidden = in_ref.shape[0] // 2
-    wide = (wide_hi, wide_lo)
-    side = (side_hi, side_lo)
-    bias = jnp.concatenate([bias_ref[...]] * 2, axis=1)
-    fields = [None, None] + [field_ref[row * channels : (row + 1) * channels, :] for row in range(2)] + [None, None]
-    sides = (
-        (-4, (either(far_across_ref, far_near_ref), either(across_ref, near_ref))),
-        (2, (either(near_ref, across_ref), either(far_near_ref, far_across_ref))),
-    )
-    rows = []
-    for after, (first, slabs) in enumerate(sides):
-        for index in range(4):
-            row = jnp.where(inside(first + index), slabs[index // 2](index % 2), 0.0)
-            rows.append(row)
-            put_windows(wide, 4 * after + index, row)
-        for ref, known in zip(side, (hid_hi, hid_lo)):
-            ref[(2 + 2 * after) * hidden : (4 + 2 * after) * hidden, :] = known[
-                2 * after * hidden : 2 * (after + 1) * hidden, :
-            ]
-    before = [to_channels(in_ref[...], wide, 4 * after, channels) + bias for after in range(2)]
-    activate(before[0], -3, side, 0, hidden, width)
-    activate(before[1], 3, side, 6, hidden, width)
-    for after in range(2):
-        moved = from_channels(out_ref[...], side, 4 * after, hidden, channels)
-        for row in range(2):
-            at = 4 * after + row
-            value = rows[2 + 2 * after + row] + moved[row]
-            fields[at] = jnp.where(inside(at - 2), value, 0.0)
-    for index in range(6):
-        put_windows(wide, index, fields[index])
-    for pair in (0, 2):
-        before = to_channels(in_ref[...], wide, pair, channels) + bias
-        before_ref[pair // 2] = before
-        activate(before, pair - 1, side, pair, hidden, width)
-    moved = from_channels(out_ref[...], side, 0, hidden, channels)
-    for row in range(2):
-        fields_ref[row * channels : (row + 1) * channels, :] = fields[2 + row]
-        fields_ref[(2 + row) * channels : (3 + row) * channels, :] = fields[2 + row] + moved[row]
-
-
-def outer(near, across, far_across, far_near, field, hid, bias, w_in, w_out):
-    channels, width = near.shape[1:]
-    hidden = w_in.shape[0] // 2
-    return pl.pallas_call(
-        outer_kernel,
-        out_shape=[
-            jax.ShapeDtypeStruct((2, hidden, 2 * width), f32),
-            jax.ShapeDtypeStruct((4 * channels, width), f32),
-        ],
-        scratch_shapes=[pltpu.VMEM((24 * channels, width), bf16)] * 2
-        + [pltpu.VMEM((8 * hidden, width), bf16)] * 2,
-        compiler_params=params,
-        name="outer",
-    )(near, across, far_across, far_near, field, *hid, bias, w_in, w_out)
+        functools.partial(forward_side_kernel, near_side),
+        out_shape=[jax.ShapeDtypeStruct((hidden, 2 * width), f32)]
+        + [jax.ShapeDtypeStruct((2, hidden, width), bf16)] * 2,
+        scratch_shapes=[pltpu.VMEM((12 * channels, width), bf16)] * 2,
+        compiler_params=params,
+        name="forward_near" if near_side else "forward_across",
+    )(own, beside, bias, w_in)
+
+
+def move_kernel(keep, field_ref, close_hi, close_lo, far_hi, far_lo, out_ref, moved_ref, hid_hi, hid_lo):
+    rows, channels, width = field_ref.shape
+    gather_hidden((hid_hi, hid_lo), (close_hi, close_lo), (far_hi, far_lo))
+    moved = from_channels(out_ref[...], (hid_hi, hid_lo), 0, close_hi.shape[1], channels)
+    for row in range(rows):
+        if keep:
+            moved_ref[row] = field_ref[row]
+        moved_ref[rows * keep + row] = field_ref[row] + moved[row]
+
+
+def move(keep, field, close, far, w_out):
+    rows, channels, width = field.shape
+    hidden = close[0].shape[1]
+    return pl.pallas_call(
+        functools.partial(move_kernel, keep),
+        out_shape=jax.ShapeDtypeStruct(((1 + keep) * rows, channels, width), f32),
+        scratch_shapes=[pltpu.VMEM((4 * hidden, width), bf16)] * 2,
+        compiler_params=params,
+        name="move",
+    )(field, *close, *far, w_out)
 
 
 def crps_kernel(weight_ref, fields_ref, targets_ref, out_ref):
@@ -392,23 +331,13 @@
 def hidden_grads(step, near_side, beside_ref, own_ref, slope_ref, weight_ref, wide):
     width = own_ref.shape[1]
     channels = (own_ref.shape[0] - slab_count) // 2
-    even = is_even()
-    below = even if near_side else jnp.logical_not(even)
-
-    def take(ref, row):
-        return ref[row * channels : (row + 1) * channels, :]
-
-    first = jnp.where(below, 0, -2)
-    for index in range(4):
-        own, beside = take(own_ref, index % 2), take(beside_ref, index % 2)
-        row = jnp.where(below, own, beside) if index < 2 else jnp.where(below, beside, own)
-        put_windows(wide, index, jnp.where(inside(first + index), row, 0.0))
-    grads = to_channels(weight_ref[...], wide, 0, channels) * slope_ref[step, jnp.where(below, 1, 0)]
-    rows = []
-    for half in range(2):
-        row = grads[:, half * width : (half + 1) * width]
-        rows.append(split(row))
-    return rows
+
+    def rows_of(ref):
+        return lambda row: ref[row * channels : (row + 1) * channels, :]
+
+    side_windows(near_side, rows_of(own_ref), rows_of(beside_ref), wide)
+    grads = to_channels(weight_ref[...], wide, 0, channels) * slope_ref[step, 0 if near_side else 1]
+    return [split(grads[:, half * width : (half + 1) * width]) for half in range(2)]
 
 
 def backward_side_kernel(step, near_side, own_ref, beside_ref, slope_ref, outb_ref, high_ref, low_ref, wide_hi,
@@ -519,21 +448,26 @@
     beside = lax.ppermute(own, LAT, near)
     crossed = lax.ppermute(own, LAT, across)
     ready = prepare(weight_in.T, weight_out, hidden_bias[None, :], lat_weight[None, :], width)
-    crossed, beside, ready = lax.optimization_barrier((crossed, beside, ready))
-    far_crossed = lax.ppermute(beside, LAT, across)
-    far_beside = lax.ppermute(crossed, LAT, near)
-    w_in, w_out, bias, lat_weights = ready
-    before_first, field, *hid = inner(own, beside, crossed, bias, w_in, w_out)
-    before_second, fields = outer(
-        beside, crossed, far_crossed, far_beside, field, hid, bias, w_in, w_out
-    )
+    w_in, w_out, bias, lat_weights, *raw = ready
+    before_near, *close = forward_side(True, own, beside, bias, w_in)
+    crossed, close = lax.optimization_barrier((crossed, close))
+    before_across, *distant = forward_side(False, own, crossed, bias, w_in)
+    before_first = (before_near, before_across)
+    field = move(0, own, close, distant, w_out)
+    beside = lax.ppermute(field, LAT, near)
+    crossed = lax.ppermute(field, LAT, across)
+    before_near, *close = forward_side(True, field, beside, bias, w_in)
+    crossed, close = lax.optimization_barrier((crossed, close))
+    before_across, *distant = forward_side(False, field, crossed, bias, w_in)
+    before_second = (before_near, before_across)
+    fields = move(1, field, close, distant, w_out)
     height = steps * slab_rows * channels // members
     chunks = lax.all_to_all(
         fields.reshape(members, height, width), MEMBER, split_axis=0, concat_axis=0, tiled=True
     )
     grads = crps(lat_weights, chunks, targets.reshape(members, height, width))
     grads = lax.all_to_all(grads, MEMBER, split_axis=0, concat_axis=0, tiled=True)
-    back = prepare_back(weight_in.T, weight_out, before_first, before_second)
+    back = prepare_back(*raw, *before_first, *before_second)
     w_out_back, w_in_back, slopes = back
     first_grads, message, known = collect(grads)
 

time: 59.6 us -> 58.9 us (0.988)
  Pallas kernels: 13.4 us -> 11.6 us
  starting transfers between devices: 13 us -> 14.4 us
    ppermute x2, starting transfers between devices: 2.13 us -> 3.77 us  [on_device(): crossed = lax.ppermute(message, LAT, across)]
    pallas_call x2 -> x6, Pallas kernels: 5.4 us -> 3.86 us  [the longest x4 2.71 us: forward_side(): pl.pallas_call(functools.partial(forward_side_kernel, near_side), out_sha...]
    ppermute x2, starting transfers between devices: 2.36 us -> 1.09 us  [on_device(): lax.ppermute(known, LAT, pairs)]
    ppermute x2, waiting for transfers between devices: 0.43 us -> 1.61 us  [the longest x1 1.61 us: on_device(): crossed = lax.ppermute(field, LAT, across)]
    ppermute x1, waiting for transfers between devices: 0.77 us -> 0.01 us  [on_device(): crossed = lax.ppermute(own, LAT, across)]
  transfers between devices with their start and end apart: 11 -> 11, of which waited for: 4 -> 3; matrix products, arithmetic and copies ran while one was open for 0% -> 0% of each run, Pallas kernels for 13% -> 12%
where the time goes in v8:
time: 58.9 us; the launch traced here: 58.7 us
  blocking collectives  26.4 us (45%)
  starting transfers between devices  14.4 us (24%)
  Pallas kernels  11.6 us (20%)
  waiting for transfers between devices  5.49 us (9%)
  between operations  0.83 us (1%)
    all_to_all x1, blocking collectives, on_device(): lax.all_to_all(fields.reshape(members, height, width), MEMBER, split_axis...  15.5 us
    all_to_all x1, blocking collectives, on_device(): lax.all_to_all(grads, MEMBER, split_axis=0, concat_axis=0, tiled=True)  10.9 us
    ppermute x1, starting transfers between devices, on_device(): crossed = lax.ppermute(own, LAT, across)  4.3 us
    ppermute x2, waiting for transfers between devices, on_device(): crossed = lax.ppermute(message, LAT, across)  3.86 us
    ppermute x2, starting transfers between devices, on_device(): crossed = lax.ppermute(message, LAT, across)  3.77 us
    ppermute x1, starting transfers between devices, on_device(): crossed = lax.ppermute(field, LAT, across)  3.76 us
    pallas_call x4, Pallas kernels, forward_side(): pl.pallas_call(functools.partial(forward_side_kernel, near_side), out_sha...  2.71 us
    pallas_call x4, Pallas kernels, backward_side(): pl.pallas_call(functools.partial(backward_side_kernel, step, near_side),...  2.5 us
  transfers between devices with their start and end apart: 11, of which 3 were waited for; matrix products, arithmetic and copies ran while one was open for 0% of the time, Pallas kernels for 12%

profile of v8, /device:TPU:0, one launch (start us, length us, event | category | flops | bytes accessed | tf_op | source)
XLA Modules:
  0.0 58.7 jit_solution(13087218104361793867)
XLA Ops:
  0.6 0.1 collective-permute-start.1
  0.7 4.3 %collective-permute-start = (f32[2,80,128]{2,1,0:T(8,128)}, f32[2,80,128]{2,1,0:T(8,128)S(1)}, u32[]{:S(2)}, u32[]{:S(2)}) collective-permute-start(f32[2,80,128]{2,1,0:T(8,128)} %bitcast.9), channel_id=1, source_target_pairs={{0,15},{1,2},{2,1},{3,4},{4,3},{5,6},{6,5},{7,8},{8,7},{9,10},{10,... | collective-permute-start | bytes 245768 | tf_op jit(solution)/shard_map/ppermute | solution.py:449
  5.0 0.0 copy-start
  5.0 1.8 %prepare.1 = (bf16[512,720]{1,0:T(8,128)(2,1)S(1)}, bf16[480,768]{1,0:T(8,128)(2,1)S(1)}, f32[256,128]{1,0:T(8,128)S(1)}, f32[16,128]{1,0:T(8,128)S(1)}, f32[720,256]{1,0:T(8,128)S(1)}, /*index=5*/f32[80,2304]{1,0:T(8,128)S(1)}) custom-call(f32[720,256]{1,0:T(8,128)} %bitcast.15, f32[80,2304]{1,0:T(8,128)} %wout_hbm.1, f32[1,256]{1,0:T(1,128)} %bitcast.16, ...), custom_call_target="tpu_custom_call" | custom-call | tf_op jit(solution)/shard_map/prepare/pallas_call | solution.py:123
  6.8 0.0 collective-permute-done.1.beside_ref
  6.8 0.0 copy-done
  6.8 0.7 %forward_near.2 = (f32[256,256]{1,0:T(8,128)S(1)}, bf16[2,256,128]{2,1,0:T(8,128)(2,1)S(1)}, bf16[2,256,128]{2,1,0:T(8,128)(2,1)S(1)}) custom-call(f32[2,80,128]{2,1,0:T(8,128)S(1)} %bitcast.10, f32[2,80,128]{2,1,0:T(8,128)S(1)} %collective-permute-done.1.beside_ref, f32[256,128]{1,0:T(8,128)S(1)} %get-tuple-element.51.bias_ref, ...), custom_call_target="tpu_custom_call" | custom-call | tf_op jit(solution)/shard_map/forward_near/pallas_call | solution.py:212
  7.5 0.0 collective-permute-done.beside_ref
  7.5 0.7 %forward_across.2 = (f32[256,256]{1,0:T(8,128)S(1)}, bf16[2,256,128]{2,1,0:T(8,128)(2,1)S(1)}, bf16[2,256,128]{2,1,0:T(8,128)(2,1)S(1)}) custom-call(f32[2,80,128]{2,1,0:T(8,128)S(1)} %bitcast.11, f32[2,80,128]{2,1,0:T(8,128)S(1)} %collective-permute-done.beside_ref, f32[256,128]{1,0:T(8,128)S(1)} %get-tuple-element.51.bias_ref, ...), custom_call_target="tpu_custom_call" | custom-call | tf_op jit(solution)/shard_map/forward_across/pallas_call | solution.py:212
  8.2 0.6 move.2.own_ref.field_ref
  8.8 0.1 collective-permute-start.3
  8.9 3.8 %collective-permute-start.2 = (f32[2,80,128]{2,1,0:T(8,128)S(1)}, f32[2,80,128]{2,1,0:T(8,128)S(1)}, u32[]{:S(2)}, u32[]{:S(2)}) collective-permute-start(f32[2,80,128]{2,1,0:T(8,128)S(1)} %move.2.own_ref.field_ref), channel_id=1, source_target_pairs={{0,15},{1,2},{2,1},{3,4},{4,3},{5,6},{6,5},{7,8},{8,7},{9,10},{10,... | collective-permute-start | bytes 245768 | tf_op jit(solution)/shard_map/ppermute | solution.py:458
  12.6 0.0 collective-permute-done.3.beside_ref
  12.7 0.7 %forward_near.3 = (f32[256,256]{1,0:T(8,128)S(1)}, bf16[2,256,128]{2,1,0:T(8,128)(2,1)S(1)}, bf16[2,256,128]{2,1,0:T(8,128)(2,1)S(1)}) custom-call(f32[2,80,128]{2,1,0:T(8,128)S(1)} %move.2.own_ref.field_ref, f32[2,80,128]{2,1,0:T(8,128)S(1)} %collective-permute-done.3.beside_ref, f32[256,128]{1,0:T(8,128)S(1)} %get-tuple-element.51.bias_ref, ...), custom_call_target="tpu_custom_call" | custom-call | tf_op jit(solution)/shard_map/forward_near/pallas_call | solution.py:212
  13.3 1.6 %collective-permute-done.2.beside_ref = f32[2,80,128]{2,1,0:T(8,128)S(1)} collective-permute-done((f32[2,80,128]{2,1,0:T(8,128)S(1)}, f32[2,80,128]{2,1,0:T(8,128)S(1)}, u32[]{:S(2)}, u32[]{:S(2)}) %collective-permute-start.2) | collective-permute-done | bytes 81952 | tf_op jit(solution)/shard_map/ppermute | solution.py:458
  14.9 0.7 %forward_across.3 = (f32[256,256]{1,0:T(8,128)S(1)}, bf16[2,256,128]{2,1,0:T(8,128)(2,1)S(1)}, bf16[2,256,128]{2,1,0:T(8,128)(2,1)S(1)}) custom-call(f32[2,80,128]{2,1,0:T(8,128)S(1)} %move.2.own_ref.field_ref, f32[2,80,128]{2,1,0:T(8,128)S(1)} %collective-permute-done.2.beside_ref, f32[256,128]{1,0:T(8,128)S(1)} %get-tuple-element.51.bias_ref, ...), custom_call_target="tpu_custom_call" | custom-call | tf_op jit(solution)/shard_map/forward_across/pallas_call | solution.py:212
  15.6 0.6 move.3
  16.2 0.0 copy-start.1
  16.2 15.5 %all_to_all.10.fields_ref = f32[8,40,128]{2,1,0:T(8,128)S(1)} all-to-all(f32[8,40,128]{2,1,0:T(8,128)S(1)} %bitcast.13), channel_id=1, replica_groups=mesh['member_0'=4,'member_1'=2,'lat_0'=2,'lat_1'=4,'lat_2'=2] {'member_0..., dimensions={0} | all-to-all | bytes 327680 | tf_op jit(solution)/shard_map/all_to_all | solution.py:465
  31.7 0.0 copy-done.1
  31.7 0.2 crps.1
  31.9 10.9 %all_to_all.11.grads_ref = f32[8,48,128]{2,1,0:T(8,128)S(1)} all-to-all(f32[8,48,128]{2,1,0:T(8,128)S(1)} %crps.1), channel_id=1, replica_groups=mesh['member_0'=4,'member_1'=2,'lat_0'=2,'lat_1'=4,'lat_2'=2] {'member_0..., dimensions={0} | all-to-all | bytes 393216 | tf_op jit(solution)/shard_map/all_to_all | solution.py:469
  42.9 0.1 collective-permute-start.5
  43.0 1.9 %collective-permute-start.4 = (f32[176,128]{1,0:T(8,128)S(1)}, f32[176,128]{1,0:T(8,128)S(1)}, u32[]{:S(2)}, u32[]{:S(2)}) collective-permute-start(f32[176,128]{1,0:T(8,128)S(1)} %get-tuple-element.68.own_ref), channel_id=1, source_target_pairs={{0,15},{1,2},{2,1},{3,4},{4,3},{5,6},{6,5},{7,8},{8,7},{9,10},{10,... | collective-permute-start | bytes 270344 | tf_op jit(solution)/shard_map/ppermute | solution.py:475
  44.8 0.7 %collective-permute-start.6 = (f32[16,128]{1,0:T(8,128)S(1)}, f32[16,128]{1,0:T(8,128)S(1)}, u32[]{:S(2)}, u32[]{:S(2)}) collective-permute-start(f32[16,128]{1,0:T(8,128)S(1)} %get-tuple-element.86), channel_id=1, source_target_pairs={{0,5},{1,12},{2,7},{3,14},{4,9},{5,0},{6,11},{7,2},{8,13},{9,4},{1... | collective-permute-start | bytes 24584 | tf_op jit(solution)/shard_map/ppermute | solution.py:479
  45.6 0.4 collective-permute-start.7
  45.9 1.3 %prepare_back.1 = (bf16[512,720]{1,0:T(8,128)(2,1)S(1)}, bf16[480,768]{1,0:T(8,128)(2,1)S(1)}, f32[2,2,256,256]{3,2,1,0:T(8,128)S(1)}) custom-call(f32[720,256]{1,0:T(8,128)S(1)} %get-tuple-element.69.win_ref, f32[80,2304]{1,0:T(8,128)S(1)} %get-tuple-element.70.wout_ref, f32[256,256]{1,0:T(8,128)S(1)} %get-tuple-element.71.rest_0_, ...), custom_call_target="tpu_custom_call" | custom-call | tf_op jit(solution)/shard_map/prepare_back/pallas_call | solution.py:166
  47.3 0.0 collective-permute-done.5.beside_ref.rest_0_
  47.3 0.6 %backward_near.2 = (bf16[2,256,128]{2,1,0:T(8,128)(2,1)S(1)}, bf16[2,256,128]{2,1,0:T(8,128)(2,1)S(1)}) custom-call(f32[176,128]{1,0:T(8,128)S(1)} %get-tuple-element.68.own_ref, f32[176,128]{1,0:T(8,128)S(1)} %collective-permute-done.5.beside_ref.rest_0_, f32[2,2,256,256]{3,2,1,0:T(8,128)S(1)} %get-tuple-element.75.slope_ref, ...), custom_call_target="tpu_custom_call" | custom-call | tf_op jit(solution)/shard_map/backward_near/pallas_call | solution.py:354
  47.9 1.3 %collective-permute-done.4.beside_ref.rest_1_ = f32[176,128]{1,0:T(8,128)S(1)} collective-permute-done((f32[176,128]{1,0:T(8,128)S(1)}, f32[176,128]{1,0:T(8,128)S(1)}, u32[]{:S(2)}, u32[]{:S(2)}) %collective-permute-start.4) | collective-permute-done | bytes 90144 | tf_op jit(solution)/shard_map/ppermute | solution.py:475
  49.3 0.6 %backward_across.2 = (bf16[2,256,128]{2,1,0:T(8,128)(2,1)S(1)}, bf16[2,256,128]{2,1,0:T(8,128)(2,1)S(1)}) custom-call(f32[176,128]{1,0:T(8,128)S(1)} %get-tuple-element.68.own_ref, f32[176,128]{1,0:T(8,128)S(1)} %collective-permute-done.4.beside_ref.rest_1_, f32[2,2,256,256]{3,2,1,0:T(8,128)S(1)} %get-tuple-element.75.slope_ref, ...), custom_call_target="tpu_custom_call" | custom-call | tf_op jit(solution)/shard_map/backward_across/pallas_call | solution.py:354
  49.9 0.0 collective-permute-done.6.rest_2_
  49.9 0.0 collective-permute-done.7.rest_3_
  49.9 0.6 join.1
  50.5 0.1 collective-permute-start.9
  50.6 1.9 %collective-permute-start.8 = (f32[176,128]{1,0:T(8,128)S(1)}, f32[176,128]{1,0:T(8,128)S(1)}, u32[]{:S(2)}, u32[]{:S(2)}) collective-permute-start(f32[176,128]{1,0:T(8,128)S(1)} %get-tuple-element.87.own_ref), channel_id=1, source_target_pairs={{0,15},{1,2},{2,1},{3,4},{4,3},{5,6},{6,5},{7,8},{8,7},{9,10},{10,... | collective-permute-start | bytes 270344 | tf_op jit(solution)/shard_map/ppermute | solution.py:487
  52.5 1.2 %collective-permute-start.10 = (f32[16,128]{1,0:T(8,128)S(1)}, f32[16,128]{1,0:T(8,128)S(1)}, u32[]{:S(2)}, u32[]{:S(2)}) collective-permute-start(f32[16,128]{1,0:T(8,128)S(1)} %get-tuple-element.95), channel_id=1, source_target_pairs={{0,8},{1,9},{2,10},{3,11},{4,12},{5,13},{6,14},{7,15},{8,0},{9,1},... | collective-permute-start | bytes 24584 | tf_op jit(solution)/shard_map/ppermute | solution.py:488
  53.7 0.0 collective-permute-done.9.beside_ref.rest_0_
  53.7 0.6 %backward_near.3 = (bf16[2,256,128]{2,1,0:T(8,128)(2,1)S(1)}, bf16[2,256,128]{2,1,0:T(8,128)(2,1)S(1)}) custom-call(f32[176,128]{1,0:T(8,128)S(1)} %get-tuple-element.87.own_ref, f32[176,128]{1,0:T(8,128)S(1)} %collective-permute-done.9.beside_ref.rest_0_, f32[2,2,256,256]{3,2,1,0:T(8,128)S(1)} %get-tuple-element.75.slope_ref, ...), custom_call_target="tpu_custom_call" | custom-call | tf_op jit(solution)/shard_map/backward_near/pallas_call | solution.py:354
  54.3 2.5 %collective-permute-done.8.beside_ref.rest_1_ = f32[176,128]{1,0:T(8,128)S(1)} collective-permute-done((f32[176,128]{1,0:T(8,128)S(1)}, f32[176,128]{1,0:T(8,128)S(1)}, u32[]{:S(2)}, u32[]{:S(2)}) %collective-permute-start.8) | collective-permute-done | bytes 90144 | tf_op jit(solution)/shard_map/ppermute | solution.py:487
  56.8 0.6 %backward_across.3 = (bf16[2,256,128]{2,1,0:T(8,128)(2,1)S(1)}, bf16[2,256,128]{2,1,0:T(8,128)(2,1)S(1)}) custom-call(f32[176,128]{1,0:T(8,128)S(1)} %get-tuple-element.87.own_ref, f32[176,128]{1,0:T(8,128)S(1)} %collective-permute-done.8.beside_ref.rest_1_, f32[2,2,256,256]{3,2,1,0:T(8,128)S(1)} %get-tuple-element.75.slope_ref, ...), custom_call_target="tpu_custom_call" | custom-call | tf_op jit(solution)/shard_map/backward_across/pallas_call | solution.py:354
  57.5 0.0 collective-permute-done.10.rest_2_
  57.5 1.2 %finish.1 = (f32[160,128]{1,0:T(8,128)}, f32[1,1]{1,0:T(1,128)}) custom-call(f32[176,128]{1,0:T(8,128)S(1)} %get-tuple-element.87.own_ref, bf16[2,256,128]{2,1,0:T(8,128)(2,1)S(1)} %get-tuple-element.90.close_hi, bf16[2,256,128]{2,1,0:T(8,128)(2,1)S(1)} %get-tuple-element.91.close_lo, bf16[2,256,128]{2,1,0:T(8,128)(2,1)S(1)} %get-tuple-element.93.far_hi, ...), custom_call_target="tpu_custom_call" | custom-call | tf_op jit(solution)/shard_map/finish/pallas_call | solution.py:423
  (1 shorter events, 0.0 us)
Async XLA Ops:
  0.6 6.2 %collective-permute-start.1 = (f32[2,80,128]{2,1,0:T(8,128)}, f32[2,80,128]{2,1,0:T(8,128)S(1)}, u32[]{:S(2)}, u32[]{:S(2)}) collective-permute-start(f32[2,80,128]{2,1,0:T(8,128)} %bitcast.8), channel_id=1, source_target_pairs={{0,1},{1,0},{2,3},{3,2},{4,5},{5,4},{6,7},{7,6},{8,9},{9,8},{10,11... | collective-permute-start | bytes 245768 | tf_op jit(solution)/shard_map/ppermute | solution.py:448
  0.7 6.8 %collective-permute-start = (f32[2,80,128]{2,1,0:T(8,128)}, f32[2,80,128]{2,1,0:T(8,128)S(1)}, u32[]{:S(2)}, u32[]{:S(2)}) collective-permute-start(f32[2,80,128]{2,1,0:T(8,128)} %bitcast.9), channel_id=1, source_target_pairs={{0,15},{1,2},{2,1},{3,4},{4,3},{5,6},{6,5},{7,8},{8,7},{9,10},{10,... | collective-permute-start | bytes 245768 | tf_op jit(solution)/shard_map/ppermute | solution.py:449
  5.0 1.8 %copy-start = (f32[1,2,80,128]{3,2,1,0:T(8,128)S(1)}, f32[1,2,80,128]{3,2,1,0:T(8,128)}, u32[]{:S(2)}) copy-start(f32[1,2,80,128]{3,2,1,0:T(8,128)} %param.6) | copy-start | bytes 245764
  8.8 3.9 %collective-permute-start.3 = (f32[2,80,128]{2,1,0:T(8,128)S(1)}, f32[2,80,128]{2,1,0:T(8,128)S(1)}, u32[]{:S(2)}, u32[]{:S(2)}) collective-permute-start(f32[2,80,128]{2,1,0:T(8,128)S(1)} %move.2.own_ref.field_ref), channel_id=1, source_target_pairs={{0,1},{1,0},{2,3},{3,2},{4,5},{5,4},{6,7},{7,6},{8,9},{9,8},{10,11... | collective-permute-start | bytes 245768 | tf_op jit(solution)/shard_map/ppermute | solution.py:457
  8.9 6.1 %collective-permute-start.2 = (f32[2,80,128]{2,1,0:T(8,128)S(1)}, f32[2,80,128]{2,1,0:T(8,128)S(1)}, u32[]{:S(2)}, u32[]{:S(2)}) collective-permute-start(f32[2,80,128]{2,1,0:T(8,128)S(1)} %move.2.own_ref.field_ref), channel_id=1, source_target_pairs={{0,15},{1,2},{2,1},{3,4},{4,3},{5,6},{6,5},{7,8},{8,7},{9,10},{10,... | collective-permute-start | bytes 245768 | tf_op jit(solution)/shard_map/ppermute | solution.py:458
  16.2 15.5 %copy-start.1 = (f32[2,2,80,128]{3,2,1,0:T(8,128)S(1)}, f32[2,2,80,128]{3,2,1,0:T(8,128)}, u32[]{:S(2)}) copy-start(f32[2,2,80,128]{3,2,1,0:T(8,128)} %param.7) | copy-start | bytes 491524
  42.9 4.4 %collective-permute-start.5 = (f32[176,128]{1,0:T(8,128)S(1)}, f32[176,128]{1,0:T(8,128)S(1)}, u32[]{:S(2)}, u32[]{:S(2)}) collective-permute-start(f32[176,128]{1,0:T(8,128)S(1)} %get-tuple-element.68.own_ref), channel_id=1, source_target_pairs={{0,1},{1,0},{2,3},{3,2},{4,5},{5,4},{6,7},{7,6},{8,9},{9,8},{10,11... | collective-permute-start | bytes 270344 | tf_op jit(solution)/shard_map/ppermute | solution.py:474
  43.0 6.3 %collective-permute-start.4 = (f32[176,128]{1,0:T(8,128)S(1)}, f32[176,128]{1,0:T(8,128)S(1)}, u32[]{:S(2)}, u32[]{:S(2)}) collective-permute-start(f32[176,128]{1,0:T(8,128)S(1)} %get-tuple-element.68.own_ref), channel_id=1, source_target_pairs={{0,15},{1,2},{2,1},{3,4},{4,3},{5,6},{6,5},{7,8},{8,7},{9,10},{10,... | collective-permute-start | bytes 270344 | tf_op jit(solution)/shard_map/ppermute | solution.py:475
  44.8 5.1 %collective-permute-start.6 = (f32[16,128]{1,0:T(8,128)S(1)}, f32[16,128]{1,0:T(8,128)S(1)}, u32[]{:S(2)}, u32[]{:S(2)}) collective-permute-start(f32[16,128]{1,0:T(8,128)S(1)} %get-tuple-element.86), channel_id=1, source_target_pairs={{0,5},{1,12},{2,7},{3,14},{4,9},{5,0},{6,11},{7,2},{8,13},{9,4},{1... | collective-permute-start | bytes 24584 | tf_op jit(solution)/shard_map/ppermute | solution.py:479
  45.6 4.4 %collective-permute-start.7 = (f32[16,128]{1,0:T(8,128)S(1)}, f32[16,128]{1,0:T(8,128)S(1)}, u32[]{:S(2)}, u32[]{:S(2)}) collective-permute-start(f32[16,128]{1,0:T(8,128)S(1)} %get-tuple-element.86), channel_id=1, source_target_pairs={{0,11},{1,6},{2,13},{3,8},{4,15},{5,10},{6,1},{7,12},{8,3},{9,14},... | collective-permute-start | bytes 24584 | tf_op jit(solution)/shard_map/ppermute | solution.py:479
  50.5 3.2 %collective-permute-start.9 = (f32[176,128]{1,0:T(8,128)S(1)}, f32[176,128]{1,0:T(8,128)S(1)}, u32[]{:S(2)}, u32[]{:S(2)}) collective-permute-start(f32[176,128]{1,0:T(8,128)S(1)} %get-tuple-element.87.own_ref), channel_id=1, source_target_pairs={{0,1},{1,0},{2,3},{3,2},{4,5},{5,4},{6,7},{7,6},{8,9},{9,8},{10,11... | collective-permute-start | bytes 270344 | tf_op jit(solution)/shard_map/ppermute | solution.py:486
  50.6 6.2 %collective-permute-start.8 = (f32[176,128]{1,0:T(8,128)S(1)}, f32[176,128]{1,0:T(8,128)S(1)}, u32[]{:S(2)}, u32[]{:S(2)}) collective-permute-start(f32[176,128]{1,0:T(8,128)S(1)} %get-tuple-element.87.own_ref), channel_id=1, source_target_pairs={{0,15},{1,2},{2,1},{3,4},{4,3},{5,6},{6,5},{7,8},{8,7},{9,10},{10,... | collective-permute-start | bytes 270344 | tf_op jit(solution)/shard_map/ppermute | solution.py:487
  52.5 5.0 %collective-permute-start.10 = (f32[16,128]{1,0:T(8,128)S(1)}, f32[16,128]{1,0:T(8,128)S(1)}, u32[]{:S(2)}, u32[]{:S(2)}) collective-permute-start(f32[16,128]{1,0:T(8,128)S(1)} %get-tuple-element.95), channel_id=1, source_target_pairs={{0,8},{1,9},{2,10},{3,11},{4,12},{5,13},{6,14},{7,15},{8,0},{9,1},... | collective-permute-start | bytes 24584 | tf_op jit(solution)/shard_map/ppermute | solution.py:488

commit v9 on v8

--- a/solution.py
+++ b/solution.py
@@ -132,18 +132,7 @@
     )(*(pltpu.with_memory_space_constraint(array, pltpu.HBM) for array in arrays))
 
 
-def prepare_back_kernel(win_ref, wout_ref, *rest):
-    before_refs, (outb_ref, inb_ref, slope_ref, stack) = rest[:4], rest[4:]
-    for side in range(2):
-        below = is_even() if side == 0 else jnp.logical_not(is_even())
-        first = jnp.where(below, 0, -2)
-        for step, before_ref in enumerate(before_refs[side::2]):
-            slope = gelu_slope(before_ref[...])
-            width = slope.shape[1] // 2
-            for half in range(2):
-                part = slope[:, half * width : (half + 1) * width]
-                part = jnp.where(inside(first + 1 + half), part, 0.0)
-                slope_ref[step, side, :, half * width : (half + 1) * width] = part
+def prepare_back_kernel(win_ref, wout_ref, outb_ref, inb_ref, stack):
     outer, width = wout_ref.shape
     hidden = width // 9
     inner = win_ref.shape[0] // 9
@@ -158,19 +147,39 @@
     outb_ref[:hidden, :], outb_ref[hidden:, :] = split(stack[...].T)
 
 
-def prepare_back(weight_in, weight_out, *before):
+def prepare_back(weight_in, weight_out):
     taps_in, hidden = weight_in.shape
     outer = weight_out.shape[0]
-    inner = taps_in // 9
-    shapes = [(2 * hidden, 9 * outer), (6 * inner, 3 * hidden)]
+    shapes = [(2 * hidden, 9 * outer), (6 * (taps_in // 9), 3 * hidden)]
     return pl.pallas_call(
         prepare_back_kernel,
-        out_shape=[jax.ShapeDtypeStruct(shape, bf16) for shape in shapes]
-        + [jax.ShapeDtypeStruct((2, 2, *before[0].shape), f32)],
+        out_shape=[jax.ShapeDtypeStruct(shape, bf16) for shape in shapes],
         scratch_shapes=[pltpu.VMEM((9 * outer, hidden), f32)],
         compiler_params=params,
         name="prepare_back",
-    )(weight_in, weight_out, *before)
+    )(weight_in, weight_out)
+
+
+def slopes_kernel(*refs):
+    *before_refs, slope_ref = refs
+    for side, before_ref in enumerate(before_refs):
+        below = is_even() if side == 0 else jnp.logical_not(is_even())
+        first = jnp.where(below, 0, -2)
+        slope = gelu_slope(before_ref[...])
+        width = slope.shape[1] // 2
+        for half in range(2):
+            part = slope[:, half * width : (half + 1) * width]
+            part = jnp.where(inside(first + 1 + half), part, 0.0)
+            slope_ref[side, :, half * width : (half + 1) * width] = part
+
+
+def slopes_of(*before):
+    return pl.pallas_call(
+        slopes_kernel,
+        out_shape=jax.ShapeDtypeStruct((2, *before[0].shape), f32),
+        compiler_params=params,
+        name="slopes",
+    )(*before)
 
 
 def inside(row):
@@ -336,7 +345,7 @@
         return lambda row: ref[row * channels : (row + 1) * channels, :]
 
     side_windows(near_side, rows_of(own_ref), rows_of(beside_ref), wide)
-    grads = to_channels(weight_ref[...], wide, 0, channels) * slope_ref[step, 0 if near_side else 1]
+    grads = to_channels(weight_ref[...], wide, 0, channels) * slope_ref[0 if near_side else 1]
     return [split(grads[:, half * width : (half + 1) * width]) for half in range(2)]
 
 
@@ -457,7 +466,10 @@
     beside = lax.ppermute(field, LAT, near)
     crossed = lax.ppermute(field, LAT, across)
     before_near, *close = forward_side(True, field, beside, bias, w_in)
-    crossed, close = lax.optimization_barrier((crossed, close))
+    raw, close = lax.optimization_barrier((raw, close))
+    back = prepare_back(*raw)
+    crossed, close, back = lax.optimization_barrier((crossed, close, back))
+    w_out_back, w_in_back = back
     before_across, *distant = forward_side(False, field, crossed, bias, w_in)
     before_second = (before_near, before_across)
     fields = move(1, field, close, distant, w_out)
@@ -467,8 +479,7 @@
     )
     grads = crps(lat_weights, chunks, targets.reshape(members, height, width))
     grads = lax.all_to_all(grads, MEMBER, split_axis=0, concat_axis=0, tiled=True)
-    back = prepare_back(*raw, *before_first, *before_second)
-    w_out_back, w_in_back, slopes = back
+    slopes = slopes_of(*before_second)
     first_grads, message, known = collect(grads)
 
     beside = lax.ppermute(message, LAT, near)
@@ -486,6 +497,8 @@
     beside = lax.ppermute(message, LAT, near)
     crossed = lax.ppermute(message, LAT, across)
     distant_tables = [lax.ppermute(known, LAT, pairs) for pairs in (opposite,)]
+    message, before_first = lax.optimization_barrier((message, before_first))
+    slopes = slopes_of(*before_first)
     close = backward_side(0, True, message, beside, slopes, w_out_back)
     crossed, close = lax.optimization_barrier((crossed, close))
     distant = backward_side(0, False, message, crossed, slopes, w_out_back)

time: 58.9 us -> 58.9 us (level)
    pallas_call x1, Pallas kernels: 1.35 us -> 0.33 us  [prepare_back(): pl.pallas_call(prepare_back_kernel, out_shape=[jax.ShapeDtypeStruct(shape...]
    ppermute x2, waiting for transfers between devices: 3.86 us -> 4.55 us  [on_device(): crossed = lax.ppermute(message, LAT, across)]
    pallas_call x0 -> x2, Pallas kernels: none -> 0.66 us  [slopes_of(): pl.pallas_call(slopes_kernel, out_shape=jax.ShapeDtypeStruct((2, *before[...]
  transfers between devices with their start and end apart: 11 -> 11, of which waited for: 3 -> 3; matrix products, arithmetic and copies ran while one was open for 0% -> 0% of each run, Pallas kernels for 12% -> 11%
where the time goes in v9:
time: 58.9 us; the launch traced here: 58.7 us
  blocking collectives  26.4 us (45%)
  starting transfers between devices  14.4 us (24%)
  Pallas kernels  11.2 us (19%)
  waiting for transfers between devices  5.84 us (10%)
  between operations  0.85 us (1%)
    all_to_all x1, blocking collectives, on_device(): lax.all_to_all(fields.reshape(members, height, width), MEMBER, split_axis...  15.5 us
    all_to_all x1, blocking collectives, on_device(): lax.all_to_all(grads, MEMBER, split_axis=0, concat_axis=0, tiled=True)  10.9 us
    ppermute x2, waiting for transfers between devices, on_device(): crossed = lax.ppermute(message, LAT, across)  4.55 us
    ppermute x1, starting transfers between devices, on_device(): crossed = lax.ppermute(own, LAT, across)  4.3 us
    ppermute x2, starting transfers between devices, on_device(): crossed = lax.ppermute(message, LAT, across)  3.77 us
    ppermute x1, starting transfers between devices, on_device(): crossed = lax.ppermute(field, LAT, across)  3.77 us
    pallas_call x4, Pallas kernels, forward_side(): pl.pallas_call(functools.partial(forward_side_kernel, near_side), out_sha...  2.7 us
    pallas_call x4, Pallas kernels, backward_side(): pl.pallas_call(functools.partial(backward_side_kernel, step, near_side),...  2.5 us
  transfers between devices with their start and end apart: 11, of which 3 were waited for; matrix products, arithmetic and copies ran while one was open for 0% of the time, Pallas kernels for 11%

profile of v9, /device:TPU:0, one launch (start us, length us, event | category | flops | bytes accessed | tf_op | source)
XLA Modules:
  0.0 58.7 jit_solution(2997067092197509288)
XLA Ops:
  0.6 0.1 collective-permute-start.1
  0.7 4.3 %collective-permute-start = (f32[2,80,128]{2,1,0:T(8,128)}, f32[2,80,128]{2,1,0:T(8,128)S(1)}, u32[]{:S(2)}, u32[]{:S(2)}) collective-permute-start(f32[2,80,128]{2,1,0:T(8,128)} %bitcast.9), channel_id=1, source_target_pairs={{0,15},{1,2},{2,1},{3,4},{4,3},{5,6},{6,5},{7,8},{8,7},{9,10},{10,... | collective-permute-start | bytes 245768 | tf_op jit(solution)/shard_map/ppermute | solution.py:458
  5.0 0.0 copy-start
  5.0 1.8 %prepare.1 = (bf16[512,720]{1,0:T(8,128)(2,1)S(1)}, bf16[480,768]{1,0:T(8,128)(2,1)S(1)}, f32[256,128]{1,0:T(8,128)S(1)}, f32[16,128]{1,0:T(8,128)S(1)}, f32[720,256]{1,0:T(8,128)S(1)}, /*index=5*/f32[80,2304]{1,0:T(8,128)S(1)}) custom-call(f32[720,256]{1,0:T(8,128)} %bitcast.15, f32[80,2304]{1,0:T(8,128)} %wout_hbm.1, f32[1,256]{1,0:T(1,128)} %bitcast.16, ...), custom_call_target="tpu_custom_call" | custom-call | tf_op jit(solution)/shard_map/prepare/pallas_call | solution.py:123
  6.8 0.0 collective-permute-done.1.beside_ref
  6.8 0.0 copy-done
  6.8 0.7 %forward_near.2 = (f32[256,256]{1,0:T(8,128)S(1)}, bf16[2,256,128]{2,1,0:T(8,128)(2,1)S(1)}, bf16[2,256,128]{2,1,0:T(8,128)(2,1)S(1)}) custom-call(f32[2,80,128]{2,1,0:T(8,128)S(1)} %bitcast.10, f32[2,80,128]{2,1,0:T(8,128)S(1)} %collective-permute-done.1.beside_ref, f32[256,128]{1,0:T(8,128)S(1)} %get-tuple-element.59.bias_ref, ...), custom_call_target="tpu_custom_call" | custom-call | tf_op jit(solution)/shard_map/forward_near/pallas_call | solution.py:221
  7.5 0.0 collective-permute-done.beside_ref
  7.5 0.7 %forward_across.2 = (f32[256,256]{1,0:T(8,128)S(1)}, bf16[2,256,128]{2,1,0:T(8,128)(2,1)S(1)}, bf16[2,256,128]{2,1,0:T(8,128)(2,1)S(1)}) custom-call(f32[2,80,128]{2,1,0:T(8,128)S(1)} %bitcast.11, f32[2,80,128]{2,1,0:T(8,128)S(1)} %collective-permute-done.beside_ref, f32[256,128]{1,0:T(8,128)S(1)} %get-tuple-element.59.bias_ref, ...), custom_call_target="tpu_custom_call" | custom-call | tf_op jit(solution)/shard_map/forward_across/pallas_call | solution.py:221
  8.2 0.6 move.2.own_ref.field_ref
  8.8 0.1 collective-permute-start.3
  8.9 3.8 %collective-permute-start.2 = (f32[2,80,128]{2,1,0:T(8,128)S(1)}, f32[2,80,128]{2,1,0:T(8,128)S(1)}, u32[]{:S(2)}, u32[]{:S(2)}) collective-permute-start(f32[2,80,128]{2,1,0:T(8,128)S(1)} %move.2.own_ref.field_ref), channel_id=1, source_target_pairs={{0,15},{1,2},{2,1},{3,4},{4,3},{5,6},{6,5},{7,8},{8,7},{9,10},{10,... | collective-permute-start | bytes 245768 | tf_op jit(solution)/shard_map/ppermute | solution.py:467
  12.6 0.0 collective-permute-done.3.beside_ref
  12.6 0.7 %forward_near.3 = (f32[256,256]{1,0:T(8,128)S(1)}, bf16[2,256,128]{2,1,0:T(8,128)(2,1)S(1)}, bf16[2,256,128]{2,1,0:T(8,128)(2,1)S(1)}) custom-call(f32[2,80,128]{2,1,0:T(8,128)S(1)} %move.2.own_ref.field_ref, f32[2,80,128]{2,1,0:T(8,128)S(1)} %collective-permute-done.3.beside_ref, f32[256,128]{1,0:T(8,128)S(1)} %get-tuple-element.59.bias_ref, ...), custom_call_target="tpu_custom_call" | custom-call | tf_op jit(solution)/shard_map/forward_near/pallas_call | solution.py:221
  13.3 0.3 prepare_back.1
  13.7 1.3 %collective-permute-done.2.beside_ref = f32[2,80,128]{2,1,0:T(8,128)S(1)} collective-permute-done((f32[2,80,128]{2,1,0:T(8,128)S(1)}, f32[2,80,128]{2,1,0:T(8,128)S(1)}, u32[]{:S(2)}, u32[]{:S(2)}) %collective-permute-start.2) | collective-permute-done | bytes 81952 | tf_op jit(solution)/shard_map/ppermute | solution.py:467
  14.9 0.7 %forward_across.3 = (f32[256,256]{1,0:T(8,128)S(1)}, bf16[2,256,128]{2,1,0:T(8,128)(2,1)S(1)}, bf16[2,256,128]{2,1,0:T(8,128)(2,1)S(1)}) custom-call(f32[2,80,128]{2,1,0:T(8,128)S(1)} %move.2.own_ref.field_ref, f32[2,80,128]{2,1,0:T(8,128)S(1)} %collective-permute-done.2.beside_ref, f32[256,128]{1,0:T(8,128)S(1)} %get-tuple-element.59.bias_ref, ...), custom_call_target="tpu_custom_call" | custom-call | tf_op jit(solution)/shard_map/forward_across/pallas_call | solution.py:221
  15.6 0.6 move.3
  16.2 0.0 copy-start.1
  16.2 15.5 %all_to_all.10.fields_ref = f32[8,40,128]{2,1,0:T(8,128)S(1)} all-to-all(f32[8,40,128]{2,1,0:T(8,128)S(1)} %bitcast.13), channel_id=1, replica_groups=mesh['member_0'=4,'member_1'=2,'lat_0'=2,'lat_1'=4,'lat_2'=2] {'member_0..., dimensions={0} | all-to-all | bytes 327680 | tf_op jit(solution)/shard_map/all_to_all | solution.py:477
  31.7 0.0 copy-done.1
  31.7 0.2 crps.1
  31.9 10.9 %all_to_all.11.grads_ref = f32[8,48,128]{2,1,0:T(8,128)S(1)} all-to-all(f32[8,48,128]{2,1,0:T(8,128)S(1)} %crps.1), channel_id=1, replica_groups=mesh['member_0'=4,'member_1'=2,'lat_0'=2,'lat_1'=4,'lat_2'=2] {'member_0..., dimensions={0} | all-to-all | bytes 393216 | tf_op jit(solution)/shard_map/all_to_all | solution.py:481
  42.9 0.1 collective-permute-start.5
  43.0 1.9 %collective-permute-start.4 = (f32[176,128]{1,0:T(8,128)S(1)}, f32[176,128]{1,0:T(8,128)S(1)}, u32[]{:S(2)}, u32[]{:S(2)}) collective-permute-start(f32[176,128]{1,0:T(8,128)S(1)} %get-tuple-element.84.own_ref), channel_id=1, source_target_pairs={{0,15},{1,2},{2,1},{3,4},{4,3},{5,6},{6,5},{7,8},{8,7},{9,10},{10,... | collective-permute-start | bytes 270344 | tf_op jit(solution)/shard_map/ppermute | solution.py:486
  44.8 0.7 %collective-permute-start.6 = (f32[16,128]{1,0:T(8,128)S(1)}, f32[16,128]{1,0:T(8,128)S(1)}, u32[]{:S(2)}, u32[]{:S(2)}) collective-permute-start(f32[16,128]{1,0:T(8,128)S(1)} %get-tuple-element.97), channel_id=1, source_target_pairs={{0,5},{1,12},{2,7},{3,14},{4,9},{5,0},{6,11},{7,2},{8,13},{9,4},{1... | collective-permute-start | bytes 24584 | tf_op jit(solution)/shard_map/ppermute | solution.py:490
  45.5 0.4 collective-permute-start.7
  45.9 0.3 slopes.2.slope_ref
  46.3 0.0 collective-permute-done.5.beside_ref.rest_0_
  46.3 0.6 %backward_near.2 = (bf16[2,256,128]{2,1,0:T(8,128)(2,1)S(1)}, bf16[2,256,128]{2,1,0:T(8,128)(2,1)S(1)}) custom-call(f32[176,128]{1,0:T(8,128)S(1)} %get-tuple-element.84.own_ref, f32[176,128]{1,0:T(8,128)S(1)} %collective-permute-done.5.beside_ref.rest_0_, f32[2,256,256]{2,1,0:T(8,128)S(1)} %slopes.2.slope_ref, bf16[512,720]{1,0:T(8,128)(2,1)S(1)} %get-tuple-element.87.outb_ref), custom_call_target="tpu_custom_call" | custom-call | tf_op jit(solution)/shard_map/backward_near/pallas_call | solution.py:363
  46.9 2.4 %collective-permute-done.4.beside_ref.rest_1_ = f32[176,128]{1,0:T(8,128)S(1)} collective-permute-done((f32[176,128]{1,0:T(8,128)S(1)}, f32[176,128]{1,0:T(8,128)S(1)}, u32[]{:S(2)}, u32[]{:S(2)}) %collective-permute-start.4) | collective-permute-done | bytes 90144 | tf_op jit(solution)/shard_map/ppermute | solution.py:486
  49.3 0.6 %backward_across.2 = (bf16[2,256,128]{2,1,0:T(8,128)(2,1)S(1)}, bf16[2,256,128]{2,1,0:T(8,128)(2,1)S(1)}) custom-call(f32[176,128]{1,0:T(8,128)S(1)} %get-tuple-element.84.own_ref, f32[176,128]{1,0:T(8,128)S(1)} %collective-permute-done.4.beside_ref.rest_1_, f32[2,256,256]{2,1,0:T(8,128)S(1)} %slopes.2.slope_ref, bf16[512,720]{1,0:T(8,128)(2,1)S(1)} %get-tuple-element.87.outb_ref), custom_call_target="tpu_custom_call" | custom-call | tf_op jit(solution)/shard_map/backward_across/pallas_call | solution.py:363
  49.9 0.0 collective-permute-done.6.rest_2_
  49.9 0.0 collective-permute-done.7.rest_3_
  49.9 0.6 join.1
  50.5 0.1 collective-permute-start.9
  50.6 1.9 %collective-permute-start.8 = (f32[176,128]{1,0:T(8,128)S(1)}, f32[176,128]{1,0:T(8,128)S(1)}, u32[]{:S(2)}, u32[]{:S(2)}) collective-permute-start(f32[176,128]{1,0:T(8,128)S(1)} %get-tuple-element.101.own_ref), channel_id=1, source_target_pairs={{0,15},{1,2},{2,1},{3,4},{4,3},{5,6},{6,5},{7,8},{8,7},{9,10},{10,... | collective-permute-start | bytes 270344 | tf_op jit(solution)/shard_map/ppermute | solution.py:498
  52.5 1.2 %collective-permute-start.10 = (f32[16,128]{1,0:T(8,128)S(1)}, f32[16,128]{1,0:T(8,128)S(1)}, u32[]{:S(2)}, u32[]{:S(2)}) collective-permute-start(f32[16,128]{1,0:T(8,128)S(1)} %get-tuple-element.111), channel_id=1, source_target_pairs={{0,8},{1,9},{2,10},{3,11},{4,12},{5,13},{6,14},{7,15},{8,0},{9,1},... | collective-permute-start | bytes 24584 | tf_op jit(solution)/shard_map/ppermute | solution.py:499
  53.7 0.3 slopes.3.slope_ref
  54.0 0.0 collective-permute-done.9.beside_ref.rest_0_
  54.0 0.6 %backward_near.3 = (bf16[2,256,128]{2,1,0:T(8,128)(2,1)S(1)}, bf16[2,256,128]{2,1,0:T(8,128)(2,1)S(1)}) custom-call(f32[176,128]{1,0:T(8,128)S(1)} %get-tuple-element.101.own_ref, f32[176,128]{1,0:T(8,128)S(1)} %collective-permute-done.9.beside_ref.rest_0_, f32[2,256,256]{2,1,0:T(8,128)S(1)} %slopes.3.slope_ref, bf16[512,720]{1,0:T(8,128)(2,1)S(1)} %get-tuple-element.87.outb_ref), custom_call_target="tpu_custom_call" | custom-call | tf_op jit(solution)/shard_map/backward_near/pallas_call | solution.py:363
  54.6 2.2 %collective-permute-done.8.beside_ref.rest_1_ = f32[176,128]{1,0:T(8,128)S(1)} collective-permute-done((f32[176,128]{1,0:T(8,128)S(1)}, f32[176,128]{1,0:T(8,128)S(1)}, u32[]{:S(2)}, u32[]{:S(2)}) %collective-permute-start.8) | collective-permute-done | bytes 90144 | tf_op jit(solution)/shard_map/ppermute | solution.py:498
  56.8 0.6 %backward_across.3 = (bf16[2,256,128]{2,1,0:T(8,128)(2,1)S(1)}, bf16[2,256,128]{2,1,0:T(8,128)(2,1)S(1)}) custom-call(f32[176,128]{1,0:T(8,128)S(1)} %get-tuple-element.101.own_ref, f32[176,128]{1,0:T(8,128)S(1)} %collective-permute-done.8.beside_ref.rest_1_, f32[2,256,256]{2,1,0:T(8,128)S(1)} %slopes.3.slope_ref, ...), custom_call_target="tpu_custom_call" | custom-call | tf_op jit(solution)/shard_map/backward_across/pallas_call | solution.py:363
  57.4 0.0 collective-permute-done.10.rest_2_
  57.5 1.2 %finish.1 = (f32[160,128]{1,0:T(8,128)}, f32[1,1]{1,0:T(1,128)}) custom-call(f32[176,128]{1,0:T(8,128)S(1)} %get-tuple-element.101.own_ref, bf16[2,256,128]{2,1,0:T(8,128)(2,1)S(1)} %get-tuple-element.106.close_hi, bf16[2,256,128]{2,1,0:T(8,128)(2,1)S(1)} %get-tuple-element.107.close_lo, bf16[2,256,128]{2,1,0:T(8,128)(2,1)S(1)} %get-tuple-element.109.far_hi, ...), custom_call_target="tpu_custom_call" | custom-call | tf_op jit(solution)/shard_map/finish/pallas_call | solution.py:432
  (1 shorter events, 0.0 us)
Async XLA Ops:
  0.6 6.2 %collective-permute-start.1 = (f32[2,80,128]{2,1,0:T(8,128)}, f32[2,80,128]{2,1,0:T(8,128)S(1)}, u32[]{:S(2)}, u32[]{:S(2)}) collective-permute-start(f32[2,80,128]{2,1,0:T(8,128)} %bitcast.8), channel_id=1, source_target_pairs={{0,1},{1,0},{2,3},{3,2},{4,5},{5,4},{6,7},{7,6},{8,9},{9,8},{10,11... | collective-permute-start | bytes 245768 | tf_op jit(solution)/shard_map/ppermute | solution.py:457
  0.7 6.8 %collective-permute-start = (f32[2,80,128]{2,1,0:T(8,128)}, f32[2,80,128]{2,1,0:T(8,128)S(1)}, u32[]{:S(2)}, u32[]{:S(2)}) collective-permute-start(f32[2,80,128]{2,1,0:T(8,128)} %bitcast.9), channel_id=1, source_target_pairs={{0,15},{1,2},{2,1},{3,4},{4,3},{5,6},{6,5},{7,8},{8,7},{9,10},{10,... | collective-permute-start | bytes 245768 | tf_op jit(solution)/shard_map/ppermute | solution.py:458
  5.0 1.8 %copy-start = (f32[1,2,80,128]{3,2,1,0:T(8,128)S(1)}, f32[1,2,80,128]{3,2,1,0:T(8,128)}, u32[]{:S(2)}) copy-start(f32[1,2,80,128]{3,2,1,0:T(8,128)} %param.6) | copy-start | bytes 245764
  8.8 3.9 %collective-permute-start.3 = (f32[2,80,128]{2,1,0:T(8,128)S(1)}, f32[2,80,128]{2,1,0:T(8,128)S(1)}, u32[]{:S(2)}, u32[]{:S(2)}) collective-permute-start(f32[2,80,128]{2,1,0:T(8,128)S(1)} %move.2.own_ref.field_ref), channel_id=1, source_target_pairs={{0,1},{1,0},{2,3},{3,2},{4,5},{5,4},{6,7},{7,6},{8,9},{9,8},{10,11... | collective-permute-start | bytes 245768 | tf_op jit(solution)/shard_map/ppermute | solution.py:466
  8.9 6.1 %collective-permute-start.2 = (f32[2,80,128]{2,1,0:T(8,128)S(1)}, f32[2,80,128]{2,1,0:T(8,128)S(1)}, u32[]{:S(2)}, u32[]{:S(2)}) collective-permute-start(f32[2,80,128]{2,1,0:T(8,128)S(1)} %move.2.own_ref.field_ref), channel_id=1, source_target_pairs={{0,15},{1,2},{2,1},{3,4},{4,3},{5,6},{6,5},{7,8},{8,7},{9,10},{10,... | collective-permute-start | bytes 245768 | tf_op jit(solution)/shard_map/ppermute | solution.py:467
  16.2 15.5 %copy-start.1 = (f32[2,2,80,128]{3,2,1,0:T(8,128)S(1)}, f32[2,2,80,128]{3,2,1,0:T(8,128)}, u32[]{:S(2)}) copy-start(f32[2,2,80,128]{3,2,1,0:T(8,128)} %param.7) | copy-start | bytes 491524
  42.9 3.4 %collective-permute-start.5 = (f32[176,128]{1,0:T(8,128)S(1)}, f32[176,128]{1,0:T(8,128)S(1)}, u32[]{:S(2)}, u32[]{:S(2)}) collective-permute-start(f32[176,128]{1,0:T(8,128)S(1)} %get-tuple-element.84.own_ref), channel_id=1, source_target_pairs={{0,1},{1,0},{2,3},{3,2},{4,5},{5,4},{6,7},{7,6},{8,9},{9,8},{10,11... | collective-permute-start | bytes 270344 | tf_op jit(solution)/shard_map/ppermute | solution.py:485
  43.0 6.3 %collective-permute-start.4 = (f32[176,128]{1,0:T(8,128)S(1)}, f32[176,128]{1,0:T(8,128)S(1)}, u32[]{:S(2)}, u32[]{:S(2)}) collective-permute-start(f32[176,128]{1,0:T(8,128)S(1)} %get-tuple-element.84.own_ref), channel_id=1, source_target_pairs={{0,15},{1,2},{2,1},{3,4},{4,3},{5,6},{6,5},{7,8},{8,7},{9,10},{10,... | collective-permute-start | bytes 270344 | tf_op jit(solution)/shard_map/ppermute | solution.py:486
  44.8 5.1 %collective-permute-start.6 = (f32[16,128]{1,0:T(8,128)S(1)}, f32[16,128]{1,0:T(8,128)S(1)}, u32[]{:S(2)}, u32[]{:S(2)}) collective-permute-start(f32[16,128]{1,0:T(8,128)S(1)} %get-tuple-element.97), channel_id=1, source_target_pairs={{0,5},{1,12},{2,7},{3,14},{4,9},{5,0},{6,11},{7,2},{8,13},{9,4},{1... | collective-permute-start | bytes 24584 | tf_op jit(solution)/shard_map/ppermute | solution.py:490
  45.5 4.4 %collective-permute-start.7 = (f32[16,128]{1,0:T(8,128)S(1)}, f32[16,128]{1,0:T(8,128)S(1)}, u32[]{:S(2)}, u32[]{:S(2)}) collective-permute-start(f32[16,128]{1,0:T(8,128)S(1)} %get-tuple-element.97), channel_id=1, source_target_pairs={{0,11},{1,6},{2,13},{3,8},{4,15},{5,10},{6,1},{7,12},{8,3},{9,14},... | collective-permute-start | bytes 24584 | tf_op jit(solution)/shard_map/ppermute | solution.py:490
  50.5 3.5 %collective-permute-start.9 = (f32[176,128]{1,0:T(8,128)S(1)}, f32[176,128]{1,0:T(8,128)S(1)}, u32[]{:S(2)}, u32[]{:S(2)}) collective-permute-start(f32[176,128]{1,0:T(8,128)S(1)} %get-tuple-element.101.own_ref), channel_id=1, source_target_pairs={{0,1},{1,0},{2,3},{3,2},{4,5},{5,4},{6,7},{7,6},{8,9},{9,8},{10,11... | collective-permute-start | bytes 270344 | tf_op jit(solution)/shard_map/ppermute | solution.py:497
  50.6 6.2 %collective-permute-start.8 = (f32[176,128]{1,0:T(8,128)S(1)}, f32[176,128]{1,0:T(8,128)S(1)}, u32[]{:S(2)}, u32[]{:S(2)}) collective-permute-start(f32[176,128]{1,0:T(8,128)S(1)} %get-tuple-element.101.own_ref), channel_id=1, source_target_pairs={{0,15},{1,2},{2,1},{3,4},{4,3},{5,6},{6,5},{7,8},{8,7},{9,10},{10,... | collective-permute-start | bytes 270344 | tf_op jit(solution)/shard_map/ppermute | solution.py:498
  52.5 5.0 %collective-permute-start.10 = (f32[16,128]{1,0:T(8,128)S(1)}, f32[16,128]{1,0:T(8,128)S(1)}, u32[]{:S(2)}, u32[]{:S(2)}) collective-permute-start(f32[16,128]{1,0:T(8,128)S(1)} %get-tuple-element.111), channel_id=1, source_target_pairs={{0,8},{1,9},{2,10},{3,11},{4,12},{5,13},{6,14},{7,15},{8,0},{9,1},... | collective-permute-start | bytes 24584 | tf_op jit(solution)/shard_map/ppermute | solution.py:499

commit v10 on v8

--- a/solution.py
+++ b/solution.py
@@ -63,8 +63,7 @@
     return product(weights, read(windows, pair * 3 * channels, 9 * channels, 3 * channels))
 
 
-def from_channels(weights, hidden, pair, channels, outer):
-    mixed = product(weights, read(hidden, pair * channels, 3 * channels, channels))
+def combined(mixed, outer):
     width = mixed.shape[1] // 2
     rows = []
     for half in range(2):
@@ -219,14 +218,16 @@
     )(own, beside, bias, w_in)
 
 
-def move_kernel(keep, field_ref, close_hi, close_lo, far_hi, far_lo, out_ref, moved_ref, hid_hi, hid_lo):
+def move_kernel(keep, field_ref, close_hi, close_lo, far_hi, far_lo, out_ref, moved_ref):
     rows, channels, width = field_ref.shape
-    gather_hidden((hid_hi, hid_lo), (close_hi, close_lo), (far_hi, far_lo))
-    moved = from_channels(out_ref[...], (hid_hi, hid_lo), 0, close_hi.shape[1], channels)
-    for row in range(rows):
-        if keep:
-            moved_ref[row] = field_ref[row]
-        moved_ref[rows * keep + row] = field_ref[row] + moved[row]
+
+    def use(moved):
+        for row in range(rows):
+            if keep:
+                moved_ref[row] = field_ref[row]
+            moved_ref[rows * keep + row] = field_ref[row] + moved[row]
+
+    from_sides(out_ref, (close_hi, close_lo), (far_hi, far_lo), channels, use)
 
 
 def move(keep, field, close, far, w_out):
@@ -235,7 +236,6 @@
     return pl.pallas_call(
         functools.partial(move_kernel, keep),
         out_shape=jax.ShapeDtypeStruct(((1 + keep) * rows, channels, width), f32),
-        scratch_shapes=[pltpu.VMEM((4 * hidden, width), bf16)] * 2,
         compiler_params=params,
         name="move",
     )(field, *close, *far, w_out)
@@ -360,25 +360,29 @@
     )(own, beside, slopes, w_out)
 
 
-def gather_hidden(hid, close, far):
-    hidden = close[0].shape[1]
-    even = is_even()
-    for half in range(2):
-        far_at = pl.multiple_of(jnp.where(even, half, 2 + half) * hidden, hidden)
-        close_at = pl.multiple_of(jnp.where(even, 2 + half, half) * hidden, hidden)
-        for ref, far_ref, close_ref in zip(hid, far, close):
-            ref[pl.ds(far_at, hidden), :] = far_ref[half]
-            ref[pl.ds(close_at, hidden), :] = close_ref[half]
+def from_sides(weights_ref, close, far, outer, use):
+    def run(first, second):
+        right = []
+        for one, two in zip(first, second):
+            rows = [one[0], one[1], two[0], two[1]]
+            stacks = [jnp.concatenate(rows[at : at + 3], axis=0) for at in range(2)]
+            right.append(jnp.concatenate(stacks, axis=1))
+        use(combined(product(weights_ref[...], right), outer))
+
+    pl.when(is_even())(lambda: run(far, close))
+    pl.when(jnp.logical_not(is_even()))(lambda: run(close, far))
 
 
 def join_kernel(own_ref, close_hi, close_lo, far_hi, far_lo, inb_ref, added_ref, *rest):
-    *tables, out_ref, known_ref, hid_hi, hid_lo = rest
+    *tables, out_ref, known_ref = rest
     channels = (own_ref.shape[0] - slab_count) // 2
-    gather_hidden((hid_hi, hid_lo), (close_hi, close_lo), (far_hi, far_lo))
-    moved = from_channels(inb_ref[...], (hid_hi, hid_lo), 0, close_hi.shape[1], channels)
-    for row in range(2):
-        part = slice(row * channels, (row + 1) * channels)
-        out_ref[part, :] = own_ref[part, :] + moved[row] + added_ref[part, :]
+
+    def use(moved):
+        for row in range(2):
+            part = slice(row * channels, (row + 1) * channels)
+            out_ref[part, :] = own_ref[part, :] + moved[row] + added_ref[part, :]
+
+    from_sides(inb_ref, (close_hi, close_lo), (far_hi, far_lo), channels, use)
     known = table_of(own_ref, *tables)
     out_ref[2 * channels :, :] = known
     known_ref[...] = known
@@ -392,26 +396,27 @@
             jax.ShapeDtypeStruct(own.shape, f32),
             jax.ShapeDtypeStruct((slab_count, width), f32),
         ],
-        scratch_shapes=[pltpu.VMEM((4 * hidden, width), bf16)] * 2,
         compiler_params=params,
         name="join",
     )(own, *close, *far, w_in, added, *tables)
 
 
 def finish_kernel(count, own_ref, close_hi, close_lo, far_hi, far_lo, inb_ref, *rest):
-    *tables, out_hbm, loss_hbm, out_ref, loss_ref, hid_hi, hid_lo, done = rest
+    *tables, out_hbm, loss_hbm, out_ref, loss_ref, done = rest
     channels = (own_ref.shape[0] - slab_count) // 2
     total = jnp.sum(table_of(own_ref, *tables), axis=0, keepdims=True)
     loss_ref[...] = jnp.sum(total, axis=1, keepdims=True) / count
     copies = [pltpu.make_async_copy(loss_ref, loss_hbm, done.at[0])]
     copies[0].start()
-    gather_hidden((hid_hi, hid_lo), (close_hi, close_lo), (far_hi, far_lo))
-    moved = from_channels(inb_ref[...], (hid_hi, hid_lo), 0, close_hi.shape[1], channels)
-    for row in range(2):
-        part = pl.ds(row * channels, channels)
-        out_ref[part, :] = own_ref[part, :] + moved[row]
-        copies.append(pltpu.make_async_copy(out_ref.at[part, :], out_hbm.at[part, :], done.at[1 + row]))
-        copies[-1].start()
+
+    def use(moved):
+        for row in range(2):
+            part = slice(row * channels, (row + 1) * channels)
+            out_ref[part, :] = own_ref[part, :] + moved[row]
+
+    from_sides(inb_ref, (close_hi, close_lo), (far_hi, far_lo), channels, use)
+    copies.append(pltpu.make_async_copy(out_ref, out_hbm, done.at[1]))
+    copies[-1].start()
     for copy in copies:
         copy.wait()
 
@@ -429,8 +434,7 @@
         in_specs=[vmem] * (6 + len(tables)),
         out_specs=[pl.BlockSpec(memory_space=pltpu.HBM)] * 2,
         scratch_shapes=[pltpu.VMEM((lines, width), f32), pltpu.VMEM((1, 1), f32)]
-        + [pltpu.VMEM((4 * hidden, width), bf16)] * 2
-        + [pltpu.SemaphoreType.DMA((3,))],
+        + [pltpu.SemaphoreType.DMA((2,))],
         compiler_params=params,
         name="finish",
     )(own, *close, *far, w_in, *tables)

time: 58.9 us -> 58.9 us (level)
  no operation moved by 1% of the time
where the time goes in v10:
time: 58.9 us; the launch traced here: 58.7 us
  blocking collectives  26.4 us (45%)
  starting transfers between devices  14.4 us (24%)
  Pallas kernels  11.5 us (20%)
  waiting for transfers between devices  5.53 us (9%)
  between operations  0.84 us (1%)
    all_to_all x1, blocking collectives, on_device(): lax.all_to_all(fields.reshape(members, height, width), MEMBER, split_axis...  15.5 us
    all_to_all x1, blocking collectives, on_device(): lax.all_to_all(grads, MEMBER, split_axis=0, concat_axis=0, tiled=True)  10.9 us
    ppermute x1, starting transfers between devices, on_device(): crossed = lax.ppermute(own, LAT, across)  4.3 us
    ppermute x2, waiting for transfers between devices, on_device(): crossed = lax.ppermute(message, LAT, across)  3.9 us
    ppermute x1, starting transfers between devices, on_device(): crossed = lax.ppermute(field, LAT, across)  3.76 us
    ppermute x2, starting transfers between devices, on_device(): crossed = lax.ppermute(message, LAT, across)  3.73 us
    pallas_call x4, Pallas kernels, forward_side(): pl.pallas_call(functools.partial(forward_side_kernel, near_side), out_sha...  2.71 us
    pallas_call x4, Pallas kernels, backward_side(): pl.pallas_call(functools.partial(backward_side_kernel, step, near_side),...  2.5 us
  transfers between devices with their start and end apart: 11, of which 3 were waited for; matrix products, arithmetic and copies ran while one was open for 0% of the time, Pallas kernels for 12%

profile of v10, /device:TPU:0, one launch (start us, length us, event | category | flops | bytes accessed | tf_op | source)
XLA Modules:
  0.0 58.7 jit_solution(12905939335760800386)
XLA Ops:
  0.6 0.1 collective-permute-start.1
  0.7 4.3 %collective-permute-start = (f32[2,80,128]{2,1,0:T(8,128)}, f32[2,80,128]{2,1,0:T(8,128)S(1)}, u32[]{:S(2)}, u32[]{:S(2)}) collective-permute-start(f32[2,80,128]{2,1,0:T(8,128)} %bitcast.9), channel_id=1, source_target_pairs={{0,15},{1,2},{2,1},{3,4},{4,3},{5,6},{6,5},{7,8},{8,7},{9,10},{10,... | collective-permute-start | bytes 245768 | tf_op jit(solution)/shard_map/ppermute | solution.py:453
  5.0 0.0 copy-start
  5.0 1.8 %prepare.1 = (bf16[512,720]{1,0:T(8,128)(2,1)S(1)}, bf16[480,768]{1,0:T(8,128)(2,1)S(1)}, f32[256,128]{1,0:T(8,128)S(1)}, f32[16,128]{1,0:T(8,128)S(1)}, f32[720,256]{1,0:T(8,128)S(1)}, /*index=5*/f32[80,2304]{1,0:T(8,128)S(1)}) custom-call(f32[720,256]{1,0:T(8,128)} %bitcast.15, f32[80,2304]{1,0:T(8,128)} %wout_hbm.1, f32[1,256]{1,0:T(1,128)} %bitcast.16, ...), custom_call_target="tpu_custom_call" | custom-call | tf_op jit(solution)/shard_map/prepare/pallas_call | solution.py:122
  6.8 0.0 collective-permute-done.1.beside_ref
  6.8 0.0 copy-done
  6.8 0.7 %forward_near.2 = (f32[256,256]{1,0:T(8,128)S(1)}, bf16[2,256,128]{2,1,0:T(8,128)(2,1)S(1)}, bf16[2,256,128]{2,1,0:T(8,128)(2,1)S(1)}) custom-call(f32[2,80,128]{2,1,0:T(8,128)S(1)} %bitcast.10, f32[2,80,128]{2,1,0:T(8,128)S(1)} %collective-permute-done.1.beside_ref, f32[256,128]{1,0:T(8,128)S(1)} %get-tuple-element.51.bias_ref, ...), custom_call_target="tpu_custom_call" | custom-call | tf_op jit(solution)/shard_map/forward_near/pallas_call | solution.py:211
  7.5 0.0 collective-permute-done.beside_ref
  7.5 0.7 %forward_across.2 = (f32[256,256]{1,0:T(8,128)S(1)}, bf16[2,256,128]{2,1,0:T(8,128)(2,1)S(1)}, bf16[2,256,128]{2,1,0:T(8,128)(2,1)S(1)}) custom-call(f32[2,80,128]{2,1,0:T(8,128)S(1)} %bitcast.11, f32[2,80,128]{2,1,0:T(8,128)S(1)} %collective-permute-done.beside_ref, f32[256,128]{1,0:T(8,128)S(1)} %get-tuple-element.51.bias_ref, ...), custom_call_target="tpu_custom_call" | custom-call | tf_op jit(solution)/shard_map/forward_across/pallas_call | solution.py:211
  8.2 0.6 move.2.own_ref.field_ref
  8.8 0.1 collective-permute-start.3
  8.9 3.8 %collective-permute-start.2 = (f32[2,80,128]{2,1,0:T(8,128)S(1)}, f32[2,80,128]{2,1,0:T(8,128)S(1)}, u32[]{:S(2)}, u32[]{:S(2)}) collective-permute-start(f32[2,80,128]{2,1,0:T(8,128)S(1)} %move.2.own_ref.field_ref), channel_id=1, source_target_pairs={{0,15},{1,2},{2,1},{3,4},{4,3},{5,6},{6,5},{7,8},{8,7},{9,10},{10,... | collective-permute-start | bytes 245768 | tf_op jit(solution)/shard_map/ppermute | solution.py:462
  12.6 0.0 collective-permute-done.3.beside_ref
  12.6 0.7 %forward_near.3 = (f32[256,256]{1,0:T(8,128)S(1)}, bf16[2,256,128]{2,1,0:T(8,128)(2,1)S(1)}, bf16[2,256,128]{2,1,0:T(8,128)(2,1)S(1)}) custom-call(f32[2,80,128]{2,1,0:T(8,128)S(1)} %move.2.own_ref.field_ref, f32[2,80,128]{2,1,0:T(8,128)S(1)} %collective-permute-done.3.beside_ref, f32[256,128]{1,0:T(8,128)S(1)} %get-tuple-element.51.bias_ref, ...), custom_call_target="tpu_custom_call" | custom-call | tf_op jit(solution)/shard_map/forward_near/pallas_call | solution.py:211
  13.3 1.6 %collective-permute-done.2.beside_ref = f32[2,80,128]{2,1,0:T(8,128)S(1)} collective-permute-done((f32[2,80,128]{2,1,0:T(8,128)S(1)}, f32[2,80,128]{2,1,0:T(8,128)S(1)}, u32[]{:S(2)}, u32[]{:S(2)}) %collective-permute-start.2) | collective-permute-done | bytes 81952 | tf_op jit(solution)/shard_map/ppermute | solution.py:462
  14.9 0.7 %forward_across.3 = (f32[256,256]{1,0:T(8,128)S(1)}, bf16[2,256,128]{2,1,0:T(8,128)(2,1)S(1)}, bf16[2,256,128]{2,1,0:T(8,128)(2,1)S(1)}) custom-call(f32[2,80,128]{2,1,0:T(8,128)S(1)} %move.2.own_ref.field_ref, f32[2,80,128]{2,1,0:T(8,128)S(1)} %collective-permute-done.2.beside_ref, f32[256,128]{1,0:T(8,128)S(1)} %get-tuple-element.51.bias_ref, ...), custom_call_target="tpu_custom_call" | custom-call | tf_op jit(solution)/shard_map/forward_across/pallas_call | solution.py:211
  15.6 0.6 move.3
  16.2 0.0 copy-start.1
  16.2 15.5 %all_to_all.10.fields_ref = f32[8,40,128]{2,1,0:T(8,128)S(1)} all-to-all(f32[8,40,128]{2,1,0:T(8,128)S(1)} %bitcast.13), channel_id=1, replica_groups=mesh['member_0'=4,'member_1'=2,'lat_0'=2,'lat_1'=4,'lat_2'=2] {'member_0..., dimensions={0} | all-to-all | bytes 327680 | tf_op jit(solution)/shard_map/all_to_all | solution.py:469
  31.6 0.0 copy-done.1
  31.6 0.2 crps.1
  31.9 10.9 %all_to_all.11.grads_ref = f32[8,48,128]{2,1,0:T(8,128)S(1)} all-to-all(f32[8,48,128]{2,1,0:T(8,128)S(1)} %crps.1), channel_id=1, replica_groups=mesh['member_0'=4,'member_1'=2,'lat_0'=2,'lat_1'=4,'lat_2'=2] {'member_0..., dimensions={0} | all-to-all | bytes 393216 | tf_op jit(solution)/shard_map/all_to_all | solution.py:473
  42.8 0.1 collective-permute-start.5
  42.9 1.9 %collective-permute-start.4 = (f32[176,128]{1,0:T(8,128)S(1)}, f32[176,128]{1,0:T(8,128)S(1)}, u32[]{:S(2)}, u32[]{:S(2)}) collective-permute-start(f32[176,128]{1,0:T(8,128)S(1)} %get-tuple-element.68.own_ref), channel_id=1, source_target_pairs={{0,15},{1,2},{2,1},{3,4},{4,3},{5,6},{6,5},{7,8},{8,7},{9,10},{10,... | collective-permute-start | bytes 270344 | tf_op jit(solution)/shard_map/ppermute | solution.py:479
  44.8 0.7 %collective-permute-start.6 = (f32[16,128]{1,0:T(8,128)S(1)}, f32[16,128]{1,0:T(8,128)S(1)}, u32[]{:S(2)}, u32[]{:S(2)}) collective-permute-start(f32[16,128]{1,0:T(8,128)S(1)} %get-tuple-element.86), channel_id=1, source_target_pairs={{0,5},{1,12},{2,7},{3,14},{4,9},{5,0},{6,11},{7,2},{8,13},{9,4},{1... | collective-permute-start | bytes 24584 | tf_op jit(solution)/shard_map/ppermute | solution.py:483
  45.5 0.4 collective-permute-start.7
  45.9 1.3 %prepare_back.1 = (bf16[512,720]{1,0:T(8,128)(2,1)S(1)}, bf16[480,768]{1,0:T(8,128)(2,1)S(1)}, f32[2,2,256,256]{3,2,1,0:T(8,128)S(1)}) custom-call(f32[720,256]{1,0:T(8,128)S(1)} %get-tuple-element.69.win_ref, f32[80,2304]{1,0:T(8,128)S(1)} %get-tuple-element.70.wout_ref, f32[256,256]{1,0:T(8,128)S(1)} %get-tuple-element.71.rest_0_, ...), custom_call_target="tpu_custom_call" | custom-call | tf_op jit(solution)/shard_map/prepare_back/pallas_call | solution.py:165
  47.3 0.0 collective-permute-done.5.beside_ref.rest_0_
  47.3 0.6 %backward_near.2 = (bf16[2,256,128]{2,1,0:T(8,128)(2,1)S(1)}, bf16[2,256,128]{2,1,0:T(8,128)(2,1)S(1)}) custom-call(f32[176,128]{1,0:T(8,128)S(1)} %get-tuple-element.68.own_ref, f32[176,128]{1,0:T(8,128)S(1)} %collective-permute-done.5.beside_ref.rest_0_, f32[2,2,256,256]{3,2,1,0:T(8,128)S(1)} %get-tuple-element.75.slope_ref, ...), custom_call_target="tpu_custom_call" | custom-call | tf_op jit(solution)/shard_map/backward_near/pallas_call | solution.py:354
  47.9 1.4 %collective-permute-done.4.beside_ref.rest_1_ = f32[176,128]{1,0:T(8,128)S(1)} collective-permute-done((f32[176,128]{1,0:T(8,128)S(1)}, f32[176,128]{1,0:T(8,128)S(1)}, u32[]{:S(2)}, u32[]{:S(2)}) %collective-permute-start.4) | collective-permute-done | bytes 90144 | tf_op jit(solution)/shard_map/ppermute | solution.py:479
  49.3 0.6 %backward_across.2 = (bf16[2,256,128]{2,1,0:T(8,128)(2,1)S(1)}, bf16[2,256,128]{2,1,0:T(8,128)(2,1)S(1)}) custom-call(f32[176,128]{1,0:T(8,128)S(1)} %get-tuple-element.68.own_ref, f32[176,128]{1,0:T(8,128)S(1)} %collective-permute-done.4.beside_ref.rest_1_, f32[2,2,256,256]{3,2,1,0:T(8,128)S(1)} %get-tuple-element.75.slope_ref, ...), custom_call_target="tpu_custom_call" | custom-call | tf_op jit(solution)/shard_map/backward_across/pallas_call | solution.py:354
  49.9 0.0 collective-permute-done.6.rest_2_
  49.9 0.0 collective-permute-done.7.rest_3_
  49.9 0.6 join.1
  50.5 0.1 collective-permute-start.9
  50.6 1.9 %collective-permute-start.8 = (f32[176,128]{1,0:T(8,128)S(1)}, f32[176,128]{1,0:T(8,128)S(1)}, u32[]{:S(2)}, u32[]{:S(2)}) collective-permute-start(f32[176,128]{1,0:T(8,128)S(1)} %get-tuple-element.87.own_ref), channel_id=1, source_target_pairs={{0,15},{1,2},{2,1},{3,4},{4,3},{5,6},{6,5},{7,8},{8,7},{9,10},{10,... | collective-permute-start | bytes 270344 | tf_op jit(solution)/shard_map/ppermute | solution.py:491
  52.4 1.2 %collective-permute-start.10 = (f32[16,128]{1,0:T(8,128)S(1)}, f32[16,128]{1,0:T(8,128)S(1)}, u32[]{:S(2)}, u32[]{:S(2)}) collective-permute-start(f32[16,128]{1,0:T(8,128)S(1)} %get-tuple-element.95), channel_id=1, source_target_pairs={{0,8},{1,9},{2,10},{3,11},{4,12},{5,13},{6,14},{7,15},{8,0},{9,1},... | collective-permute-start | bytes 24584 | tf_op jit(solution)/shard_map/ppermute | solution.py:492
  53.6 0.0 collective-permute-done.9.beside_ref.rest_0_
  53.6 0.6 %backward_near.3 = (bf16[2,256,128]{2,1,0:T(8,128)(2,1)S(1)}, bf16[2,256,128]{2,1,0:T(8,128)(2,1)S(1)}) custom-call(f32[176,128]{1,0:T(8,128)S(1)} %get-tuple-element.87.own_ref, f32[176,128]{1,0:T(8,128)S(1)} %collective-permute-done.9.beside_ref.rest_0_, f32[2,2,256,256]{3,2,1,0:T(8,128)S(1)} %get-tuple-element.75.slope_ref, ...), custom_call_target="tpu_custom_call" | custom-call | tf_op jit(solution)/shard_map/backward_near/pallas_call | solution.py:354
  54.2 2.5 %collective-permute-done.8.beside_ref.rest_1_ = f32[176,128]{1,0:T(8,128)S(1)} collective-permute-done((f32[176,128]{1,0:T(8,128)S(1)}, f32[176,128]{1,0:T(8,128)S(1)}, u32[]{:S(2)}, u32[]{:S(2)}) %collective-permute-start.8) | collective-permute-done | bytes 90144 | tf_op jit(solution)/shard_map/ppermute | solution.py:491
  56.8 0.6 %backward_across.3 = (bf16[2,256,128]{2,1,0:T(8,128)(2,1)S(1)}, bf16[2,256,128]{2,1,0:T(8,128)(2,1)S(1)}) custom-call(f32[176,128]{1,0:T(8,128)S(1)} %get-tuple-element.87.own_ref, f32[176,128]{1,0:T(8,128)S(1)} %collective-permute-done.8.beside_ref.rest_1_, f32[2,2,256,256]{3,2,1,0:T(8,128)S(1)} %get-tuple-element.75.slope_ref, ...), custom_call_target="tpu_custom_call" | custom-call | tf_op jit(solution)/shard_map/backward_across/pallas_call | solution.py:354
  57.4 0.0 collective-permute-done.10.rest_2_
  57.4 1.3 %finish.1 = (f32[160,128]{1,0:T(8,128)}, f32[1,1]{1,0:T(1,128)}) custom-call(f32[176,128]{1,0:T(8,128)S(1)} %get-tuple-element.87.own_ref, bf16[2,256,128]{2,1,0:T(8,128)(2,1)S(1)} %get-tuple-element.90.close_hi, bf16[2,256,128]{2,1,0:T(8,128)(2,1)S(1)} %get-tuple-element.91.close_lo, bf16[2,256,128]{2,1,0:T(8,128)(2,1)S(1)} %get-tuple-element.93.far_hi, ...), custom_call_target="tpu_custom_call" | custom-call | tf_op jit(solution)/shard_map/finish/pallas_call | solution.py:428
  (1 shorter events, 0.0 us)
Async XLA Ops:
  0.6 6.2 %collective-permute-start.1 = (f32[2,80,128]{2,1,0:T(8,128)}, f32[2,80,128]{2,1,0:T(8,128)S(1)}, u32[]{:S(2)}, u32[]{:S(2)}) collective-permute-start(f32[2,80,128]{2,1,0:T(8,128)} %bitcast.8), channel_id=1, source_target_pairs={{0,1},{1,0},{2,3},{3,2},{4,5},{5,4},{6,7},{7,6},{8,9},{9,8},{10,11... | collective-permute-start | bytes 245768 | tf_op jit(solution)/shard_map/ppermute | solution.py:452
  0.7 6.8 %collective-permute-start = (f32[2,80,128]{2,1,0:T(8,128)}, f32[2,80,128]{2,1,0:T(8,128)S(1)}, u32[]{:S(2)}, u32[]{:S(2)}) collective-permute-start(f32[2,80,128]{2,1,0:T(8,128)} %bitcast.9), channel_id=1, source_target_pairs={{0,15},{1,2},{2,1},{3,4},{4,3},{5,6},{6,5},{7,8},{8,7},{9,10},{10,... | collective-permute-start | bytes 245768 | tf_op jit(solution)/shard_map/ppermute | solution.py:453
  5.0 1.8 %copy-start = (f32[1,2,80,128]{3,2,1,0:T(8,128)S(1)}, f32[1,2,80,128]{3,2,1,0:T(8,128)}, u32[]{:S(2)}) copy-start(f32[1,2,80,128]{3,2,1,0:T(8,128)} %param.6) | copy-start | bytes 245764
  8.8 3.9 %collective-permute-start.3 = (f32[2,80,128]{2,1,0:T(8,128)S(1)}, f32[2,80,128]{2,1,0:T(8,128)S(1)}, u32[]{:S(2)}, u32[]{:S(2)}) collective-permute-start(f32[2,80,128]{2,1,0:T(8,128)S(1)} %move.2.own_ref.field_ref), channel_id=1, source_target_pairs={{0,1},{1,0},{2,3},{3,2},{4,5},{5,4},{6,7},{7,6},{8,9},{9,8},{10,11... | collective-permute-start | bytes 245768 | tf_op jit(solution)/shard_map/ppermute | solution.py:461
  8.9 6.1 %collective-permute-start.2 = (f32[2,80,128]{2,1,0:T(8,128)S(1)}, f32[2,80,128]{2,1,0:T(8,128)S(1)}, u32[]{:S(2)}, u32[]{:S(2)}) collective-permute-start(f32[2,80,128]{2,1,0:T(8,128)S(1)} %move.2.own_ref.field_ref), channel_id=1, source_target_pairs={{0,15},{1,2},{2,1},{3,4},{4,3},{5,6},{6,5},{7,8},{8,7},{9,10},{10,... | collective-permute-start | bytes 245768 | tf_op jit(solution)/shard_map/ppermute | solution.py:462
  16.2 15.5 %copy-start.1 = (f32[2,2,80,128]{3,2,1,0:T(8,128)S(1)}, f32[2,2,80,128]{3,2,1,0:T(8,128)}, u32[]{:S(2)}) copy-start(f32[2,2,80,128]{3,2,1,0:T(8,128)} %param.7) | copy-start | bytes 491524
  42.8 4.4 %collective-permute-start.5 = (f32[176,128]{1,0:T(8,128)S(1)}, f32[176,128]{1,0:T(8,128)S(1)}, u32[]{:S(2)}, u32[]{:S(2)}) collective-permute-start(f32[176,128]{1,0:T(8,128)S(1)} %get-tuple-element.68.own_ref), channel_id=1, source_target_pairs={{0,1},{1,0},{2,3},{3,2},{4,5},{5,4},{6,7},{7,6},{8,9},{9,8},{10,11... | collective-permute-start | bytes 270344 | tf_op jit(solution)/shard_map/ppermute | solution.py:478
  42.9 6.3 %collective-permute-start.4 = (f32[176,128]{1,0:T(8,128)S(1)}, f32[176,128]{1,0:T(8,128)S(1)}, u32[]{:S(2)}, u32[]{:S(2)}) collective-permute-start(f32[176,128]{1,0:T(8,128)S(1)} %get-tuple-element.68.own_ref), channel_id=1, source_target_pairs={{0,15},{1,2},{2,1},{3,4},{4,3},{5,6},{6,5},{7,8},{8,7},{9,10},{10,... | collective-permute-start | bytes 270344 | tf_op jit(solution)/shard_map/ppermute | solution.py:479
  44.8 5.1 %collective-permute-start.6 = (f32[16,128]{1,0:T(8,128)S(1)}, f32[16,128]{1,0:T(8,128)S(1)}, u32[]{:S(2)}, u32[]{:S(2)}) collective-permute-start(f32[16,128]{1,0:T(8,128)S(1)} %get-tuple-element.86), channel_id=1, source_target_pairs={{0,5},{1,12},{2,7},{3,14},{4,9},{5,0},{6,11},{7,2},{8,13},{9,4},{1... | collective-permute-start | bytes 24584 | tf_op jit(solution)/shard_map/ppermute | solution.py:483
  45.5 4.4 %collective-permute-start.7 = (f32[16,128]{1,0:T(8,128)S(1)}, f32[16,128]{1,0:T(8,128)S(1)}, u32[]{:S(2)}, u32[]{:S(2)}) collective-permute-start(f32[16,128]{1,0:T(8,128)S(1)} %get-tuple-element.86), channel_id=1, source_target_pairs={{0,11},{1,6},{2,13},{3,8},{4,15},{5,10},{6,1},{7,12},{8,3},{9,14},... | collective-permute-start | bytes 24584 | tf_op jit(solution)/shard_map/ppermute | solution.py:483
  50.5 3.1 %collective-permute-start.9 = (f32[176,128]{1,0:T(8,128)S(1)}, f32[176,128]{1,0:T(8,128)S(1)}, u32[]{:S(2)}, u32[]{:S(2)}) collective-permute-start(f32[176,128]{1,0:T(8,128)S(1)} %get-tuple-element.87.own_ref), channel_id=1, source_target_pairs={{0,1},{1,0},{2,3},{3,2},{4,5},{5,4},{6,7},{7,6},{8,9},{9,8},{10,11... | collective-permute-start | bytes 270344 | tf_op jit(solution)/shard_map/ppermute | solution.py:490
  50.6 6.2 %collective-permute-start.8 = (f32[176,128]{1,0:T(8,128)S(1)}, f32[176,128]{1,0:T(8,128)S(1)}, u32[]{:S(2)}, u32[]{:S(2)}) collective-permute-start(f32[176,128]{1,0:T(8,128)S(1)} %get-tuple-element.87.own_ref), channel_id=1, source_target_pairs={{0,15},{1,2},{2,1},{3,4},{4,3},{5,6},{6,5},{7,8},{8,7},{9,10},{10,... | collective-permute-start | bytes 270344 | tf_op jit(solution)/shard_map/ppermute | solution.py:491
  52.4 5.0 %collective-permute-start.10 = (f32[16,128]{1,0:T(8,128)S(1)}, f32[16,128]{1,0:T(8,128)S(1)}, u32[]{:S(2)}, u32[]{:S(2)}) collective-permute-start(f32[16,128]{1,0:T(8,128)S(1)} %get-tuple-element.95), channel_id=1, source_target_pairs={{0,8},{1,9},{2,10},{3,11},{4,12},{5,13},{6,14},{7,15},{8,0},{9,1},... | collective-permute-start | bytes 24584 | tf_op jit(solution)/shard_map/ppermute | solution.py:492

commit v11 on v9

--- a/solution.py
+++ b/solution.py
@@ -162,21 +162,22 @@
 
 def slopes_kernel(*refs):
     *before_refs, slope_ref = refs
-    for side, before_ref in enumerate(before_refs):
+    for side in range(2):
         below = is_even() if side == 0 else jnp.logical_not(is_even())
         first = jnp.where(below, 0, -2)
-        slope = gelu_slope(before_ref[...])
-        width = slope.shape[1] // 2
-        for half in range(2):
-            part = slope[:, half * width : (half + 1) * width]
-            part = jnp.where(inside(first + 1 + half), part, 0.0)
-            slope_ref[side, :, half * width : (half + 1) * width] = part
+        for step, before_ref in enumerate(before_refs[side::2]):
+            slope = gelu_slope(before_ref[...])
+            width = slope.shape[1] // 2
+            for half in range(2):
+                part = slope[:, half * width : (half + 1) * width]
+                part = jnp.where(inside(first + 1 + half), part, 0.0)
+                slope_ref[step, side, :, half * width : (half + 1) * width] = part
 
 
 def slopes_of(*before):
     return pl.pallas_call(
         slopes_kernel,
-        out_shape=jax.ShapeDtypeStruct((2, *before[0].shape), f32),
+        out_shape=jax.ShapeDtypeStruct((2, 2, *before[0].shape), f32),
         compiler_params=params,
         name="slopes",
     )(*before)
@@ -345,7 +346,7 @@
         return lambda row: ref[row * channels : (row + 1) * channels, :]
 
     side_windows(near_side, rows_of(own_ref), rows_of(beside_ref), wide)
-    grads = to_channels(weight_ref[...], wide, 0, channels) * slope_ref[0 if near_side else 1]
+    grads = to_channels(weight_ref[...], wide, 0, channels) * slope_ref[step, 0 if near_side else 1]
     return [split(grads[:, half * width : (half + 1) * width]) for half in range(2)]
 
 
@@ -479,7 +480,7 @@
     )
     grads = crps(lat_weights, chunks, targets.reshape(members, height, width))
     grads = lax.all_to_all(grads, MEMBER, split_axis=0, concat_axis=0, tiled=True)
-    slopes = slopes_of(*before_second)
+    slopes = slopes_of(*before_first, *before_second)
     first_grads, message, known = collect(grads)
 
     beside = lax.ppermute(message, LAT, near)
@@ -497,8 +498,6 @@
     beside = lax.ppermute(message, LAT, near)
     crossed = lax.ppermute(message, LAT, across)
     distant_tables = [lax.ppermute(known, LAT, pairs) for pairs in (opposite,)]
-    message, before_first = lax.optimization_barrier((message, before_first))
-    slopes = slopes_of(*before_first)
     close = backward_side(0, True, message, beside, slopes, w_out_back)
     crossed, close = lax.optimization_barrier((crossed, close))
     distant = backward_side(0, False, message, crossed, slopes, w_out_back)

time: 58.9 us -> 58.9 us (level)
  no operation moved by 1% of the time
where the time goes in v11:
time: 58.9 us; the launch traced here: 58.7 us
  blocking collectives  26.4 us (45%)
  starting transfers between devices  14.4 us (24%)
  Pallas kernels  11.2 us (19%)
  waiting for transfers between devices  5.87 us (10%)
  between operations  0.84 us (1%)
    all_to_all x1, blocking collectives, on_device(): lax.all_to_all(fields.reshape(members, height, width), MEMBER, split_axis...  15.5 us
    all_to_all x1, blocking collectives, on_device(): lax.all_to_all(grads, MEMBER, split_axis=0, concat_axis=0, tiled=True)  10.9 us
    ppermute x2, waiting for transfers between devices, on_device(): crossed = lax.ppermute(message, LAT, across)  4.58 us
    ppermute x1, starting transfers between devices, on_device(): crossed = lax.ppermute(own, LAT, across)  4.3 us
    ppermute x1, starting transfers between devices, on_device(): crossed = lax.ppermute(field, LAT, across)  3.76 us
    ppermute x2, starting transfers between devices, on_device(): crossed = lax.ppermute(message, LAT, across)  3.76 us
    pallas_call x4, Pallas kernels, forward_side(): pl.pallas_call(functools.partial(forward_side_kernel, near_side), out_sha...  2.71 us
    pallas_call x4, Pallas kernels, backward_side(): pl.pallas_call(functools.partial(backward_side_kernel, step, near_side),...  2.5 us
  transfers between devices with their start and end apart: 11, of which 3 were waited for; matrix products, arithmetic and copies ran while one was open for 0% of the time, Pallas kernels for 11%

profile of v11, /device:TPU:0, one launch (start us, length us, event | category | flops | bytes accessed | tf_op | source)
XLA Modules:
  0.0 58.7 jit_solution(4335683407800905515)
XLA Ops:
  0.6 0.1 collective-permute-start.1
  0.7 4.3 %collective-permute-start = (f32[2,80,128]{2,1,0:T(8,128)}, f32[2,80,128]{2,1,0:T(8,128)S(1)}, u32[]{:S(2)}, u32[]{:S(2)}) collective-permute-start(f32[2,80,128]{2,1,0:T(8,128)} %bitcast.9), channel_id=1, source_target_pairs={{0,15},{1,2},{2,1},{3,4},{4,3},{5,6},{6,5},{7,8},{8,7},{9,10},{10,... | collective-permute-start | bytes 245768 | tf_op jit(solution)/shard_map/ppermute | solution.py:459
  5.0 0.0 copy-start
  5.0 1.8 %prepare.1 = (bf16[512,720]{1,0:T(8,128)(2,1)S(1)}, bf16[480,768]{1,0:T(8,128)(2,1)S(1)}, f32[256,128]{1,0:T(8,128)S(1)}, f32[16,128]{1,0:T(8,128)S(1)}, f32[720,256]{1,0:T(8,128)S(1)}, /*index=5*/f32[80,2304]{1,0:T(8,128)S(1)}) custom-call(f32[720,256]{1,0:T(8,128)} %bitcast.15, f32[80,2304]{1,0:T(8,128)} %wout_hbm.1, f32[1,256]{1,0:T(1,128)} %bitcast.16, ...), custom_call_target="tpu_custom_call" | custom-call | tf_op jit(solution)/shard_map/prepare/pallas_call | solution.py:123
  6.8 0.0 collective-permute-done.1.beside_ref
  6.8 0.0 copy-done
  6.8 0.7 %forward_near.2 = (f32[256,256]{1,0:T(8,128)S(1)}, bf16[2,256,128]{2,1,0:T(8,128)(2,1)S(1)}, bf16[2,256,128]{2,1,0:T(8,128)(2,1)S(1)}) custom-call(f32[2,80,128]{2,1,0:T(8,128)S(1)} %bitcast.10, f32[2,80,128]{2,1,0:T(8,128)S(1)} %collective-permute-done.1.beside_ref, f32[256,128]{1,0:T(8,128)S(1)} %get-tuple-element.56.bias_ref, ...), custom_call_target="tpu_custom_call" | custom-call | tf_op jit(solution)/shard_map/forward_near/pallas_call | solution.py:222
  7.5 0.0 collective-permute-done.beside_ref
  7.5 0.7 %forward_across.2 = (f32[256,256]{1,0:T(8,128)S(1)}, bf16[2,256,128]{2,1,0:T(8,128)(2,1)S(1)}, bf16[2,256,128]{2,1,0:T(8,128)(2,1)S(1)}) custom-call(f32[2,80,128]{2,1,0:T(8,128)S(1)} %bitcast.11, f32[2,80,128]{2,1,0:T(8,128)S(1)} %collective-permute-done.beside_ref, f32[256,128]{1,0:T(8,128)S(1)} %get-tuple-element.56.bias_ref, ...), custom_call_target="tpu_custom_call" | custom-call | tf_op jit(solution)/shard_map/forward_across/pallas_call | solution.py:222
  8.2 0.6 move.2.own_ref.field_ref
  8.8 0.1 collective-permute-start.3
  8.9 3.8 %collective-permute-start.2 = (f32[2,80,128]{2,1,0:T(8,128)S(1)}, f32[2,80,128]{2,1,0:T(8,128)S(1)}, u32[]{:S(2)}, u32[]{:S(2)}) collective-permute-start(f32[2,80,128]{2,1,0:T(8,128)S(1)} %move.2.own_ref.field_ref), channel_id=1, source_target_pairs={{0,15},{1,2},{2,1},{3,4},{4,3},{5,6},{6,5},{7,8},{8,7},{9,10},{10,... | collective-permute-start | bytes 245768 | tf_op jit(solution)/shard_map/ppermute | solution.py:468
  12.7 0.0 collective-permute-done.3.beside_ref
  12.7 0.7 %forward_near.3 = (f32[256,256]{1,0:T(8,128)S(1)}, bf16[2,256,128]{2,1,0:T(8,128)(2,1)S(1)}, bf16[2,256,128]{2,1,0:T(8,128)(2,1)S(1)}) custom-call(f32[2,80,128]{2,1,0:T(8,128)S(1)} %move.2.own_ref.field_ref, f32[2,80,128]{2,1,0:T(8,128)S(1)} %collective-permute-done.3.beside_ref, f32[256,128]{1,0:T(8,128)S(1)} %get-tuple-element.56.bias_ref, ...), custom_call_target="tpu_custom_call" | custom-call | tf_op jit(solution)/shard_map/forward_near/pallas_call | solution.py:222
  13.3 0.3 prepare_back.1
  13.7 1.3 %collective-permute-done.2.beside_ref = f32[2,80,128]{2,1,0:T(8,128)S(1)} collective-permute-done((f32[2,80,128]{2,1,0:T(8,128)S(1)}, f32[2,80,128]{2,1,0:T(8,128)S(1)}, u32[]{:S(2)}, u32[]{:S(2)}) %collective-permute-start.2) | collective-permute-done | bytes 81952 | tf_op jit(solution)/shard_map/ppermute | solution.py:468
  14.9 0.7 %forward_across.3 = (f32[256,256]{1,0:T(8,128)S(1)}, bf16[2,256,128]{2,1,0:T(8,128)(2,1)S(1)}, bf16[2,256,128]{2,1,0:T(8,128)(2,1)S(1)}) custom-call(f32[2,80,128]{2,1,0:T(8,128)S(1)} %move.2.own_ref.field_ref, f32[2,80,128]{2,1,0:T(8,128)S(1)} %collective-permute-done.2.beside_ref, f32[256,128]{1,0:T(8,128)S(1)} %get-tuple-element.56.bias_ref, ...), custom_call_target="tpu_custom_call" | custom-call | tf_op jit(solution)/shard_map/forward_across/pallas_call | solution.py:222
  15.6 0.6 move.3
  16.2 0.0 copy-start.1
  16.2 15.5 %all_to_all.10.fields_ref = f32[8,40,128]{2,1,0:T(8,128)S(1)} all-to-all(f32[8,40,128]{2,1,0:T(8,128)S(1)} %bitcast.13), channel_id=1, replica_groups=mesh['member_0'=4,'member_1'=2,'lat_0'=2,'lat_1'=4,'lat_2'=2] {'member_0..., dimensions={0} | all-to-all | bytes 327680 | tf_op jit(solution)/shard_map/all_to_all | solution.py:478
  31.7 0.0 copy-done.1
  31.7 0.2 crps.1
  31.9 10.9 %all_to_all.11.grads_ref = f32[8,48,128]{2,1,0:T(8,128)S(1)} all-to-all(f32[8,48,128]{2,1,0:T(8,128)S(1)} %crps.1), channel_id=1, replica_groups=mesh['member_0'=4,'member_1'=2,'lat_0'=2,'lat_1'=4,'lat_2'=2] {'member_0..., dimensions={0} | all-to-all | bytes 393216 | tf_op jit(solution)/shard_map/all_to_all | solution.py:482
  42.9 0.1 collective-permute-start.5
  43.0 1.9 %collective-permute-start.4 = (f32[176,128]{1,0:T(8,128)S(1)}, f32[176,128]{1,0:T(8,128)S(1)}, u32[]{:S(2)}, u32[]{:S(2)}) collective-permute-start(f32[176,128]{1,0:T(8,128)S(1)} %get-tuple-element.81.own_ref), channel_id=1, source_target_pairs={{0,15},{1,2},{2,1},{3,4},{4,3},{5,6},{6,5},{7,8},{8,7},{9,10},{10,... | collective-permute-start | bytes 270344 | tf_op jit(solution)/shard_map/ppermute | solution.py:487
  44.9 0.7 %collective-permute-start.6 = (f32[16,128]{1,0:T(8,128)S(1)}, f32[16,128]{1,0:T(8,128)S(1)}, u32[]{:S(2)}, u32[]{:S(2)}) collective-permute-start(f32[16,128]{1,0:T(8,128)S(1)} %get-tuple-element.96), channel_id=1, source_target_pairs={{0,5},{1,12},{2,7},{3,14},{4,9},{5,0},{6,11},{7,2},{8,13},{9,4},{1... | collective-permute-start | bytes 24584 | tf_op jit(solution)/shard_map/ppermute | solution.py:491
  45.6 0.4 collective-permute-start.7
  45.9 0.6 %slopes.1.slope_ref = f32[2,2,256,256]{3,2,1,0:T(8,128)S(1)} custom-call(f32[256,256]{1,0:T(8,128)S(1)} %get-tuple-element.82.refs_0_, f32[256,256]{1,0:T(8,128)S(1)} %get-tuple-element.83.refs_1_, f32[256,256]{1,0:T(8,128)S(1)} %get-tuple-element.84.refs_2_, f32[256,256]{1,0:T(8,128)S(1)} %get-tuple-element.85.refs_3_), custom_call_target="tpu_custom_call" | custom-call | tf_op jit(solution)/shard_map/slopes/pallas_call | solution.py:178
  46.6 0.0 collective-permute-done.5.beside_ref.rest_0_
  46.6 0.6 %backward_near.2 = (bf16[2,256,128]{2,1,0:T(8,128)(2,1)S(1)}, bf16[2,256,128]{2,1,0:T(8,128)(2,1)S(1)}) custom-call(f32[176,128]{1,0:T(8,128)S(1)} %get-tuple-element.81.own_ref, f32[176,128]{1,0:T(8,128)S(1)} %collective-permute-done.5.beside_ref.rest_0_, f32[2,2,256,256]{3,2,1,0:T(8,128)S(1)} %slopes.1.slope_ref, ...), custom_call_target="tpu_custom_call" | custom-call | tf_op jit(solution)/shard_map/backward_near/pallas_call | solution.py:364
  47.2 2.1 %collective-permute-done.4.beside_ref.rest_1_ = f32[176,128]{1,0:T(8,128)S(1)} collective-permute-done((f32[176,128]{1,0:T(8,128)S(1)}, f32[176,128]{1,0:T(8,128)S(1)}, u32[]{:S(2)}, u32[]{:S(2)}) %collective-permute-start.4) | collective-permute-done | bytes 90144 | tf_op jit(solution)/shard_map/ppermute | solution.py:487
  49.3 0.6 %backward_across.2 = (bf16[2,256,128]{2,1,0:T(8,128)(2,1)S(1)}, bf16[2,256,128]{2,1,0:T(8,128)(2,1)S(1)}) custom-call(f32[176,128]{1,0:T(8,128)S(1)} %get-tuple-element.81.own_ref, f32[176,128]{1,0:T(8,128)S(1)} %collective-permute-done.4.beside_ref.rest_1_, f32[2,2,256,256]{3,2,1,0:T(8,128)S(1)} %slopes.1.slope_ref, ...), custom_call_target="tpu_custom_call" | custom-call | tf_op jit(solution)/shard_map/backward_across/pallas_call | solution.py:364
  49.9 0.0 collective-permute-done.6.rest_2_
  49.9 0.0 collective-permute-done.7.rest_3_
  50.0 0.6 join.1
  50.5 0.1 collective-permute-start.9
  50.6 1.9 %collective-permute-start.8 = (f32[176,128]{1,0:T(8,128)S(1)}, f32[176,128]{1,0:T(8,128)S(1)}, u32[]{:S(2)}, u32[]{:S(2)}) collective-permute-start(f32[176,128]{1,0:T(8,128)S(1)} %get-tuple-element.97.own_ref), channel_id=1, source_target_pairs={{0,15},{1,2},{2,1},{3,4},{4,3},{5,6},{6,5},{7,8},{8,7},{9,10},{10,... | collective-permute-start | bytes 270344 | tf_op jit(solution)/shard_map/ppermute | solution.py:499
  52.5 1.2 %collective-permute-start.10 = (f32[16,128]{1,0:T(8,128)S(1)}, f32[16,128]{1,0:T(8,128)S(1)}, u32[]{:S(2)}, u32[]{:S(2)}) collective-permute-start(f32[16,128]{1,0:T(8,128)S(1)} %get-tuple-element.105), channel_id=1, source_target_pairs={{0,8},{1,9},{2,10},{3,11},{4,12},{5,13},{6,14},{7,15},{8,0},{9,1},... | collective-permute-start | bytes 24584 | tf_op jit(solution)/shard_map/ppermute | solution.py:500
  53.7 0.0 collective-permute-done.9.beside_ref.rest_0_
  53.7 0.6 %backward_near.3 = (bf16[2,256,128]{2,1,0:T(8,128)(2,1)S(1)}, bf16[2,256,128]{2,1,0:T(8,128)(2,1)S(1)}) custom-call(f32[176,128]{1,0:T(8,128)S(1)} %get-tuple-element.97.own_ref, f32[176,128]{1,0:T(8,128)S(1)} %collective-permute-done.9.beside_ref.rest_0_, f32[2,2,256,256]{3,2,1,0:T(8,128)S(1)} %slopes.1.slope_ref, ...), custom_call_target="tpu_custom_call" | custom-call | tf_op jit(solution)/shard_map/backward_near/pallas_call | solution.py:364
  54.3 2.5 %collective-permute-done.8.beside_ref.rest_1_ = f32[176,128]{1,0:T(8,128)S(1)} collective-permute-done((f32[176,128]{1,0:T(8,128)S(1)}, f32[176,128]{1,0:T(8,128)S(1)}, u32[]{:S(2)}, u32[]{:S(2)}) %collective-permute-start.8) | collective-permute-done | bytes 90144 | tf_op jit(solution)/shard_map/ppermute | solution.py:499
  56.9 0.6 %backward_across.3 = (bf16[2,256,128]{2,1,0:T(8,128)(2,1)S(1)}, bf16[2,256,128]{2,1,0:T(8,128)(2,1)S(1)}) custom-call(f32[176,128]{1,0:T(8,128)S(1)} %get-tuple-element.97.own_ref, f32[176,128]{1,0:T(8,128)S(1)} %collective-permute-done.8.beside_ref.rest_1_, f32[2,2,256,256]{3,2,1,0:T(8,128)S(1)} %slopes.1.slope_ref, ...), custom_call_target="tpu_custom_call" | custom-call | tf_op jit(solution)/shard_map/backward_across/pallas_call | solution.py:364
  57.5 0.0 collective-permute-done.10.rest_2_
  57.5 1.2 %finish.1 = (f32[160,128]{1,0:T(8,128)}, f32[1,1]{1,0:T(1,128)}) custom-call(f32[176,128]{1,0:T(8,128)S(1)} %get-tuple-element.97.own_ref, bf16[2,256,128]{2,1,0:T(8,128)(2,1)S(1)} %get-tuple-element.100.close_hi, bf16[2,256,128]{2,1,0:T(8,128)(2,1)S(1)} %get-tuple-element.101.close_lo, bf16[2,256,128]{2,1,0:T(8,128)(2,1)S(1)} %get-tuple-element.103.far_hi, ...), custom_call_target="tpu_custom_call" | custom-call | tf_op jit(solution)/shard_map/finish/pallas_call | solution.py:433
  (1 shorter events, 0.0 us)
Async XLA Ops:
  0.6 6.2 %collective-permute-start.1 = (f32[2,80,128]{2,1,0:T(8,128)}, f32[2,80,128]{2,1,0:T(8,128)S(1)}, u32[]{:S(2)}, u32[]{:S(2)}) collective-permute-start(f32[2,80,128]{2,1,0:T(8,128)} %bitcast.8), channel_id=1, source_target_pairs={{0,1},{1,0},{2,3},{3,2},{4,5},{5,4},{6,7},{7,6},{8,9},{9,8},{10,11... | collective-permute-start | bytes 245768 | tf_op jit(solution)/shard_map/ppermute | solution.py:458
  0.7 6.8 %collective-permute-start = (f32[2,80,128]{2,1,0:T(8,128)}, f32[2,80,128]{2,1,0:T(8,128)S(1)}, u32[]{:S(2)}, u32[]{:S(2)}) collective-permute-start(f32[2,80,128]{2,1,0:T(8,128)} %bitcast.9), channel_id=1, source_target_pairs={{0,15},{1,2},{2,1},{3,4},{4,3},{5,6},{6,5},{7,8},{8,7},{9,10},{10,... | collective-permute-start | bytes 245768 | tf_op jit(solution)/shard_map/ppermute | solution.py:459
  5.0 1.8 %copy-start = (f32[1,2,80,128]{3,2,1,0:T(8,128)S(1)}, f32[1,2,80,128]{3,2,1,0:T(8,128)}, u32[]{:S(2)}) copy-start(f32[1,2,80,128]{3,2,1,0:T(8,128)} %param.6) | copy-start | bytes 245764
  8.8 3.9 %collective-permute-start.3 = (f32[2,80,128]{2,1,0:T(8,128)S(1)}, f32[2,80,128]{2,1,0:T(8,128)S(1)}, u32[]{:S(2)}, u32[]{:S(2)}) collective-permute-start(f32[2,80,128]{2,1,0:T(8,128)S(1)} %move.2.own_ref.field_ref), channel_id=1, source_target_pairs={{0,1},{1,0},{2,3},{3,2},{4,5},{5,4},{6,7},{7,6},{8,9},{9,8},{10,11... | collective-permute-start | bytes 245768 | tf_op jit(solution)/shard_map/ppermute | solution.py:467
  8.9 6.1 %collective-permute-start.2 = (f32[2,80,128]{2,1,0:T(8,128)S(1)}, f32[2,80,128]{2,1,0:T(8,128)S(1)}, u32[]{:S(2)}, u32[]{:S(2)}) collective-permute-start(f32[2,80,128]{2,1,0:T(8,128)S(1)} %move.2.own_ref.field_ref), channel_id=1, source_target_pairs={{0,15},{1,2},{2,1},{3,4},{4,3},{5,6},{6,5},{7,8},{8,7},{9,10},{10,... | collective-permute-start | bytes 245768 | tf_op jit(solution)/shard_map/ppermute | solution.py:468
  16.2 15.5 %copy-start.1 = (f32[2,2,80,128]{3,2,1,0:T(8,128)S(1)}, f32[2,2,80,128]{3,2,1,0:T(8,128)}, u32[]{:S(2)}) copy-start(f32[2,2,80,128]{3,2,1,0:T(8,128)} %param.7) | copy-start | bytes 491524
  42.9 3.7 %collective-permute-start.5 = (f32[176,128]{1,0:T(8,128)S(1)}, f32[176,128]{1,0:T(8,128)S(1)}, u32[]{:S(2)}, u32[]{:S(2)}) collective-permute-start(f32[176,128]{1,0:T(8,128)S(1)} %get-tuple-element.81.own_ref), channel_id=1, source_target_pairs={{0,1},{1,0},{2,3},{3,2},{4,5},{5,4},{6,7},{7,6},{8,9},{9,8},{10,11... | collective-permute-start | bytes 270344 | tf_op jit(solution)/shard_map/ppermute | solution.py:486
  43.0 6.3 %collective-permute-start.4 = (f32[176,128]{1,0:T(8,128)S(1)}, f32[176,128]{1,0:T(8,128)S(1)}, u32[]{:S(2)}, u32[]{:S(2)}) collective-permute-start(f32[176,128]{1,0:T(8,128)S(1)} %get-tuple-element.81.own_ref), channel_id=1, source_target_pairs={{0,15},{1,2},{2,1},{3,4},{4,3},{5,6},{6,5},{7,8},{8,7},{9,10},{10,... | collective-permute-start | bytes 270344 | tf_op jit(solution)/shard_map/ppermute | solution.py:487
  44.9 5.1 %collective-permute-start.6 = (f32[16,128]{1,0:T(8,128)S(1)}, f32[16,128]{1,0:T(8,128)S(1)}, u32[]{:S(2)}, u32[]{:S(2)}) collective-permute-start(f32[16,128]{1,0:T(8,128)S(1)} %get-tuple-element.96), channel_id=1, source_target_pairs={{0,5},{1,12},{2,7},{3,14},{4,9},{5,0},{6,11},{7,2},{8,13},{9,4},{1... | collective-permute-start | bytes 24584 | tf_op jit(solution)/shard_map/ppermute | solution.py:491
  45.6 4.4 %collective-permute-start.7 = (f32[16,128]{1,0:T(8,128)S(1)}, f32[16,128]{1,0:T(8,128)S(1)}, u32[]{:S(2)}, u32[]{:S(2)}) collective-permute-start(f32[16,128]{1,0:T(8,128)S(1)} %get-tuple-element.96), channel_id=1, source_target_pairs={{0,11},{1,6},{2,13},{3,8},{4,15},{5,10},{6,1},{7,12},{8,3},{9,14},... | collective-permute-start | bytes 24584 | tf_op jit(solution)/shard_map/ppermute | solution.py:491
  50.5 3.2 %collective-permute-start.9 = (f32[176,128]{1,0:T(8,128)S(1)}, f32[176,128]{1,0:T(8,128)S(1)}, u32[]{:S(2)}, u32[]{:S(2)}) collective-permute-start(f32[176,128]{1,0:T(8,128)S(1)} %get-tuple-element.97.own_ref), channel_id=1, source_target_pairs={{0,1},{1,0},{2,3},{3,2},{4,5},{5,4},{6,7},{7,6},{8,9},{9,8},{10,11... | collective-permute-start | bytes 270344 | tf_op jit(solution)/shard_map/ppermute | solution.py:498
  50.6 6.2 %collective-permute-start.8 = (f32[176,128]{1,0:T(8,128)S(1)}, f32[176,128]{1,0:T(8,128)S(1)}, u32[]{:S(2)}, u32[]{:S(2)}) collective-permute-start(f32[176,128]{1,0:T(8,128)S(1)} %get-tuple-element.97.own_ref), channel_id=1, source_target_pairs={{0,15},{1,2},{2,1},{3,4},{4,3},{5,6},{6,5},{7,8},{8,7},{9,10},{10,... | collective-permute-start | bytes 270344 | tf_op jit(solution)/shard_map/ppermute | solution.py:499
  52.5 5.0 %collective-permute-start.10 = (f32[16,128]{1,0:T(8,128)S(1)}, f32[16,128]{1,0:T(8,128)S(1)}, u32[]{:S(2)}, u32[]{:S(2)}) collective-permute-start(f32[16,128]{1,0:T(8,128)S(1)} %get-tuple-element.105), channel_id=1, source_target_pairs={{0,8},{1,9},{2,10},{3,11},{4,12},{5,13},{6,14},{7,15},{8,0},{9,1},... | collective-permute-start | bytes 24584 | tf_op jit(solution)/shard_map/ppermute | solution.py:500
